TPU v7x, 32 devices: a whole 2x2x4 slice. The times are simulated.
32 devices in a mesh: blk: 2 (over y), tm: 4 (over z), fsdp: 4 (over x, core).
Axes of the slice: x: 2, y: 2, z: 4, core: 2. Of those that a mesh axis runs over, the one named last changes fastest.
Arguments:
- features: bfloat16 [4, 4, 320, 512], P('fsdp', 'tm', 'blk'), may hold values from -6 to 6
- neighbours: int32 [320, 8], P('blk'), may hold values from 0 to 319, as said below
- conv_taps: float32 [9, 512], replicated, may hold values from -3 to 3
- norm_gain: float32 [512], replicated, may hold values from 0.25 to 1.75
- qkv_weight: bfloat16 [512, 1536], P('fsdp'), as said below
- out_weight: bfloat16 [512, 512], P('fsdp'), may hold values from -0.25 to 0.25
- cotangent: bfloat16 [4, 4, 320, 512], P('fsdp', 'tm', 'blk'), may hold values from -0.083496094 to 0.083496094
Outputs:
- weight_grads: float32 [1048576], P(('blk', 'tm', 'fsdp'))
Inputs may be any that keep to these rules, and one draw needn't show every extreme that they name: `neighbours`: row p holds p - 1, p + 1, three neighbouring pixels near p - 128 and three near p + 128, clipped to the window; every entry lies within 130 of p, and one lies exactly 130 away. `qkv_weight`: projection weights of order 512 ** -0.5 per entry.
All inputs are finite; a program needn't handle non-finite values.
Results may differ from a plain program's by a relative error of at most 0.0086.
Values may be sent and summed in bfloat16 or wider, within the bound.
No kernel may reach another device: no remote copies, remote signals or barrier semaphores. Data moves between devices by JAX's collectives and lax.ppermute only.
A program may use at most 64 MiB of HBM per device.

v0:
```python
import jax
import jax.numpy as jnp
from jax import lax
from jax.experimental import pallas as pl
from jax.experimental.pallas import tpu as pltpu
from jax.sharding import PartitionSpec as P


HEADS = 8
HALO = 130
VMEM = pltpu.MemorySpace.VMEM


def swap(values, axis, mask):
    return lax.ppermute(values, axis, [(i, i ^ mask) for i in range(lax.axis_size(axis))])


def pick(values, index, dim=0):
    return lax.dynamic_index_in_dim(values, index, dim, keepdims=False)


def place():
    t, f = lax.axis_index("tm"), lax.axis_index("fsdp")
    return lax.axis_index("blk"), t, t >> 1, t & 1, f >> 1, f & 1


def start_all(copies):
    for copy in copies:
        copy.start()


def prep_kernel(up_ref, qkv_ref, out_w_ref, mine_ref, other_ref, cut_ref, sems):
    _, _, zp, zh, _, _ = place()
    half = mine_ref.shape[0]
    width = out_w_ref.shape[1] // 2
    rows = lambda h: up_ref.at[pl.ds(pl.multiple_of(h * half, 16), half)]
    copies = [
        pltpu.make_async_copy(rows(zp), mine_ref, sems.at[0]),
        pltpu.make_async_copy(rows(1 - zp), other_ref, sems.at[1]),
        pltpu.make_async_copy(out_w_ref, cut_ref.at[:, pl.ds(3 * width, 2 * width)], sems.at[2]),
    ]
    for m in range(3):
        start = pl.multiple_of((2 * m + zh) * width, 128)
        copies.append(
            pltpu.make_async_copy(
                qkv_ref.at[:, pl.ds(start, width)],
                cut_ref.at[:, pl.ds(m * width, width)],
                sems.at[3 + m],
            )
        )
    start_all(copies)
    for copy in copies:
        copy.wait()


def conv_kernel(
    near_hbm, own_hbm, band_hbm, taps_hbm, gain_hbm, mine_ref, other_ref,
    near_ref, table_ref, taps_ref, gain_ref, sems,
):
    y, _, zp, _, _, _ = place()
    pixels, _ = own_hbm.shape
    half = pixels // 2
    pairs = [
        (near_hbm, near_ref),
        (taps_hbm, taps_ref),
        (gain_hbm, gain_ref),
        (own_hbm, table_ref.at[pl.ds(0, pixels)]),
        (band_hbm, table_ref.at[pl.ds(pixels, pixels)]),
    ]
    copies = [pltpu.make_async_copy(a, b, sems.at[i]) for i, (a, b) in enumerate(pairs)]
    start_all(copies)
    copies[0].wait()
    near = near_ref[...].T
    neighbours = near.shape[1]
    local = near - y * pixels
    local = jnp.where(local < 0, local + 2 * pixels, local)
    slots = lax.broadcasted_iota(jnp.int32, (pixels, 2 * pixels), 1)
    chosen = jnp.concatenate(
        [
            jnp.where(local[:, k : k + 1] == slots, 1.0, 0.0).astype(jnp.bfloat16)
            for k in range(neighbours)
        ],
        axis=0,
    )
    for copy in copies[1:]:
        copy.wait()
    gathered = jnp.dot(chosen, table_ref[...], preferred_element_type=jnp.float32)
    own = table_ref[:pixels, :].astype(jnp.float32)
    spatial = taps_ref[0:1, :] * own
    for k in range(neighbours):
        spatial = spatial + taps_ref[k + 1 : k + 2, :] * gathered[k * pixels : (k + 1) * pixels]
    hidden = (own + spatial).astype(jnp.bfloat16).astype(jnp.float32)
    inverse = lax.rsqrt(jnp.mean(hidden * hidden, axis=-1, keepdims=True) + 1e-05)
    normed = (hidden * inverse * gain_ref[...]).astype(jnp.bfloat16)
    low, high = normed[:half], normed[half:]

    @pl.when(zp == 0)
    def _():
        mine_ref[...] = low
        other_ref[...] = high

    @pl.when(zp == 1)
    def _():
        mine_ref[...] = high
        other_ref[...] = low


def block_kernel(*refs):
    frames = 4
    sources, refs = refs[: 3 * frames], refs[3 * frames :]
    keep_ref, send_ref, n_ref, u_ref, qkv_ref, out_w_ref, sums_ref, out_sums_ref, sems = refs
    _, t, _, zh, x, core = place()
    pixels, channels = sources[0].shape
    width, depth = out_w_ref.shape[0], channels // HEADS
    rows = sources[-1].shape[0]
    up_copies, row_copies, qkv_copies = [], [], []
    for k in range(frames):
        row_copies.append(pltpu.make_async_copy(sources[k], n_ref.at[t ^ k], sems.at[k]))
        up_copies.append(
            pltpu.make_async_copy(sources[frames + k], u_ref.at[t ^ k], sems.at[frames + k])
        )
    shards = sources[2 * frames :]
    for k, shard in enumerate(shards):
        f = (2 * x + core) ^ (2 * (k & 1) + (k >> 1))
        qkv_copies.append(
            pltpu.make_async_copy(
                shard.at[:, pl.ds(0, 3 * width)],
                qkv_ref.at[pl.ds(pl.multiple_of(f * rows, 128), rows)],
                sems.at[2 * frames + k],
            )
        )

    def out_copy(shard, k):
        start = pl.multiple_of((core ^ k) * rows, 128)
        return pltpu.make_async_copy(
            shard.at[:, pl.ds(3 * width, channels)],
            out_w_ref.at[pl.ds(start, rows)],
            sems.at[3 * frames + k],
        )

    start_all(row_copies + qkv_copies + up_copies)
    for k in range(2):

        @pl.when(x == zh)
        def _(k=k):
            out_copy(shards[2 * k], k).start()

        @pl.when(x != zh)
        def _(k=k):
            out_copy(shards[2 * k + 1], k).start()

    for copy in row_copies + qkv_copies:
        copy.wait()
    normed = n_ref[...].reshape(frames * pixels, channels)
    qkv = jnp.dot(normed, qkv_ref[...], preferred_element_type=jnp.float32).astype(jnp.bfloat16)
    for copy in up_copies + [out_copy(shards[2 * k], k) for k in range(2)]:
        copy.wait()
    upstream = u_ref[...].reshape(frames * pixels, channels)
    grads = lax.dot_general(
        upstream, out_w_ref[...], (((1,), (1,)), ((), ())), preferred_element_type=jnp.float32
    ).astype(jnp.bfloat16)

    def part(values, frame, third=0):
        rows = values[frame * pixels : (frame + 1) * pixels]
        return rows[:, third * width : (third + 1) * width].astype(jnp.float32)

    q = [part(qkv, i, 0) for i in range(frames)]
    k = [part(qkv, i, 1) for i in range(frames)]
    v = [part(qkv, i, 2) for i in range(frames)]
    g = [part(grads, i) for i in range(frames)]
    row_head = lax.broadcasted_iota(jnp.int32, (width, width), 0) // depth
    col_head = lax.broadcasted_iota(jnp.int32, (width, width), 1) // depth
    same = jnp.where(row_head == col_head, 1.0, 0.0).astype(jnp.bfloat16)

    def head_sums(products):
        stacked = jnp.concatenate(products, axis=0)
        high = stacked.astype(jnp.bfloat16)
        low = (stacked - high.astype(jnp.float32)).astype(jnp.bfloat16)
        total = jnp.dot(high, same, preferred_element_type=jnp.float32)
        total = total + jnp.dot(low, same, preferred_element_type=jnp.float32)
        return [total[i * pixels : (i + 1) * pixels] for i in range(len(products))]

    def rounded(values):
        return values.astype(jnp.bfloat16).astype(jnp.float32)

    attended, dq = [], []
    dk, dv = [None] * frames, [None] * frames

    def plus(total, term):
        return term if total is None else total + term

    for i in range(frames):
        scores = head_sums([q[i] * k[u] for u in range(i + 1)])
        scores = [s * 0.125 for s in scores]
        largest = scores[0]
        for s in scores[1:]:
            largest = jnp.maximum(largest, s)
        powers = [jnp.exp(s - largest) for s in scores]
        total = powers[0]
        for p in powers[1:]:
            total = total + p
        scale = 1.0 / total
        weights = [rounded(p * scale) for p in powers]
        dprob = head_sums([g[i] * v[u] for u in range(i + 1)])
        delta = weights[0] * dprob[0]
        for u in range(1, i + 1):
            delta = delta + weights[u] * dprob[u]
        seen, grad_q = None, None
        for u in range(i + 1):
            ds = rounded(weights[u] * (dprob[u] - delta) * 0.125)
            seen = plus(seen, weights[u] * v[u])
            grad_q = plus(grad_q, ds * k[u])
            dk[u] = plus(dk[u], ds * q[i])
            dv[u] = plus(dv[u], weights[u] * g[i])
        attended.append(seen.astype(jnp.bfloat16))
        dq.append(grad_q.astype(jnp.bfloat16))
    thirds = (dq, [d.astype(jnp.bfloat16) for d in dk], [d.astype(jnp.bfloat16) for d in dv])

    def over_rows(lhs, rhs):
        return lax.dot_general(
            lhs, rhs, (((0,), (0,)), ((), ())), preferred_element_type=jnp.float32
        )

    for m, pieces in enumerate(thirds):
        grad = over_rows(normed, jnp.concatenate(pieces, axis=0))
        for lane in range(0, width, 128):
            sums_ref[lane // 128, pl.ds(m, channels, stride=3), :] = grad[:, lane : lane + 128]
    out_sums_ref[...] = over_rows(jnp.concatenate(attended, axis=0), upstream)

    block = 64
    for x in range(2):
        for y in range(2):
            for zp in range(2):
                slot = (x * 2 + y) * 2 + zp
                for side, ref in ((core, keep_ref), (1 - core, send_ref)):
                    if y == 1 and zp == 1:
                        start = pl.multiple_of((2 * x + side) * block, block)
                        rows = out_sums_ref[pl.ds(start, block), :]
                        pieces = (rows[:, :width], rows[:, width:])
                    else:
                        pieces = []
                        for low in range(2):
                            index = y * 16 + (2 * zp + low) * 4 + 2 * x + side
                            start = pl.multiple_of(index * block, block)
                            pieces.append(
                                jnp.concatenate(
                                    [
                                        sums_ref[lane, pl.ds(start, block), :]
                                        for lane in range(width // 128)
                                    ],
                                    axis=1,
                                )
                            )
                    for low in range(2):
                        ref[slot, low * block : (low + 1) * block, :] = pieces[low].astype(ref.dtype)


def split_form(features, neighbours, conv_taps, norm_gain, qkv_weight, out_weight, cotangent):
    own = features[0, 0]
    pixels, channels = own.shape
    half, width, block = pixels // 2, channels // 2, channels // HEADS
    y, _, zp, zh, x, _ = place()
    narrow_type = jnp.bfloat16
    anywhere = pl.BlockSpec(memory_space=pl.ANY)
    in_vmem = pl.BlockSpec(memory_space=VMEM)
    piece = jax.ShapeDtypeStruct((half, channels), narrow_type)

    band = swap(own, "blk", 1)
    up_mine, up_other, cut = pl.pallas_call(
        prep_kernel,
        out_shape=(
            piece,
            piece,
            jax.ShapeDtypeStruct((qkv_weight.shape[0], 3 * width + channels), narrow_type),
        ),
        in_specs=[anywhere] * 3,
        out_specs=(in_vmem,) * 3,
        scratch_shapes=[pltpu.SemaphoreType.DMA((6,))],
        compiler_params=pltpu.CompilerParams(vmem_limit_bytes=4 << 20),
        name="prep",
    )(cotangent[0, 0], qkv_weight, out_weight)

    def spread(mine, other):
        far = swap(other, "tm", 3)
        middle = swap(other, "tm", 2)
        near = swap(mine, "tm", 1)
        return [mine, near, middle, far]

    ups = spread(up_mine, up_other)
    cut_x = swap(cut, "fsdp", 2)
    n_mine, n_other = pl.pallas_call(
        conv_kernel,
        out_shape=(piece, piece),
        in_specs=[anywhere] * 5,
        out_specs=(in_vmem,) * 2,
        scratch_shapes=[
            pltpu.VMEM((neighbours.shape[1], pixels), jnp.int32),
            pltpu.VMEM((2 * pixels, channels), narrow_type),
            pltpu.VMEM(conv_taps.shape, jnp.float32),
            pltpu.VMEM((1, channels), jnp.float32),
            pltpu.SemaphoreType.DMA((5,)),
        ],
        compiler_params=pltpu.CompilerParams(vmem_limit_bytes=16 << 20),
        name="conv",
    )(neighbours.T, own, band, conv_taps, norm_gain.reshape(1, channels))
    rows = spread(n_mine, n_other)
    cut_c = swap(cut, "fsdp", 1)
    cut_xc = swap(cut_x, "fsdp", 1)

    keep, send = pl.pallas_call(
        block_kernel,
        out_shape=(
            jax.ShapeDtypeStruct((8, 2 * block, width), jnp.float32),
            jax.ShapeDtypeStruct((8, 2 * block, width), narrow_type),
        ),
        in_specs=[anywhere] * 12,
        out_specs=(in_vmem, in_vmem),
        scratch_shapes=[
            pltpu.VMEM((4, half, channels), narrow_type),
            pltpu.VMEM((4, half, channels), narrow_type),
            pltpu.VMEM((channels, 3 * width), narrow_type),
            pltpu.VMEM((width, channels), narrow_type),
            pltpu.VMEM((width // 128, 3 * channels, 128), jnp.float32),
            pltpu.VMEM((width, channels), jnp.float32),
            pltpu.SemaphoreType.DMA((14,)),
        ],
        compiler_params=pltpu.CompilerParams(vmem_limit_bytes=32 << 20),
        name="attend",
    )(*rows, *ups, cut, cut_x, cut_c, cut_xc)

    def narrow(values):
        return values.astype(jnp.bfloat16)

    total = keep + swap(send, "fsdp", 1).astype(jnp.float32)
    total = total.reshape(2, 2, 2, 2 * block, width)
    first, second = total[..., : width // 2], total[..., width // 2 :]
    got_first = swap(narrow(pick(first, 1 - x, 0)), "fsdp", 2)
    got_second = swap(narrow(pick(second, 1 - y, 1)), "blk", 1)
    first = pick(first, x, 0) + got_first.astype(jnp.float32)
    second = pick(second, y, 1) + got_second.astype(jnp.float32)
    got_first = swap(narrow(pick(first, 1 - y, 0)), "blk", 1)
    got_second = swap(narrow(pick(second, 1 - x, 0)), "fsdp", 2)
    first = pick(first, y, 0) + got_first.astype(jnp.float32)
    second = pick(second, x, 0) + got_second.astype(jnp.float32)
    total = jnp.concatenate([first, second], axis=-1)
    total = pick(total, zp) + swap(narrow(pick(total, 1 - zp)), "tm", 2).astype(jnp.float32)
    total = total.reshape(2, block, width)
    mine = pick(total, zh)
    got = swap(pick(total, 1 - zh), "tm", 1)
    is_out = (y == 1) & (zp == 1)
    left = jnp.where(is_out, total[0], jnp.where(zh == 0, mine, got))
    right = jnp.where(is_out, total[1], jnp.where(zh == 0, got, mine))
    return jnp.concatenate([left, right], axis=1).reshape(-1)


def with_halo(cells, sides, width):
    for axis, dim in sides:
        count = lax.axis_size(axis)
        ends = count - 1
        head = lax.slice_in_dim(cells, 0, width, axis=dim)
        tail = lax.slice_in_dim(cells, cells.shape[dim] - width, cells.shape[dim], axis=dim)
        cells = jnp.concatenate(
            [
                lax.ppermute(tail, axis, [(i, (i + 1) % count) for i in range(ends)]),
                cells,
                lax.ppermute(head, axis, [((i + 1) % count, i) for i in range(ends)]),
            ],
            axis=dim,
        )
    return cells


def halved(partial, axis, bit):
    count = lax.axis_size(axis)
    mine = (lax.axis_index(axis) >> bit) & 1
    keep = lax.dynamic_index_in_dim(partial, mine, 0, keepdims=False)
    send = lax.dynamic_index_in_dim(partial, 1 - mine, 0, keepdims=False)
    got = lax.ppermute(send.astype(jnp.bfloat16), axis, [(i, i ^ (1 << bit)) for i in range(count)])
    return keep + got.astype(jnp.float32)


def scattered_sum(summands):
    counts = [lax.axis_size(axis) for axis in ("blk", "tm", "fsdp")]
    bits = [count.bit_length() - 1 for count in counts]
    order = [("fsdp", bit) for bit in range(bits[2])]
    order += [("blk", bit) for bit in range(bits[0])]
    order += [("tm", bit) for bit in range(bits[1])]
    labels = [(axis, bit) for axis, many in zip(("blk", "tm", "fsdp"), bits) for bit in reversed(range(many))]
    partial = summands.reshape((2,) * len(labels) + (-1, 128))
    for axis, bit in order:
        place = labels.index((axis, bit))
        labels.pop(place)
        partial = halved(jnp.moveaxis(partial, place, 0), axis, bit)
    return partial.reshape(-1)


def rounded(values):
    return lax.optimization_barrier(values.astype(jnp.bfloat16)).astype(jnp.float32)


def attend_all(qkv_rows, grad_rows):
    frames, pixels, width = qkv_rows.shape
    channels = width // 3

    def split_heads(block):
        return block.reshape(frames, pixels, HEADS, channels // HEADS).astype(jnp.float32)

    queries = split_heads(qkv_rows[:, :, :channels])
    keys_all = split_heads(qkv_rows[:, :, channels : 2 * channels])
    values = split_heads(qkv_rows[:, :, 2 * channels :])
    grads = split_heads(grad_rows)
    scores = jnp.einsum("tpeh,upeh->petu", queries, keys_all) * 0.125
    causal = jnp.arange(frames)[:, None] >= jnp.arange(frames)[None, :]
    masked = jnp.where(causal, scores, -1e30)
    largest = jnp.max(masked, axis=-1, keepdims=True)
    totals = jnp.sum(jnp.exp(masked - largest), axis=-1, keepdims=True)
    log_total = largest + jnp.log(totals)
    weights = rounded(jnp.exp(masked - log_total))
    attended = jnp.einsum("petu,upeh->tpeh", weights, values)
    dprob = jnp.einsum("tpeh,upeh->petu", grads, values)
    delta = jnp.sum(weights * dprob, axis=-1, keepdims=True)
    dscore = rounded(weights * (dprob - delta) * 0.125)
    grad_query = jnp.einsum("petu,upeh->tpeh", dscore, keys_all)
    grad_key = jnp.einsum("petu,tpeh->upeh", dscore, queries)
    grad_value = jnp.einsum("petu,tpeh->upeh", weights, grads)
    joined = jnp.concatenate(
        [part.reshape(frames, pixels, channels) for part in (grad_query, grad_key, grad_value)],
        axis=-1,
    )
    return (
        attended.reshape(frames, pixels, channels).astype(jnp.bfloat16),
        joined.astype(jnp.bfloat16),
    )


def general_form(features, neighbours, conv_taps, norm_gain, qkv_weight, out_weight, cotangent):
    inputs = features[0, 0]
    upstream = cotangent[0, 0]
    pixels, channels = inputs.shape
    padded = with_halo(inputs, (("blk", 0),), HALO)
    first_pixel = lax.axis_index("blk") * pixels
    local_rows = neighbours - first_pixel + HALO
    inputs_f = inputs.astype(jnp.float32)
    spatial = conv_taps[0] * inputs_f
    for column in range(8):
        spatial = spatial + conv_taps[column + 1] * jnp.take(
            padded, local_rows[:, column], axis=0
        ).astype(jnp.float32)
    hidden_f = rounded(inputs_f + spatial)
    inverse = lax.rsqrt(jnp.mean(hidden_f * hidden_f, axis=-1, keepdims=True) + 1e-05)
    normed = (hidden_f * inverse * norm_gain).astype(jnp.bfloat16)
    full_qkv, full_out = (
        lax.all_gather(qkv_weight, "fsdp", axis=0, tiled=True),
        lax.all_gather(out_weight, "fsdp", axis=0, tiled=True),
    )
    att_grads = jnp.dot(upstream, full_out.T, preferred_element_type=jnp.float32).astype(
        jnp.bfloat16
    )
    swap_normed, swap_grads, swap_upstream = (
        lax.all_to_all(normed[None], "tm", split_axis=1, concat_axis=0, tiled=True),
        lax.all_to_all(att_grads[None], "tm", split_axis=1, concat_axis=0, tiled=True),
        lax.all_to_all(upstream[None], "tm", split_axis=1, concat_axis=0, tiled=True),
    )
    frames = swap_normed.shape[0]
    few_pixels = swap_normed.shape[1]
    flat_normed = swap_normed.reshape(-1, channels)
    qkv_rows = jnp.dot(flat_normed, full_qkv, preferred_element_type=jnp.float32).astype(
        jnp.bfloat16
    )
    qkv_rows = qkv_rows.reshape(frames, few_pixels, 3 * channels)
    attended_x, dqkv_x = attend_all(qkv_rows, swap_grads)
    grad_in = jnp.einsum(
        "pc,pd->cd",
        flat_normed,
        dqkv_x.reshape(-1, 3 * channels),
        preferred_element_type=jnp.float32,
    )
    grad_out = jnp.einsum(
        "pc,pd->cd",
        attended_x.reshape(-1, channels),
        swap_upstream.reshape(-1, channels),
        preferred_element_type=jnp.float32,
    )
    summands = jnp.concatenate([grad_in.reshape(-1), grad_out.reshape(-1)])
    return scattered_sum(summands)


def solution(mesh):
    sizes = mesh.shape

    def per_device(*arrays):
        pixels, channels = arrays[0].shape[-2:]
        devices = sizes["blk"] * sizes["tm"] * sizes["fsdp"]
        fits = (
            sizes["blk"] == 2
            and sizes["tm"] == sizes["fsdp"] == arrays[0].shape[0] * 4
            and devices == 4 * HEADS
            and pixels >= HALO
            and pixels % 32 == 0
            and channels == 64 * HEADS
        )
        if not fits:
            return general_form(*arrays)
        return split_form(*arrays)

    return jax.shard_map(
        per_device,
        mesh=mesh,
        in_specs=(
            P("fsdp", "tm", "blk", None),
            P("blk", None),
            P(),
            P(),
            P("fsdp", None),
            P("fsdp", None),
            P("fsdp", "tm", "blk", None),
        ),
        out_specs=P(("blk", "tm", "fsdp")),
        check_vma=False,
    )
```

profile of v0, /device:TPU:0, one launch (start us, length us, event | category | flops | bytes accessed | tf_op | source)
XLA Modules:
  0.0 61.0 jit_solution(7138360539702638297)
XLA Ops:
  0.0 1.0 %copy-done = bf16[128,1536]{1,0:T(8,128)(2,1)S(1)} copy-done((bf16[128,1536]{1,0:T(8,128)(2,1)S(1)}, bf16[128,1536]{1,0:T(8,128)(2,1)}, u32[]{:S(2)}) %copy-start) | copy-done | bytes 393240
  1.0 0.9 %copy-done.2 = bf16[1,1,160,512]{3,2,1,0:T(8,128)(2,1)S(1)} copy-done((bf16[1,1,160,512]{3,2,1,0:T(8,128)(2,1)S(1)}, bf16[1,1,160,512]{3,2,1,0:T(8,128)(2,1)}, u32[]{:S(2)}) %copy-start.2) | copy-done | bytes 163864
  1.9 0.9 %copy-done.3 = bf16[128,512]{1,0:T(8,128)(2,1)S(1)} copy-done((bf16[128,512]{1,0:T(8,128)(2,1)S(1)}, bf16[128,512]{1,0:T(8,128)(2,1)}, u32[]{:S(2)}) %copy-start.3) | copy-done | bytes 131096
  2.8 0.3 prep.1
  3.1 0.0 copy-start.5
  3.1 3.0 %collective-permute-start.7 = (bf16[128,1280]{1,0:T(8,128)(2,1)S(1)}, bf16[128,1280]{1,0:T(8,128)(2,1)S(1)}, u32[]{:S(2)}, u32[]{:S(2)}) collective-permute-start(bf16[128,1280]{1,0:T(8,128)(2,1)S(1)} %get-tuple-element.16.refs_8_), channel_id=1, source_target_pairs={{0,2},{1,3},{2,0},{3,1},{4,6},{5,7},{6,4},{7,5},{8,10},{9,11},{10,... | collective-permute-start | bytes 983048 | tf_op jit(solution)/shard_map/ppermute | solution.py:15
  6.2 1.5 %collective-permute-start = (bf16[160,512]{1,0:T(8,128)(2,1)S(1)}, bf16[160,512]{1,0:T(8,128)(2,1)S(1)}, u32[]{:S(2)}, u32[]{:S(2)}) collective-permute-start(bf16[160,512]{1,0:T(8,128)(2,1)S(1)} %bitcast.40), channel_id=1, source_target_pairs={{0,16},{16,0},{1,17},{17,1},{2,18},{18,2},{3,19},{19,3},{4,20},{20... | collective-permute-start | bytes 491528 | tf_op jit(solution)/shard_map/ppermute | solution.py:15
  7.7 6.2 %collective-permute-done.7.refs_9_ = bf16[128,1280]{1,0:T(8,128)(2,1)S(1)} collective-permute-done((bf16[128,1280]{1,0:T(8,128)(2,1)S(1)}, bf16[128,1280]{1,0:T(8,128)(2,1)S(1)}, u32[]{:S(2)}, u32[]{:S(2)}) %collective-permute-start.7) | collective-permute-done | bytes 327712 | tf_op jit(solution)/shard_map/ppermute | solution.py:15
  13.9 1.8 %collective-permute-start.4 = (bf16[80,512]{1,0:T(8,128)(2,1)S(1)}, bf16[80,512]{1,0:T(8,128)(2,1)S(1)}, u32[]{:S(2)}, u32[]{:S(2)}) collective-permute-start(bf16[80,512]{1,0:T(8,128)(2,1)S(1)} %get-tuple-element.14.refs_4_), channel_id=1, source_target_pairs={{0,4},{4,0},{8,12},{12,8},{1,5},{5,1},{9,13},{13,9},{2,6},{6,2},{1... | collective-permute-start | bytes 245768 | tf_op jit(solution)/shard_map/ppermute | solution.py:15
  15.7 2.6 %collective-permute-start.5 = (bf16[80,512]{1,0:T(8,128)(2,1)S(1)}, bf16[80,512]{1,0:T(8,128)(2,1)S(1)}, u32[]{:S(2)}, u32[]{:S(2)}) collective-permute-start(bf16[80,512]{1,0:T(8,128)(2,1)S(1)} %get-tuple-element.15), channel_id=1, source_target_pairs={{0,8},{4,12},{8,0},{12,4},{1,9},{5,13},{9,1},{13,5},{2,10},{6,14},... | collective-permute-start | bytes 245768 | tf_op jit(solution)/shard_map/ppermute | solution.py:15
  18.3 1.9 %conv.1 = (bf16[80,512]{1,0:T(8,128)(2,1)S(1)}, bf16[80,512]{1,0:T(8,128)(2,1)S(1)}) custom-call(s32[8,160]{1,0:T(8,128)S(1)} %bitcast.43, bf16[160,512]{1,0:T(8,128)(2,1)S(1)} %bitcast.41, bf16[160,512]{1,0:T(8,128)(2,1)S(1)} %collective-permute-done.band_hbm, f32[9,512]{1,0:T(8,128)S(1)} %copy-done.4, f32[1,512]{1,0:T(1,128)S(1)} %bitcast.44), custom_call_target="tpu_custom_call" | custom-call | tf_op jit(solution)/shard_map/conv/pallas_call | solution.py:291
  20.3 0.9 %collective-permute-start.1 = (bf16[80,512]{1,0:T(8,128)(2,1)S(1)}, bf16[80,512]{1,0:T(8,128)(2,1)S(1)}, u32[]{:S(2)}, u32[]{:S(2)}) collective-permute-start(bf16[80,512]{1,0:T(8,128)(2,1)S(1)} %get-tuple-element.12.refs_0_), channel_id=1, source_target_pairs={{0,4},{4,0},{8,12},{12,8},{1,5},{5,1},{9,13},{13,9},{2,6},{6,2},{1... | collective-permute-start | bytes 245768 | tf_op jit(solution)/shard_map/ppermute | solution.py:15
  21.2 4.0 %collective-permute-done.5.refs_6_ = bf16[80,512]{1,0:T(8,128)(2,1)S(1)} collective-permute-done((bf16[80,512]{1,0:T(8,128)(2,1)S(1)}, bf16[80,512]{1,0:T(8,128)(2,1)S(1)}, u32[]{:S(2)}, u32[]{:S(2)}) %collective-permute-start.5) | collective-permute-done | bytes 81952 | tf_op jit(solution)/shard_map/ppermute | solution.py:15
  25.3 2.7 %collective-permute-start.3 = (bf16[80,512]{1,0:T(8,128)(2,1)S(1)}, bf16[80,512]{1,0:T(8,128)(2,1)S(1)}, u32[]{:S(2)}, u32[]{:S(2)}) collective-permute-start(bf16[80,512]{1,0:T(8,128)(2,1)S(1)} %get-tuple-element.13), channel_id=1, source_target_pairs={{0,12},{4,8},{8,4},{12,0},{1,13},{5,9},{9,5},{13,1},{2,14},{6,10},... | collective-permute-start | bytes 245768 | tf_op jit(solution)/shard_map/ppermute | solution.py:15
  28.0 4.7 %collective-permute-done.2.refs_2_ = bf16[80,512]{1,0:T(8,128)(2,1)S(1)} collective-permute-done((bf16[80,512]{1,0:T(8,128)(2,1)S(1)}, bf16[80,512]{1,0:T(8,128)(2,1)S(1)}, u32[]{:S(2)}, u32[]{:S(2)}) %collective-permute-start.2) | collective-permute-done | bytes 81952 | tf_op jit(solution)/shard_map/ppermute | solution.py:15
  32.6 3.6 %attend.1 = (f32[8,128,256]{2,1,0:T(8,128)S(1)}, bf16[8,128,256]{2,1,0:T(8,128)(2,1)S(1)}) custom-call(bf16[80,512]{1,0:T(8,128)(2,1)S(1)} %get-tuple-element.12.refs_0_, bf16[80,512]{1,0:T(8,128)(2,1)S(1)} %collective-permute-done.1.refs_1_, bf16[80,512]{1,0:T(8,128)(2,1)S(1)} %collective-permute-done.2.refs_2_, ...), custom_call_target="tpu_custom_call" | custom-call | tf_op jit(solution)/shard_map/attend/pallas_call | solution.py:310
  36.3 0.1 collective-permute-start.10
  36.3 1.9 %collective-permute-done.10 = bf16[8,128,256]{2,1,0:T(8,128)(2,1)S(1)} collective-permute-done((bf16[8,128,256]{2,1,0:T(8,128)(2,1)S(1)}, bf16[8,128,256]{2,1,0:T(8,128)(2,1)S(1)}, u32[]{:S(2)}, u32[]{:S(2)}) %collective-permute-start.10) | collective-permute-done | bytes 524320 | tf_op jit(solution)/shard_map/ppermute | solution.py:15
  38.2 0.1 convert_add_fusion
  38.4 0.1 fusion.10
  38.5 1.6 %collective-permute-start.13 = (bf16[2,2,128,128]{3,2,1,0:T(8,128)(2,1)S(1)}, bf16[2,2,128,128]{3,2,1,0:T(8,128)(2,1)S(1)}, u32[]{:S(2)}, u32[]{:S(2)}) collective-permute-start(bf16[2,2,128,128]{3,2,1,0:T(8,128)(2,1)S(1)} %fusion.1), channel_id=1, source_target_pairs={{0,16},{16,0},{1,17},{17,1},{2,18},{18,2},{3,19},{19,3},{4,20},{20... | collective-permute-start | bytes 393224 | tf_op jit(solution)/shard_map/ppermute | solution.py:15
  40.1 1.6 %collective-permute-start.11 = (bf16[2,2,128,128]{3,2,1,0:T(8,128)(2,1)S(1)}, bf16[2,2,128,128]{3,2,1,0:T(8,128)(2,1)S(1)}, u32[]{:S(2)}, u32[]{:S(2)}) collective-permute-start(bf16[2,2,128,128]{3,2,1,0:T(8,128)(2,1)S(1)} %fusion), channel_id=1, source_target_pairs={{0,2},{1,3},{2,0},{3,1},{4,6},{5,7},{6,4},{7,5},{8,10},{9,11},{10,... | collective-permute-start | bytes 393224 | tf_op jit(solution)/shard_map/ppermute | solution.py:15
  41.7 2.4 %collective-permute-done.13 = bf16[2,2,128,128]{3,2,1,0:T(8,128)(2,1)S(1)} collective-permute-done((bf16[2,2,128,128]{3,2,1,0:T(8,128)(2,1)S(1)}, bf16[2,2,128,128]{3,2,1,0:T(8,128)(2,1)S(1)}, u32[]{:S(2)}, u32[]{:S(2)}) %collective-permute-start.13) | collective-permute-done | bytes 131104 | tf_op jit(solution)/shard_map/ppermute | solution.py:15
  44.2 1.6 %collective-permute-start.14 = (bf16[2,128,128]{2,1,0:T(8,128)(2,1)S(1)}, bf16[2,128,128]{2,1,0:T(8,128)(2,1)S(1)}, u32[]{:S(2)}, u32[]{:S(2)}) collective-permute-start(bf16[2,128,128]{2,1,0:T(8,128)(2,1)S(1)} %fusion.8), channel_id=1, source_target_pairs={{0,2},{1,3},{2,0},{3,1},{4,6},{5,7},{6,4},{7,5},{8,10},{9,11},{10,... | collective-permute-start | bytes 196616 | tf_op jit(solution)/shard_map/ppermute | solution.py:15
  45.8 1.6 %collective-permute-start.12 = (bf16[2,128,128]{2,1,0:T(8,128)(2,1)S(1)}, bf16[2,128,128]{2,1,0:T(8,128)(2,1)S(1)}, u32[]{:S(2)}, u32[]{:S(2)}) collective-permute-start(bf16[2,128,128]{2,1,0:T(8,128)(2,1)S(1)} %fusion.7), channel_id=1, source_target_pairs={{0,16},{16,0},{1,17},{17,1},{2,18},{18,2},{3,19},{19,3},{4,20},{20... | collective-permute-start | bytes 196616 | tf_op jit(solution)/shard_map/ppermute | solution.py:15
  47.4 1.1 %collective-permute-done.14 = bf16[2,128,128]{2,1,0:T(8,128)(2,1)S(1)} collective-permute-done((bf16[2,128,128]{2,1,0:T(8,128)(2,1)S(1)}, bf16[2,128,128]{2,1,0:T(8,128)(2,1)S(1)}, u32[]{:S(2)}, u32[]{:S(2)}) %collective-permute-start.14) | collective-permute-done | bytes 65568 | tf_op jit(solution)/shard_map/ppermute | solution.py:15
  48.5 1.6 %collective-permute-done.12 = bf16[2,128,128]{2,1,0:T(8,128)(2,1)S(1)} collective-permute-done((bf16[2,128,128]{2,1,0:T(8,128)(2,1)S(1)}, bf16[2,128,128]{2,1,0:T(8,128)(2,1)S(1)}, u32[]{:S(2)}, u32[]{:S(2)}) %collective-permute-start.12) | collective-permute-done | bytes 65568 | tf_op jit(solution)/shard_map/ppermute | solution.py:15
  50.2 3.3 %collective-permute-start.15 = (bf16[128,256]{1,0:T(8,128)(2,1)S(1)}, bf16[128,256]{1,0:T(8,128)(2,1)S(1)}, u32[]{:S(2)}, u32[]{:S(2)}) collective-permute-start(bf16[128,256]{1,0:T(8,128)(2,1)S(1)} %fusion.9), channel_id=1, source_target_pairs={{0,8},{4,12},{8,0},{12,4},{1,9},{5,13},{9,1},{13,5},{2,10},{6,14},... | collective-permute-start | bytes 196616 | tf_op jit(solution)/shard_map/ppermute | solution.py:15
  53.4 2.4 %collective-permute-done.15 = bf16[128,256]{1,0:T(8,128)(2,1)S(1)} collective-permute-done((bf16[128,256]{1,0:T(8,128)(2,1)S(1)}, bf16[128,256]{1,0:T(8,128)(2,1)S(1)}, u32[]{:S(2)}, u32[]{:S(2)}) %collective-permute-start.15) | collective-permute-done | bytes 65568 | tf_op jit(solution)/shard_map/ppermute | solution.py:15
  55.9 1.3 %collective-permute-start.16 = (f32[64,256]{1,0:T(8,128)S(1)}, f32[64,256]{1,0:T(8,128)S(1)}, u32[]{:S(2)}, u32[]{:S(2)}) collective-permute-start(f32[64,256]{1,0:T(8,128)S(1)} %dynamic-slice_bitcast_fusion), channel_id=1, source_target_pairs={{0,4},{4,0},{8,12},{12,8},{1,5},{5,1},{9,13},{13,9},{2,6},{6,2},{1... | collective-permute-start | bytes 196616 | tf_op jit(solution)/shard_map/ppermute | solution.py:15
  57.3 3.0 %collective-permute-done.16 = f32[64,256]{1,0:T(8,128)S(1)} collective-permute-done((f32[64,256]{1,0:T(8,128)S(1)}, f32[64,256]{1,0:T(8,128)S(1)}, u32[]{:S(2)}, u32[]{:S(2)}) %collective-permute-start.16) | collective-permute-done | bytes 65568 | tf_op jit(solution)/shard_map/ppermute | solution.py:15
  60.3 0.7 %copy.8 = f32[8,4,8,128]{3,1,2,0:T(4,128)} copy(f32[8,4,8,128]{3,2,1,0:T(8,128)S(1)} %maximum_bitcast_fusion) | data formatting | bytes 262144
  (35 shorter events, 0.3 us)
Async XLA Ops:
  0.0 1.0 %copy-start = (bf16[128,1536]{1,0:T(8,128)(2,1)S(1)}, bf16[128,1536]{1,0:T(8,128)(2,1)}, u32[]{:S(2)}) copy-start(bf16[128,1536]{1,0:T(8,128)(2,1)} %qkv_ref.1) | copy-start | bytes 1179652
  1.0 0.9 %copy-start.2 = (bf16[1,1,160,512]{3,2,1,0:T(8,128)(2,1)S(1)}, bf16[1,1,160,512]{3,2,1,0:T(8,128)(2,1)}, u32[]{:S(2)}) copy-start(bf16[1,1,160,512]{3,2,1,0:T(8,128)(2,1)} %param.13) | copy-start | bytes 491524
  1.9 0.9 %copy-start.3 = (bf16[128,512]{1,0:T(8,128)(2,1)S(1)}, bf16[128,512]{1,0:T(8,128)(2,1)}, u32[]{:S(2)}) copy-start(bf16[128,512]{1,0:T(8,128)(2,1)} %out_w_ref.1) | copy-start | bytes 393220
  2.8 3.3 %copy-start.1 = (bf16[1,1,160,512]{3,2,1,0:T(8,128)(2,1)S(1)}, bf16[1,1,160,512]{3,2,1,0:T(8,128)(2,1)}, u32[]{:S(2)}) copy-start(bf16[1,1,160,512]{3,2,1,0:T(8,128)(2,1)} %param.7) | copy-start | bytes 491524
  2.8 15.5 %copy-start.4 = (f32[9,512]{1,0:T(8,128)S(1)}, f32[9,512]{1,0:T(8,128)}, u32[]{:S(2)}) copy-start(f32[9,512]{1,0:T(8,128)} %taps_hbm.1) | copy-start | bytes 55300
  3.1 15.2 %copy-start.5 = (s32[160,8]{0,1:T(8,128)S(1)}, s32[160,8]{0,1:T(8,128)}, u32[]{:S(2)}) copy-start(s32[160,8]{0,1:T(8,128)} %param.8) | copy-start | bytes 15364
  3.1 10.7 %collective-permute-start.7 = (bf16[128,1280]{1,0:T(8,128)(2,1)S(1)}, bf16[128,1280]{1,0:T(8,128)(2,1)S(1)}, u32[]{:S(2)}, u32[]{:S(2)}) collective-permute-start(bf16[128,1280]{1,0:T(8,128)(2,1)S(1)} %get-tuple-element.16.refs_8_), channel_id=1, source_target_pairs={{0,2},{1,3},{2,0},{3,1},{4,6},{5,7},{6,4},{7,5},{8,10},{9,11},{10,... | collective-permute-start | bytes 983048 | tf_op jit(solution)/shard_map/ppermute | solution.py:15
  6.2 12.1 %collective-permute-start = (bf16[160,512]{1,0:T(8,128)(2,1)S(1)}, bf16[160,512]{1,0:T(8,128)(2,1)S(1)}, u32[]{:S(2)}, u32[]{:S(2)}) collective-permute-start(bf16[160,512]{1,0:T(8,128)(2,1)S(1)} %bitcast.40), channel_id=1, source_target_pairs={{0,16},{16,0},{1,17},{17,1},{2,18},{18,2},{3,19},{19,3},{4,20},{20... | collective-permute-start | bytes 491528 | tf_op jit(solution)/shard_map/ppermute | solution.py:15
  7.7 24.9 %collective-permute-start.8 = (bf16[128,1280]{1,0:T(8,128)(2,1)S(1)}, bf16[128,1280]{1,0:T(8,128)(2,1)S(1)}, u32[]{:S(2)}, u32[]{:S(2)}) collective-permute-start(bf16[128,1280]{1,0:T(8,128)(2,1)S(1)} %get-tuple-element.16.refs_8_), channel_id=1, source_target_pairs={{0,1},{1,0},{2,3},{3,2},{4,5},{5,4},{6,7},{7,6},{8,9},{9,8},{10,11... | collective-permute-start | bytes 983048 | tf_op jit(solution)/shard_map/ppermute | solution.py:15
  13.9 18.8 %collective-permute-start.9 = (bf16[128,1280]{1,0:T(8,128)(2,1)S(1)}, bf16[128,1280]{1,0:T(8,128)(2,1)S(1)}, u32[]{:S(2)}, u32[]{:S(2)}) collective-permute-start(bf16[128,1280]{1,0:T(8,128)(2,1)S(1)} %collective-permute-done.7.refs_9_), channel_id=1, source_target_pairs={{0,1},{1,0},{2,3},{3,2},{4,5},{5,4},{6,7},{7,6},{8,9},{9,8},{10,11... | collective-permute-start | bytes 983048 | tf_op jit(solution)/shard_map/ppermute | solution.py:15
  13.9 6.4 %collective-permute-start.4 = (bf16[80,512]{1,0:T(8,128)(2,1)S(1)}, bf16[80,512]{1,0:T(8,128)(2,1)S(1)}, u32[]{:S(2)}, u32[]{:S(2)}) collective-permute-start(bf16[80,512]{1,0:T(8,128)(2,1)S(1)} %get-tuple-element.14.refs_4_), channel_id=1, source_target_pairs={{0,4},{4,0},{8,12},{12,8},{1,5},{5,1},{9,13},{13,9},{2,6},{6,2},{1... | collective-permute-start | bytes 245768 | tf_op jit(solution)/shard_map/ppermute | solution.py:15
  15.7 2.6 %copy-start.6 = (f32[512]{0:T(512)S(1)}, f32[512]{0:T(512)}, u32[]{:S(2)}) copy-start(f32[512]{0:T(512)} %param.10) | copy-start | bytes 6148
  15.7 9.6 %collective-permute-start.5 = (bf16[80,512]{1,0:T(8,128)(2,1)S(1)}, bf16[80,512]{1,0:T(8,128)(2,1)S(1)}, u32[]{:S(2)}, u32[]{:S(2)}) collective-permute-start(bf16[80,512]{1,0:T(8,128)(2,1)S(1)} %get-tuple-element.15), channel_id=1, source_target_pairs={{0,8},{4,12},{8,0},{12,4},{1,9},{5,13},{9,1},{13,5},{2,10},{6,14},... | collective-permute-start | bytes 245768 | tf_op jit(solution)/shard_map/ppermute | solution.py:15
  18.3 7.0 %collective-permute-start.6 = (bf16[80,512]{1,0:T(8,128)(2,1)S(1)}, bf16[80,512]{1,0:T(8,128)(2,1)S(1)}, u32[]{:S(2)}, u32[]{:S(2)}) collective-permute-start(bf16[80,512]{1,0:T(8,128)(2,1)S(1)} %get-tuple-element.15), channel_id=1, source_target_pairs={{0,12},{4,8},{8,4},{12,0},{1,13},{5,9},{9,5},{13,1},{2,14},{6,10},... | collective-permute-start | bytes 245768 | tf_op jit(solution)/shard_map/ppermute | solution.py:15
  20.3 7.7 %collective-permute-start.1 = (bf16[80,512]{1,0:T(8,128)(2,1)S(1)}, bf16[80,512]{1,0:T(8,128)(2,1)S(1)}, u32[]{:S(2)}, u32[]{:S(2)}) collective-permute-start(bf16[80,512]{1,0:T(8,128)(2,1)S(1)} %get-tuple-element.12.refs_0_), channel_id=1, source_target_pairs={{0,4},{4,0},{8,12},{12,8},{1,5},{5,1},{9,13},{13,9},{2,6},{6,2},{1... | collective-permute-start | bytes 245768 | tf_op jit(solution)/shard_map/ppermute | solution.py:15
  25.3 7.4 %collective-permute-start.2 = (bf16[80,512]{1,0:T(8,128)(2,1)S(1)}, bf16[80,512]{1,0:T(8,128)(2,1)S(1)}, u32[]{:S(2)}, u32[]{:S(2)}) collective-permute-start(bf16[80,512]{1,0:T(8,128)(2,1)S(1)} %get-tuple-element.13), channel_id=1, source_target_pairs={{0,8},{4,12},{8,0},{12,4},{1,9},{5,13},{9,1},{13,5},{2,10},{6,14},... | collective-permute-start | bytes 245768 | tf_op jit(solution)/shard_map/ppermute | solution.py:15
  25.3 7.4 %collective-permute-start.3 = (bf16[80,512]{1,0:T(8,128)(2,1)S(1)}, bf16[80,512]{1,0:T(8,128)(2,1)S(1)}, u32[]{:S(2)}, u32[]{:S(2)}) collective-permute-start(bf16[80,512]{1,0:T(8,128)(2,1)S(1)} %get-tuple-element.13), channel_id=1, source_target_pairs={{0,12},{4,8},{8,4},{12,0},{1,13},{5,9},{9,5},{13,1},{2,14},{6,10},... | collective-permute-start | bytes 245768 | tf_op jit(solution)/shard_map/ppermute | solution.py:15
  36.3 2.0 %collective-permute-start.10 = (bf16[8,128,256]{2,1,0:T(8,128)(2,1)S(1)}, bf16[8,128,256]{2,1,0:T(8,128)(2,1)S(1)}, u32[]{:S(2)}, u32[]{:S(2)}) collective-permute-start(bf16[8,128,256]{2,1,0:T(8,128)(2,1)S(1)} %get-tuple-element.18), channel_id=1, source_target_pairs={{0,1},{1,0},{2,3},{3,2},{4,5},{5,4},{6,7},{7,6},{8,9},{9,8},{10,11... | collective-permute-start | bytes 1572872 | tf_op jit(solution)/shard_map/ppermute | solution.py:15
  38.5 5.6 %collective-permute-start.13 = (bf16[2,2,128,128]{3,2,1,0:T(8,128)(2,1)S(1)}, bf16[2,2,128,128]{3,2,1,0:T(8,128)(2,1)S(1)}, u32[]{:S(2)}, u32[]{:S(2)}) collective-permute-start(bf16[2,2,128,128]{3,2,1,0:T(8,128)(2,1)S(1)} %fusion.1), channel_id=1, source_target_pairs={{0,16},{16,0},{1,17},{17,1},{2,18},{18,2},{3,19},{19,3},{4,20},{20... | collective-permute-start | bytes 393224 | tf_op jit(solution)/shard_map/ppermute | solution.py:15
  40.1 5.6 %collective-permute-start.11 = (bf16[2,2,128,128]{3,2,1,0:T(8,128)(2,1)S(1)}, bf16[2,2,128,128]{3,2,1,0:T(8,128)(2,1)S(1)}, u32[]{:S(2)}, u32[]{:S(2)}) collective-permute-start(bf16[2,2,128,128]{3,2,1,0:T(8,128)(2,1)S(1)} %fusion), channel_id=1, source_target_pairs={{0,2},{1,3},{2,0},{3,1},{4,6},{5,7},{6,4},{7,5},{8,10},{9,11},{10,... | collective-permute-start | bytes 393224 | tf_op jit(solution)/shard_map/ppermute | solution.py:15
  44.2 4.3 %collective-permute-start.14 = (bf16[2,128,128]{2,1,0:T(8,128)(2,1)S(1)}, bf16[2,128,128]{2,1,0:T(8,128)(2,1)S(1)}, u32[]{:S(2)}, u32[]{:S(2)}) collective-permute-start(bf16[2,128,128]{2,1,0:T(8,128)(2,1)S(1)} %fusion.8), channel_id=1, source_target_pairs={{0,2},{1,3},{2,0},{3,1},{4,6},{5,7},{6,4},{7,5},{8,10},{9,11},{10,... | collective-permute-start | bytes 196616 | tf_op jit(solution)/shard_map/ppermute | solution.py:15
  45.8 4.3 %collective-permute-start.12 = (bf16[2,128,128]{2,1,0:T(8,128)(2,1)S(1)}, bf16[2,128,128]{2,1,0:T(8,128)(2,1)S(1)}, u32[]{:S(2)}, u32[]{:S(2)}) collective-permute-start(bf16[2,128,128]{2,1,0:T(8,128)(2,1)S(1)} %fusion.7), channel_id=1, source_target_pairs={{0,16},{16,0},{1,17},{17,1},{2,18},{18,2},{3,19},{19,3},{4,20},{20... | collective-permute-start | bytes 196616 | tf_op jit(solution)/shard_map/ppermute | solution.py:15
  50.2 5.7 %collective-permute-start.15 = (bf16[128,256]{1,0:T(8,128)(2,1)S(1)}, bf16[128,256]{1,0:T(8,128)(2,1)S(1)}, u32[]{:S(2)}, u32[]{:S(2)}) collective-permute-start(bf16[128,256]{1,0:T(8,128)(2,1)S(1)} %fusion.9), channel_id=1, source_target_pairs={{0,8},{4,12},{8,0},{12,4},{1,9},{5,13},{9,1},{13,5},{2,10},{6,14},... | collective-permute-start | bytes 196616 | tf_op jit(solution)/shard_map/ppermute | solution.py:15
  55.9 4.3 %collective-permute-start.16 = (f32[64,256]{1,0:T(8,128)S(1)}, f32[64,256]{1,0:T(8,128)S(1)}, u32[]{:S(2)}, u32[]{:S(2)}) collective-permute-start(f32[64,256]{1,0:T(8,128)S(1)} %dynamic-slice_bitcast_fusion), channel_id=1, source_target_pairs={{0,4},{4,0},{8,12},{12,8},{1,5},{5,1},{9,13},{13,9},{2,6},{6,2},{1... | collective-permute-start | bytes 196616 | tf_op jit(solution)/shard_map/ppermute | solution.py:15
where the time goes:
time: 61.2 us; the launch traced here: 61 us
  waiting for transfers between devices  27.4 us (45%)
  starting transfers between devices  23.6 us (39%)
  Pallas kernels  5.84 us (10%)
  local copies, waits for them, and re-layouts  3.73 us (6%)
    ppermute x17, waiting for transfers between devices, swap(): lax.ppermute(values, axis, [(i, i ^ mask) for i in range(lax.axis_size(ax...  27.4 us
    ppermute x17, starting transfers between devices, swap(): lax.ppermute(values, axis, [(i, i ^ mask) for i in range(lax.axis_size(ax...  23.6 us
    pallas_call x1, Pallas kernels, split_form(): pl.pallas_call(block_kernel, out_shape=(jax.ShapeDtypeStruct((8, 2 * bloc...  3.6 us
    unnamed x15, local copies, waits for them, and re-layouts  3.52 us
    pallas_call x1, Pallas kernels, split_form(): pl.pallas_call(conv_kernel, out_shape=(piece, piece), in_specs=[anywhere]...  1.95 us
  transfers between devices with their start and end apart: 17, of which 9 were waited for; matrix products, arithmetic and copies ran while one was open for 0% of the time, Pallas kernels for 3%

commit v1 on v0

--- a/solution.py
+++ b/solution.py
@@ -255,6 +255,20 @@
                         ref[slot, low * block : (low + 1) * block, :] = pieces[low].astype(ref.dtype)
 
 
+def join_kernel(total_ref, got_ref, out_ref):
+    y, _, zp, zh, _, _ = place()
+    lanes = out_ref.shape[1]
+    rows, width = got_ref.shape
+    is_out = (y == 1) & (zp == 1)
+    got = got_ref[...].astype(jnp.float32)
+    for side in range(2):
+        joined = jnp.where(is_out | (zh == side), total_ref[side], got)
+        for lane in range(0, width, lanes):
+            first = (side * width + lane) // lanes
+            step = 2 * width // lanes
+            out_ref[pl.ds(first, rows, stride=step), :] = joined[:, lane : lane + lanes]
+
+
 def split_form(features, neighbours, conv_taps, norm_gain, qkv_weight, out_weight, cotangent):
     own = features[0, 0]
     pixels, channels = own.shape
@@ -276,18 +290,12 @@
         in_specs=[anywhere] * 3,
         out_specs=(in_vmem,) * 3,
         scratch_shapes=[pltpu.SemaphoreType.DMA((6,))],
-        compiler_params=pltpu.CompilerParams(vmem_limit_bytes=4 << 20),
         name="prep",
     )(cotangent[0, 0], qkv_weight, out_weight)
 
-    def spread(mine, other):
-        far = swap(other, "tm", 3)
-        middle = swap(other, "tm", 2)
-        near = swap(mine, "tm", 1)
-        return [mine, near, middle, far]
-
-    ups = spread(up_mine, up_other)
     cut_x = swap(cut, "fsdp", 2)
+    up_2 = swap(up_other, "tm", 2)
+    up_1 = swap(up_mine, "tm", 1)
     n_mine, n_other = pl.pallas_call(
         conv_kernel,
         out_shape=(piece, piece),
@@ -303,7 +311,10 @@
         compiler_params=pltpu.CompilerParams(vmem_limit_bytes=16 << 20),
         name="conv",
     )(neighbours.T, own, band, conv_taps, norm_gain.reshape(1, channels))
-    rows = spread(n_mine, n_other)
+    row_3 = swap(n_other, "tm", 3)
+    row_2 = swap(n_other, "tm", 2)
+    row_1 = swap(n_mine, "tm", 1)
+    up_3 = swap(up_2, "tm", 1)
     cut_c = swap(cut, "fsdp", 1)
     cut_xc = swap(cut_x, "fsdp", 1)
 
@@ -326,7 +337,9 @@
         ],
         compiler_params=pltpu.CompilerParams(vmem_limit_bytes=32 << 20),
         name="attend",
-    )(*rows, *ups, cut, cut_x, cut_c, cut_xc)
+    )(
+        *(n_mine, row_1, row_2, row_3), *(up_mine, up_1, up_2, up_3), *(cut, cut_x, cut_c, cut_xc)
+    )
 
     def narrow(values):
         return values.astype(jnp.bfloat16)
@@ -345,12 +358,17 @@
     total = jnp.concatenate([first, second], axis=-1)
     total = pick(total, zp) + swap(narrow(pick(total, 1 - zp)), "tm", 2).astype(jnp.float32)
     total = total.reshape(2, block, width)
-    mine = pick(total, zh)
-    got = swap(pick(total, 1 - zh), "tm", 1)
-    is_out = (y == 1) & (zp == 1)
-    left = jnp.where(is_out, total[0], jnp.where(zh == 0, mine, got))
-    right = jnp.where(is_out, total[1], jnp.where(zh == 0, got, mine))
-    return jnp.concatenate([left, right], axis=1).reshape(-1)
+    got = swap(narrow(pick(total, 1 - zh)), "tm", 1)
+    lanes = 128
+    out = pl.pallas_call(
+        join_kernel,
+        out_shape=jax.ShapeDtypeStruct((block * channels // lanes, lanes), jnp.float32),
+        in_specs=[in_vmem] * 2,
+        out_specs=in_vmem,
+        compiler_params=pltpu.CompilerParams(vmem_limit_bytes=4 << 20),
+        name="join",
+    )(total, got)
+    return out.reshape(-1)
 
 
 def with_halo(cells, sides, width):

time: 61.2 us -> 64.1 us (1.047)
  waiting for transfers between devices: 27.4 us -> 30.2 us
  local copies, waits for them, and re-layouts: 3.73 us -> 1.11 us
  Pallas kernels: 5.84 us -> 8.1 us
    ppermute x17, waiting for transfers between devices: 27.4 us -> 30.2 us  [swap(): lax.ppermute(values, axis, [(i, i ^ mask) for i in range(lax.axis_size(ax...]
    unnamed x15 -> x12, local copies, waits for them, and re-layouts: 3.52 us -> 0.9 us
    pallas_call x1, Pallas kernels: 0.29 us -> 1.93 us  [split_form(): pl.pallas_call(prep_kernel, out_shape=(piece, piece, jax.ShapeDtypeStruct...]
    pallas_call x0 -> x1, Pallas kernels: none -> 0.67 us  [split_form(): pl.pallas_call(join_kernel, out_shape=jax.ShapeDtypeStruct((block * chann...]
  transfers between devices with their start and end apart: 17 -> 17, of which waited for: 9 -> 10; matrix products, arithmetic and copies ran while one was open for 0% -> 0% of each run, Pallas kernels for 3% -> 3%
where the time goes in v1:
time: 64.1 us; the launch traced here: 64 us
  waiting for transfers between devices  30.2 us (47%)
  starting transfers between devices  24.2 us (38%)
  Pallas kernels  8.1 us (13%)
  local copies, waits for them, and re-layouts  1.11 us (2%)
    ppermute x17, waiting for transfers between devices, swap(): lax.ppermute(values, axis, [(i, i ^ mask) for i in range(lax.axis_size(ax...  30.2 us
    ppermute x17, starting transfers between devices, swap(): lax.ppermute(values, axis, [(i, i ^ mask) for i in range(lax.axis_size(ax...  24.2 us
    pallas_call x1, Pallas kernels, split_form(): pl.pallas_call(block_kernel, out_shape=(jax.ShapeDtypeStruct((8, 2 * bloc...  3.55 us
    pallas_call x1, Pallas kernels, split_form(): pl.pallas_call(conv_kernel, out_shape=(piece, piece), in_specs=[anywhere]...  1.95 us
    pallas_call x1, Pallas kernels, split_form(): pl.pallas_call(prep_kernel, out_shape=(piece, piece, jax.ShapeDtypeStruct...  1.93 us
  transfers between devices with their start and end apart: 17, of which 10 were waited for; matrix products, arithmetic and copies ran while one was open for 0% of the time, Pallas kernels for 3%

profile of v1, /device:TPU:0, one launch (start us, length us, event | category | flops | bytes accessed | tf_op | source)
XLA Modules:
  0.0 64.0 jit_solution(13142541558064989427)
XLA Ops:
  0.0 1.9 %prep.1 = (bf16[80,512]{1,0:T(8,128)(2,1)}, bf16[80,512]{1,0:T(8,128)(2,1)}, bf16[128,1280]{1,0:T(8,128)(2,1)}) custom-call(bf16[160,512]{1,0:T(8,128)(2,1)} %bitcast.44, bf16[128,1536]{1,0:T(8,128)(2,1)} %qkv_ref.1, bf16[128,512]{1,0:T(8,128)(2,1)} %out_w_ref.1), custom_call_target="tpu_custom_call" | custom-call | tf_op jit(solution)/shard_map/prep/pallas_call | solution.py:283
  2.0 3.1 %collective-permute-start.7 = (bf16[128,1280]{1,0:T(8,128)(2,1)}, bf16[128,1280]{1,0:T(8,128)(2,1)S(1)}, u32[]{:S(2)}, u32[]{:S(2)}) collective-permute-start(bf16[128,1280]{1,0:T(8,128)(2,1)} %get-tuple-element.16.refs_8_), channel_id=1, source_target_pairs={{0,2},{1,3},{2,0},{3,1},{4,6},{5,7},{6,4},{7,5},{8,10},{9,11},{10,... | collective-permute-start | bytes 983048 | tf_op jit(solution)/shard_map/ppermute | solution.py:15
  5.0 7.9 %collective-permute-done.7.refs_9_ = bf16[128,1280]{1,0:T(8,128)(2,1)S(1)} collective-permute-done((bf16[128,1280]{1,0:T(8,128)(2,1)}, bf16[128,1280]{1,0:T(8,128)(2,1)S(1)}, u32[]{:S(2)}, u32[]{:S(2)}) %collective-permute-start.7) | collective-permute-done | bytes 327712 | tf_op jit(solution)/shard_map/ppermute | solution.py:15
  12.9 1.8 %collective-permute-start = (bf16[160,512]{1,0:T(8,128)(2,1)S(1)}, bf16[160,512]{1,0:T(8,128)(2,1)S(1)}, u32[]{:S(2)}, u32[]{:S(2)}) collective-permute-start(bf16[160,512]{1,0:T(8,128)(2,1)S(1)} %bitcast.39), channel_id=1, source_target_pairs={{0,16},{16,0},{1,17},{17,1},{2,18},{18,2},{3,19},{19,3},{4,20},{20... | collective-permute-start | bytes 491528 | tf_op jit(solution)/shard_map/ppermute | solution.py:15
  14.7 2.6 %collective-permute-start.5 = (bf16[80,512]{1,0:T(8,128)(2,1)}, bf16[80,512]{1,0:T(8,128)(2,1)S(1)}, u32[]{:S(2)}, u32[]{:S(2)}) collective-permute-start(bf16[80,512]{1,0:T(8,128)(2,1)} %get-tuple-element.15), channel_id=1, source_target_pairs={{0,8},{4,12},{8,0},{12,4},{1,9},{5,13},{9,1},{13,5},{2,10},{6,14},... | collective-permute-start | bytes 245768 | tf_op jit(solution)/shard_map/ppermute | solution.py:15
  17.3 1.6 %collective-permute-start.4 = (bf16[80,512]{1,0:T(8,128)(2,1)}, bf16[80,512]{1,0:T(8,128)(2,1)S(1)}, u32[]{:S(2)}, u32[]{:S(2)}) collective-permute-start(bf16[80,512]{1,0:T(8,128)(2,1)} %get-tuple-element.14.refs_4_), channel_id=1, source_target_pairs={{0,4},{4,0},{8,12},{12,8},{1,5},{5,1},{9,13},{13,9},{2,6},{6,2},{1... | collective-permute-start | bytes 245768 | tf_op jit(solution)/shard_map/ppermute | solution.py:15
  18.9 3.2 %collective-permute-done.5.refs_6_ = bf16[80,512]{1,0:T(8,128)(2,1)S(1)} collective-permute-done((bf16[80,512]{1,0:T(8,128)(2,1)}, bf16[80,512]{1,0:T(8,128)(2,1)S(1)}, u32[]{:S(2)}, u32[]{:S(2)}) %collective-permute-start.5) | collective-permute-done | bytes 81952 | tf_op jit(solution)/shard_map/ppermute | solution.py:15
  22.1 0.8 %collective-permute-start.6 = (bf16[80,512]{1,0:T(8,128)(2,1)S(1)}, bf16[80,512]{1,0:T(8,128)(2,1)S(1)}, u32[]{:S(2)}, u32[]{:S(2)}) collective-permute-start(bf16[80,512]{1,0:T(8,128)(2,1)S(1)} %collective-permute-done.5.refs_6_), channel_id=1, source_target_pairs={{0,4},{4,0},{8,12},{12,8},{1,5},{5,1},{9,13},{13,9},{2,6},{6,2},{1... | collective-permute-start | bytes 245768 | tf_op jit(solution)/shard_map/ppermute | solution.py:15
  22.9 1.9 %conv.1 = (bf16[80,512]{1,0:T(8,128)(2,1)S(1)}, bf16[80,512]{1,0:T(8,128)(2,1)S(1)}) custom-call(s32[8,160]{1,0:T(8,128)S(1)} %bitcast.41, bf16[160,512]{1,0:T(8,128)(2,1)S(1)} %bitcast.40, bf16[160,512]{1,0:T(8,128)(2,1)S(1)} %collective-permute-done.band_hbm, f32[9,512]{1,0:T(8,128)S(1)} %copy-done.3, f32[1,512]{1,0:T(1,128)S(1)} %bitcast.42), custom_call_target="tpu_custom_call" | custom-call | tf_op jit(solution)/shard_map/conv/pallas_call | solution.py:299
  24.9 1.3 %collective-permute-start.1 = (bf16[80,512]{1,0:T(8,128)(2,1)S(1)}, bf16[80,512]{1,0:T(8,128)(2,1)S(1)}, u32[]{:S(2)}, u32[]{:S(2)}) collective-permute-start(bf16[80,512]{1,0:T(8,128)(2,1)S(1)} %get-tuple-element.12.refs_0_), channel_id=1, source_target_pairs={{0,4},{4,0},{8,12},{12,8},{1,5},{5,1},{9,13},{13,9},{2,6},{6,2},{1... | collective-permute-start | bytes 245768 | tf_op jit(solution)/shard_map/ppermute | solution.py:15
  26.2 2.2 %collective-permute-start.2 = (bf16[80,512]{1,0:T(8,128)(2,1)S(1)}, bf16[80,512]{1,0:T(8,128)(2,1)S(1)}, u32[]{:S(2)}, u32[]{:S(2)}) collective-permute-start(bf16[80,512]{1,0:T(8,128)(2,1)S(1)} %get-tuple-element.13), channel_id=1, source_target_pairs={{0,8},{4,12},{8,0},{12,4},{1,9},{5,13},{9,1},{13,5},{2,10},{6,14},... | collective-permute-start | bytes 245768 | tf_op jit(solution)/shard_map/ppermute | solution.py:15
  28.3 1.7 %collective-permute-start.3 = (bf16[80,512]{1,0:T(8,128)(2,1)S(1)}, bf16[80,512]{1,0:T(8,128)(2,1)S(1)}, u32[]{:S(2)}, u32[]{:S(2)}) collective-permute-start(bf16[80,512]{1,0:T(8,128)(2,1)S(1)} %get-tuple-element.13), channel_id=1, source_target_pairs={{0,12},{4,8},{8,4},{12,0},{1,13},{5,9},{9,5},{13,1},{2,14},{6,10},... | collective-permute-start | bytes 245768 | tf_op jit(solution)/shard_map/ppermute | solution.py:15
  30.1 0.2 collective-permute-done.1.refs_1_
  30.3 5.2 %collective-permute-done.2.refs_2_ = bf16[80,512]{1,0:T(8,128)(2,1)S(1)} collective-permute-done((bf16[80,512]{1,0:T(8,128)(2,1)S(1)}, bf16[80,512]{1,0:T(8,128)(2,1)S(1)}, u32[]{:S(2)}, u32[]{:S(2)}) %collective-permute-start.2) | collective-permute-done | bytes 81952 | tf_op jit(solution)/shard_map/ppermute | solution.py:15
  35.5 0.9 %copy-done.2 = bf16[80,512]{1,0:T(8,128)(2,1)S(1)} copy-done((bf16[80,512]{1,0:T(8,128)(2,1)S(1)}, bf16[80,512]{1,0:T(8,128)(2,1)}, u32[]{:S(2)}) %copy-start.2) | copy-done | bytes 81944
  36.4 3.5 %attend.1 = (f32[8,128,256]{2,1,0:T(8,128)S(1)}, bf16[8,128,256]{2,1,0:T(8,128)(2,1)S(1)}) custom-call(bf16[80,512]{1,0:T(8,128)(2,1)S(1)} %get-tuple-element.12.refs_0_, bf16[80,512]{1,0:T(8,128)(2,1)S(1)} %collective-permute-done.1.refs_1_, bf16[80,512]{1,0:T(8,128)(2,1)S(1)} %collective-permute-done.2.refs_2_, ...), custom_call_target="tpu_custom_call" | custom-call | tf_op jit(solution)/shard_map/attend/pallas_call | solution.py:321
  40.0 0.1 collective-permute-start.10
  40.0 1.9 %collective-permute-done.10 = bf16[8,128,256]{2,1,0:T(8,128)(2,1)S(1)} collective-permute-done((bf16[8,128,256]{2,1,0:T(8,128)(2,1)S(1)}, bf16[8,128,256]{2,1,0:T(8,128)(2,1)S(1)}, u32[]{:S(2)}, u32[]{:S(2)}) %collective-permute-start.10) | collective-permute-done | bytes 524320 | tf_op jit(solution)/shard_map/ppermute | solution.py:15
  41.9 0.1 convert_add_fusion
  42.1 0.1 fusion.11
  42.2 0.4 collective-permute-start.13
  42.6 1.8 %collective-permute-start.11 = (bf16[2,2,128,128]{3,2,1,0:T(8,128)(2,1)S(1)}, bf16[2,2,128,128]{3,2,1,0:T(8,128)(2,1)S(1)}, u32[]{:S(2)}, u32[]{:S(2)}) collective-permute-start(bf16[2,2,128,128]{3,2,1,0:T(8,128)(2,1)S(1)} %fusion), channel_id=1, source_target_pairs={{0,2},{1,3},{2,0},{3,1},{4,6},{5,7},{6,4},{7,5},{8,10},{9,11},{10,... | collective-permute-start | bytes 393224 | tf_op jit(solution)/shard_map/ppermute | solution.py:15
  44.4 3.5 %collective-permute-done.13 = bf16[2,2,128,128]{3,2,1,0:T(8,128)(2,1)S(1)} collective-permute-done((bf16[2,2,128,128]{3,2,1,0:T(8,128)(2,1)S(1)}, bf16[2,2,128,128]{3,2,1,0:T(8,128)(2,1)S(1)}, u32[]{:S(2)}, u32[]{:S(2)}) %collective-permute-start.13) | collective-permute-done | bytes 131104 | tf_op jit(solution)/shard_map/ppermute | solution.py:15
  47.9 1.6 %collective-permute-start.14 = (bf16[2,128,128]{2,1,0:T(8,128)(2,1)S(1)}, bf16[2,128,128]{2,1,0:T(8,128)(2,1)S(1)}, u32[]{:S(2)}, u32[]{:S(2)}) collective-permute-start(bf16[2,128,128]{2,1,0:T(8,128)(2,1)S(1)} %fusion.8), channel_id=1, source_target_pairs={{0,2},{1,3},{2,0},{3,1},{4,6},{5,7},{6,4},{7,5},{8,10},{9,11},{10,... | collective-permute-start | bytes 196616 | tf_op jit(solution)/shard_map/ppermute | solution.py:15
  49.5 0.6 collective-permute-start.12
  50.1 2.1 %collective-permute-done.14 = bf16[2,128,128]{2,1,0:T(8,128)(2,1)S(1)} collective-permute-done((bf16[2,128,128]{2,1,0:T(8,128)(2,1)S(1)}, bf16[2,128,128]{2,1,0:T(8,128)(2,1)S(1)}, u32[]{:S(2)}, u32[]{:S(2)}) %collective-permute-start.14) | collective-permute-done | bytes 65568 | tf_op jit(solution)/shard_map/ppermute | solution.py:15
  52.2 1.6 %collective-permute-done.12 = bf16[2,128,128]{2,1,0:T(8,128)(2,1)S(1)} collective-permute-done((bf16[2,128,128]{2,1,0:T(8,128)(2,1)S(1)}, bf16[2,128,128]{2,1,0:T(8,128)(2,1)S(1)}, u32[]{:S(2)}, u32[]{:S(2)}) %collective-permute-start.12) | collective-permute-done | bytes 65568 | tf_op jit(solution)/shard_map/ppermute | solution.py:15
  53.9 3.2 %collective-permute-start.15 = (bf16[128,256]{1,0:T(8,128)(2,1)S(1)}, bf16[128,256]{1,0:T(8,128)(2,1)S(1)}, u32[]{:S(2)}, u32[]{:S(2)}) collective-permute-start(bf16[128,256]{1,0:T(8,128)(2,1)S(1)} %fusion.9), channel_id=1, source_target_pairs={{0,8},{4,12},{8,0},{12,4},{1,9},{5,13},{9,1},{13,5},{2,10},{6,14},... | collective-permute-start | bytes 196616 | tf_op jit(solution)/shard_map/ppermute | solution.py:15
  57.0 2.2 %collective-permute-done.15 = bf16[128,256]{1,0:T(8,128)(2,1)S(1)} collective-permute-done((bf16[128,256]{1,0:T(8,128)(2,1)S(1)}, bf16[128,256]{1,0:T(8,128)(2,1)S(1)}, u32[]{:S(2)}, u32[]{:S(2)}) %collective-permute-start.15) | collective-permute-done | bytes 65568 | tf_op jit(solution)/shard_map/ppermute | solution.py:15
  59.3 1.7 %collective-permute-start.16 = (bf16[64,256]{1,0:T(8,128)(2,1)S(1)}, bf16[64,256]{1,0:T(8,128)(2,1)S(1)}, u32[]{:S(2)}, u32[]{:S(2)}) collective-permute-start(bf16[64,256]{1,0:T(8,128)(2,1)S(1)} %fusion.10), channel_id=1, source_target_pairs={{0,4},{4,0},{8,12},{12,8},{1,5},{5,1},{9,13},{13,9},{2,6},{6,2},{1... | collective-permute-start | bytes 98312 | tf_op jit(solution)/shard_map/ppermute | solution.py:15
  61.0 2.3 %collective-permute-done.16.got_ref = bf16[64,256]{1,0:T(8,128)(2,1)S(1)} collective-permute-done((bf16[64,256]{1,0:T(8,128)(2,1)S(1)}, bf16[64,256]{1,0:T(8,128)(2,1)S(1)}, u32[]{:S(2)}, u32[]{:S(2)}) %collective-permute-start.16) | collective-permute-done | bytes 32800 | tf_op jit(solution)/shard_map/ppermute | solution.py:15
  63.3 0.7 %join.1 = f32[256,128]{1,0:T(8,128)} custom-call(f32[2,64,256]{2,1,0:T(8,128)S(1)} %bitcast.38, bf16[64,256]{1,0:T(8,128)(2,1)S(1)} %collective-permute-done.16.got_ref), custom_call_target="tpu_custom_call" | custom-call | tf_op jit(solution)/shard_map/join/pallas_call | solution.py:363
  (31 shorter events, 0.3 us)
Async XLA Ops:
  0.0 12.9 %copy-start.1 = (bf16[1,1,160,512]{3,2,1,0:T(8,128)(2,1)S(1)}, bf16[1,1,160,512]{3,2,1,0:T(8,128)(2,1)}, u32[]{:S(2)}) copy-start(bf16[1,1,160,512]{3,2,1,0:T(8,128)(2,1)} %param.7) | copy-start | bytes 491524
  0.0 22.9 %copy-start.3 = (f32[9,512]{1,0:T(8,128)S(1)}, f32[9,512]{1,0:T(8,128)}, u32[]{:S(2)}) copy-start(f32[9,512]{1,0:T(8,128)} %taps_hbm.1) | copy-start | bytes 55300
  0.0 22.9 %copy-start.4 = (s32[160,8]{0,1:T(8,128)S(1)}, s32[160,8]{0,1:T(8,128)}, u32[]{:S(2)}) copy-start(s32[160,8]{0,1:T(8,128)} %param.8) | copy-start | bytes 15364
  0.0 22.9 %copy-start.5 = (f32[512]{0:T(512)S(1)}, f32[512]{0:T(512)}, u32[]{:S(2)}) copy-start(f32[512]{0:T(512)} %param.10) | copy-start | bytes 6148
  1.9 33.6 %copy-start = (bf16[128,1280]{1,0:T(8,128)(2,1)S(1)}, bf16[128,1280]{1,0:T(8,128)(2,1)}, u32[]{:S(2)}) copy-start(bf16[128,1280]{1,0:T(8,128)(2,1)} %get-tuple-element.16.refs_8_) | copy-start | bytes 983044
  2.0 11.0 %collective-permute-start.7 = (bf16[128,1280]{1,0:T(8,128)(2,1)}, bf16[128,1280]{1,0:T(8,128)(2,1)S(1)}, u32[]{:S(2)}, u32[]{:S(2)}) collective-permute-start(bf16[128,1280]{1,0:T(8,128)(2,1)} %get-tuple-element.16.refs_8_), channel_id=1, source_target_pairs={{0,2},{1,3},{2,0},{3,1},{4,6},{5,7},{6,4},{7,5},{8,10},{9,11},{10,... | collective-permute-start | bytes 983048 | tf_op jit(solution)/shard_map/ppermute | solution.py:15
  5.0 30.5 %collective-permute-start.8 = (bf16[128,1280]{1,0:T(8,128)(2,1)}, bf16[128,1280]{1,0:T(8,128)(2,1)S(1)}, u32[]{:S(2)}, u32[]{:S(2)}) collective-permute-start(bf16[128,1280]{1,0:T(8,128)(2,1)} %get-tuple-element.16.refs_8_), channel_id=1, source_target_pairs={{0,1},{1,0},{2,3},{3,2},{4,5},{5,4},{6,7},{7,6},{8,9},{9,8},{10,11... | collective-permute-start | bytes 983048 | tf_op jit(solution)/shard_map/ppermute | solution.py:15
  12.9 22.6 %collective-permute-start.9 = (bf16[128,1280]{1,0:T(8,128)(2,1)S(1)}, bf16[128,1280]{1,0:T(8,128)(2,1)S(1)}, u32[]{:S(2)}, u32[]{:S(2)}) collective-permute-start(bf16[128,1280]{1,0:T(8,128)(2,1)S(1)} %collective-permute-done.7.refs_9_), channel_id=1, source_target_pairs={{0,1},{1,0},{2,3},{3,2},{4,5},{5,4},{6,7},{7,6},{8,9},{9,8},{10,11... | collective-permute-start | bytes 983048 | tf_op jit(solution)/shard_map/ppermute | solution.py:15
  12.9 10.0 %collective-permute-start = (bf16[160,512]{1,0:T(8,128)(2,1)S(1)}, bf16[160,512]{1,0:T(8,128)(2,1)S(1)}, u32[]{:S(2)}, u32[]{:S(2)}) collective-permute-start(bf16[160,512]{1,0:T(8,128)(2,1)S(1)} %bitcast.39), channel_id=1, source_target_pairs={{0,16},{16,0},{1,17},{17,1},{2,18},{18,2},{3,19},{19,3},{4,20},{20... | collective-permute-start | bytes 491528 | tf_op jit(solution)/shard_map/ppermute | solution.py:15
  14.7 7.4 %collective-permute-start.5 = (bf16[80,512]{1,0:T(8,128)(2,1)}, bf16[80,512]{1,0:T(8,128)(2,1)S(1)}, u32[]{:S(2)}, u32[]{:S(2)}) collective-permute-start(bf16[80,512]{1,0:T(8,128)(2,1)} %get-tuple-element.15), channel_id=1, source_target_pairs={{0,8},{4,12},{8,0},{12,4},{1,9},{5,13},{9,1},{13,5},{2,10},{6,14},... | collective-permute-start | bytes 245768 | tf_op jit(solution)/shard_map/ppermute | solution.py:15
  17.3 8.9 %collective-permute-start.4 = (bf16[80,512]{1,0:T(8,128)(2,1)}, bf16[80,512]{1,0:T(8,128)(2,1)S(1)}, u32[]{:S(2)}, u32[]{:S(2)}) collective-permute-start(bf16[80,512]{1,0:T(8,128)(2,1)} %get-tuple-element.14.refs_4_), channel_id=1, source_target_pairs={{0,4},{4,0},{8,12},{12,8},{1,5},{5,1},{9,13},{13,9},{2,6},{6,2},{1... | collective-permute-start | bytes 245768 | tf_op jit(solution)/shard_map/ppermute | solution.py:15
  22.1 6.2 %collective-permute-start.6 = (bf16[80,512]{1,0:T(8,128)(2,1)S(1)}, bf16[80,512]{1,0:T(8,128)(2,1)S(1)}, u32[]{:S(2)}, u32[]{:S(2)}) collective-permute-start(bf16[80,512]{1,0:T(8,128)(2,1)S(1)} %collective-permute-done.5.refs_6_), channel_id=1, source_target_pairs={{0,4},{4,0},{8,12},{12,8},{1,5},{5,1},{9,13},{13,9},{2,6},{6,2},{1... | collective-permute-start | bytes 245768 | tf_op jit(solution)/shard_map/ppermute | solution.py:15
  24.9 5.4 %collective-permute-start.1 = (bf16[80,512]{1,0:T(8,128)(2,1)S(1)}, bf16[80,512]{1,0:T(8,128)(2,1)S(1)}, u32[]{:S(2)}, u32[]{:S(2)}) collective-permute-start(bf16[80,512]{1,0:T(8,128)(2,1)S(1)} %get-tuple-element.12.refs_0_), channel_id=1, source_target_pairs={{0,4},{4,0},{8,12},{12,8},{1,5},{5,1},{9,13},{13,9},{2,6},{6,2},{1... | collective-permute-start | bytes 245768 | tf_op jit(solution)/shard_map/ppermute | solution.py:15
  26.2 9.3 %collective-permute-start.2 = (bf16[80,512]{1,0:T(8,128)(2,1)S(1)}, bf16[80,512]{1,0:T(8,128)(2,1)S(1)}, u32[]{:S(2)}, u32[]{:S(2)}) collective-permute-start(bf16[80,512]{1,0:T(8,128)(2,1)S(1)} %get-tuple-element.13), channel_id=1, source_target_pairs={{0,8},{4,12},{8,0},{12,4},{1,9},{5,13},{9,1},{13,5},{2,10},{6,14},... | collective-permute-start | bytes 245768 | tf_op jit(solution)/shard_map/ppermute | solution.py:15
  28.3 7.2 %collective-permute-start.3 = (bf16[80,512]{1,0:T(8,128)(2,1)S(1)}, bf16[80,512]{1,0:T(8,128)(2,1)S(1)}, u32[]{:S(2)}, u32[]{:S(2)}) collective-permute-start(bf16[80,512]{1,0:T(8,128)(2,1)S(1)} %get-tuple-element.13), channel_id=1, source_target_pairs={{0,12},{4,8},{8,4},{12,0},{1,13},{5,9},{9,5},{13,1},{2,14},{6,10},... | collective-permute-start | bytes 245768 | tf_op jit(solution)/shard_map/ppermute | solution.py:15
  35.5 0.9 %copy-start.2 = (bf16[80,512]{1,0:T(8,128)(2,1)S(1)}, bf16[80,512]{1,0:T(8,128)(2,1)}, u32[]{:S(2)}) copy-start(bf16[80,512]{1,0:T(8,128)(2,1)} %get-tuple-element.14.refs_4_) | copy-start | bytes 245764
  40.0 2.0 %collective-permute-start.10 = (bf16[8,128,256]{2,1,0:T(8,128)(2,1)S(1)}, bf16[8,128,256]{2,1,0:T(8,128)(2,1)S(1)}, u32[]{:S(2)}, u32[]{:S(2)}) collective-permute-start(bf16[8,128,256]{2,1,0:T(8,128)(2,1)S(1)} %get-tuple-element.18), channel_id=1, source_target_pairs={{0,1},{1,0},{2,3},{3,2},{4,5},{5,4},{6,7},{7,6},{8,9},{9,8},{10,11... | collective-permute-start | bytes 1572872 | tf_op jit(solution)/shard_map/ppermute | solution.py:15
  42.2 5.6 %collective-permute-start.13 = (bf16[2,2,128,128]{3,2,1,0:T(8,128)(2,1)S(1)}, bf16[2,2,128,128]{3,2,1,0:T(8,128)(2,1)S(1)}, u32[]{:S(2)}, u32[]{:S(2)}) collective-permute-start(bf16[2,2,128,128]{3,2,1,0:T(8,128)(2,1)S(1)} %fusion.1), channel_id=1, source_target_pairs={{0,16},{16,0},{1,17},{17,1},{2,18},{18,2},{3,19},{19,3},{4,20},{20... | collective-permute-start | bytes 393224 | tf_op jit(solution)/shard_map/ppermute | solution.py:15
  42.6 6.8 %collective-permute-start.11 = (bf16[2,2,128,128]{3,2,1,0:T(8,128)(2,1)S(1)}, bf16[2,2,128,128]{3,2,1,0:T(8,128)(2,1)S(1)}, u32[]{:S(2)}, u32[]{:S(2)}) collective-permute-start(bf16[2,2,128,128]{3,2,1,0:T(8,128)(2,1)S(1)} %fusion), channel_id=1, source_target_pairs={{0,2},{1,3},{2,0},{3,1},{4,6},{5,7},{6,4},{7,5},{8,10},{9,11},{10,... | collective-permute-start | bytes 393224 | tf_op jit(solution)/shard_map/ppermute | solution.py:15
  47.9 4.3 %collective-permute-start.14 = (bf16[2,128,128]{2,1,0:T(8,128)(2,1)S(1)}, bf16[2,128,128]{2,1,0:T(8,128)(2,1)S(1)}, u32[]{:S(2)}, u32[]{:S(2)}) collective-permute-start(bf16[2,128,128]{2,1,0:T(8,128)(2,1)S(1)} %fusion.8), channel_id=1, source_target_pairs={{0,2},{1,3},{2,0},{3,1},{4,6},{5,7},{6,4},{7,5},{8,10},{9,11},{10,... | collective-permute-start | bytes 196616 | tf_op jit(solution)/shard_map/ppermute | solution.py:15
  49.5 4.3 %collective-permute-start.12 = (bf16[2,128,128]{2,1,0:T(8,128)(2,1)S(1)}, bf16[2,128,128]{2,1,0:T(8,128)(2,1)S(1)}, u32[]{:S(2)}, u32[]{:S(2)}) collective-permute-start(bf16[2,128,128]{2,1,0:T(8,128)(2,1)S(1)} %fusion.7), channel_id=1, source_target_pairs={{0,16},{16,0},{1,17},{17,1},{2,18},{18,2},{3,19},{19,3},{4,20},{20... | collective-permute-start | bytes 196616 | tf_op jit(solution)/shard_map/ppermute | solution.py:15
  53.9 5.4 %collective-permute-start.15 = (bf16[128,256]{1,0:T(8,128)(2,1)S(1)}, bf16[128,256]{1,0:T(8,128)(2,1)S(1)}, u32[]{:S(2)}, u32[]{:S(2)}) collective-permute-start(bf16[128,256]{1,0:T(8,128)(2,1)S(1)} %fusion.9), channel_id=1, source_target_pairs={{0,8},{4,12},{8,0},{12,4},{1,9},{5,13},{9,1},{13,5},{2,10},{6,14},... | collective-permute-start | bytes 196616 | tf_op jit(solution)/shard_map/ppermute | solution.py:15
  59.3 4.0 %collective-permute-start.16 = (bf16[64,256]{1,0:T(8,128)(2,1)S(1)}, bf16[64,256]{1,0:T(8,128)(2,1)S(1)}, u32[]{:S(2)}, u32[]{:S(2)}) collective-permute-start(bf16[64,256]{1,0:T(8,128)(2,1)S(1)} %fusion.10), channel_id=1, source_target_pairs={{0,4},{4,0},{8,12},{12,8},{1,5},{5,1},{9,13},{13,9},{2,6},{6,2},{1... | collective-permute-start | bytes 98312 | tf_op jit(solution)/shard_map/ppermute | solution.py:15

commit v2 on v1

--- a/solution.py
+++ b/solution.py
@@ -1,3 +1,5 @@
+import functools
+
 import jax
 import jax.numpy as jnp
 from jax import lax
@@ -54,12 +56,13 @@
 
 
 def conv_kernel(
-    near_hbm, own_hbm, band_hbm, taps_hbm, gain_hbm, mine_ref, other_ref,
-    near_ref, table_ref, taps_ref, gain_ref, sems,
+    far, near_hbm, own_hbm, band_hbm, taps_hbm, gain_hbm, out_ref,
+    near_ref, turned_ref, table_ref, taps_ref, gain_ref, sems,
 ):
     y, _, zp, _, _, _ = place()
     pixels, _ = own_hbm.shape
     half = pixels // 2
+    begin = pl.multiple_of((1 - zp if far else zp) * half, 16)
     pairs = [
         (near_hbm, near_ref),
         (taps_hbm, taps_ref),
@@ -70,11 +73,12 @@
     copies = [pltpu.make_async_copy(a, b, sems.at[i]) for i, (a, b) in enumerate(pairs)]
     start_all(copies)
     copies[0].wait()
-    near = near_ref[...].T
+    turned_ref[...] = near_ref[...].T
+    near = turned_ref[pl.ds(begin, half), :]
     neighbours = near.shape[1]
     local = near - y * pixels
     local = jnp.where(local < 0, local + 2 * pixels, local)
-    slots = lax.broadcasted_iota(jnp.int32, (pixels, 2 * pixels), 1)
+    slots = lax.broadcasted_iota(jnp.int32, (half, 2 * pixels), 1)
     chosen = jnp.concatenate(
         [
             jnp.where(local[:, k : k + 1] == slots, 1.0, 0.0).astype(jnp.bfloat16)
@@ -85,41 +89,31 @@
     for copy in copies[1:]:
         copy.wait()
     gathered = jnp.dot(chosen, table_ref[...], preferred_element_type=jnp.float32)
-    own = table_ref[:pixels, :].astype(jnp.float32)
+    own = table_ref[pl.ds(begin, half), :].astype(jnp.float32)
     spatial = taps_ref[0:1, :] * own
     for k in range(neighbours):
-        spatial = spatial + taps_ref[k + 1 : k + 2, :] * gathered[k * pixels : (k + 1) * pixels]
+        spatial = spatial + taps_ref[k + 1 : k + 2, :] * gathered[k * half : (k + 1) * half]
     hidden = (own + spatial).astype(jnp.bfloat16).astype(jnp.float32)
     inverse = lax.rsqrt(jnp.mean(hidden * hidden, axis=-1, keepdims=True) + 1e-05)
-    normed = (hidden * inverse * gain_ref[...]).astype(jnp.bfloat16)
-    low, high = normed[:half], normed[half:]
-
-    @pl.when(zp == 0)
-    def _():
-        mine_ref[...] = low
-        other_ref[...] = high
-
-    @pl.when(zp == 1)
-    def _():
-        mine_ref[...] = high
-        other_ref[...] = low
+    out_ref[...] = (hidden * inverse * gain_ref[...]).astype(jnp.bfloat16)
 
 
 def block_kernel(*refs):
     frames = 4
-    sources, refs = refs[: 3 * frames], refs[3 * frames :]
+    row_refs, pair_refs, shards, refs = refs[:4], refs[4:6], refs[6:10], refs[10:]
     keep_ref, send_ref, n_ref, u_ref, qkv_ref, out_w_ref, sums_ref, out_sums_ref, sems = refs
     _, t, _, zh, x, core = place()
-    pixels, channels = sources[0].shape
+    pixels, channels = row_refs[0].shape
     width, depth = out_w_ref.shape[0], channels // HEADS
-    rows = sources[-1].shape[0]
+    rows = shards[0].shape[0]
     up_copies, row_copies, qkv_copies = [], [], []
     for k in range(frames):
-        row_copies.append(pltpu.make_async_copy(sources[k], n_ref.at[t ^ k], sems.at[k]))
+        row_copies.append(pltpu.make_async_copy(row_refs[k], n_ref.at[t ^ k], sems.at[k]))
         up_copies.append(
-            pltpu.make_async_copy(sources[frames + k], u_ref.at[t ^ k], sems.at[frames + k])
-        )
-    shards = sources[2 * frames :]
+            pltpu.make_async_copy(
+                pair_refs[k & 1].at[k >> 1], u_ref.at[t ^ k], sems.at[frames + k]
+            )
+        )
     for k, shard in enumerate(shards):
         f = (2 * x + core) ^ (2 * (k & 1) + (k >> 1))
         qkv_copies.append(
@@ -295,26 +289,32 @@
 
     cut_x = swap(cut, "fsdp", 2)
     up_2 = swap(up_other, "tm", 2)
-    up_1 = swap(up_mine, "tm", 1)
-    n_mine, n_other = pl.pallas_call(
-        conv_kernel,
-        out_shape=(piece, piece),
-        in_specs=[anywhere] * 5,
-        out_specs=(in_vmem,) * 2,
-        scratch_shapes=[
-            pltpu.VMEM((neighbours.shape[1], pixels), jnp.int32),
-            pltpu.VMEM((2 * pixels, channels), narrow_type),
-            pltpu.VMEM(conv_taps.shape, jnp.float32),
-            pltpu.VMEM((1, channels), jnp.float32),
-            pltpu.SemaphoreType.DMA((5,)),
-        ],
-        compiler_params=pltpu.CompilerParams(vmem_limit_bytes=16 << 20),
-        name="conv",
-    )(neighbours.T, own, band, conv_taps, norm_gain.reshape(1, channels))
+
+    def conv(far):
+        return pl.pallas_call(
+            functools.partial(conv_kernel, far),
+            out_shape=piece,
+            in_specs=[anywhere] * 5,
+            out_specs=in_vmem,
+            scratch_shapes=[
+                pltpu.VMEM((neighbours.shape[1], pixels), jnp.int32),
+                pltpu.VMEM((pixels, neighbours.shape[1]), jnp.int32),
+                pltpu.VMEM((2 * pixels, channels), narrow_type),
+                pltpu.VMEM(conv_taps.shape, jnp.float32),
+                pltpu.VMEM((1, channels), jnp.float32),
+                pltpu.SemaphoreType.DMA((5,)),
+            ],
+            compiler_params=pltpu.CompilerParams(vmem_limit_bytes=16 << 20),
+            name="conv_far" if far else "conv_near",
+        )(neighbours.T, own, band, conv_taps, norm_gain.reshape(1, channels))
+
+    n_other = conv(True)
     row_3 = swap(n_other, "tm", 3)
     row_2 = swap(n_other, "tm", 2)
+    n_mine = conv(False)
     row_1 = swap(n_mine, "tm", 1)
-    up_3 = swap(up_2, "tm", 1)
+    up_own = jnp.stack([up_mine, up_2])
+    up_got = swap(up_own, "tm", 1)
     cut_c = swap(cut, "fsdp", 1)
     cut_xc = swap(cut_x, "fsdp", 1)
 
@@ -324,7 +324,7 @@
             jax.ShapeDtypeStruct((8, 2 * block, width), jnp.float32),
             jax.ShapeDtypeStruct((8, 2 * block, width), narrow_type),
         ),
-        in_specs=[anywhere] * 12,
+        in_specs=[anywhere] * 10,
         out_specs=(in_vmem, in_vmem),
         scratch_shapes=[
             pltpu.VMEM((4, half, channels), narrow_type),
@@ -338,7 +338,7 @@
         compiler_params=pltpu.CompilerParams(vmem_limit_bytes=32 << 20),
         name="attend",
     )(
-        *(n_mine, row_1, row_2, row_3), *(up_mine, up_1, up_2, up_3), *(cut, cut_x, cut_c, cut_xc)
+        n_mine, row_1, row_2, row_3, up_own, up_got, cut, cut_x, cut_c, cut_xc
     )
 
     def narrow(values):

time: 64.1 us -> 56.3 us (0.88)
  waiting for transfers between devices: 30.2 us -> 20.9 us
  starting transfers between devices: 24.2 us -> 25.5 us
  Pallas kernels: 8.1 us -> 9.09 us
  local copies, waits for them, and re-layouts: 1.11 us -> 0.23 us
    ppermute x17 -> x16, waiting for transfers between devices: 30.2 us -> 20.9 us  [swap(): lax.ppermute(values, axis, [(i, i ^ mask) for i in range(lax.axis_size(ax...]
    ppermute x17 -> x16, starting transfers between devices: 24.2 us -> 25.5 us  [swap(): lax.ppermute(values, axis, [(i, i ^ mask) for i in range(lax.axis_size(ax...]
    pallas_call x1 -> x2, Pallas kernels: 1.95 us -> 2.91 us  [conv(): pl.pallas_call(functools.partial(conv_kernel, far), out_shape=piece, in_s...]
    unnamed x12, local copies, waits for them, and re-layouts: 0.9 us -> 0.03 us
  transfers between devices with their start and end apart: 17 -> 16, of which waited for: 10 -> 9; matrix products, arithmetic and copies ran while one was open for 0% -> 0% of each run, Pallas kernels for 3% -> 5%
where the time goes in v2:
time: 56.3 us; the launch traced here: 56.2 us
  starting transfers between devices  25.5 us (45%)
  waiting for transfers between devices  20.9 us (37%)
  Pallas kernels  9.09 us (16%)
    ppermute x16, starting transfers between devices, swap(): lax.ppermute(values, axis, [(i, i ^ mask) for i in range(lax.axis_size(ax...  25.5 us
    ppermute x16, waiting for transfers between devices, swap(): lax.ppermute(values, axis, [(i, i ^ mask) for i in range(lax.axis_size(ax...  20.9 us
    pallas_call x1, Pallas kernels, split_form(): pl.pallas_call(block_kernel, out_shape=(jax.ShapeDtypeStruct((8, 2 * bloc...  3.59 us
    pallas_call x2, Pallas kernels, conv(): pl.pallas_call(functools.partial(conv_kernel, far), out_shape=piece, in_s...  2.91 us
    pallas_call x1, Pallas kernels, split_form(): pl.pallas_call(prep_kernel, out_shape=(piece, piece, jax.ShapeDtypeStruct...  1.92 us
  transfers between devices with their start and end apart: 16, of which 9 were waited for; matrix products, arithmetic and copies ran while one was open for 0% of the time, Pallas kernels for 5%

profile of v2, /device:TPU:0, one launch (start us, length us, event | category | flops | bytes accessed | tf_op | source)
XLA Modules:
  0.0 56.2 jit_solution(14222951090564616574)
XLA Ops:
  0.0 1.9 %prep.1 = (bf16[80,512]{1,0:T(8,128)(2,1)}, bf16[80,512]{1,0:T(8,128)(2,1)}, bf16[128,1280]{1,0:T(8,128)(2,1)}) custom-call(bf16[160,512]{1,0:T(8,128)(2,1)} %bitcast.49, bf16[128,1536]{1,0:T(8,128)(2,1)} %qkv_ref.1, bf16[128,512]{1,0:T(8,128)(2,1)} %out_w_ref.1), custom_call_target="tpu_custom_call" | custom-call | tf_op jit(solution)/shard_map/prep/pallas_call | solution.py:277
  1.9 0.0 copy-start.3
  1.9 3.0 %collective-permute-start.6 = (bf16[128,1280]{1,0:T(8,128)(2,1)}, bf16[128,1280]{1,0:T(8,128)(2,1)S(1)}, u32[]{:S(2)}, u32[]{:S(2)}) collective-permute-start(bf16[128,1280]{1,0:T(8,128)(2,1)} %get-tuple-element.12.refs_6_), channel_id=1, source_target_pairs={{0,2},{1,3},{2,0},{3,1},{4,6},{5,7},{6,4},{7,5},{8,10},{9,11},{10,... | collective-permute-start | bytes 983048 | tf_op jit(solution)/shard_map/ppermute | solution.py:17
  5.0 1.5 %collective-permute-start = (bf16[160,512]{1,0:T(8,128)(2,1)S(1)}, bf16[160,512]{1,0:T(8,128)(2,1)S(1)}, u32[]{:S(2)}, u32[]{:S(2)}) collective-permute-start(bf16[160,512]{1,0:T(8,128)(2,1)S(1)} %bitcast.41), channel_id=1, source_target_pairs={{0,16},{16,0},{1,17},{17,1},{2,18},{18,2},{3,19},{19,3},{4,20},{20... | collective-permute-start | bytes 491528 | tf_op jit(solution)/shard_map/ppermute | solution.py:17
  6.5 2.6 %collective-permute-start.4 = (bf16[80,512]{1,0:T(8,128)(2,1)}, bf16[80,512]{1,0:T(8,128)(2,1)S(1)}, u32[]{:S(2)}, u32[]{:S(2)}) collective-permute-start(bf16[80,512]{1,0:T(8,128)(2,1)} %get-tuple-element.11), channel_id=1, source_target_pairs={{0,8},{4,12},{8,0},{12,4},{1,9},{5,13},{9,1},{13,5},{2,10},{6,14},... | collective-permute-start | bytes 245768 | tf_op jit(solution)/shard_map/ppermute | solution.py:17
  9.1 3.8 %collective-permute-done.6.refs_7_ = bf16[128,1280]{1,0:T(8,128)(2,1)S(1)} collective-permute-done((bf16[128,1280]{1,0:T(8,128)(2,1)}, bf16[128,1280]{1,0:T(8,128)(2,1)S(1)}, u32[]{:S(2)}, u32[]{:S(2)}) %collective-permute-start.6) | collective-permute-done | bytes 327712 | tf_op jit(solution)/shard_map/ppermute | solution.py:17
  12.9 0.0 copy-start.5
  13.0 1.5 %conv_near.1.refs_0_ = bf16[80,512]{1,0:T(8,128)(2,1)S(1)} custom-call(s32[8,160]{1,0:T(8,128)S(1)} %bitcast.44, bf16[160,512]{1,0:T(8,128)(2,1)S(1)} %bitcast.42, bf16[160,512]{1,0:T(8,128)(2,1)S(1)} %collective-permute-done.band_hbm, f32[9,512]{1,0:T(8,128)S(1)} %copy-done.2, f32[1,512]{1,0:T(1,128)S(1)} %bitcast.46), custom_call_target="tpu_custom_call" | custom-call | tf_op jit(solution)/shard_map/conv_near/pallas_call | solution.py:294
  14.4 1.9 %collective-permute-start.1 = (bf16[80,512]{1,0:T(8,128)(2,1)S(1)}, bf16[80,512]{1,0:T(8,128)(2,1)S(1)}, u32[]{:S(2)}, u32[]{:S(2)}) collective-permute-start(bf16[80,512]{1,0:T(8,128)(2,1)S(1)} %conv_near.1.refs_0_), channel_id=1, source_target_pairs={{0,4},{4,0},{8,12},{12,8},{1,5},{5,1},{9,13},{13,9},{2,6},{6,2},{1... | collective-permute-start | bytes 245768 | tf_op jit(solution)/shard_map/ppermute | solution.py:17
  16.4 0.3 collective-permute-start.5
  16.6 1.4 %conv_far.1 = bf16[80,512]{1,0:T(8,128)(2,1)S(1)} custom-call(s32[8,160]{1,0:T(8,128)S(1)} %bitcast.45, bf16[160,512]{1,0:T(8,128)(2,1)S(1)} %bitcast.43, bf16[160,512]{1,0:T(8,128)(2,1)S(1)} %collective-permute-done.band_hbm, f32[9,512]{1,0:T(8,128)S(1)} %copy-done.2, f32[1,512]{1,0:T(1,128)S(1)} %bitcast.47), custom_call_target="tpu_custom_call" | custom-call | tf_op jit(solution)/shard_map/conv_far/pallas_call | solution.py:294
  18.1 2.9 %collective-permute-start.2 = (bf16[80,512]{1,0:T(8,128)(2,1)S(1)}, bf16[80,512]{1,0:T(8,128)(2,1)S(1)}, u32[]{:S(2)}, u32[]{:S(2)}) collective-permute-start(bf16[80,512]{1,0:T(8,128)(2,1)S(1)} %conv_far.1), channel_id=1, source_target_pairs={{0,8},{4,12},{8,0},{12,4},{1,9},{5,13},{9,1},{13,5},{2,10},{6,14},... | collective-permute-start | bytes 245768 | tf_op jit(solution)/shard_map/ppermute | solution.py:17
  21.0 2.7 %collective-permute-start.3 = (bf16[80,512]{1,0:T(8,128)(2,1)S(1)}, bf16[80,512]{1,0:T(8,128)(2,1)S(1)}, u32[]{:S(2)}, u32[]{:S(2)}) collective-permute-start(bf16[80,512]{1,0:T(8,128)(2,1)S(1)} %conv_far.1), channel_id=1, source_target_pairs={{0,12},{4,8},{8,4},{12,0},{1,13},{5,9},{9,5},{13,1},{2,14},{6,10},... | collective-permute-start | bytes 245768 | tf_op jit(solution)/shard_map/ppermute | solution.py:17
  23.7 0.8 %collective-permute-done.2.refs_2_ = bf16[80,512]{1,0:T(8,128)(2,1)S(1)} collective-permute-done((bf16[80,512]{1,0:T(8,128)(2,1)S(1)}, bf16[80,512]{1,0:T(8,128)(2,1)S(1)}, u32[]{:S(2)}, u32[]{:S(2)}) %collective-permute-start.2) | collective-permute-done | bytes 81952 | tf_op jit(solution)/shard_map/ppermute | solution.py:17
  24.5 4.3 %collective-permute-done.3.refs_3_ = bf16[80,512]{1,0:T(8,128)(2,1)S(1)} collective-permute-done((bf16[80,512]{1,0:T(8,128)(2,1)S(1)}, bf16[80,512]{1,0:T(8,128)(2,1)S(1)}, u32[]{:S(2)}, u32[]{:S(2)}) %collective-permute-start.3) | collective-permute-done | bytes 81952 | tf_op jit(solution)/shard_map/ppermute | solution.py:17
  28.8 3.6 %attend.1 = (f32[8,128,256]{2,1,0:T(8,128)S(1)}, bf16[8,128,256]{2,1,0:T(8,128)(2,1)S(1)}) custom-call(bf16[80,512]{1,0:T(8,128)(2,1)S(1)} %conv_near.1.refs_0_, bf16[80,512]{1,0:T(8,128)(2,1)S(1)} %collective-permute-done.1.refs_1_, bf16[80,512]{1,0:T(8,128)(2,1)S(1)} %collective-permute-done.2.refs_2_, bf16[80,512]{1,0:T(8,128)(2,1)S(1)} %collective-permute-done.3.refs_3_, ...), custom_call_target="tpu_custom_call" | custom-call | tf_op jit(solution)/shard_map/attend/pallas_call | solution.py:321
  32.4 0.1 collective-permute-start.9
  32.5 1.9 %collective-permute-done.9 = bf16[8,128,256]{2,1,0:T(8,128)(2,1)S(1)} collective-permute-done((bf16[8,128,256]{2,1,0:T(8,128)(2,1)S(1)}, bf16[8,128,256]{2,1,0:T(8,128)(2,1)S(1)}, u32[]{:S(2)}, u32[]{:S(2)}) %collective-permute-start.9) | collective-permute-done | bytes 524320 | tf_op jit(solution)/shard_map/ppermute | solution.py:17
  34.3 0.1 convert_add_fusion
  34.5 0.1 fusion.11
  34.6 1.6 %collective-permute-start.12 = (bf16[2,2,128,128]{3,2,1,0:T(8,128)(2,1)S(1)}, bf16[2,2,128,128]{3,2,1,0:T(8,128)(2,1)S(1)}, u32[]{:S(2)}, u32[]{:S(2)}) collective-permute-start(bf16[2,2,128,128]{3,2,1,0:T(8,128)(2,1)S(1)} %fusion.1), channel_id=1, source_target_pairs={{0,16},{16,0},{1,17},{17,1},{2,18},{18,2},{3,19},{19,3},{4,20},{20... | collective-permute-start | bytes 393224 | tf_op jit(solution)/shard_map/ppermute | solution.py:17
  36.2 1.6 %collective-permute-start.10 = (bf16[2,2,128,128]{3,2,1,0:T(8,128)(2,1)S(1)}, bf16[2,2,128,128]{3,2,1,0:T(8,128)(2,1)S(1)}, u32[]{:S(2)}, u32[]{:S(2)}) collective-permute-start(bf16[2,2,128,128]{3,2,1,0:T(8,128)(2,1)S(1)} %fusion), channel_id=1, source_target_pairs={{0,2},{1,3},{2,0},{3,1},{4,6},{5,7},{6,4},{7,5},{8,10},{9,11},{10,... | collective-permute-start | bytes 393224 | tf_op jit(solution)/shard_map/ppermute | solution.py:17
  37.8 2.4 %collective-permute-done.12 = bf16[2,2,128,128]{3,2,1,0:T(8,128)(2,1)S(1)} collective-permute-done((bf16[2,2,128,128]{3,2,1,0:T(8,128)(2,1)S(1)}, bf16[2,2,128,128]{3,2,1,0:T(8,128)(2,1)S(1)}, u32[]{:S(2)}, u32[]{:S(2)}) %collective-permute-start.12) | collective-permute-done | bytes 131104 | tf_op jit(solution)/shard_map/ppermute | solution.py:17
  40.3 1.6 %collective-permute-start.13 = (bf16[2,128,128]{2,1,0:T(8,128)(2,1)S(1)}, bf16[2,128,128]{2,1,0:T(8,128)(2,1)S(1)}, u32[]{:S(2)}, u32[]{:S(2)}) collective-permute-start(bf16[2,128,128]{2,1,0:T(8,128)(2,1)S(1)} %fusion.8), channel_id=1, source_target_pairs={{0,2},{1,3},{2,0},{3,1},{4,6},{5,7},{6,4},{7,5},{8,10},{9,11},{10,... | collective-permute-start | bytes 196616 | tf_op jit(solution)/shard_map/ppermute | solution.py:17
  41.9 1.6 %collective-permute-start.11 = (bf16[2,128,128]{2,1,0:T(8,128)(2,1)S(1)}, bf16[2,128,128]{2,1,0:T(8,128)(2,1)S(1)}, u32[]{:S(2)}, u32[]{:S(2)}) collective-permute-start(bf16[2,128,128]{2,1,0:T(8,128)(2,1)S(1)} %fusion.7), channel_id=1, source_target_pairs={{0,16},{16,0},{1,17},{17,1},{2,18},{18,2},{3,19},{19,3},{4,20},{20... | collective-permute-start | bytes 196616 | tf_op jit(solution)/shard_map/ppermute | solution.py:17
  43.5 1.1 %collective-permute-done.13 = bf16[2,128,128]{2,1,0:T(8,128)(2,1)S(1)} collective-permute-done((bf16[2,128,128]{2,1,0:T(8,128)(2,1)S(1)}, bf16[2,128,128]{2,1,0:T(8,128)(2,1)S(1)}, u32[]{:S(2)}, u32[]{:S(2)}) %collective-permute-start.13) | collective-permute-done | bytes 65568 | tf_op jit(solution)/shard_map/ppermute | solution.py:17
  44.6 1.6 %collective-permute-done.11 = bf16[2,128,128]{2,1,0:T(8,128)(2,1)S(1)} collective-permute-done((bf16[2,128,128]{2,1,0:T(8,128)(2,1)S(1)}, bf16[2,128,128]{2,1,0:T(8,128)(2,1)S(1)}, u32[]{:S(2)}, u32[]{:S(2)}) %collective-permute-start.11) | collective-permute-done | bytes 65568 | tf_op jit(solution)/shard_map/ppermute | solution.py:17
  46.3 2.9 %collective-permute-start.14 = (bf16[128,256]{1,0:T(8,128)(2,1)S(1)}, bf16[128,256]{1,0:T(8,128)(2,1)S(1)}, u32[]{:S(2)}, u32[]{:S(2)}) collective-permute-start(bf16[128,256]{1,0:T(8,128)(2,1)S(1)} %fusion.9), channel_id=1, source_target_pairs={{0,8},{4,12},{8,0},{12,4},{1,9},{5,13},{9,1},{13,5},{2,10},{6,14},... | collective-permute-start | bytes 196616 | tf_op jit(solution)/shard_map/ppermute | solution.py:17
  49.1 2.4 %collective-permute-done.14 = bf16[128,256]{1,0:T(8,128)(2,1)S(1)} collective-permute-done((bf16[128,256]{1,0:T(8,128)(2,1)S(1)}, bf16[128,256]{1,0:T(8,128)(2,1)S(1)}, u32[]{:S(2)}, u32[]{:S(2)}) %collective-permute-start.14) | collective-permute-done | bytes 65568 | tf_op jit(solution)/shard_map/ppermute | solution.py:17
  51.6 1.4 %collective-permute-start.15 = (bf16[64,256]{1,0:T(8,128)(2,1)S(1)}, bf16[64,256]{1,0:T(8,128)(2,1)S(1)}, u32[]{:S(2)}, u32[]{:S(2)}) collective-permute-start(bf16[64,256]{1,0:T(8,128)(2,1)S(1)} %fusion.10), channel_id=1, source_target_pairs={{0,4},{4,0},{8,12},{12,8},{1,5},{5,1},{9,13},{13,9},{2,6},{6,2},{1... | collective-permute-start | bytes 98312 | tf_op jit(solution)/shard_map/ppermute | solution.py:17
  52.9 2.6 %collective-permute-done.15.got_ref = bf16[64,256]{1,0:T(8,128)(2,1)S(1)} collective-permute-done((bf16[64,256]{1,0:T(8,128)(2,1)S(1)}, bf16[64,256]{1,0:T(8,128)(2,1)S(1)}, u32[]{:S(2)}, u32[]{:S(2)}) %collective-permute-start.15) | collective-permute-done | bytes 32800 | tf_op jit(solution)/shard_map/ppermute | solution.py:17
  55.5 0.7 %join.1 = f32[256,128]{1,0:T(8,128)} custom-call(f32[2,64,256]{2,1,0:T(8,128)S(1)} %bitcast.40, bf16[64,256]{1,0:T(8,128)(2,1)S(1)} %collective-permute-done.15.got_ref), custom_call_target="tpu_custom_call" | custom-call | tf_op jit(solution)/shard_map/join/pallas_call | solution.py:363
  (31 shorter events, 0.3 us)
Async XLA Ops:
  0.0 5.0 %copy-start = (bf16[1,1,160,512]{3,2,1,0:T(8,128)(2,1)S(1)}, bf16[1,1,160,512]{3,2,1,0:T(8,128)(2,1)}, u32[]{:S(2)}) copy-start(bf16[1,1,160,512]{3,2,1,0:T(8,128)(2,1)} %param.7) | copy-start | bytes 491524
  0.0 12.9 %copy-start.2 = (f32[9,512]{1,0:T(8,128)S(1)}, f32[9,512]{1,0:T(8,128)}, u32[]{:S(2)}) copy-start(f32[9,512]{1,0:T(8,128)} %taps_hbm.3) | copy-start | bytes 55300
  0.0 12.9 %copy-start.4 = (f32[512]{0:T(512)S(1)}, f32[512]{0:T(512)}, u32[]{:S(2)}) copy-start(f32[512]{0:T(512)} %param.10) | copy-start | bytes 6148
  1.9 11.0 %copy-start.3 = (s32[160,8]{0,1:T(8,128)S(1)}, s32[160,8]{0,1:T(8,128)}, u32[]{:S(2)}) copy-start(s32[160,8]{0,1:T(8,128)} %param.8) | copy-start | bytes 15364
  1.9 11.0 %collective-permute-start.6 = (bf16[128,1280]{1,0:T(8,128)(2,1)}, bf16[128,1280]{1,0:T(8,128)(2,1)S(1)}, u32[]{:S(2)}, u32[]{:S(2)}) collective-permute-start(bf16[128,1280]{1,0:T(8,128)(2,1)} %get-tuple-element.12.refs_6_), channel_id=1, source_target_pairs={{0,2},{1,3},{2,0},{3,1},{4,6},{5,7},{6,4},{7,5},{8,10},{9,11},{10,... | collective-permute-start | bytes 983048 | tf_op jit(solution)/shard_map/ppermute | solution.py:17
  5.0 7.9 %collective-permute-start = (bf16[160,512]{1,0:T(8,128)(2,1)S(1)}, bf16[160,512]{1,0:T(8,128)(2,1)S(1)}, u32[]{:S(2)}, u32[]{:S(2)}) collective-permute-start(bf16[160,512]{1,0:T(8,128)(2,1)S(1)} %bitcast.41), channel_id=1, source_target_pairs={{0,16},{16,0},{1,17},{17,1},{2,18},{18,2},{3,19},{19,3},{4,20},{20... | collective-permute-start | bytes 491528 | tf_op jit(solution)/shard_map/ppermute | solution.py:17
  6.5 9.8 %collective-permute-start.4 = (bf16[80,512]{1,0:T(8,128)(2,1)}, bf16[80,512]{1,0:T(8,128)(2,1)S(1)}, u32[]{:S(2)}, u32[]{:S(2)}) collective-permute-start(bf16[80,512]{1,0:T(8,128)(2,1)} %get-tuple-element.11), channel_id=1, source_target_pairs={{0,8},{4,12},{8,0},{12,4},{1,9},{5,13},{9,1},{13,5},{2,10},{6,14},... | collective-permute-start | bytes 245768 | tf_op jit(solution)/shard_map/ppermute | solution.py:17
  9.1 19.6 %collective-permute-start.7 = (bf16[128,1280]{1,0:T(8,128)(2,1)}, bf16[128,1280]{1,0:T(8,128)(2,1)S(1)}, u32[]{:S(2)}, u32[]{:S(2)}) collective-permute-start(bf16[128,1280]{1,0:T(8,128)(2,1)} %get-tuple-element.12.refs_6_), channel_id=1, source_target_pairs={{0,1},{1,0},{2,3},{3,2},{4,5},{5,4},{6,7},{7,6},{8,9},{9,8},{10,11... | collective-permute-start | bytes 983048 | tf_op jit(solution)/shard_map/ppermute | solution.py:17
  12.9 15.8 %collective-permute-start.8 = (bf16[128,1280]{1,0:T(8,128)(2,1)S(1)}, bf16[128,1280]{1,0:T(8,128)(2,1)S(1)}, u32[]{:S(2)}, u32[]{:S(2)}) collective-permute-start(bf16[128,1280]{1,0:T(8,128)(2,1)S(1)} %collective-permute-done.6.refs_7_), channel_id=1, source_target_pairs={{0,1},{1,0},{2,3},{3,2},{4,5},{5,4},{6,7},{7,6},{8,9},{9,8},{10,11... | collective-permute-start | bytes 983048 | tf_op jit(solution)/shard_map/ppermute | solution.py:17
  12.9 3.4 %copy-start.5 = (bf16[80,512]{1,0:T(8,128)(2,1)S(1)}, bf16[80,512]{1,0:T(8,128)(2,1)}, u32[]{:S(2)}) copy-start(bf16[80,512]{1,0:T(8,128)(2,1)} %get-tuple-element.10) | copy-start | bytes 245764
  14.4 6.5 %collective-permute-start.1 = (bf16[80,512]{1,0:T(8,128)(2,1)S(1)}, bf16[80,512]{1,0:T(8,128)(2,1)S(1)}, u32[]{:S(2)}, u32[]{:S(2)}) collective-permute-start(bf16[80,512]{1,0:T(8,128)(2,1)S(1)} %conv_near.1.refs_0_), channel_id=1, source_target_pairs={{0,4},{4,0},{8,12},{12,8},{1,5},{5,1},{9,13},{13,9},{2,6},{6,2},{1... | collective-permute-start | bytes 245768 | tf_op jit(solution)/shard_map/ppermute | solution.py:17
  16.3 12.4 %copy-start.1 = (bf16[128,1280]{1,0:T(8,128)(2,1)S(1)}, bf16[128,1280]{1,0:T(8,128)(2,1)}, u32[]{:S(2)}) copy-start(bf16[128,1280]{1,0:T(8,128)(2,1)} %get-tuple-element.12.refs_6_) | copy-start | bytes 983044
  16.4 12.4 %collective-permute-start.5 = (bf16[2,80,512]{2,1,0:T(8,128)(2,1)S(1)}, bf16[2,80,512]{2,1,0:T(8,128)(2,1)S(1)}, u32[]{:S(2)}, u32[]{:S(2)}) collective-permute-start(bf16[2,80,512]{2,1,0:T(8,128)(2,1)S(1)} %pad_maximum_fusion.refs_4_), channel_id=1, source_target_pairs={{0,4},{4,0},{8,12},{12,8},{1,5},{5,1},{9,13},{13,9},{2,6},{6,2},{1... | collective-permute-start | bytes 491528 | tf_op jit(solution)/shard_map/ppermute | solution.py:17
  18.1 6.4 %collective-permute-start.2 = (bf16[80,512]{1,0:T(8,128)(2,1)S(1)}, bf16[80,512]{1,0:T(8,128)(2,1)S(1)}, u32[]{:S(2)}, u32[]{:S(2)}) collective-permute-start(bf16[80,512]{1,0:T(8,128)(2,1)S(1)} %conv_far.1), channel_id=1, source_target_pairs={{0,8},{4,12},{8,0},{12,4},{1,9},{5,13},{9,1},{13,5},{2,10},{6,14},... | collective-permute-start | bytes 245768 | tf_op jit(solution)/shard_map/ppermute | solution.py:17
  21.0 7.8 %collective-permute-start.3 = (bf16[80,512]{1,0:T(8,128)(2,1)S(1)}, bf16[80,512]{1,0:T(8,128)(2,1)S(1)}, u32[]{:S(2)}, u32[]{:S(2)}) collective-permute-start(bf16[80,512]{1,0:T(8,128)(2,1)S(1)} %conv_far.1), channel_id=1, source_target_pairs={{0,12},{4,8},{8,4},{12,0},{1,13},{5,9},{9,5},{13,1},{2,14},{6,10},... | collective-permute-start | bytes 245768 | tf_op jit(solution)/shard_map/ppermute | solution.py:17
  32.4 2.0 %collective-permute-start.9 = (bf16[8,128,256]{2,1,0:T(8,128)(2,1)S(1)}, bf16[8,128,256]{2,1,0:T(8,128)(2,1)S(1)}, u32[]{:S(2)}, u32[]{:S(2)}) collective-permute-start(bf16[8,128,256]{2,1,0:T(8,128)(2,1)S(1)} %get-tuple-element.14), channel_id=1, source_target_pairs={{0,1},{1,0},{2,3},{3,2},{4,5},{5,4},{6,7},{7,6},{8,9},{9,8},{10,11... | collective-permute-start | bytes 1572872 | tf_op jit(solution)/shard_map/ppermute | solution.py:17
  34.6 5.6 %collective-permute-start.12 = (bf16[2,2,128,128]{3,2,1,0:T(8,128)(2,1)S(1)}, bf16[2,2,128,128]{3,2,1,0:T(8,128)(2,1)S(1)}, u32[]{:S(2)}, u32[]{:S(2)}) collective-permute-start(bf16[2,2,128,128]{3,2,1,0:T(8,128)(2,1)S(1)} %fusion.1), channel_id=1, source_target_pairs={{0,16},{16,0},{1,17},{17,1},{2,18},{18,2},{3,19},{19,3},{4,20},{20... | collective-permute-start | bytes 393224 | tf_op jit(solution)/shard_map/ppermute | solution.py:17
  36.2 5.6 %collective-permute-start.10 = (bf16[2,2,128,128]{3,2,1,0:T(8,128)(2,1)S(1)}, bf16[2,2,128,128]{3,2,1,0:T(8,128)(2,1)S(1)}, u32[]{:S(2)}, u32[]{:S(2)}) collective-permute-start(bf16[2,2,128,128]{3,2,1,0:T(8,128)(2,1)S(1)} %fusion), channel_id=1, source_target_pairs={{0,2},{1,3},{2,0},{3,1},{4,6},{5,7},{6,4},{7,5},{8,10},{9,11},{10,... | collective-permute-start | bytes 393224 | tf_op jit(solution)/shard_map/ppermute | solution.py:17
  40.3 4.3 %collective-permute-start.13 = (bf16[2,128,128]{2,1,0:T(8,128)(2,1)S(1)}, bf16[2,128,128]{2,1,0:T(8,128)(2,1)S(1)}, u32[]{:S(2)}, u32[]{:S(2)}) collective-permute-start(bf16[2,128,128]{2,1,0:T(8,128)(2,1)S(1)} %fusion.8), channel_id=1, source_target_pairs={{0,2},{1,3},{2,0},{3,1},{4,6},{5,7},{6,4},{7,5},{8,10},{9,11},{10,... | collective-permute-start | bytes 196616 | tf_op jit(solution)/shard_map/ppermute | solution.py:17
  41.9 4.3 %collective-permute-start.11 = (bf16[2,128,128]{2,1,0:T(8,128)(2,1)S(1)}, bf16[2,128,128]{2,1,0:T(8,128)(2,1)S(1)}, u32[]{:S(2)}, u32[]{:S(2)}) collective-permute-start(bf16[2,128,128]{2,1,0:T(8,128)(2,1)S(1)} %fusion.7), channel_id=1, source_target_pairs={{0,16},{16,0},{1,17},{17,1},{2,18},{18,2},{3,19},{19,3},{4,20},{20... | collective-permute-start | bytes 196616 | tf_op jit(solution)/shard_map/ppermute | solution.py:17
  46.3 5.2 %collective-permute-start.14 = (bf16[128,256]{1,0:T(8,128)(2,1)S(1)}, bf16[128,256]{1,0:T(8,128)(2,1)S(1)}, u32[]{:S(2)}, u32[]{:S(2)}) collective-permute-start(bf16[128,256]{1,0:T(8,128)(2,1)S(1)} %fusion.9), channel_id=1, source_target_pairs={{0,8},{4,12},{8,0},{12,4},{1,9},{5,13},{9,1},{13,5},{2,10},{6,14},... | collective-permute-start | bytes 196616 | tf_op jit(solution)/shard_map/ppermute | solution.py:17
  51.6 4.0 %collective-permute-start.15 = (bf16[64,256]{1,0:T(8,128)(2,1)S(1)}, bf16[64,256]{1,0:T(8,128)(2,1)S(1)}, u32[]{:S(2)}, u32[]{:S(2)}) collective-permute-start(bf16[64,256]{1,0:T(8,128)(2,1)S(1)} %fusion.10), channel_id=1, source_target_pairs={{0,4},{4,0},{8,12},{12,8},{1,5},{5,1},{9,13},{13,9},{2,6},{6,2},{1... | collective-permute-start | bytes 98312 | tf_op jit(solution)/shard_map/ppermute | solution.py:17

commit v3 on v2

--- a/solution.py
+++ b/solution.py
@@ -98,94 +98,59 @@
     out_ref[...] = (hidden * inverse * gain_ref[...]).astype(jnp.bfloat16)
 
 
-def block_kernel(*refs):
+def head_sums(products, width):
+    depth = width * 2 // HEADS
+    row_head = lax.broadcasted_iota(jnp.int32, (width, width), 0) // depth
+    col_head = lax.broadcasted_iota(jnp.int32, (width, width), 1) // depth
+    same = jnp.where(row_head == col_head, 0.125, 0.0).astype(jnp.bfloat16)
+    pixels = products[0].shape[0]
+    stacked = jnp.concatenate(products, axis=0)
+    high = stacked.astype(jnp.bfloat16)
+    low = (stacked - high.astype(jnp.float32)).astype(jnp.bfloat16)
+    total = jnp.dot(high, same, preferred_element_type=jnp.float32)
+    total = total + jnp.dot(low, same, preferred_element_type=jnp.float32)
+    return [total[i * pixels : (i + 1) * pixels] for i in range(len(products))]
+
+
+def wide(ref, frame, third, width, pixels):
+    rows = ref[frame * pixels : (frame + 1) * pixels, third * width : (third + 1) * width]
+    return rows.astype(jnp.float32)
+
+
+def shard_rows(k, rows):
+    _, _, _, _, x, core = place()
+    f = (2 * x + core) ^ (2 * (k & 1) + (k >> 1))
+    return pl.ds(pl.multiple_of(f * rows, 128), rows)
+
+
+def forward_kernel(*refs):
     frames = 4
-    row_refs, pair_refs, shards, refs = refs[:4], refs[4:6], refs[6:10], refs[10:]
-    keep_ref, send_ref, n_ref, u_ref, qkv_ref, out_w_ref, sums_ref, out_sums_ref, sems = refs
-    _, t, _, zh, x, core = place()
+    row_refs, shards, refs = refs[:4], refs[4:8], refs[8:]
+    qkv_ref, weights_ref, attended_ref, n_ref, w_ref, sems = refs
+    _, t, _, _, _, _ = place()
     pixels, channels = row_refs[0].shape
-    width, depth = out_w_ref.shape[0], channels // HEADS
+    width = channels // 2
     rows = shards[0].shape[0]
-    up_copies, row_copies, qkv_copies = [], [], []
-    for k in range(frames):
-        row_copies.append(pltpu.make_async_copy(row_refs[k], n_ref.at[t ^ k], sems.at[k]))
-        up_copies.append(
-            pltpu.make_async_copy(
-                pair_refs[k & 1].at[k >> 1], u_ref.at[t ^ k], sems.at[frames + k]
-            )
+    copies = [pltpu.make_async_copy(row_refs[k], n_ref.at[t ^ k], sems.at[k]) for k in range(frames)]
+    copies += [
+        pltpu.make_async_copy(
+            shards[k].at[:, pl.ds(0, 3 * width)], w_ref.at[shard_rows(k, rows)], sems.at[frames + k]
         )
-    for k, shard in enumerate(shards):
-        f = (2 * x + core) ^ (2 * (k & 1) + (k >> 1))
-        qkv_copies.append(
-            pltpu.make_async_copy(
-                shard.at[:, pl.ds(0, 3 * width)],
-                qkv_ref.at[pl.ds(pl.multiple_of(f * rows, 128), rows)],
-                sems.at[2 * frames + k],
-            )
-        )
-
-    def out_copy(shard, k):
-        start = pl.multiple_of((core ^ k) * rows, 128)
-        return pltpu.make_async_copy(
-            shard.at[:, pl.ds(3 * width, channels)],
-            out_w_ref.at[pl.ds(start, rows)],
-            sems.at[3 * frames + k],
-        )
-
-    start_all(row_copies + qkv_copies + up_copies)
-    for k in range(2):
-
-        @pl.when(x == zh)
-        def _(k=k):
-            out_copy(shards[2 * k], k).start()
-
-        @pl.when(x != zh)
-        def _(k=k):
-            out_copy(shards[2 * k + 1], k).start()
-
-    for copy in row_copies + qkv_copies:
+        for k in range(4)
+    ]
+    start_all(copies)
+    for copy in copies:
         copy.wait()
     normed = n_ref[...].reshape(frames * pixels, channels)
-    qkv = jnp.dot(normed, qkv_ref[...], preferred_element_type=jnp.float32).astype(jnp.bfloat16)
-    for copy in up_copies + [out_copy(shards[2 * k], k) for k in range(2)]:
-        copy.wait()
-    upstream = u_ref[...].reshape(frames * pixels, channels)
-    grads = lax.dot_general(
-        upstream, out_w_ref[...], (((1,), (1,)), ((), ())), preferred_element_type=jnp.float32
-    ).astype(jnp.bfloat16)
-
-    def part(values, frame, third=0):
-        rows = values[frame * pixels : (frame + 1) * pixels]
-        return rows[:, third * width : (third + 1) * width].astype(jnp.float32)
-
-    q = [part(qkv, i, 0) for i in range(frames)]
-    k = [part(qkv, i, 1) for i in range(frames)]
-    v = [part(qkv, i, 2) for i in range(frames)]
-    g = [part(grads, i) for i in range(frames)]
-    row_head = lax.broadcasted_iota(jnp.int32, (width, width), 0) // depth
-    col_head = lax.broadcasted_iota(jnp.int32, (width, width), 1) // depth
-    same = jnp.where(row_head == col_head, 1.0, 0.0).astype(jnp.bfloat16)
-
-    def head_sums(products):
-        stacked = jnp.concatenate(products, axis=0)
-        high = stacked.astype(jnp.bfloat16)
-        low = (stacked - high.astype(jnp.float32)).astype(jnp.bfloat16)
-        total = jnp.dot(high, same, preferred_element_type=jnp.float32)
-        total = total + jnp.dot(low, same, preferred_element_type=jnp.float32)
-        return [total[i * pixels : (i + 1) * pixels] for i in range(len(products))]
-
-    def rounded(values):
-        return values.astype(jnp.bfloat16).astype(jnp.float32)
-
-    attended, dq = [], []
-    dk, dv = [None] * frames, [None] * frames
-
-    def plus(total, term):
-        return term if total is None else total + term
-
+    qkv_ref[...] = jnp.dot(normed, w_ref[...], preferred_element_type=jnp.float32).astype(
+        jnp.bfloat16
+    )
+    q, k, v = (
+        [wide(qkv_ref, i, third, width, pixels) for i in range(frames)] for third in range(3)
+    )
+    slot = 0
     for i in range(frames):
-        scores = head_sums([q[i] * k[u] for u in range(i + 1)])
-        scores = [s * 0.125 for s in scores]
+        scores = head_sums([q[i] * k[u] for u in range(i + 1)], width)
         largest = scores[0]
         for s in scores[1:]:
             largest = jnp.maximum(largest, s)
@@ -194,20 +159,86 @@
         for p in powers[1:]:
             total = total + p
         scale = 1.0 / total
-        weights = [rounded(p * scale) for p in powers]
-        dprob = head_sums([g[i] * v[u] for u in range(i + 1)])
+        seen = None
+        for u in range(i + 1):
+            weights = (powers[u] * scale).astype(jnp.bfloat16)
+            weights_ref[slot] = weights
+            slot += 1
+            term = weights.astype(jnp.float32) * v[u]
+            seen = term if seen is None else seen + term
+        attended_ref[i * pixels : (i + 1) * pixels, :] = seen.astype(jnp.bfloat16)
+
+
+def backward_kernel(*refs):
+    frames = 4
+    row_refs, pair_refs, shards, refs = refs[:4], refs[4:6], refs[6:10], refs[10:]
+    qkv_ref, weights_ref, attended_ref, refs = refs[0], refs[1], refs[2], refs[3:]
+    keep_ref, send_ref, n_ref, u_ref, out_w_ref, sums_ref, out_sums_ref, sems = refs
+    _, t, _, zh, x, core = place()
+    pixels, channels = row_refs[0].shape
+    width = out_w_ref.shape[0]
+    rows = shards[0].shape[0]
+    row_copies = [
+        pltpu.make_async_copy(row_refs[k], n_ref.at[t ^ k], sems.at[k]) for k in range(frames)
+    ]
+    up_copies = [
+        pltpu.make_async_copy(pair_refs[k & 1].at[k >> 1], u_ref.at[t ^ k], sems.at[frames + k])
+        for k in range(frames)
+    ]
+
+    def out_copy(shard, k):
+        start = pl.multiple_of((core ^ k) * rows, 128)
+        return pltpu.make_async_copy(
+            shard.at[:, pl.ds(3 * width, channels)],
+            out_w_ref.at[pl.ds(start, rows)],
+            sems.at[2 * frames + k],
+        )
+
+    start_all(up_copies)
+    for k in range(2):
+
+        @pl.when(x == zh)
+        def _(k=k):
+            out_copy(shards[2 * k], k).start()
+
+        @pl.when(x != zh)
+        def _(k=k):
+            out_copy(shards[2 * k + 1], k).start()
+
+    start_all(row_copies)
+    for copy in up_copies + [out_copy(shards[2 * k], k) for k in range(2)]:
+        copy.wait()
+    upstream = u_ref[...].reshape(frames * pixels, channels)
+    grads = lax.dot_general(
+        upstream, out_w_ref[...], (((1,), (1,)), ((), ())), preferred_element_type=jnp.float32
+    ).astype(jnp.bfloat16)
+    g = [grads[i * pixels : (i + 1) * pixels].astype(jnp.float32) for i in range(frames)]
+    q, k, v = (
+        [wide(qkv_ref, i, third, width, pixels) for i in range(frames)] for third in range(3)
+    )
+    dq, dk, dv = [], [None] * frames, [None] * frames
+
+    def plus(total, term):
+        return term if total is None else total + term
+
+    slot = 0
+    for i in range(frames):
+        dprob = head_sums([g[i] * v[u] for u in range(i + 1)], width)
+        weights = [weights_ref[slot + u].astype(jnp.float32) for u in range(i + 1)]
+        slot += i + 1
         delta = weights[0] * dprob[0]
         for u in range(1, i + 1):
             delta = delta + weights[u] * dprob[u]
-        seen, grad_q = None, None
+        grad_q = None
         for u in range(i + 1):
-            ds = rounded(weights[u] * (dprob[u] - delta) * 0.125)
-            seen = plus(seen, weights[u] * v[u])
+            ds = (weights[u] * (dprob[u] - delta)).astype(jnp.bfloat16).astype(jnp.float32)
             grad_q = plus(grad_q, ds * k[u])
             dk[u] = plus(dk[u], ds * q[i])
             dv[u] = plus(dv[u], weights[u] * g[i])
-        attended.append(seen.astype(jnp.bfloat16))
         dq.append(grad_q.astype(jnp.bfloat16))
+    for copy in row_copies:
+        copy.wait()
+    normed = n_ref[...].reshape(frames * pixels, channels)
     thirds = (dq, [d.astype(jnp.bfloat16) for d in dk], [d.astype(jnp.bfloat16) for d in dv])
 
     def over_rows(lhs, rhs):
@@ -219,7 +250,7 @@
         grad = over_rows(normed, jnp.concatenate(pieces, axis=0))
         for lane in range(0, width, 128):
             sums_ref[lane // 128, pl.ds(m, channels, stride=3), :] = grad[:, lane : lane + 128]
-    out_sums_ref[...] = over_rows(jnp.concatenate(attended, axis=0), upstream)
+    out_sums_ref[...] = over_rows(attended_ref[...], upstream)
 
     block = 64
     for x in range(2):
@@ -318,27 +349,44 @@
     cut_c = swap(cut, "fsdp", 1)
     cut_xc = swap(cut_x, "fsdp", 1)
 
+    qkv, weights, attended = pl.pallas_call(
+        forward_kernel,
+        out_shape=(
+            jax.ShapeDtypeStruct((4 * half, 3 * width), narrow_type),
+            jax.ShapeDtypeStruct((10, half, width), narrow_type),
+            jax.ShapeDtypeStruct((4 * half, width), narrow_type),
+        ),
+        in_specs=[anywhere] * 8,
+        out_specs=(in_vmem,) * 3,
+        scratch_shapes=[
+            pltpu.VMEM((4, half, channels), narrow_type),
+            pltpu.VMEM((channels, 3 * width), narrow_type),
+            pltpu.SemaphoreType.DMA((8,)),
+        ],
+        compiler_params=pltpu.CompilerParams(vmem_limit_bytes=24 << 20),
+        name="forward",
+    )(n_mine, row_1, row_2, row_3, cut, cut_x, cut_c, cut_xc)
     keep, send = pl.pallas_call(
-        block_kernel,
+        backward_kernel,
         out_shape=(
             jax.ShapeDtypeStruct((8, 2 * block, width), jnp.float32),
             jax.ShapeDtypeStruct((8, 2 * block, width), narrow_type),
         ),
-        in_specs=[anywhere] * 10,
+        in_specs=[anywhere] * 10 + [in_vmem] * 3,
         out_specs=(in_vmem, in_vmem),
         scratch_shapes=[
             pltpu.VMEM((4, half, channels), narrow_type),
             pltpu.VMEM((4, half, channels), narrow_type),
-            pltpu.VMEM((channels, 3 * width), narrow_type),
             pltpu.VMEM((width, channels), narrow_type),
             pltpu.VMEM((width // 128, 3 * channels, 128), jnp.float32),
             pltpu.VMEM((width, channels), jnp.float32),
-            pltpu.SemaphoreType.DMA((14,)),
+            pltpu.SemaphoreType.DMA((10,)),
         ],
-        compiler_params=pltpu.CompilerParams(vmem_limit_bytes=32 << 20),
-        name="attend",
+        compiler_params=pltpu.CompilerParams(vmem_limit_bytes=28 << 20),
+        name="backward",
     )(
-        n_mine, row_1, row_2, row_3, up_own, up_got, cut, cut_x, cut_c, cut_xc
+        n_mine, row_1, row_2, row_3, up_own, up_got, cut, cut_x, cut_c, cut_xc,
+        qkv, weights, attended,
     )
 
     def narrow(values):

time: 56.3 us -> 57 us (1.012)
  Pallas kernels: 9.09 us -> 9.77 us
    pallas_call x1 -> x2, Pallas kernels: 3.59 us -> 4.29 us  [the longest x1 2.82 us: split_form(): pl.pallas_call(backward_kernel, out_shape=(jax.ShapeDtypeStruct((8, 2 * b...]
  transfers between devices with their start and end apart: 16 -> 16, of which waited for: 9 -> 9; matrix products, arithmetic and copies ran while one was open for 0% -> 0% of each run, Pallas kernels for 5% -> 8%
where the time goes in v3:
time: 57 us; the launch traced here: 56.9 us
  starting transfers between devices  25.5 us (45%)
  waiting for transfers between devices  20.9 us (37%)
  Pallas kernels  9.77 us (17%)
    ppermute x16, starting transfers between devices, swap(): lax.ppermute(values, axis, [(i, i ^ mask) for i in range(lax.axis_size(ax...  25.5 us
    ppermute x16, waiting for transfers between devices, swap(): lax.ppermute(values, axis, [(i, i ^ mask) for i in range(lax.axis_size(ax...  20.9 us
    pallas_call x2, Pallas kernels, conv(): pl.pallas_call(functools.partial(conv_kernel, far), out_shape=piece, in_s...  2.9 us
    pallas_call x1, Pallas kernels, split_form(): pl.pallas_call(backward_kernel, out_shape=(jax.ShapeDtypeStruct((8, 2 * b...  2.82 us
    pallas_call x1, Pallas kernels, split_form(): pl.pallas_call(prep_kernel, out_shape=(piece, piece, jax.ShapeDtypeStruct...  1.91 us
    pallas_call x1, Pallas kernels, split_form(): pl.pallas_call(forward_kernel, out_shape=(jax.ShapeDtypeStruct((4 * half,...  1.47 us
  transfers between devices with their start and end apart: 16, of which 9 were waited for; matrix products, arithmetic and copies ran while one was open for 0% of the time, Pallas kernels for 8%

profile of v3, /device:TPU:0, one launch (start us, length us, event | category | flops | bytes accessed | tf_op | source)
XLA Modules:
  0.0 56.9 jit_solution(8673972906284785925)
XLA Ops:
  0.0 1.9 %prep.1 = (bf16[80,512]{1,0:T(8,128)(2,1)}, bf16[80,512]{1,0:T(8,128)(2,1)}, bf16[128,1280]{1,0:T(8,128)(2,1)}) custom-call(bf16[160,512]{1,0:T(8,128)(2,1)} %bitcast.49, bf16[128,1536]{1,0:T(8,128)(2,1)} %qkv_ref.1, bf16[128,512]{1,0:T(8,128)(2,1)} %out_w_ref.1), custom_call_target="tpu_custom_call" | custom-call | tf_op jit(solution)/shard_map/prep/pallas_call | solution.py:308
  1.9 0.0 copy-start.3
  1.9 3.0 %collective-permute-start.6 = (bf16[128,1280]{1,0:T(8,128)(2,1)}, bf16[128,1280]{1,0:T(8,128)(2,1)S(1)}, u32[]{:S(2)}, u32[]{:S(2)}) collective-permute-start(bf16[128,1280]{1,0:T(8,128)(2,1)} %get-tuple-element.15.refs_4_.refs_6_), channel_id=1, source_target_pairs={{0,2},{1,3},{2,0},{3,1},{4,6},{5,7},{6,4},{7,5},{8,10},{9,11},{10,... | collective-permute-start | bytes 983048 | tf_op jit(solution)/shard_map/ppermute | solution.py:17
  5.0 1.5 %collective-permute-start = (bf16[160,512]{1,0:T(8,128)(2,1)S(1)}, bf16[160,512]{1,0:T(8,128)(2,1)S(1)}, u32[]{:S(2)}, u32[]{:S(2)}) collective-permute-start(bf16[160,512]{1,0:T(8,128)(2,1)S(1)} %bitcast.41), channel_id=1, source_target_pairs={{0,16},{16,0},{1,17},{17,1},{2,18},{18,2},{3,19},{19,3},{4,20},{20... | collective-permute-start | bytes 491528 | tf_op jit(solution)/shard_map/ppermute | solution.py:17
  6.5 2.6 %collective-permute-start.4 = (bf16[80,512]{1,0:T(8,128)(2,1)}, bf16[80,512]{1,0:T(8,128)(2,1)S(1)}, u32[]{:S(2)}, u32[]{:S(2)}) collective-permute-start(bf16[80,512]{1,0:T(8,128)(2,1)} %get-tuple-element.14), channel_id=1, source_target_pairs={{0,8},{4,12},{8,0},{12,4},{1,9},{5,13},{9,1},{13,5},{2,10},{6,14},... | collective-permute-start | bytes 245768 | tf_op jit(solution)/shard_map/ppermute | solution.py:17
  9.1 3.8 %collective-permute-done.6.refs_5_.refs_7_ = bf16[128,1280]{1,0:T(8,128)(2,1)S(1)} collective-permute-done((bf16[128,1280]{1,0:T(8,128)(2,1)}, bf16[128,1280]{1,0:T(8,128)(2,1)S(1)}, u32[]{:S(2)}, u32[]{:S(2)}) %collective-permute-start.6) | collective-permute-done | bytes 327712 | tf_op jit(solution)/shard_map/ppermute | solution.py:17
  12.9 1.5 %conv_near.1.refs_0_ = bf16[80,512]{1,0:T(8,128)(2,1)S(1)} custom-call(s32[8,160]{1,0:T(8,128)S(1)} %bitcast.44, bf16[160,512]{1,0:T(8,128)(2,1)S(1)} %bitcast.42, bf16[160,512]{1,0:T(8,128)(2,1)S(1)} %collective-permute-done.band_hbm, f32[9,512]{1,0:T(8,128)S(1)} %copy-done.2, f32[1,512]{1,0:T(1,128)S(1)} %bitcast.46), custom_call_target="tpu_custom_call" | custom-call | tf_op jit(solution)/shard_map/conv_near/pallas_call | solution.py:325
  14.4 1.9 %collective-permute-start.1 = (bf16[80,512]{1,0:T(8,128)(2,1)S(1)}, bf16[80,512]{1,0:T(8,128)(2,1)S(1)}, u32[]{:S(2)}, u32[]{:S(2)}) collective-permute-start(bf16[80,512]{1,0:T(8,128)(2,1)S(1)} %conv_near.1.refs_0_), channel_id=1, source_target_pairs={{0,4},{4,0},{8,12},{12,8},{1,5},{5,1},{9,13},{13,9},{2,6},{6,2},{1... | collective-permute-start | bytes 245768 | tf_op jit(solution)/shard_map/ppermute | solution.py:17
  16.3 0.3 collective-permute-start.5
  16.6 1.4 %conv_far.1 = bf16[80,512]{1,0:T(8,128)(2,1)S(1)} custom-call(s32[8,160]{1,0:T(8,128)S(1)} %bitcast.45, bf16[160,512]{1,0:T(8,128)(2,1)S(1)} %bitcast.43, bf16[160,512]{1,0:T(8,128)(2,1)S(1)} %collective-permute-done.band_hbm, f32[9,512]{1,0:T(8,128)S(1)} %copy-done.2, f32[1,512]{1,0:T(1,128)S(1)} %bitcast.47), custom_call_target="tpu_custom_call" | custom-call | tf_op jit(solution)/shard_map/conv_far/pallas_call | solution.py:325
  18.1 2.9 %collective-permute-start.2 = (bf16[80,512]{1,0:T(8,128)(2,1)S(1)}, bf16[80,512]{1,0:T(8,128)(2,1)S(1)}, u32[]{:S(2)}, u32[]{:S(2)}) collective-permute-start(bf16[80,512]{1,0:T(8,128)(2,1)S(1)} %conv_far.1), channel_id=1, source_target_pairs={{0,8},{4,12},{8,0},{12,4},{1,9},{5,13},{9,1},{13,5},{2,10},{6,14},... | collective-permute-start | bytes 245768 | tf_op jit(solution)/shard_map/ppermute | solution.py:17
  21.0 2.7 %collective-permute-start.3 = (bf16[80,512]{1,0:T(8,128)(2,1)S(1)}, bf16[80,512]{1,0:T(8,128)(2,1)S(1)}, u32[]{:S(2)}, u32[]{:S(2)}) collective-permute-start(bf16[80,512]{1,0:T(8,128)(2,1)S(1)} %conv_far.1), channel_id=1, source_target_pairs={{0,12},{4,8},{8,4},{12,0},{1,13},{5,9},{9,5},{13,1},{2,14},{6,10},... | collective-permute-start | bytes 245768 | tf_op jit(solution)/shard_map/ppermute | solution.py:17
  23.7 0.8 %collective-permute-done.2.refs_2_ = bf16[80,512]{1,0:T(8,128)(2,1)S(1)} collective-permute-done((bf16[80,512]{1,0:T(8,128)(2,1)S(1)}, bf16[80,512]{1,0:T(8,128)(2,1)S(1)}, u32[]{:S(2)}, u32[]{:S(2)}) %collective-permute-start.2) | collective-permute-done | bytes 81952 | tf_op jit(solution)/shard_map/ppermute | solution.py:17
  24.5 4.3 %collective-permute-done.3.refs_3_ = bf16[80,512]{1,0:T(8,128)(2,1)S(1)} collective-permute-done((bf16[80,512]{1,0:T(8,128)(2,1)S(1)}, bf16[80,512]{1,0:T(8,128)(2,1)S(1)}, u32[]{:S(2)}, u32[]{:S(2)}) %collective-permute-start.3) | collective-permute-done | bytes 81952 | tf_op jit(solution)/shard_map/ppermute | solution.py:17
  28.8 1.5 %forward.1 = (bf16[320,768]{1,0:T(8,128)(2,1)S(1)}, bf16[10,80,256]{2,1,0:T(8,128)(2,1)S(1)}, bf16[320,256]{1,0:T(8,128)(2,1)S(1)}) custom-call(bf16[80,512]{1,0:T(8,128)(2,1)S(1)} %conv_near.1.refs_0_, bf16[80,512]{1,0:T(8,128)(2,1)S(1)} %collective-permute-done.1.refs_1_, bf16[80,512]{1,0:T(8,128)(2,1)S(1)} %collective-permute-done.2.refs_2_, ...), custom_call_target="tpu_custom_call" | custom-call | tf_op jit(solution)/shard_map/forward/pallas_call | solution.py:352
  30.2 2.8 %backward.1 = (f32[8,128,256]{2,1,0:T(8,128)S(1)}, bf16[8,128,256]{2,1,0:T(8,128)(2,1)S(1)}) custom-call(bf16[80,512]{1,0:T(8,128)(2,1)S(1)} %conv_near.1.refs_0_, bf16[80,512]{1,0:T(8,128)(2,1)S(1)} %collective-permute-done.1.refs_1_, bf16[80,512]{1,0:T(8,128)(2,1)S(1)} %collective-permute-done.2.refs_2_, ...), custom_call_target="tpu_custom_call" | custom-call | tf_op jit(solution)/shard_map/backward/pallas_call | solution.py:369
  33.1 0.1 collective-permute-start.9
  33.2 1.9 %collective-permute-done.9 = bf16[8,128,256]{2,1,0:T(8,128)(2,1)S(1)} collective-permute-done((bf16[8,128,256]{2,1,0:T(8,128)(2,1)S(1)}, bf16[8,128,256]{2,1,0:T(8,128)(2,1)S(1)}, u32[]{:S(2)}, u32[]{:S(2)}) %collective-permute-start.9) | collective-permute-done | bytes 524320 | tf_op jit(solution)/shard_map/ppermute | solution.py:17
  35.0 0.1 convert_add_fusion
  35.2 0.1 fusion.11
  35.3 1.6 %collective-permute-start.12 = (bf16[2,2,128,128]{3,2,1,0:T(8,128)(2,1)S(1)}, bf16[2,2,128,128]{3,2,1,0:T(8,128)(2,1)S(1)}, u32[]{:S(2)}, u32[]{:S(2)}) collective-permute-start(bf16[2,2,128,128]{3,2,1,0:T(8,128)(2,1)S(1)} %fusion.1), channel_id=1, source_target_pairs={{0,16},{16,0},{1,17},{17,1},{2,18},{18,2},{3,19},{19,3},{4,20},{20... | collective-permute-start | bytes 393224 | tf_op jit(solution)/shard_map/ppermute | solution.py:17
  36.9 1.6 %collective-permute-start.10 = (bf16[2,2,128,128]{3,2,1,0:T(8,128)(2,1)S(1)}, bf16[2,2,128,128]{3,2,1,0:T(8,128)(2,1)S(1)}, u32[]{:S(2)}, u32[]{:S(2)}) collective-permute-start(bf16[2,2,128,128]{3,2,1,0:T(8,128)(2,1)S(1)} %fusion), channel_id=1, source_target_pairs={{0,2},{1,3},{2,0},{3,1},{4,6},{5,7},{6,4},{7,5},{8,10},{9,11},{10,... | collective-permute-start | bytes 393224 | tf_op jit(solution)/shard_map/ppermute | solution.py:17
  38.5 2.4 %collective-permute-done.12 = bf16[2,2,128,128]{3,2,1,0:T(8,128)(2,1)S(1)} collective-permute-done((bf16[2,2,128,128]{3,2,1,0:T(8,128)(2,1)S(1)}, bf16[2,2,128,128]{3,2,1,0:T(8,128)(2,1)S(1)}, u32[]{:S(2)}, u32[]{:S(2)}) %collective-permute-start.12) | collective-permute-done | bytes 131104 | tf_op jit(solution)/shard_map/ppermute | solution.py:17
  41.0 1.6 %collective-permute-start.13 = (bf16[2,128,128]{2,1,0:T(8,128)(2,1)S(1)}, bf16[2,128,128]{2,1,0:T(8,128)(2,1)S(1)}, u32[]{:S(2)}, u32[]{:S(2)}) collective-permute-start(bf16[2,128,128]{2,1,0:T(8,128)(2,1)S(1)} %fusion.8), channel_id=1, source_target_pairs={{0,2},{1,3},{2,0},{3,1},{4,6},{5,7},{6,4},{7,5},{8,10},{9,11},{10,... | collective-permute-start | bytes 196616 | tf_op jit(solution)/shard_map/ppermute | solution.py:17
  42.6 1.6 %collective-permute-start.11 = (bf16[2,128,128]{2,1,0:T(8,128)(2,1)S(1)}, bf16[2,128,128]{2,1,0:T(8,128)(2,1)S(1)}, u32[]{:S(2)}, u32[]{:S(2)}) collective-permute-start(bf16[2,128,128]{2,1,0:T(8,128)(2,1)S(1)} %fusion.7), channel_id=1, source_target_pairs={{0,16},{16,0},{1,17},{17,1},{2,18},{18,2},{3,19},{19,3},{4,20},{20... | collective-permute-start | bytes 196616 | tf_op jit(solution)/shard_map/ppermute | solution.py:17
  44.2 1.1 %collective-permute-done.13 = bf16[2,128,128]{2,1,0:T(8,128)(2,1)S(1)} collective-permute-done((bf16[2,128,128]{2,1,0:T(8,128)(2,1)S(1)}, bf16[2,128,128]{2,1,0:T(8,128)(2,1)S(1)}, u32[]{:S(2)}, u32[]{:S(2)}) %collective-permute-start.13) | collective-permute-done | bytes 65568 | tf_op jit(solution)/shard_map/ppermute | solution.py:17
  45.3 1.6 %collective-permute-done.11 = bf16[2,128,128]{2,1,0:T(8,128)(2,1)S(1)} collective-permute-done((bf16[2,128,128]{2,1,0:T(8,128)(2,1)S(1)}, bf16[2,128,128]{2,1,0:T(8,128)(2,1)S(1)}, u32[]{:S(2)}, u32[]{:S(2)}) %collective-permute-start.11) | collective-permute-done | bytes 65568 | tf_op jit(solution)/shard_map/ppermute | solution.py:17
  47.0 2.9 %collective-permute-start.14 = (bf16[128,256]{1,0:T(8,128)(2,1)S(1)}, bf16[128,256]{1,0:T(8,128)(2,1)S(1)}, u32[]{:S(2)}, u32[]{:S(2)}) collective-permute-start(bf16[128,256]{1,0:T(8,128)(2,1)S(1)} %fusion.9), channel_id=1, source_target_pairs={{0,8},{4,12},{8,0},{12,4},{1,9},{5,13},{9,1},{13,5},{2,10},{6,14},... | collective-permute-start | bytes 196616 | tf_op jit(solution)/shard_map/ppermute | solution.py:17
  49.8 2.4 %collective-permute-done.14 = bf16[128,256]{1,0:T(8,128)(2,1)S(1)} collective-permute-done((bf16[128,256]{1,0:T(8,128)(2,1)S(1)}, bf16[128,256]{1,0:T(8,128)(2,1)S(1)}, u32[]{:S(2)}, u32[]{:S(2)}) %collective-permute-start.14) | collective-permute-done | bytes 65568 | tf_op jit(solution)/shard_map/ppermute | solution.py:17
  52.3 1.4 %collective-permute-start.15 = (bf16[64,256]{1,0:T(8,128)(2,1)S(1)}, bf16[64,256]{1,0:T(8,128)(2,1)S(1)}, u32[]{:S(2)}, u32[]{:S(2)}) collective-permute-start(bf16[64,256]{1,0:T(8,128)(2,1)S(1)} %fusion.10), channel_id=1, source_target_pairs={{0,4},{4,0},{8,12},{12,8},{1,5},{5,1},{9,13},{13,9},{2,6},{6,2},{1... | collective-permute-start | bytes 98312 | tf_op jit(solution)/shard_map/ppermute | solution.py:17
  53.6 2.6 %collective-permute-done.15.got_ref = bf16[64,256]{1,0:T(8,128)(2,1)S(1)} collective-permute-done((bf16[64,256]{1,0:T(8,128)(2,1)S(1)}, bf16[64,256]{1,0:T(8,128)(2,1)S(1)}, u32[]{:S(2)}, u32[]{:S(2)}) %collective-permute-start.15) | collective-permute-done | bytes 32800 | tf_op jit(solution)/shard_map/ppermute | solution.py:17
  56.2 0.7 %join.1 = f32[256,128]{1,0:T(8,128)} custom-call(f32[2,64,256]{2,1,0:T(8,128)S(1)} %bitcast.40, bf16[64,256]{1,0:T(8,128)(2,1)S(1)} %collective-permute-done.15.got_ref), custom_call_target="tpu_custom_call" | custom-call | tf_op jit(solution)/shard_map/join/pallas_call | solution.py:411
  (32 shorter events, 0.3 us)
Async XLA Ops:
  0.0 5.0 %copy-start.1 = (bf16[1,1,160,512]{3,2,1,0:T(8,128)(2,1)S(1)}, bf16[1,1,160,512]{3,2,1,0:T(8,128)(2,1)}, u32[]{:S(2)}) copy-start(bf16[1,1,160,512]{3,2,1,0:T(8,128)(2,1)} %param.7) | copy-start | bytes 491524
  0.0 12.9 %copy-start.2 = (f32[9,512]{1,0:T(8,128)S(1)}, f32[9,512]{1,0:T(8,128)}, u32[]{:S(2)}) copy-start(f32[9,512]{1,0:T(8,128)} %taps_hbm.3) | copy-start | bytes 55300
  0.0 12.9 %copy-start.4 = (f32[512]{0:T(512)S(1)}, f32[512]{0:T(512)}, u32[]{:S(2)}) copy-start(f32[512]{0:T(512)} %param.10) | copy-start | bytes 6148
  1.9 11.0 %copy-start.3 = (s32[160,8]{0,1:T(8,128)S(1)}, s32[160,8]{0,1:T(8,128)}, u32[]{:S(2)}) copy-start(s32[160,8]{0,1:T(8,128)} %param.8) | copy-start | bytes 15364
  1.9 11.0 %collective-permute-start.6 = (bf16[128,1280]{1,0:T(8,128)(2,1)}, bf16[128,1280]{1,0:T(8,128)(2,1)S(1)}, u32[]{:S(2)}, u32[]{:S(2)}) collective-permute-start(bf16[128,1280]{1,0:T(8,128)(2,1)} %get-tuple-element.15.refs_4_.refs_6_), channel_id=1, source_target_pairs={{0,2},{1,3},{2,0},{3,1},{4,6},{5,7},{6,4},{7,5},{8,10},{9,11},{10,... | collective-permute-start | bytes 983048 | tf_op jit(solution)/shard_map/ppermute | solution.py:17
  5.0 7.9 %collective-permute-start = (bf16[160,512]{1,0:T(8,128)(2,1)S(1)}, bf16[160,512]{1,0:T(8,128)(2,1)S(1)}, u32[]{:S(2)}, u32[]{:S(2)}) collective-permute-start(bf16[160,512]{1,0:T(8,128)(2,1)S(1)} %bitcast.41), channel_id=1, source_target_pairs={{0,16},{16,0},{1,17},{17,1},{2,18},{18,2},{3,19},{19,3},{4,20},{20... | collective-permute-start | bytes 491528 | tf_op jit(solution)/shard_map/ppermute | solution.py:17
  6.5 9.8 %collective-permute-start.4 = (bf16[80,512]{1,0:T(8,128)(2,1)}, bf16[80,512]{1,0:T(8,128)(2,1)S(1)}, u32[]{:S(2)}, u32[]{:S(2)}) collective-permute-start(bf16[80,512]{1,0:T(8,128)(2,1)} %get-tuple-element.14), channel_id=1, source_target_pairs={{0,8},{4,12},{8,0},{12,4},{1,9},{5,13},{9,1},{13,5},{2,10},{6,14},... | collective-permute-start | bytes 245768 | tf_op jit(solution)/shard_map/ppermute | solution.py:17
  9.1 19.6 %collective-permute-start.7 = (bf16[128,1280]{1,0:T(8,128)(2,1)}, bf16[128,1280]{1,0:T(8,128)(2,1)S(1)}, u32[]{:S(2)}, u32[]{:S(2)}) collective-permute-start(bf16[128,1280]{1,0:T(8,128)(2,1)} %get-tuple-element.15.refs_4_.refs_6_), channel_id=1, source_target_pairs={{0,1},{1,0},{2,3},{3,2},{4,5},{5,4},{6,7},{7,6},{8,9},{9,8},{10,11... | collective-permute-start | bytes 983048 | tf_op jit(solution)/shard_map/ppermute | solution.py:17
  12.9 15.8 %collective-permute-start.8 = (bf16[128,1280]{1,0:T(8,128)(2,1)S(1)}, bf16[128,1280]{1,0:T(8,128)(2,1)S(1)}, u32[]{:S(2)}, u32[]{:S(2)}) collective-permute-start(bf16[128,1280]{1,0:T(8,128)(2,1)S(1)} %collective-permute-done.6.refs_5_.refs_7_), channel_id=1, source_target_pairs={{0,1},{1,0},{2,3},{3,2},{4,5},{5,4},{6,7},{7,6},{8,9},{9,8},{10,11... | collective-permute-start | bytes 983048 | tf_op jit(solution)/shard_map/ppermute | solution.py:17
  12.9 3.4 %copy-start.5 = (bf16[80,512]{1,0:T(8,128)(2,1)S(1)}, bf16[80,512]{1,0:T(8,128)(2,1)}, u32[]{:S(2)}) copy-start(bf16[80,512]{1,0:T(8,128)(2,1)} %get-tuple-element.13) | copy-start | bytes 245764
  14.4 6.5 %collective-permute-start.1 = (bf16[80,512]{1,0:T(8,128)(2,1)S(1)}, bf16[80,512]{1,0:T(8,128)(2,1)S(1)}, u32[]{:S(2)}, u32[]{:S(2)}) collective-permute-start(bf16[80,512]{1,0:T(8,128)(2,1)S(1)} %conv_near.1.refs_0_), channel_id=1, source_target_pairs={{0,4},{4,0},{8,12},{12,8},{1,5},{5,1},{9,13},{13,9},{2,6},{6,2},{1... | collective-permute-start | bytes 245768 | tf_op jit(solution)/shard_map/ppermute | solution.py:17
  16.3 12.4 %copy-start = (bf16[128,1280]{1,0:T(8,128)(2,1)S(1)}, bf16[128,1280]{1,0:T(8,128)(2,1)}, u32[]{:S(2)}) copy-start(bf16[128,1280]{1,0:T(8,128)(2,1)} %get-tuple-element.15.refs_4_.refs_6_) | copy-start | bytes 983044
  16.3 13.9 %collective-permute-start.5 = (bf16[2,80,512]{2,1,0:T(8,128)(2,1)S(1)}, bf16[2,80,512]{2,1,0:T(8,128)(2,1)S(1)}, u32[]{:S(2)}, u32[]{:S(2)}) collective-permute-start(bf16[2,80,512]{2,1,0:T(8,128)(2,1)S(1)} %pad_maximum_fusion.refs_4_), channel_id=1, source_target_pairs={{0,4},{4,0},{8,12},{12,8},{1,5},{5,1},{9,13},{13,9},{2,6},{6,2},{1... | collective-permute-start | bytes 491528 | tf_op jit(solution)/shard_map/ppermute | solution.py:17
  18.1 6.4 %collective-permute-start.2 = (bf16[80,512]{1,0:T(8,128)(2,1)S(1)}, bf16[80,512]{1,0:T(8,128)(2,1)S(1)}, u32[]{:S(2)}, u32[]{:S(2)}) collective-permute-start(bf16[80,512]{1,0:T(8,128)(2,1)S(1)} %conv_far.1), channel_id=1, source_target_pairs={{0,8},{4,12},{8,0},{12,4},{1,9},{5,13},{9,1},{13,5},{2,10},{6,14},... | collective-permute-start | bytes 245768 | tf_op jit(solution)/shard_map/ppermute | solution.py:17
  21.0 7.8 %collective-permute-start.3 = (bf16[80,512]{1,0:T(8,128)(2,1)S(1)}, bf16[80,512]{1,0:T(8,128)(2,1)S(1)}, u32[]{:S(2)}, u32[]{:S(2)}) collective-permute-start(bf16[80,512]{1,0:T(8,128)(2,1)S(1)} %conv_far.1), channel_id=1, source_target_pairs={{0,12},{4,8},{8,4},{12,0},{1,13},{5,9},{9,5},{13,1},{2,14},{6,10},... | collective-permute-start | bytes 245768 | tf_op jit(solution)/shard_map/ppermute | solution.py:17
  33.1 2.0 %collective-permute-start.9 = (bf16[8,128,256]{2,1,0:T(8,128)(2,1)S(1)}, bf16[8,128,256]{2,1,0:T(8,128)(2,1)S(1)}, u32[]{:S(2)}, u32[]{:S(2)}) collective-permute-start(bf16[8,128,256]{2,1,0:T(8,128)(2,1)S(1)} %get-tuple-element.20), channel_id=1, source_target_pairs={{0,1},{1,0},{2,3},{3,2},{4,5},{5,4},{6,7},{7,6},{8,9},{9,8},{10,11... | collective-permute-start | bytes 1572872 | tf_op jit(solution)/shard_map/ppermute | solution.py:17
  35.3 5.6 %collective-permute-start.12 = (bf16[2,2,128,128]{3,2,1,0:T(8,128)(2,1)S(1)}, bf16[2,2,128,128]{3,2,1,0:T(8,128)(2,1)S(1)}, u32[]{:S(2)}, u32[]{:S(2)}) collective-permute-start(bf16[2,2,128,128]{3,2,1,0:T(8,128)(2,1)S(1)} %fusion.1), channel_id=1, source_target_pairs={{0,16},{16,0},{1,17},{17,1},{2,18},{18,2},{3,19},{19,3},{4,20},{20... | collective-permute-start | bytes 393224 | tf_op jit(solution)/shard_map/ppermute | solution.py:17
  36.9 5.6 %collective-permute-start.10 = (bf16[2,2,128,128]{3,2,1,0:T(8,128)(2,1)S(1)}, bf16[2,2,128,128]{3,2,1,0:T(8,128)(2,1)S(1)}, u32[]{:S(2)}, u32[]{:S(2)}) collective-permute-start(bf16[2,2,128,128]{3,2,1,0:T(8,128)(2,1)S(1)} %fusion), channel_id=1, source_target_pairs={{0,2},{1,3},{2,0},{3,1},{4,6},{5,7},{6,4},{7,5},{8,10},{9,11},{10,... | collective-permute-start | bytes 393224 | tf_op jit(solution)/shard_map/ppermute | solution.py:17
  41.0 4.3 %collective-permute-start.13 = (bf16[2,128,128]{2,1,0:T(8,128)(2,1)S(1)}, bf16[2,128,128]{2,1,0:T(8,128)(2,1)S(1)}, u32[]{:S(2)}, u32[]{:S(2)}) collective-permute-start(bf16[2,128,128]{2,1,0:T(8,128)(2,1)S(1)} %fusion.8), channel_id=1, source_target_pairs={{0,2},{1,3},{2,0},{3,1},{4,6},{5,7},{6,4},{7,5},{8,10},{9,11},{10,... | collective-permute-start | bytes 196616 | tf_op jit(solution)/shard_map/ppermute | solution.py:17
  42.6 4.3 %collective-permute-start.11 = (bf16[2,128,128]{2,1,0:T(8,128)(2,1)S(1)}, bf16[2,128,128]{2,1,0:T(8,128)(2,1)S(1)}, u32[]{:S(2)}, u32[]{:S(2)}) collective-permute-start(bf16[2,128,128]{2,1,0:T(8,128)(2,1)S(1)} %fusion.7), channel_id=1, source_target_pairs={{0,16},{16,0},{1,17},{17,1},{2,18},{18,2},{3,19},{19,3},{4,20},{20... | collective-permute-start | bytes 196616 | tf_op jit(solution)/shard_map/ppermute | solution.py:17
  47.0 5.2 %collective-permute-start.14 = (bf16[128,256]{1,0:T(8,128)(2,1)S(1)}, bf16[128,256]{1,0:T(8,128)(2,1)S(1)}, u32[]{:S(2)}, u32[]{:S(2)}) collective-permute-start(bf16[128,256]{1,0:T(8,128)(2,1)S(1)} %fusion.9), channel_id=1, source_target_pairs={{0,8},{4,12},{8,0},{12,4},{1,9},{5,13},{9,1},{13,5},{2,10},{6,14},... | collective-permute-start | bytes 196616 | tf_op jit(solution)/shard_map/ppermute | solution.py:17
  52.3 4.0 %collective-permute-start.15 = (bf16[64,256]{1,0:T(8,128)(2,1)S(1)}, bf16[64,256]{1,0:T(8,128)(2,1)S(1)}, u32[]{:S(2)}, u32[]{:S(2)}) collective-permute-start(bf16[64,256]{1,0:T(8,128)(2,1)S(1)} %fusion.10), channel_id=1, source_target_pairs={{0,4},{4,0},{8,12},{12,8},{1,5},{5,1},{9,13},{13,9},{2,6},{6,2},{1... | collective-permute-start | bytes 98312 | tf_op jit(solution)/shard_map/ppermute | solution.py:17

commit v4 on v3

--- a/solution.py
+++ b/solution.py
@@ -15,6 +15,18 @@
 
 def swap(values, axis, mask):
     return lax.ppermute(values, axis, [(i, i ^ mask) for i in range(lax.axis_size(axis))])
+
+
+def shift(values, axis, mask, to_core=1):
+    cores = lax.axis_size("fsdp")
+    if axis == "fsdp":
+        return lax.ppermute(values, axis, [(i, i ^ mask) for i in range(1, cores, 2)])
+    pairs = [
+        (i * cores + j, (i ^ mask) * cores + j + to_core - 1)
+        for i in range(lax.axis_size(axis))
+        for j in range(1, cores, 2)
+    ]
+    return lax.ppermute(values, (axis, "fsdp"), pairs)
 
 
 def pick(values, index, dim=0):
@@ -173,7 +185,8 @@
     frames = 4
     row_refs, pair_refs, shards, refs = refs[:4], refs[4:6], refs[6:10], refs[10:]
     qkv_ref, weights_ref, attended_ref, refs = refs[0], refs[1], refs[2], refs[3:]
-    keep_ref, send_ref, n_ref, u_ref, out_w_ref, sums_ref, out_sums_ref, sems = refs
+    keep_refs, send_refs, refs = refs[:2], refs[2:4], refs[4:]
+    n_ref, u_ref, out_w_ref, sums_ref, out_sums_ref, sems = refs
     _, t, _, zh, x, core = place()
     pixels, channels = row_refs[0].shape
     width = out_w_ref.shape[0]
@@ -252,46 +265,56 @@
             sums_ref[lane // 128, pl.ds(m, channels, stride=3), :] = grad[:, lane : lane + 128]
     out_sums_ref[...] = over_rows(attended_ref[...], upstream)
 
-    block = 64
-    for x in range(2):
-        for y in range(2):
-            for zp in range(2):
-                slot = (x * 2 + y) * 2 + zp
-                for side, ref in ((core, keep_ref), (1 - core, send_ref)):
-                    if y == 1 and zp == 1:
-                        start = pl.multiple_of((2 * x + side) * block, block)
-                        rows = out_sums_ref[pl.ds(start, block), :]
-                        pieces = (rows[:, :width], rows[:, width:])
-                    else:
-                        pieces = []
-                        for low in range(2):
-                            index = y * 16 + (2 * zp + low) * 4 + 2 * x + side
-                            start = pl.multiple_of(index * block, block)
-                            pieces.append(
-                                jnp.concatenate(
-                                    [
-                                        sums_ref[lane, pl.ds(start, block), :]
-                                        for lane in range(width // 128)
-                                    ],
-                                    axis=1,
-                                )
-                            )
-                    for low in range(2):
-                        ref[slot, low * block : (low + 1) * block, :] = pieces[low].astype(ref.dtype)
-
-
-def join_kernel(total_ref, got_ref, out_ref):
-    y, _, zp, zh, _, _ = place()
-    lanes = out_ref.shape[1]
-    rows, width = got_ref.shape
+    block = depth = channels // HEADS
+
+    def store(path_refs):
+        for side in range(2):
+            for slot in range(8):
+                at_x, at_y, at_zp = slot >> 2, (slot >> 1) & 1, slot & 1
+                for low in range(2):
+                    index = at_y * 16 + (2 * at_zp + low) * 4 + 2 * at_x + side
+                    for path in range(2):
+                        if index < 3 * HEADS:
+                            first = index * block
+                            piece = sums_ref[path, first : first + block, :]
+                        else:
+                            first = (2 * at_x + side) * block
+                            lane = low * width + path * 128
+                            piece = out_sums_ref[first : first + block, lane : lane + 128]
+                        a, b = (at_x, at_y) if path == 0 else (at_y, at_x)
+                        rows_at = slice(low * block, (low + 1) * block)
+                        ref = path_refs[path]
+                        ref[a, b, at_zp, side, rows_at, :] = piece.astype(ref.dtype)
+
+    @pl.when(core == 0)
+    def _():
+        store(send_refs)
+
+    @pl.when(core == 1)
+    def _():
+        store(keep_refs)
+
+
+def join_kernel(total_0_ref, total_1_ref, handed_ref, got_ref, got_handed_ref, out_ref):
+    y, _, zp, zh, _, core = place()
+    paths, rows, _ = got_ref.shape
     is_out = (y == 1) & (zp == 1)
-    got = got_ref[...].astype(jnp.float32)
-    for side in range(2):
-        joined = jnp.where(is_out | (zh == side), total_ref[side], got)
-        for lane in range(0, width, lanes):
-            first = (side * width + lane) // lanes
-            step = 2 * width // lanes
-            out_ref[pl.ds(first, rows, stride=step), :] = joined[:, lane : lane + lanes]
+
+    def join(totals, other):
+        for path in range(paths):
+            got = other[path].astype(jnp.float32)
+            for side in range(2):
+                mine = totals[path][side * rows : (side + 1) * rows, :]
+                joined = jnp.where(is_out | (zh == side), mine, got)
+                out_ref[pl.ds(side * paths + path, rows, stride=2 * paths), :] = joined
+
+    @pl.when(core == 0)
+    def _():
+        join([handed_ref.at[0], handed_ref.at[1]], got_handed_ref)
+
+    @pl.when(core == 1)
+    def _():
+        join([total_0_ref.at[1], total_1_ref.at[1]], got_ref)
 
 
 def split_form(features, neighbours, conv_taps, norm_gain, qkv_weight, out_weight, cotangent):
@@ -366,14 +389,14 @@
         compiler_params=pltpu.CompilerParams(vmem_limit_bytes=24 << 20),
         name="forward",
     )(n_mine, row_1, row_2, row_3, cut, cut_x, cut_c, cut_xc)
-    keep, send = pl.pallas_call(
+    *keep, send_0, send_1 = pl.pallas_call(
         backward_kernel,
         out_shape=(
-            jax.ShapeDtypeStruct((8, 2 * block, width), jnp.float32),
-            jax.ShapeDtypeStruct((8, 2 * block, width), narrow_type),
+            *(jax.ShapeDtypeStruct((2,) * 4 + (2 * block, 128), jnp.float32),) * 2,
+            *(jax.ShapeDtypeStruct((2,) * 4 + (2 * block, 128), narrow_type),) * 2,
         ),
         in_specs=[anywhere] * 10 + [in_vmem] * 3,
-        out_specs=(in_vmem, in_vmem),
+        out_specs=(in_vmem,) * 4,
         scratch_shapes=[
             pltpu.VMEM((4, half, channels), narrow_type),
             pltpu.VMEM((4, half, channels), narrow_type),
@@ -392,30 +415,51 @@
     def narrow(values):
         return values.astype(jnp.bfloat16)
 
-    total = keep + swap(send, "fsdp", 1).astype(jnp.float32)
-    total = total.reshape(2, 2, 2, 2 * block, width)
-    first, second = total[..., : width // 2], total[..., width // 2 :]
-    got_first = swap(narrow(pick(first, 1 - x, 0)), "fsdp", 2)
-    got_second = swap(narrow(pick(second, 1 - y, 1)), "blk", 1)
-    first = pick(first, x, 0) + got_first.astype(jnp.float32)
-    second = pick(second, y, 1) + got_second.astype(jnp.float32)
-    got_first = swap(narrow(pick(first, 1 - y, 0)), "blk", 1)
-    got_second = swap(narrow(pick(second, 1 - x, 0)), "fsdp", 2)
-    first = pick(first, y, 0) + got_first.astype(jnp.float32)
-    second = pick(second, x, 0) + got_second.astype(jnp.float32)
-    total = jnp.concatenate([first, second], axis=-1)
-    total = pick(total, zp) + swap(narrow(pick(total, 1 - zp)), "tm", 2).astype(jnp.float32)
-    total = total.reshape(2, block, width)
-    got = swap(narrow(pick(total, 1 - zh)), "tm", 1)
-    lanes = 128
+    def plus(*terms):
+        total = terms[0].astype(jnp.float32)
+        for term in terms[1:]:
+            total = total + term.astype(jnp.float32)
+        return total
+
+    cores = lax.axis_size("fsdp")
+    up = [(i, i + 1) for i in range(0, cores, 2)]
+    paths = [
+        [keep[0], lax.ppermute(send_0, "fsdp", up)],
+        [keep[1], lax.ppermute(send_1, "fsdp", up)],
+    ]
+    hops = (("fsdp", 2, x), ("blk", 1, y))
+    for stage in range(2):
+        got = []
+        for path in range(2):
+            axis, mask, index = hops[path ^ stage]
+            far = plus(*(pick(part, 1 - index) for part in paths[path]))
+            got.append(shift(narrow(far), axis, mask))
+        for path in range(2):
+            index = hops[path ^ stage][2]
+            paths[path] = [pick(part, index) for part in paths[path]] + [got[path]]
+    far = jnp.stack([plus(*(pick(part, 1 - zp) for part in path)) for path in paths])
+    got = shift(narrow(far), "tm", 2)
+    totals = [
+        plus(*(pick(part, zp) for part in path), got[i]) for i, path in enumerate(paths)
+    ]
+
+    def both(core):
+        rows = [pick(total[core].reshape(2, block, 128), 1 - zh) for total in totals]
+        return narrow(jnp.stack(rows))
+
+    got = shift(both(1), "tm", 1)
+    got_handed = shift(both(0), "tm", 1, 0)
+    handed = lax.ppermute(
+        jnp.stack([total[0] for total in totals]), "fsdp", [(j, i) for i, j in up]
+    )
     out = pl.pallas_call(
         join_kernel,
-        out_shape=jax.ShapeDtypeStruct((block * channels // lanes, lanes), jnp.float32),
-        in_specs=[in_vmem] * 2,
+        out_shape=jax.ShapeDtypeStruct((block * channels // 128, 128), jnp.float32),
+        in_specs=[in_vmem] * 5,
         out_specs=in_vmem,
         compiler_params=pltpu.CompilerParams(vmem_limit_bytes=4 << 20),
         name="join",
-    )(total, got)
+    )(*totals, handed, got, got_handed)
     return out.reshape(-1)
 
 

time: 57 us -> 73.6 us (1.29)
  the two profiles are of different devices: /device:TPU:0 before, /device:TPU:1 now
where the time goes in v4:
time: 73.6 us; the launch traced here: 73.1 us
  starting transfers between devices  38 us (52%)
  waiting for transfers between devices  18.1 us (25%)
  Pallas kernels  9.79 us (13%)
  other arithmetic  6.69 us (9%)
    ppermute x9, starting transfers between devices, swap(): lax.ppermute(values, axis, [(i, i ^ mask) for i in range(lax.axis_size(ax...  14.5 us
    ppermute x5, starting transfers between devices, shift(): return lax.ppermute(values, (axis, 'fsdp'), pairs)  13.4 us
    ppermute x9, waiting for transfers between devices, swap(): lax.ppermute(values, axis, [(i, i ^ mask) for i in range(lax.axis_size(ax...  8.43 us
    ppermute x5, waiting for transfers between devices, shift(): return lax.ppermute(values, (axis, 'fsdp'), pairs)  6.67 us
    ppermute x2, starting transfers between devices, shift(): lax.ppermute(values, axis, [(i, i ^ mask) for i in range(1, cores, 2)])  6.22 us
    convert_element_type x4, other arithmetic, narrow(): return values.astype(jnp.bfloat16)  3.93 us
    pallas_call x2, Pallas kernels, conv(): pl.pallas_call(functools.partial(conv_kernel, far), out_shape=piece, in_s...  2.92 us
    pallas_call x1, Pallas kernels, split_form(): pl.pallas_call(backward_kernel, out_shape=(*(jax.ShapeDtypeStruct((2,) *...  2.8 us
  transfers between devices with their start and end apart: 19, of which 7 were waited for; matrix products, arithmetic and copies ran while one was open for 7% of the time, Pallas kernels for 6%

profile of v4, /device:TPU:1, one launch (start us, length us, event | category | flops | bytes accessed | tf_op | source)
XLA Modules:
  0.0 73.1 jit_solution(4186719767250615959)
XLA Ops:
  0.0 1.9 %prep.1 = (bf16[80,512]{1,0:T(8,128)(2,1)}, bf16[80,512]{1,0:T(8,128)(2,1)}, bf16[128,1280]{1,0:T(8,128)(2,1)}) custom-call(bf16[160,512]{1,0:T(8,128)(2,1)} %bitcast.70, bf16[128,1536]{1,0:T(8,128)(2,1)} %qkv_ref.1, bf16[128,512]{1,0:T(8,128)(2,1)} %out_w_ref.1), custom_call_target="tpu_custom_call" | custom-call | tf_op jit(solution)/shard_map/prep/pallas_call | solution.py:331
  2.0 2.1 %collective-permute-start.6 = (bf16[128,1280]{1,0:T(8,128)(2,1)}, bf16[128,1280]{1,0:T(8,128)(2,1)S(1)}, u32[]{:S(2)}, u32[]{:S(2)}) collective-permute-start(bf16[128,1280]{1,0:T(8,128)(2,1)} %get-tuple-element.17.refs_4_.refs_6_), channel_id=1, source_target_pairs={{0,2},{1,3},{2,0},{3,1},{4,6},{5,7},{6,4},{7,5},{8,10},{9,11},{10,... | collective-permute-start | bytes 983048 | tf_op jit(solution)/shard_map/ppermute | solution.py:17
  4.1 1.2 %collective-permute-start = (bf16[160,512]{1,0:T(8,128)(2,1)S(1)}, bf16[160,512]{1,0:T(8,128)(2,1)S(1)}, u32[]{:S(2)}, u32[]{:S(2)}) collective-permute-start(bf16[160,512]{1,0:T(8,128)(2,1)S(1)} %bitcast.61), channel_id=1, source_target_pairs={{0,16},{16,0},{1,17},{17,1},{2,18},{18,2},{3,19},{19,3},{4,20},{20... | collective-permute-start | bytes 491528 | tf_op jit(solution)/shard_map/ppermute | solution.py:17
  5.3 2.3 %collective-permute-start.4 = (bf16[80,512]{1,0:T(8,128)(2,1)}, bf16[80,512]{1,0:T(8,128)(2,1)S(1)}, u32[]{:S(2)}, u32[]{:S(2)}) collective-permute-start(bf16[80,512]{1,0:T(8,128)(2,1)} %get-tuple-element.16), channel_id=1, source_target_pairs={{0,8},{4,12},{8,0},{12,4},{1,9},{5,13},{9,1},{13,5},{2,10},{6,14},... | collective-permute-start | bytes 245768 | tf_op jit(solution)/shard_map/ppermute | solution.py:17
  7.6 1.5 %collective-permute-start.7 = (bf16[128,1280]{1,0:T(8,128)(2,1)}, bf16[128,1280]{1,0:T(8,128)(2,1)S(1)}, u32[]{:S(2)}, u32[]{:S(2)}) collective-permute-start(bf16[128,1280]{1,0:T(8,128)(2,1)} %get-tuple-element.17.refs_4_.refs_6_), channel_id=1, source_target_pairs={{0,1},{1,0},{2,3},{3,2},{4,5},{5,4},{6,7},{7,6},{8,9},{9,8},{10,11... | collective-permute-start | bytes 983048 | tf_op jit(solution)/shard_map/ppermute | solution.py:17
  9.1 2.6 %collective-permute-done.6.refs_5_.refs_7_ = bf16[128,1280]{1,0:T(8,128)(2,1)S(1)} collective-permute-done((bf16[128,1280]{1,0:T(8,128)(2,1)}, bf16[128,1280]{1,0:T(8,128)(2,1)S(1)}, u32[]{:S(2)}, u32[]{:S(2)}) %collective-permute-start.6) | collective-permute-done | bytes 327712 | tf_op jit(solution)/shard_map/ppermute | solution.py:17
  11.7 1.3 %collective-permute-start.8 = (bf16[128,1280]{1,0:T(8,128)(2,1)S(1)}, bf16[128,1280]{1,0:T(8,128)(2,1)S(1)}, u32[]{:S(2)}, u32[]{:S(2)}) collective-permute-start(bf16[128,1280]{1,0:T(8,128)(2,1)S(1)} %collective-permute-done.6.refs_5_.refs_7_), channel_id=1, source_target_pairs={{0,1},{1,0},{2,3},{3,2},{4,5},{5,4},{6,7},{7,6},{8,9},{9,8},{10,11... | collective-permute-start | bytes 983048 | tf_op jit(solution)/shard_map/ppermute | solution.py:17
  13.0 1.5 %conv_near.1.refs_0_ = bf16[80,512]{1,0:T(8,128)(2,1)S(1)} custom-call(s32[8,160]{1,0:T(8,128)S(1)} %bitcast.64, bf16[160,512]{1,0:T(8,128)(2,1)S(1)} %bitcast.62, bf16[160,512]{1,0:T(8,128)(2,1)S(1)} %collective-permute-done.band_hbm, f32[9,512]{1,0:T(8,128)S(1)} %copy-done.2, f32[1,512]{1,0:T(1,128)S(1)} %bitcast.66), custom_call_target="tpu_custom_call" | custom-call | tf_op jit(solution)/shard_map/conv_near/pallas_call | solution.py:348
  14.4 1.6 %collective-permute-start.1 = (bf16[80,512]{1,0:T(8,128)(2,1)S(1)}, bf16[80,512]{1,0:T(8,128)(2,1)S(1)}, u32[]{:S(2)}, u32[]{:S(2)}) collective-permute-start(bf16[80,512]{1,0:T(8,128)(2,1)S(1)} %conv_near.1.refs_0_), channel_id=1, source_target_pairs={{0,4},{4,0},{8,12},{12,8},{1,5},{5,1},{9,13},{13,9},{2,6},{6,2},{1... | collective-permute-start | bytes 245768 | tf_op jit(solution)/shard_map/ppermute | solution.py:17
  16.2 1.4 %conv_far.1 = bf16[80,512]{1,0:T(8,128)(2,1)S(1)} custom-call(s32[8,160]{1,0:T(8,128)S(1)} %bitcast.65, bf16[160,512]{1,0:T(8,128)(2,1)S(1)} %bitcast.63, bf16[160,512]{1,0:T(8,128)(2,1)S(1)} %collective-permute-done.band_hbm, f32[9,512]{1,0:T(8,128)S(1)} %copy-done.2, f32[1,512]{1,0:T(1,128)S(1)} %bitcast.67), custom_call_target="tpu_custom_call" | custom-call | tf_op jit(solution)/shard_map/conv_far/pallas_call | solution.py:348
  17.6 2.5 %collective-permute-start.2 = (bf16[80,512]{1,0:T(8,128)(2,1)S(1)}, bf16[80,512]{1,0:T(8,128)(2,1)S(1)}, u32[]{:S(2)}, u32[]{:S(2)}) collective-permute-start(bf16[80,512]{1,0:T(8,128)(2,1)S(1)} %conv_far.1), channel_id=1, source_target_pairs={{0,8},{4,12},{8,0},{12,4},{1,9},{5,13},{9,1},{13,5},{2,10},{6,14},... | collective-permute-start | bytes 245768 | tf_op jit(solution)/shard_map/ppermute | solution.py:17
  20.1 1.9 %collective-permute-start.3 = (bf16[80,512]{1,0:T(8,128)(2,1)S(1)}, bf16[80,512]{1,0:T(8,128)(2,1)S(1)}, u32[]{:S(2)}, u32[]{:S(2)}) collective-permute-start(bf16[80,512]{1,0:T(8,128)(2,1)S(1)} %conv_far.1), channel_id=1, source_target_pairs={{0,12},{4,8},{8,4},{12,0},{1,13},{5,9},{9,5},{13,1},{2,14},{6,10},... | collective-permute-start | bytes 245768 | tf_op jit(solution)/shard_map/ppermute | solution.py:17
  22.1 1.0 %collective-permute-done.2.refs_2_ = bf16[80,512]{1,0:T(8,128)(2,1)S(1)} collective-permute-done((bf16[80,512]{1,0:T(8,128)(2,1)S(1)}, bf16[80,512]{1,0:T(8,128)(2,1)S(1)}, u32[]{:S(2)}, u32[]{:S(2)}) %collective-permute-start.2) | collective-permute-done | bytes 81952 | tf_op jit(solution)/shard_map/ppermute | solution.py:17
  23.1 4.8 %collective-permute-done.3.refs_3_ = bf16[80,512]{1,0:T(8,128)(2,1)S(1)} collective-permute-done((bf16[80,512]{1,0:T(8,128)(2,1)S(1)}, bf16[80,512]{1,0:T(8,128)(2,1)S(1)}, u32[]{:S(2)}, u32[]{:S(2)}) %collective-permute-start.3) | collective-permute-done | bytes 81952 | tf_op jit(solution)/shard_map/ppermute | solution.py:17
  27.9 1.5 %forward.1 = (bf16[320,768]{1,0:T(8,128)(2,1)S(1)}, bf16[10,80,256]{2,1,0:T(8,128)(2,1)S(1)}, bf16[320,256]{1,0:T(8,128)(2,1)S(1)}) custom-call(bf16[80,512]{1,0:T(8,128)(2,1)S(1)} %conv_near.1.refs_0_, bf16[80,512]{1,0:T(8,128)(2,1)S(1)} %collective-permute-done.1.refs_1_, bf16[80,512]{1,0:T(8,128)(2,1)S(1)} %collective-permute-done.2.refs_2_, ...), custom_call_target="tpu_custom_call" | custom-call | tf_op jit(solution)/shard_map/forward/pallas_call | solution.py:375
  29.4 2.8 %backward.1 = (f32[2,2,2,2,128,128]{5,4,3,2,1,0:T(8,128)S(1)}, f32[2,2,2,2,128,128]{5,4,3,2,1,0:T(8,128)S(1)}, bf16[2,2,2,2,128,128]{5,4,3,2,1,0:T(8,128)(2,1)S(1)}, bf16[2,2,2,2,128,128]{5,4,3,2,1,0:T(8,128)(2,1)S(1)}) custom-call(bf16[80,512]{1,0:T(8,128)(2,1)S(1)} %conv_near.1.refs_0_, bf16[80,512]{1,0:T(8,128)(2,1)S(1)} %collective-permute-done.1.refs_1_, ...), custom_call_target="tpu_custom_call" | custom-call | tf_op jit(solution)/shard_map/backward/pallas_call | solution.py:392
  32.2 1.3 %collective-permute-start.9 = (bf16[2,2,2,2,128,128]{5,4,3,2,1,0:T(8,128)(2,1)S(1)}, bf16[2,2,2,2,128,128]{5,4,3,2,1,0:T(8,128)(2,1)}, u32[]{:S(2)}, u32[]{:S(2)}) collective-permute-start(bf16[2,2,2,2,128,128]{5,4,3,2,1,0:T(8,128)(2,1)S(1)} %get-tuple-element.22), channel_id=1, source_target_pairs={{0,1},{2,3},{4,5},{6,7},{8,9},{10,11},{12,13},{14,15},{16,17},{18,... | collective-permute-start | bytes 1572872 | tf_op jit(solution)/shard_map/ppermute | solution.py:427
  33.5 1.3 %collective-permute-start.12 = (bf16[2,2,2,2,128,128]{5,4,3,2,1,0:T(8,128)(2,1)S(1)}, bf16[2,2,2,2,128,128]{5,4,3,2,1,0:T(8,128)(2,1)}, u32[]{:S(2)}, u32[]{:S(2)}) collective-permute-start(bf16[2,2,2,2,128,128]{5,4,3,2,1,0:T(8,128)(2,1)S(1)} %get-tuple-element.24), channel_id=1, source_target_pairs={{0,1},{2,3},{4,5},{6,7},{8,9},{10,11},{12,13},{14,15},{16,17},{18,... | collective-permute-start | bytes 1572872 | tf_op jit(solution)/shard_map/ppermute | solution.py:428
  34.8 1.3 %collective-permute-done.9 = bf16[2,2,2,2,128,128]{5,4,3,2,1,0:T(8,128)(2,1)} collective-permute-done((bf16[2,2,2,2,128,128]{5,4,3,2,1,0:T(8,128)(2,1)S(1)}, bf16[2,2,2,2,128,128]{5,4,3,2,1,0:T(8,128)(2,1)}, u32[]{:S(2)}, u32[]{:S(2)}) %collective-permute-start.9) | collective-permute-done | bytes 524320 | tf_op jit(solution)/shard_map/ppermute | solution.py:427
  36.2 1.0 %fusion = bf16[2,2,2,128,128]{4,3,2,1,0:T(8,128)(2,1)S(1)} fusion(f32[2,2,2,2,128,128]{5,4,3,2,1,0:T(8,128)S(1)} %get-tuple-element.21, s32[]{:T(128)S(6)} %select_n.79, bf16[2,2,2,2,128,128]{5,4,3,2,1,0:T(8,128)(2,1)} %collective-permute-done.9), kind=kLoop, calls=%fused_computation.2 | loop fusion | flops 393216 | bytes 1048580 | tf_op jit(solution)/shard_map/convert_element_type | solution.py:416
  37.2 3.1 %collective-permute-start.10 = (bf16[2,2,2,128,128]{4,3,2,1,0:T(8,128)(2,1)S(1)}, bf16[2,2,2,128,128]{4,3,2,1,0:T(8,128)(2,1)S(1)}, u32[]{:S(2)}, u32[]{:S(2)}) collective-permute-start(bf16[2,2,2,128,128]{4,3,2,1,0:T(8,128)(2,1)S(1)} %fusion), channel_id=1, source_target_pairs={{1,3},{3,1},{5,7},{7,5},{9,11},{11,9},{13,15},{15,13},{17,19},{19,... | collective-permute-start | bytes 786440 | tf_op jit(solution)/shard_map/ppermute | solution.py:23
  40.3 1.0 %fusion.1 = bf16[2,2,2,128,128]{4,3,2,1,0:T(8,128)(2,1)S(1)} fusion(f32[2,2,2,2,128,128]{5,4,3,2,1,0:T(8,128)S(1)} %get-tuple-element.23, s32[]{:T(128)S(6)} %select_n.80, bf16[2,2,2,2,128,128]{5,4,3,2,1,0:T(8,128)(2,1)} %collective-permute-done.12), kind=kLoop, calls=%fused_computation.3 | loop fusion | flops 393216 | bytes 1048580 | tf_op jit(solution)/shard_map/convert_element_type | solution.py:416
  41.3 3.2 %collective-permute-start.13 = (bf16[2,2,2,128,128]{4,3,2,1,0:T(8,128)(2,1)S(1)}, bf16[2,2,2,128,128]{4,3,2,1,0:T(8,128)(2,1)S(1)}, u32[]{:S(2)}, u32[]{:S(2)}) collective-permute-start(bf16[2,2,2,128,128]{4,3,2,1,0:T(8,128)(2,1)S(1)} %fusion.1), channel_id=1, source_target_pairs={{1,17},{3,19},{17,1},{19,3},{5,21},{7,23},{21,5},{23,7},{9,25},{11... | collective-permute-start | bytes 786440 | tf_op jit(solution)/shard_map/ppermute | solution.py:29
  45.5 2.9 %collective-permute-start.11 = (bf16[2,2,128,128]{3,2,1,0:T(8,128)(2,1)S(1)}, bf16[2,2,128,128]{3,2,1,0:T(8,128)(2,1)S(1)}, u32[]{:S(2)}, u32[]{:S(2)}) collective-permute-start(bf16[2,2,128,128]{3,2,1,0:T(8,128)(2,1)S(1)} %fusion.3), channel_id=1, source_target_pairs={{1,17},{3,19},{17,1},{19,3},{5,21},{7,23},{21,5},{23,7},{9,25},{11... | collective-permute-start | bytes 393224 | tf_op jit(solution)/shard_map/ppermute | solution.py:29
  49.4 3.1 %collective-permute-start.14 = (bf16[2,2,128,128]{3,2,1,0:T(8,128)(2,1)S(1)}, bf16[2,2,128,128]{3,2,1,0:T(8,128)(2,1)S(1)}, u32[]{:S(2)}, u32[]{:S(2)}) collective-permute-start(bf16[2,2,128,128]{3,2,1,0:T(8,128)(2,1)S(1)} %fusion.2), channel_id=1, source_target_pairs={{1,3},{3,1},{5,7},{7,5},{9,11},{11,9},{13,15},{15,13},{17,19},{19,... | collective-permute-start | bytes 393224 | tf_op jit(solution)/shard_map/ppermute | solution.py:23
  53.4 1.7 %collective-permute-done.14 = bf16[2,2,128,128]{3,2,1,0:T(8,128)(2,1)S(1)} collective-permute-done((bf16[2,2,128,128]{3,2,1,0:T(8,128)(2,1)S(1)}, bf16[2,2,128,128]{3,2,1,0:T(8,128)(2,1)S(1)}, u32[]{:S(2)}, u32[]{:S(2)}) %collective-permute-start.14) | collective-permute-done | bytes 131104 | tf_op jit(solution)/shard_map/ppermute | solution.py:23
  56.0 4.1 %collective-permute-start.15 = (bf16[2,2,128,128]{3,2,1,0:T(8,128)(2,1)S(1)}, bf16[2,2,128,128]{3,2,1,0:T(8,128)(2,1)S(1)}, u32[]{:S(2)}, u32[]{:S(2)}) collective-permute-start(bf16[2,2,128,128]{3,2,1,0:T(8,128)(2,1)S(1)} %pad_maximum_fusion.1), channel_id=1, source_target_pairs={{1,9},{3,11},{5,13},{7,15},{9,1},{11,3},{13,5},{15,7},{17,25},{19,... | collective-permute-start | bytes 393224 | tf_op jit(solution)/shard_map/ppermute | solution.py:29
  60.1 3.9 %collective-permute-done.15 = bf16[2,2,128,128]{3,2,1,0:T(8,128)(2,1)S(1)} collective-permute-done((bf16[2,2,128,128]{3,2,1,0:T(8,128)(2,1)S(1)}, bf16[2,2,128,128]{3,2,1,0:T(8,128)(2,1)S(1)}, u32[]{:S(2)}, u32[]{:S(2)}) %collective-permute-start.15) | collective-permute-done | bytes 131104 | tf_op jit(solution)/shard_map/ppermute | solution.py:29
  65.1 1.3 %collective-permute-start.18 = (bf16[2,64,128]{2,1,0:T(8,128)(2,1)S(1)}, bf16[2,64,128]{2,1,0:T(8,128)(2,1)S(1)}, u32[]{:S(2)}, u32[]{:S(2)}) collective-permute-start(bf16[2,64,128]{2,1,0:T(8,128)(2,1)S(1)} %pad_maximum_fusion.4), channel_id=1, source_target_pairs={{1,4},{3,6},{5,0},{7,2},{9,12},{11,14},{13,8},{15,10},{17,20},{19,... | collective-permute-start | bytes 98312 | tf_op jit(solution)/shard_map/ppermute | solution.py:29
  66.4 1.3 %collective-permute-start.16 = (f32[2,128,128]{2,1,0:T(8,128)S(1)}, f32[2,128,128]{2,1,0:T(8,128)S(1)}, u32[]{:S(2)}, u32[]{:S(2)}) collective-permute-start(f32[2,128,128]{2,1,0:T(8,128)S(1)} %pad_maximum_fusion.2), channel_id=1, source_target_pairs={{1,0},{3,2},{5,4},{7,6},{9,8},{11,10},{13,12},{15,14},{17,16},{19,... | collective-permute-start | bytes 393224 | tf_op jit(solution)/shard_map/ppermute | solution.py:452
  67.7 1.9 %collective-permute-start.17 = (bf16[2,64,128]{2,1,0:T(8,128)(2,1)S(1)}, bf16[2,64,128]{2,1,0:T(8,128)(2,1)S(1)}, u32[]{:S(2)}, u32[]{:S(2)}) collective-permute-start(bf16[2,64,128]{2,1,0:T(8,128)(2,1)S(1)} %pad_maximum_fusion.3), channel_id=1, source_target_pairs={{1,5},{3,7},{5,1},{7,3},{9,13},{11,15},{13,9},{15,11},{17,21},{19,... | collective-permute-start | bytes 98312 | tf_op jit(solution)/shard_map/ppermute | solution.py:29
  69.7 2.7 %collective-permute-done.17.got_ref = bf16[2,64,128]{2,1,0:T(8,128)(2,1)S(1)} collective-permute-done((bf16[2,64,128]{2,1,0:T(8,128)(2,1)S(1)}, bf16[2,64,128]{2,1,0:T(8,128)(2,1)S(1)}, u32[]{:S(2)}, u32[]{:S(2)}) %collective-permute-start.17) | collective-permute-done | bytes 32800 | tf_op jit(solution)/shard_map/ppermute | solution.py:29
  (42 shorter events, 5.6 us)
Async XLA Ops:
  0.0 4.0 %copy-start.1 = (bf16[1,1,160,512]{3,2,1,0:T(8,128)(2,1)S(1)}, bf16[1,1,160,512]{3,2,1,0:T(8,128)(2,1)}, u32[]{:S(2)}) copy-start(bf16[1,1,160,512]{3,2,1,0:T(8,128)(2,1)} %param.7) | copy-start | bytes 491524
  0.0 12.9 %copy-start.2 = (f32[9,512]{1,0:T(8,128)S(1)}, f32[9,512]{1,0:T(8,128)}, u32[]{:S(2)}) copy-start(f32[9,512]{1,0:T(8,128)} %taps_hbm.3) | copy-start | bytes 55300
  0.0 12.9 %copy-start.4 = (f32[512]{0:T(512)S(1)}, f32[512]{0:T(512)}, u32[]{:S(2)}) copy-start(f32[512]{0:T(512)} %param.10) | copy-start | bytes 6148
  1.9 11.0 %copy-start.3 = (s32[160,8]{0,1:T(8,128)S(1)}, s32[160,8]{0,1:T(8,128)}, u32[]{:S(2)}) copy-start(s32[160,8]{0,1:T(8,128)} %param.8) | copy-start | bytes 15364
  2.0 9.7 %collective-permute-start.6 = (bf16[128,1280]{1,0:T(8,128)(2,1)}, bf16[128,1280]{1,0:T(8,128)(2,1)S(1)}, u32[]{:S(2)}, u32[]{:S(2)}) collective-permute-start(bf16[128,1280]{1,0:T(8,128)(2,1)} %get-tuple-element.17.refs_4_.refs_6_), channel_id=1, source_target_pairs={{0,2},{1,3},{2,0},{3,1},{4,6},{5,7},{6,4},{7,5},{8,10},{9,11},{10,... | collective-permute-start | bytes 983048 | tf_op jit(solution)/shard_map/ppermute | solution.py:17
  4.1 8.9 %collective-permute-start = (bf16[160,512]{1,0:T(8,128)(2,1)S(1)}, bf16[160,512]{1,0:T(8,128)(2,1)S(1)}, u32[]{:S(2)}, u32[]{:S(2)}) collective-permute-start(bf16[160,512]{1,0:T(8,128)(2,1)S(1)} %bitcast.61), channel_id=1, source_target_pairs={{0,16},{16,0},{1,17},{17,1},{2,18},{18,2},{3,19},{19,3},{4,20},{20... | collective-permute-start | bytes 491528 | tf_op jit(solution)/shard_map/ppermute | solution.py:17
  5.3 10.8 %collective-permute-start.4 = (bf16[80,512]{1,0:T(8,128)(2,1)}, bf16[80,512]{1,0:T(8,128)(2,1)S(1)}, u32[]{:S(2)}, u32[]{:S(2)}) collective-permute-start(bf16[80,512]{1,0:T(8,128)(2,1)} %get-tuple-element.16), channel_id=1, source_target_pairs={{0,8},{4,12},{8,0},{12,4},{1,9},{5,13},{9,1},{13,5},{2,10},{6,14},... | collective-permute-start | bytes 245768 | tf_op jit(solution)/shard_map/ppermute | solution.py:17
  7.6 20.3 %collective-permute-start.7 = (bf16[128,1280]{1,0:T(8,128)(2,1)}, bf16[128,1280]{1,0:T(8,128)(2,1)S(1)}, u32[]{:S(2)}, u32[]{:S(2)}) collective-permute-start(bf16[128,1280]{1,0:T(8,128)(2,1)} %get-tuple-element.17.refs_4_.refs_6_), channel_id=1, source_target_pairs={{0,1},{1,0},{2,3},{3,2},{4,5},{5,4},{6,7},{7,6},{8,9},{9,8},{10,11... | collective-permute-start | bytes 983048 | tf_op jit(solution)/shard_map/ppermute | solution.py:17
  11.7 16.3 %collective-permute-start.8 = (bf16[128,1280]{1,0:T(8,128)(2,1)S(1)}, bf16[128,1280]{1,0:T(8,128)(2,1)S(1)}, u32[]{:S(2)}, u32[]{:S(2)}) collective-permute-start(bf16[128,1280]{1,0:T(8,128)(2,1)S(1)} %collective-permute-done.6.refs_5_.refs_7_), channel_id=1, source_target_pairs={{0,1},{1,0},{2,3},{3,2},{4,5},{5,4},{6,7},{7,6},{8,9},{9,8},{10,11... | collective-permute-start | bytes 983048 | tf_op jit(solution)/shard_map/ppermute | solution.py:17
  12.9 3.1 %copy-start.5 = (bf16[80,512]{1,0:T(8,128)(2,1)S(1)}, bf16[80,512]{1,0:T(8,128)(2,1)}, u32[]{:S(2)}) copy-start(bf16[80,512]{1,0:T(8,128)(2,1)} %get-tuple-element.15) | copy-start | bytes 245764
  14.4 5.7 %collective-permute-start.1 = (bf16[80,512]{1,0:T(8,128)(2,1)S(1)}, bf16[80,512]{1,0:T(8,128)(2,1)S(1)}, u32[]{:S(2)}, u32[]{:S(2)}) collective-permute-start(bf16[80,512]{1,0:T(8,128)(2,1)S(1)} %conv_near.1.refs_0_), channel_id=1, source_target_pairs={{0,4},{4,0},{8,12},{12,8},{1,5},{5,1},{9,13},{13,9},{2,6},{6,2},{1... | collective-permute-start | bytes 245768 | tf_op jit(solution)/shard_map/ppermute | solution.py:17
  16.1 11.9 %copy-start = (bf16[128,1280]{1,0:T(8,128)(2,1)S(1)}, bf16[128,1280]{1,0:T(8,128)(2,1)}, u32[]{:S(2)}) copy-start(bf16[128,1280]{1,0:T(8,128)(2,1)} %get-tuple-element.17.refs_4_.refs_6_) | copy-start | bytes 983044
  16.1 13.3 %collective-permute-start.5 = (bf16[2,80,512]{2,1,0:T(8,128)(2,1)S(1)}, bf16[2,80,512]{2,1,0:T(8,128)(2,1)S(1)}, u32[]{:S(2)}, u32[]{:S(2)}) collective-permute-start(bf16[2,80,512]{2,1,0:T(8,128)(2,1)S(1)} %pad_maximum_fusion.refs_4_), channel_id=1, source_target_pairs={{0,4},{4,0},{8,12},{12,8},{1,5},{5,1},{9,13},{13,9},{2,6},{6,2},{1... | collective-permute-start | bytes 491528 | tf_op jit(solution)/shard_map/ppermute | solution.py:17
  17.6 5.5 %collective-permute-start.2 = (bf16[80,512]{1,0:T(8,128)(2,1)S(1)}, bf16[80,512]{1,0:T(8,128)(2,1)S(1)}, u32[]{:S(2)}, u32[]{:S(2)}) collective-permute-start(bf16[80,512]{1,0:T(8,128)(2,1)S(1)} %conv_far.1), channel_id=1, source_target_pairs={{0,8},{4,12},{8,0},{12,4},{1,9},{5,13},{9,1},{13,5},{2,10},{6,14},... | collective-permute-start | bytes 245768 | tf_op jit(solution)/shard_map/ppermute | solution.py:17
  20.1 7.8 %collective-permute-start.3 = (bf16[80,512]{1,0:T(8,128)(2,1)S(1)}, bf16[80,512]{1,0:T(8,128)(2,1)S(1)}, u32[]{:S(2)}, u32[]{:S(2)}) collective-permute-start(bf16[80,512]{1,0:T(8,128)(2,1)S(1)} %conv_far.1), channel_id=1, source_target_pairs={{0,12},{4,8},{8,4},{12,0},{1,13},{5,9},{9,5},{13,1},{2,14},{6,10},... | collective-permute-start | bytes 245768 | tf_op jit(solution)/shard_map/ppermute | solution.py:17
  32.2 3.9 %collective-permute-start.9 = (bf16[2,2,2,2,128,128]{5,4,3,2,1,0:T(8,128)(2,1)S(1)}, bf16[2,2,2,2,128,128]{5,4,3,2,1,0:T(8,128)(2,1)}, u32[]{:S(2)}, u32[]{:S(2)}) collective-permute-start(bf16[2,2,2,2,128,128]{5,4,3,2,1,0:T(8,128)(2,1)S(1)} %get-tuple-element.22), channel_id=1, source_target_pairs={{0,1},{2,3},{4,5},{6,7},{8,9},{10,11},{12,13},{14,15},{16,17},{18,... | collective-permute-start | bytes 1572872 | tf_op jit(solution)/shard_map/ppermute | solution.py:427
  33.5 6.8 %collective-permute-start.12 = (bf16[2,2,2,2,128,128]{5,4,3,2,1,0:T(8,128)(2,1)S(1)}, bf16[2,2,2,2,128,128]{5,4,3,2,1,0:T(8,128)(2,1)}, u32[]{:S(2)}, u32[]{:S(2)}) collective-permute-start(bf16[2,2,2,2,128,128]{5,4,3,2,1,0:T(8,128)(2,1)S(1)} %get-tuple-element.24), channel_id=1, source_target_pairs={{0,1},{2,3},{4,5},{6,7},{8,9},{10,11},{12,13},{14,15},{16,17},{18,... | collective-permute-start | bytes 1572872 | tf_op jit(solution)/shard_map/ppermute | solution.py:428
  37.2 7.3 %collective-permute-start.10 = (bf16[2,2,2,128,128]{4,3,2,1,0:T(8,128)(2,1)S(1)}, bf16[2,2,2,128,128]{4,3,2,1,0:T(8,128)(2,1)S(1)}, u32[]{:S(2)}, u32[]{:S(2)}) collective-permute-start(bf16[2,2,2,128,128]{4,3,2,1,0:T(8,128)(2,1)S(1)} %fusion), channel_id=1, source_target_pairs={{1,3},{3,1},{5,7},{7,5},{9,11},{11,9},{13,15},{15,13},{17,19},{19,... | collective-permute-start | bytes 786440 | tf_op jit(solution)/shard_map/ppermute | solution.py:23
  41.3 7.1 %collective-permute-start.13 = (bf16[2,2,2,128,128]{4,3,2,1,0:T(8,128)(2,1)S(1)}, bf16[2,2,2,128,128]{4,3,2,1,0:T(8,128)(2,1)S(1)}, u32[]{:S(2)}, u32[]{:S(2)}) collective-permute-start(bf16[2,2,2,128,128]{4,3,2,1,0:T(8,128)(2,1)S(1)} %fusion.1), channel_id=1, source_target_pairs={{1,17},{3,19},{17,1},{19,3},{5,21},{7,23},{21,5},{23,7},{9,25},{11... | collective-permute-start | bytes 786440 | tf_op jit(solution)/shard_map/ppermute | solution.py:29
  45.5 7.0 %collective-permute-start.11 = (bf16[2,2,128,128]{3,2,1,0:T(8,128)(2,1)S(1)}, bf16[2,2,128,128]{3,2,1,0:T(8,128)(2,1)S(1)}, u32[]{:S(2)}, u32[]{:S(2)}) collective-permute-start(bf16[2,2,128,128]{3,2,1,0:T(8,128)(2,1)S(1)} %fusion.3), channel_id=1, source_target_pairs={{1,17},{3,19},{17,1},{19,3},{5,21},{7,23},{21,5},{23,7},{9,25},{11... | collective-permute-start | bytes 393224 | tf_op jit(solution)/shard_map/ppermute | solution.py:29
  49.4 5.7 %collective-permute-start.14 = (bf16[2,2,128,128]{3,2,1,0:T(8,128)(2,1)S(1)}, bf16[2,2,128,128]{3,2,1,0:T(8,128)(2,1)S(1)}, u32[]{:S(2)}, u32[]{:S(2)}) collective-permute-start(bf16[2,2,128,128]{3,2,1,0:T(8,128)(2,1)S(1)} %fusion.2), channel_id=1, source_target_pairs={{1,3},{3,1},{5,7},{7,5},{9,11},{11,9},{13,15},{15,13},{17,19},{19,... | collective-permute-start | bytes 393224 | tf_op jit(solution)/shard_map/ppermute | solution.py:23
  56.0 8.0 %collective-permute-start.15 = (bf16[2,2,128,128]{3,2,1,0:T(8,128)(2,1)S(1)}, bf16[2,2,128,128]{3,2,1,0:T(8,128)(2,1)S(1)}, u32[]{:S(2)}, u32[]{:S(2)}) collective-permute-start(bf16[2,2,128,128]{3,2,1,0:T(8,128)(2,1)S(1)} %pad_maximum_fusion.1), channel_id=1, source_target_pairs={{1,9},{3,11},{5,13},{7,15},{9,1},{11,3},{13,5},{15,7},{17,25},{19,... | collective-permute-start | bytes 393224 | tf_op jit(solution)/shard_map/ppermute | solution.py:29
  65.1 4.6 %collective-permute-start.18 = (bf16[2,64,128]{2,1,0:T(8,128)(2,1)S(1)}, bf16[2,64,128]{2,1,0:T(8,128)(2,1)S(1)}, u32[]{:S(2)}, u32[]{:S(2)}) collective-permute-start(bf16[2,64,128]{2,1,0:T(8,128)(2,1)S(1)} %pad_maximum_fusion.4), channel_id=1, source_target_pairs={{1,4},{3,6},{5,0},{7,2},{9,12},{11,14},{13,8},{15,10},{17,20},{19,... | collective-permute-start | bytes 98312 | tf_op jit(solution)/shard_map/ppermute | solution.py:29
  66.4 6.0 %collective-permute-start.16 = (f32[2,128,128]{2,1,0:T(8,128)S(1)}, f32[2,128,128]{2,1,0:T(8,128)S(1)}, u32[]{:S(2)}, u32[]{:S(2)}) collective-permute-start(f32[2,128,128]{2,1,0:T(8,128)S(1)} %pad_maximum_fusion.2), channel_id=1, source_target_pairs={{1,0},{3,2},{5,4},{7,6},{9,8},{11,10},{13,12},{15,14},{17,16},{19,... | collective-permute-start | bytes 393224 | tf_op jit(solution)/shard_map/ppermute | solution.py:452
  67.7 4.7 %collective-permute-start.17 = (bf16[2,64,128]{2,1,0:T(8,128)(2,1)S(1)}, bf16[2,64,128]{2,1,0:T(8,128)(2,1)S(1)}, u32[]{:S(2)}, u32[]{:S(2)}) collective-permute-start(bf16[2,64,128]{2,1,0:T(8,128)(2,1)S(1)} %pad_maximum_fusion.3), channel_id=1, source_target_pairs={{1,5},{3,7},{5,1},{7,3},{9,13},{11,15},{13,9},{15,11},{17,21},{19,... | collective-permute-start | bytes 98312 | tf_op jit(solution)/shard_map/ppermute | solution.py:29

commit v5 on v3

--- a/solution.py
+++ b/solution.py
@@ -29,30 +29,6 @@
 def start_all(copies):
     for copy in copies:
         copy.start()
-
-
-def prep_kernel(up_ref, qkv_ref, out_w_ref, mine_ref, other_ref, cut_ref, sems):
-    _, _, zp, zh, _, _ = place()
-    half = mine_ref.shape[0]
-    width = out_w_ref.shape[1] // 2
-    rows = lambda h: up_ref.at[pl.ds(pl.multiple_of(h * half, 16), half)]
-    copies = [
-        pltpu.make_async_copy(rows(zp), mine_ref, sems.at[0]),
-        pltpu.make_async_copy(rows(1 - zp), other_ref, sems.at[1]),
-        pltpu.make_async_copy(out_w_ref, cut_ref.at[:, pl.ds(3 * width, 2 * width)], sems.at[2]),
-    ]
-    for m in range(3):
-        start = pl.multiple_of((2 * m + zh) * width, 128)
-        copies.append(
-            pltpu.make_async_copy(
-                qkv_ref.at[:, pl.ds(start, width)],
-                cut_ref.at[:, pl.ds(m * width, width)],
-                sems.at[3 + m],
-            )
-        )
-    start_all(copies)
-    for copy in copies:
-        copy.wait()
 
 
 def conv_kernel(
@@ -127,17 +103,21 @@
     frames = 4
     row_refs, shards, refs = refs[:4], refs[4:8], refs[8:]
     qkv_ref, weights_ref, attended_ref, n_ref, w_ref, sems = refs
-    _, t, _, _, _, _ = place()
+    _, t, _, zh, _, _ = place()
     pixels, channels = row_refs[0].shape
     width = channels // 2
     rows = shards[0].shape[0]
     copies = [pltpu.make_async_copy(row_refs[k], n_ref.at[t ^ k], sems.at[k]) for k in range(frames)]
-    copies += [
-        pltpu.make_async_copy(
-            shards[k].at[:, pl.ds(0, 3 * width)], w_ref.at[shard_rows(k, rows)], sems.at[frames + k]
-        )
-        for k in range(4)
-    ]
+    for k in range(4):
+        for m in range(3):
+            columns = pl.ds(pl.multiple_of((2 * m + zh) * width, 128), width)
+            copies.append(
+                pltpu.make_async_copy(
+                    shards[k].at[:, columns],
+                    w_ref.at[shard_rows(k, rows), pl.ds(m * width, width)],
+                    sems.at[frames + 3 * k + m],
+                )
+            )
     start_all(copies)
     for copy in copies:
         copy.wait()
@@ -171,13 +151,13 @@
 
 def backward_kernel(*refs):
     frames = 4
-    row_refs, pair_refs, shards, refs = refs[:4], refs[4:6], refs[6:10], refs[10:]
+    row_refs, pair_refs, out_refs, refs = refs[:4], refs[4:6], refs[6:8], refs[8:]
     qkv_ref, weights_ref, attended_ref, refs = refs[0], refs[1], refs[2], refs[3:]
     keep_ref, send_ref, n_ref, u_ref, out_w_ref, sums_ref, out_sums_ref, sems = refs
-    _, t, _, zh, x, core = place()
+    _, t, _, zh, _, core = place()
     pixels, channels = row_refs[0].shape
     width = out_w_ref.shape[0]
-    rows = shards[0].shape[0]
+    rows = out_refs[0].shape[0]
     row_copies = [
         pltpu.make_async_copy(row_refs[k], n_ref.at[t ^ k], sems.at[k]) for k in range(frames)
     ]
@@ -186,27 +166,16 @@
         for k in range(frames)
     ]
 
-    def out_copy(shard, k):
+    for k in range(2):
         start = pl.multiple_of((core ^ k) * rows, 128)
-        return pltpu.make_async_copy(
-            shard.at[:, pl.ds(3 * width, channels)],
-            out_w_ref.at[pl.ds(start, rows)],
-            sems.at[2 * frames + k],
+        up_copies.append(
+            pltpu.make_async_copy(
+                out_refs[k], out_w_ref.at[pl.ds(start, rows)], sems.at[2 * frames + k]
+            )
         )
-
     start_all(up_copies)
-    for k in range(2):
-
-        @pl.when(x == zh)
-        def _(k=k):
-            out_copy(shards[2 * k], k).start()
-
-        @pl.when(x != zh)
-        def _(k=k):
-            out_copy(shards[2 * k + 1], k).start()
-
     start_all(row_copies)
-    for copy in up_copies + [out_copy(shards[2 * k], k) for k in range(2)]:
+    for copy in up_copies:
         copy.wait()
     upstream = u_ref[...].reshape(frames * pixels, channels)
     grads = lax.dot_general(
@@ -252,32 +221,23 @@
             sums_ref[lane // 128, pl.ds(m, channels, stride=3), :] = grad[:, lane : lane + 128]
     out_sums_ref[...] = over_rows(attended_ref[...], upstream)
 
-    block = 64
-    for x in range(2):
-        for y in range(2):
-            for zp in range(2):
-                slot = (x * 2 + y) * 2 + zp
-                for side, ref in ((core, keep_ref), (1 - core, send_ref)):
-                    if y == 1 and zp == 1:
-                        start = pl.multiple_of((2 * x + side) * block, block)
-                        rows = out_sums_ref[pl.ds(start, block), :]
-                        pieces = (rows[:, :width], rows[:, width:])
-                    else:
-                        pieces = []
-                        for low in range(2):
-                            index = y * 16 + (2 * zp + low) * 4 + 2 * x + side
-                            start = pl.multiple_of(index * block, block)
-                            pieces.append(
-                                jnp.concatenate(
-                                    [
-                                        sums_ref[lane, pl.ds(start, block), :]
-                                        for lane in range(width // 128)
-                                    ],
-                                    axis=1,
-                                )
-                            )
-                    for low in range(2):
-                        ref[slot, low * block : (low + 1) * block, :] = pieces[low].astype(ref.dtype)
+    block = channels // HEADS
+    for slot in range(8):
+        at_x, at_y, at_zp = slot >> 2, (slot >> 1) & 1, slot & 1
+        for side, ref in ((core, keep_ref), (1 - core, send_ref)):
+            for low in range(2):
+                rows_at = slice(low * block, (low + 1) * block)
+                first = at_y * 16 + (2 * at_zp + low) * 4 + 2 * at_x
+                if first < 3 * HEADS:
+                    start = pl.multiple_of((first + (side ^ zh ^ low)) * block, block)
+                    for lane in range(width // 128):
+                        piece = sums_ref[lane, pl.ds(start, block), :]
+                        lanes_at = slice(lane * 128, (lane + 1) * 128)
+                        ref[slot, rows_at, lanes_at] = piece.astype(ref.dtype)
+                else:
+                    start = pl.multiple_of((2 * at_x + side) * block, block)
+                    piece = out_sums_ref[pl.ds(start, block), low * width : (low + 1) * width]
+                    ref[slot, rows_at, :] = piece.astype(ref.dtype)
 
 
 def join_kernel(total_ref, got_ref, out_ref):
@@ -305,21 +265,10 @@
     piece = jax.ShapeDtypeStruct((half, channels), narrow_type)
 
     band = swap(own, "blk", 1)
-    up_mine, up_other, cut = pl.pallas_call(
-        prep_kernel,
-        out_shape=(
-            piece,
-            piece,
-            jax.ShapeDtypeStruct((qkv_weight.shape[0], 3 * width + channels), narrow_type),
-        ),
-        in_specs=[anywhere] * 3,
-        out_specs=(in_vmem,) * 3,
-        scratch_shapes=[pltpu.SemaphoreType.DMA((6,))],
-        name="prep",
-    )(cotangent[0, 0], qkv_weight, out_weight)
-
-    cut_x = swap(cut, "fsdp", 2)
-    up_2 = swap(up_other, "tm", 2)
+    qkv_x = swap(qkv_weight, "fsdp", 2)
+    out_x = swap(out_weight, "fsdp", 2)
+    halves = cotangent[0, 0].reshape(2, half, channels)
+    up_2 = swap(pick(halves, 1 - zp), "tm", 2)
 
     def conv(far):
         return pl.pallas_call(
@@ -344,10 +293,12 @@
     row_2 = swap(n_other, "tm", 2)
     n_mine = conv(False)
     row_1 = swap(n_mine, "tm", 1)
-    up_own = jnp.stack([up_mine, up_2])
+    up_own = jnp.stack([pick(halves, zp), up_2])
     up_got = swap(up_own, "tm", 1)
-    cut_c = swap(cut, "fsdp", 1)
-    cut_xc = swap(cut_x, "fsdp", 1)
+    qkv_c = swap(qkv_weight, "fsdp", 1)
+    qkv_xc = swap(qkv_x, "fsdp", 1)
+    out_rows = jnp.where(x == zh, out_weight, out_x)
+    out_c = swap(out_rows, "fsdp", 1)
 
     qkv, weights, attended = pl.pallas_call(
         forward_kernel,
@@ -361,18 +312,18 @@
         scratch_shapes=[
             pltpu.VMEM((4, half, channels), narrow_type),
             pltpu.VMEM((channels, 3 * width), narrow_type),
-            pltpu.SemaphoreType.DMA((8,)),
+            pltpu.SemaphoreType.DMA((16,)),
         ],
         compiler_params=pltpu.CompilerParams(vmem_limit_bytes=24 << 20),
         name="forward",
-    )(n_mine, row_1, row_2, row_3, cut, cut_x, cut_c, cut_xc)
+    )(n_mine, row_1, row_2, row_3, qkv_weight, qkv_x, qkv_c, qkv_xc)
     keep, send = pl.pallas_call(
         backward_kernel,
         out_shape=(
             jax.ShapeDtypeStruct((8, 2 * block, width), jnp.float32),
             jax.ShapeDtypeStruct((8, 2 * block, width), narrow_type),
         ),
-        in_specs=[anywhere] * 10 + [in_vmem] * 3,
+        in_specs=[anywhere] * 8 + [in_vmem] * 3,
         out_specs=(in_vmem, in_vmem),
         scratch_shapes=[
             pltpu.VMEM((4, half, channels), narrow_type),
@@ -385,8 +336,7 @@
         compiler_params=pltpu.CompilerParams(vmem_limit_bytes=28 << 20),
         name="backward",
     )(
-        n_mine, row_1, row_2, row_3, up_own, up_got, cut, cut_x, cut_c, cut_xc,
-        qkv, weights, attended,
+        n_mine, row_1, row_2, row_3, up_own, up_got, out_rows, out_c, qkv, weights, attended
     )
 
     def narrow(values):
@@ -406,7 +356,9 @@
     total = jnp.concatenate([first, second], axis=-1)
     total = pick(total, zp) + swap(narrow(pick(total, 1 - zp)), "tm", 2).astype(jnp.float32)
     total = total.reshape(2, block, width)
-    got = swap(narrow(pick(total, 1 - zh)), "tm", 1)
+    cores = lax.axis_size("fsdp")
+    crossed = [(i, i ^ cores ^ 1) for i in range(lax.axis_size("tm") * cores)]
+    got = lax.ppermute(narrow(pick(total, 1 - zh)), ("tm", "fsdp"), crossed)
     lanes = 128
     out = pl.pallas_call(
         join_kernel,

time: 57 us -> 61.3 us (1.075)
  waiting for transfers between devices: 20.9 us -> 28.4 us
  starting transfers between devices: 25.5 us -> 22.8 us
  Pallas kernels: 9.77 us -> 8.22 us
  local copies, waits for them, and re-layouts: 0.23 us -> 1.22 us
    ppermute x16 -> x17, waiting for transfers between devices: 20.9 us -> 25.1 us  [swap(): lax.ppermute(values, axis, [(i, i ^ mask) for i in range(lax.axis_size(ax...]
    ppermute x0 -> x1, waiting for transfers between devices: none -> 3.33 us  [split_form(): got = lax.ppermute(narrow(pick(total, 1 - zh)), ('tm', 'fsdp'), crossed)]
    ppermute x16 -> x17, starting transfers between devices: 25.5 us -> 22.8 us  [swap(): lax.ppermute(values, axis, [(i, i ^ mask) for i in range(lax.axis_size(ax...]
    pallas_call x1 -> x0, Pallas kernels: 1.91 us -> none  [split_form(): pl.pallas_call(prep_kernel, out_shape=(piece, piece, jax.ShapeDtypeStruct...]
    dynamic_slice x0 -> x1, local copies, waits for them, and re-layouts: none -> 0.98 us  [pick(): return lax.dynamic_index_in_dim(values, index, dim, keepdims=False)]
  transfers between devices with their start and end apart: 16 -> 18, of which waited for: 9 -> 10; matrix products, arithmetic and copies ran while one was open for 0% -> 2% of each run, Pallas kernels for 8% -> 7%
where the time goes in v5:
time: 61.3 us; the launch traced here: 61.2 us
  waiting for transfers between devices  28.4 us (46%)
  starting transfers between devices  22.8 us (37%)
  Pallas kernels  8.22 us (13%)
  local copies, waits for them, and re-layouts  1.22 us (2%)
    ppermute x17, waiting for transfers between devices, swap(): lax.ppermute(values, axis, [(i, i ^ mask) for i in range(lax.axis_size(ax...  25.1 us
    ppermute x17, starting transfers between devices, swap(): lax.ppermute(values, axis, [(i, i ^ mask) for i in range(lax.axis_size(ax...  22.8 us
    ppermute x1, waiting for transfers between devices, split_form(): got = lax.ppermute(narrow(pick(total, 1 - zh)), ('tm', 'fsdp'), crossed)  3.33 us
    pallas_call x1, Pallas kernels, split_form(): pl.pallas_call(backward_kernel, out_shape=(jax.ShapeDtypeStruct((8, 2 * b...  3.07 us
    pallas_call x2, Pallas kernels, conv(): pl.pallas_call(functools.partial(conv_kernel, far), out_shape=piece, in_s...  2.91 us
    pallas_call x1, Pallas kernels, split_form(): pl.pallas_call(forward_kernel, out_shape=(jax.ShapeDtypeStruct((4 * half,...  1.57 us
  transfers between devices with their start and end apart: 18, of which 10 were waited for; matrix products, arithmetic and copies ran while one was open for 2% of the time, Pallas kernels for 7%

profile of v5, /device:TPU:0, one launch (start us, length us, event | category | flops | bytes accessed | tf_op | source)
XLA Modules:
  0.0 61.2 jit_solution(12198035729837161383)
XLA Ops:
  0.0 3.0 %collective-permute-start.8 = (bf16[128,1536]{1,0:T(8,128)(2,1)}, bf16[128,1536]{1,0:T(8,128)(2,1)S(1)}, u32[]{:S(2)}, u32[]{:S(2)}) collective-permute-start(bf16[128,1536]{1,0:T(8,128)(2,1)} %refs_4_.1), channel_id=1, source_target_pairs={{0,2},{1,3},{2,0},{3,1},{4,6},{5,7},{6,4},{7,5},{8,10},{9,11},{10,... | collective-permute-start | bytes 1179656 | tf_op jit(solution)/shard_map/ppermute | solution.py:17
  3.0 1.0 %constant_dynamic-slice_fusion = (bf16[1,80,512]{2,1,0:T(8,128)(2,1)S(1)}, bf16[80,512]{1,0:T(8,128)(2,1)S(1)}) fusion(bf16[2,80,512]{2,1,0:T(8,128)(2,1)} %bitcast.50, s32[]{:T(128)S(6)} %select_n.41, s32[]{:T(128)S(6)} %select_n.42), kind=kLoop, calls=%fused_computation.28 | loop fusion | bytes 327688 | tf_op jit(solution)/shard_map/jit(dynamic_index_in_dim)/dynamic_slice | solution.py:21
  4.0 2.7 %collective-permute-start.4 = (bf16[80,512]{1,0:T(8,128)(2,1)S(1)}, bf16[80,512]{1,0:T(8,128)(2,1)S(1)}, u32[]{:S(2)}, u32[]{:S(2)}) collective-permute-start(bf16[80,512]{1,0:T(8,128)(2,1)S(1)} %get-tuple-element.18), channel_id=1, source_target_pairs={{0,8},{4,12},{8,0},{12,4},{1,9},{5,13},{9,1},{13,5},{2,10},{6,14},... | collective-permute-start | bytes 245768 | tf_op jit(solution)/shard_map/ppermute | solution.py:17
  6.6 1.5 %collective-permute-start = (bf16[160,512]{1,0:T(8,128)(2,1)S(1)}, bf16[160,512]{1,0:T(8,128)(2,1)S(1)}, u32[]{:S(2)}, u32[]{:S(2)}) collective-permute-start(bf16[160,512]{1,0:T(8,128)(2,1)S(1)} %bitcast.42), channel_id=1, source_target_pairs={{0,16},{16,0},{1,17},{17,1},{2,18},{18,2},{3,19},{19,3},{4,20},{20... | collective-permute-start | bytes 491528 | tf_op jit(solution)/shard_map/ppermute | solution.py:17
  8.1 0.5 collective-permute-start.6
  8.7 4.5 %collective-permute-done.8.refs_5_ = bf16[128,1536]{1,0:T(8,128)(2,1)S(1)} collective-permute-done((bf16[128,1536]{1,0:T(8,128)(2,1)}, bf16[128,1536]{1,0:T(8,128)(2,1)S(1)}, u32[]{:S(2)}, u32[]{:S(2)}) %collective-permute-start.8) | collective-permute-done | bytes 393248 | tf_op jit(solution)/shard_map/ppermute | solution.py:17
  13.2 2.2 %collective-permute-start.5 = (bf16[2,80,512]{2,1,0:T(8,128)(2,1)S(1)}, bf16[2,80,512]{2,1,0:T(8,128)(2,1)S(1)}, u32[]{:S(2)}, u32[]{:S(2)}) collective-permute-start(bf16[2,80,512]{2,1,0:T(8,128)(2,1)S(1)} %pad_maximum_fusion.refs_4_), channel_id=1, source_target_pairs={{0,4},{4,0},{8,12},{12,8},{1,5},{5,1},{9,13},{13,9},{2,6},{6,2},{1... | collective-permute-start | bytes 491528 | tf_op jit(solution)/shard_map/ppermute | solution.py:17
  15.4 1.5 %conv_near.1.refs_0_ = bf16[80,512]{1,0:T(8,128)(2,1)S(1)} custom-call(s32[8,160]{1,0:T(8,128)S(1)} %bitcast.45, bf16[160,512]{1,0:T(8,128)(2,1)S(1)} %bitcast.43, bf16[160,512]{1,0:T(8,128)(2,1)S(1)} %collective-permute-done.band_hbm, f32[9,512]{1,0:T(8,128)S(1)} %copy-done.2, f32[1,512]{1,0:T(1,128)S(1)} %bitcast.47), custom_call_target="tpu_custom_call" | custom-call | tf_op jit(solution)/shard_map/conv_near/pallas_call | solution.py:274
  16.9 0.7 %collective-permute-start.1 = (bf16[80,512]{1,0:T(8,128)(2,1)S(1)}, bf16[80,512]{1,0:T(8,128)(2,1)S(1)}, u32[]{:S(2)}, u32[]{:S(2)}) collective-permute-start(bf16[80,512]{1,0:T(8,128)(2,1)S(1)} %conv_near.1.refs_0_), channel_id=1, source_target_pairs={{0,4},{4,0},{8,12},{12,8},{1,5},{5,1},{9,13},{13,9},{2,6},{6,2},{1... | collective-permute-start | bytes 245768 | tf_op jit(solution)/shard_map/ppermute | solution.py:17
  17.6 1.4 %conv_far.1 = bf16[80,512]{1,0:T(8,128)(2,1)S(1)} custom-call(s32[8,160]{1,0:T(8,128)S(1)} %bitcast.46, bf16[160,512]{1,0:T(8,128)(2,1)S(1)} %bitcast.44, bf16[160,512]{1,0:T(8,128)(2,1)S(1)} %collective-permute-done.band_hbm, f32[9,512]{1,0:T(8,128)S(1)} %copy-done.2, f32[1,512]{1,0:T(1,128)S(1)} %bitcast.48), custom_call_target="tpu_custom_call" | custom-call | tf_op jit(solution)/shard_map/conv_far/pallas_call | solution.py:274
  19.0 2.7 %collective-permute-start.2 = (bf16[80,512]{1,0:T(8,128)(2,1)S(1)}, bf16[80,512]{1,0:T(8,128)(2,1)S(1)}, u32[]{:S(2)}, u32[]{:S(2)}) collective-permute-start(bf16[80,512]{1,0:T(8,128)(2,1)S(1)} %conv_far.1), channel_id=1, source_target_pairs={{0,8},{4,12},{8,0},{12,4},{1,9},{5,13},{9,1},{13,5},{2,10},{6,14},... | collective-permute-start | bytes 245768 | tf_op jit(solution)/shard_map/ppermute | solution.py:17
  21.7 0.3 collective-permute-done.1.refs_1_
  22.0 4.3 %collective-permute-done.2.refs_2_ = bf16[80,512]{1,0:T(8,128)(2,1)S(1)} collective-permute-done((bf16[80,512]{1,0:T(8,128)(2,1)S(1)}, bf16[80,512]{1,0:T(8,128)(2,1)S(1)}, u32[]{:S(2)}, u32[]{:S(2)}) %collective-permute-start.2) | collective-permute-done | bytes 81952 | tf_op jit(solution)/shard_map/ppermute | solution.py:17
  26.3 3.2 %collective-permute-start.3 = (bf16[80,512]{1,0:T(8,128)(2,1)S(1)}, bf16[80,512]{1,0:T(8,128)(2,1)S(1)}, u32[]{:S(2)}, u32[]{:S(2)}) collective-permute-start(bf16[80,512]{1,0:T(8,128)(2,1)S(1)} %conv_far.1), channel_id=1, source_target_pairs={{0,12},{4,8},{8,4},{12,0},{1,13},{5,9},{9,5},{13,1},{2,14},{6,10},... | collective-permute-start | bytes 245768 | tf_op jit(solution)/shard_map/ppermute | solution.py:17
  29.5 3.1 %collective-permute-done.3.refs_3_ = bf16[80,512]{1,0:T(8,128)(2,1)S(1)} collective-permute-done((bf16[80,512]{1,0:T(8,128)(2,1)S(1)}, bf16[80,512]{1,0:T(8,128)(2,1)S(1)}, u32[]{:S(2)}, u32[]{:S(2)}) %collective-permute-start.3) | collective-permute-done | bytes 81952 | tf_op jit(solution)/shard_map/ppermute | solution.py:17
  32.6 1.6 %forward.1 = (bf16[320,768]{1,0:T(8,128)(2,1)S(1)}, bf16[10,80,256]{2,1,0:T(8,128)(2,1)S(1)}, bf16[320,256]{1,0:T(8,128)(2,1)S(1)}) custom-call(bf16[80,512]{1,0:T(8,128)(2,1)S(1)} %conv_near.1.refs_0_, bf16[80,512]{1,0:T(8,128)(2,1)S(1)} %collective-permute-done.1.refs_1_, bf16[80,512]{1,0:T(8,128)(2,1)S(1)} %collective-permute-done.2.refs_2_, ...), custom_call_target="tpu_custom_call" | custom-call | tf_op jit(solution)/shard_map/forward/pallas_call | solution.py:303
  34.1 3.1 %backward.1 = (f32[8,128,256]{2,1,0:T(8,128)S(1)}, bf16[8,128,256]{2,1,0:T(8,128)(2,1)S(1)}) custom-call(bf16[80,512]{1,0:T(8,128)(2,1)S(1)} %conv_near.1.refs_0_, bf16[80,512]{1,0:T(8,128)(2,1)S(1)} %collective-permute-done.1.refs_1_, bf16[80,512]{1,0:T(8,128)(2,1)S(1)} %collective-permute-done.2.refs_2_, ...), custom_call_target="tpu_custom_call" | custom-call | tf_op jit(solution)/shard_map/backward/pallas_call | solution.py:320
  37.2 0.1 collective-permute-start.11
  37.3 1.9 %collective-permute-done.11 = bf16[8,128,256]{2,1,0:T(8,128)(2,1)S(1)} collective-permute-done((bf16[8,128,256]{2,1,0:T(8,128)(2,1)S(1)}, bf16[8,128,256]{2,1,0:T(8,128)(2,1)S(1)}, u32[]{:S(2)}, u32[]{:S(2)}) %collective-permute-start.11) | collective-permute-done | bytes 524320 | tf_op jit(solution)/shard_map/ppermute | solution.py:17
  39.2 0.1 convert_add_fusion
  39.3 0.1 fusion.11
  39.5 1.6 %collective-permute-start.14 = (bf16[2,2,128,128]{3,2,1,0:T(8,128)(2,1)S(1)}, bf16[2,2,128,128]{3,2,1,0:T(8,128)(2,1)S(1)}, u32[]{:S(2)}, u32[]{:S(2)}) collective-permute-start(bf16[2,2,128,128]{3,2,1,0:T(8,128)(2,1)S(1)} %fusion.1), channel_id=1, source_target_pairs={{0,16},{16,0},{1,17},{17,1},{2,18},{18,2},{3,19},{19,3},{4,20},{20... | collective-permute-start | bytes 393224 | tf_op jit(solution)/shard_map/ppermute | solution.py:17
  41.1 1.5 %collective-permute-start.12 = (bf16[2,2,128,128]{3,2,1,0:T(8,128)(2,1)S(1)}, bf16[2,2,128,128]{3,2,1,0:T(8,128)(2,1)S(1)}, u32[]{:S(2)}, u32[]{:S(2)}) collective-permute-start(bf16[2,2,128,128]{3,2,1,0:T(8,128)(2,1)S(1)} %fusion), channel_id=1, source_target_pairs={{0,2},{1,3},{2,0},{3,1},{4,6},{5,7},{6,4},{7,5},{8,10},{9,11},{10,... | collective-permute-start | bytes 393224 | tf_op jit(solution)/shard_map/ppermute | solution.py:17
  42.6 2.4 %collective-permute-done.14 = bf16[2,2,128,128]{3,2,1,0:T(8,128)(2,1)S(1)} collective-permute-done((bf16[2,2,128,128]{3,2,1,0:T(8,128)(2,1)S(1)}, bf16[2,2,128,128]{3,2,1,0:T(8,128)(2,1)S(1)}, u32[]{:S(2)}, u32[]{:S(2)}) %collective-permute-start.14) | collective-permute-done | bytes 131104 | tf_op jit(solution)/shard_map/ppermute | solution.py:17
  45.1 1.6 %collective-permute-start.15 = (bf16[2,128,128]{2,1,0:T(8,128)(2,1)S(1)}, bf16[2,128,128]{2,1,0:T(8,128)(2,1)S(1)}, u32[]{:S(2)}, u32[]{:S(2)}) collective-permute-start(bf16[2,128,128]{2,1,0:T(8,128)(2,1)S(1)} %fusion.8), channel_id=1, source_target_pairs={{0,2},{1,3},{2,0},{3,1},{4,6},{5,7},{6,4},{7,5},{8,10},{9,11},{10,... | collective-permute-start | bytes 196616 | tf_op jit(solution)/shard_map/ppermute | solution.py:17
  46.8 1.6 %collective-permute-start.13 = (bf16[2,128,128]{2,1,0:T(8,128)(2,1)S(1)}, bf16[2,128,128]{2,1,0:T(8,128)(2,1)S(1)}, u32[]{:S(2)}, u32[]{:S(2)}) collective-permute-start(bf16[2,128,128]{2,1,0:T(8,128)(2,1)S(1)} %fusion.7), channel_id=1, source_target_pairs={{0,16},{16,0},{1,17},{17,1},{2,18},{18,2},{3,19},{19,3},{4,20},{20... | collective-permute-start | bytes 196616 | tf_op jit(solution)/shard_map/ppermute | solution.py:17
  48.3 1.1 %collective-permute-done.15 = bf16[2,128,128]{2,1,0:T(8,128)(2,1)S(1)} collective-permute-done((bf16[2,128,128]{2,1,0:T(8,128)(2,1)S(1)}, bf16[2,128,128]{2,1,0:T(8,128)(2,1)S(1)}, u32[]{:S(2)}, u32[]{:S(2)}) %collective-permute-start.15) | collective-permute-done | bytes 65568 | tf_op jit(solution)/shard_map/ppermute | solution.py:17
  49.5 1.6 %collective-permute-done.13 = bf16[2,128,128]{2,1,0:T(8,128)(2,1)S(1)} collective-permute-done((bf16[2,128,128]{2,1,0:T(8,128)(2,1)S(1)}, bf16[2,128,128]{2,1,0:T(8,128)(2,1)S(1)}, u32[]{:S(2)}, u32[]{:S(2)}) %collective-permute-start.13) | collective-permute-done | bytes 65568 | tf_op jit(solution)/shard_map/ppermute | solution.py:17
  51.1 0.1 collective-permute-start.16
  51.2 5.8 %collective-permute-done.16 = bf16[128,256]{1,0:T(8,128)(2,1)S(1)} collective-permute-done((bf16[128,256]{1,0:T(8,128)(2,1)S(1)}, bf16[128,256]{1,0:T(8,128)(2,1)S(1)}, u32[]{:S(2)}, u32[]{:S(2)}) %collective-permute-start.16) | collective-permute-done | bytes 65568 | tf_op jit(solution)/shard_map/ppermute | solution.py:17
  57.2 3.3 %collective-permute-done.17.got_ref = bf16[64,256]{1,0:T(8,128)(2,1)S(1)} collective-permute-done((bf16[64,256]{1,0:T(8,128)(2,1)S(1)}, bf16[64,256]{1,0:T(8,128)(2,1)S(1)}, u32[]{:S(2)}, u32[]{:S(2)}) %collective-permute-start.17) | collective-permute-done | bytes 32800 | tf_op jit(solution)/shard_map/ppermute | solution.py:361
  60.5 0.7 %join.1 = f32[256,128]{1,0:T(8,128)} custom-call(f32[2,64,256]{2,1,0:T(8,128)S(1)} %bitcast.41, bf16[64,256]{1,0:T(8,128)(2,1)S(1)} %collective-permute-done.17.got_ref), custom_call_target="tpu_custom_call" | custom-call | tf_op jit(solution)/shard_map/join/pallas_call | solution.py:363
  (37 shorter events, 0.4 us)
Async XLA Ops:
  0.0 13.1 %collective-permute-start.8 = (bf16[128,1536]{1,0:T(8,128)(2,1)}, bf16[128,1536]{1,0:T(8,128)(2,1)S(1)}, u32[]{:S(2)}, u32[]{:S(2)}) collective-permute-start(bf16[128,1536]{1,0:T(8,128)(2,1)} %refs_4_.1), channel_id=1, source_target_pairs={{0,2},{1,3},{2,0},{3,1},{4,6},{5,7},{6,4},{7,5},{8,10},{9,11},{10,... | collective-permute-start | bytes 1179656 | tf_op jit(solution)/shard_map/ppermute | solution.py:17
  3.0 3.6 %copy-start = (bf16[1,1,160,512]{3,2,1,0:T(8,128)(2,1)S(1)}, bf16[1,1,160,512]{3,2,1,0:T(8,128)(2,1)}, u32[]{:S(2)}) copy-start(bf16[1,1,160,512]{3,2,1,0:T(8,128)(2,1)} %param.7) | copy-start | bytes 491524
  3.0 5.2 %copy-start.5 = (bf16[128,512]{1,0:T(8,128)(2,1)S(1)}, bf16[128,512]{1,0:T(8,128)(2,1)}, u32[]{:S(2)}) copy-start(bf16[128,512]{1,0:T(8,128)(2,1)} %param.12) | copy-start | bytes 393220
  4.0 9.2 %collective-permute-start.4 = (bf16[80,512]{1,0:T(8,128)(2,1)S(1)}, bf16[80,512]{1,0:T(8,128)(2,1)S(1)}, u32[]{:S(2)}, u32[]{:S(2)}) collective-permute-start(bf16[80,512]{1,0:T(8,128)(2,1)S(1)} %get-tuple-element.18), channel_id=1, source_target_pairs={{0,8},{4,12},{8,0},{12,4},{1,9},{5,13},{9,1},{13,5},{2,10},{6,14},... | collective-permute-start | bytes 245768 | tf_op jit(solution)/shard_map/ppermute | solution.py:17
  6.6 8.8 %collective-permute-start = (bf16[160,512]{1,0:T(8,128)(2,1)S(1)}, bf16[160,512]{1,0:T(8,128)(2,1)S(1)}, u32[]{:S(2)}, u32[]{:S(2)}) collective-permute-start(bf16[160,512]{1,0:T(8,128)(2,1)S(1)} %bitcast.42), channel_id=1, source_target_pairs={{0,16},{16,0},{1,17},{17,1},{2,18},{18,2},{3,19},{19,3},{4,20},{20... | collective-permute-start | bytes 491528 | tf_op jit(solution)/shard_map/ppermute | solution.py:17
  8.1 10.9 %collective-permute-start.6 = (bf16[128,512]{1,0:T(8,128)(2,1)S(1)}, bf16[128,512]{1,0:T(8,128)(2,1)S(1)}, u32[]{:S(2)}, u32[]{:S(2)}) collective-permute-start(bf16[128,512]{1,0:T(8,128)(2,1)S(1)} %copy-done.5), channel_id=1, source_target_pairs={{0,2},{1,3},{2,0},{3,1},{4,6},{5,7},{6,4},{7,5},{8,10},{9,11},{10,... | collective-permute-start | bytes 393224 | tf_op jit(solution)/shard_map/ppermute | solution.py:17
  8.7 23.9 %collective-permute-start.9 = (bf16[128,1536]{1,0:T(8,128)(2,1)}, bf16[128,1536]{1,0:T(8,128)(2,1)S(1)}, u32[]{:S(2)}, u32[]{:S(2)}) collective-permute-start(bf16[128,1536]{1,0:T(8,128)(2,1)} %refs_4_.1), channel_id=1, source_target_pairs={{0,1},{1,0},{2,3},{3,2},{4,5},{5,4},{6,7},{7,6},{8,9},{9,8},{10,11... | collective-permute-start | bytes 1179656 | tf_op jit(solution)/shard_map/ppermute | solution.py:17
  13.1 19.4 %collective-permute-start.10 = (bf16[128,1536]{1,0:T(8,128)(2,1)S(1)}, bf16[128,1536]{1,0:T(8,128)(2,1)S(1)}, u32[]{:S(2)}, u32[]{:S(2)}) collective-permute-start(bf16[128,1536]{1,0:T(8,128)(2,1)S(1)} %collective-permute-done.8.refs_5_), channel_id=1, source_target_pairs={{0,1},{1,0},{2,3},{3,2},{4,5},{5,4},{6,7},{7,6},{8,9},{9,8},{10,11... | collective-permute-start | bytes 1179656 | tf_op jit(solution)/shard_map/ppermute | solution.py:17
  13.1 2.2 %copy-start.2 = (f32[9,512]{1,0:T(8,128)S(1)}, f32[9,512]{1,0:T(8,128)}, u32[]{:S(2)}) copy-start(f32[9,512]{1,0:T(8,128)} %taps_hbm.3) | copy-start | bytes 55300
  13.2 2.2 %copy-start.3 = (s32[160,8]{0,1:T(8,128)S(1)}, s32[160,8]{0,1:T(8,128)}, u32[]{:S(2)}) copy-start(s32[160,8]{0,1:T(8,128)} %param.8) | copy-start | bytes 15364
  13.2 2.2 %copy-start.4 = (f32[512]{0:T(512)S(1)}, f32[512]{0:T(512)}, u32[]{:S(2)}) copy-start(f32[512]{0:T(512)} %param.10) | copy-start | bytes 6148
  13.2 20.9 %collective-permute-start.5 = (bf16[2,80,512]{2,1,0:T(8,128)(2,1)S(1)}, bf16[2,80,512]{2,1,0:T(8,128)(2,1)S(1)}, u32[]{:S(2)}, u32[]{:S(2)}) collective-permute-start(bf16[2,80,512]{2,1,0:T(8,128)(2,1)S(1)} %pad_maximum_fusion.refs_4_), channel_id=1, source_target_pairs={{0,4},{4,0},{8,12},{12,8},{1,5},{5,1},{9,13},{13,9},{2,6},{6,2},{1... | collective-permute-start | bytes 491528 | tf_op jit(solution)/shard_map/ppermute | solution.py:17
  16.9 15.7 %copy-start.1 = (bf16[128,1536]{1,0:T(8,128)(2,1)S(1)}, bf16[128,1536]{1,0:T(8,128)(2,1)}, u32[]{:S(2)}) copy-start(bf16[128,1536]{1,0:T(8,128)(2,1)} %refs_4_.1) | copy-start | bytes 1179652
  16.9 5.1 %collective-permute-start.1 = (bf16[80,512]{1,0:T(8,128)(2,1)S(1)}, bf16[80,512]{1,0:T(8,128)(2,1)S(1)}, u32[]{:S(2)}, u32[]{:S(2)}) collective-permute-start(bf16[80,512]{1,0:T(8,128)(2,1)S(1)} %conv_near.1.refs_0_), channel_id=1, source_target_pairs={{0,4},{4,0},{8,12},{12,8},{1,5},{5,1},{9,13},{13,9},{2,6},{6,2},{1... | collective-permute-start | bytes 245768 | tf_op jit(solution)/shard_map/ppermute | solution.py:17
  19.0 7.3 %collective-permute-start.2 = (bf16[80,512]{1,0:T(8,128)(2,1)S(1)}, bf16[80,512]{1,0:T(8,128)(2,1)S(1)}, u32[]{:S(2)}, u32[]{:S(2)}) collective-permute-start(bf16[80,512]{1,0:T(8,128)(2,1)S(1)} %conv_far.1), channel_id=1, source_target_pairs={{0,8},{4,12},{8,0},{12,4},{1,9},{5,13},{9,1},{13,5},{2,10},{6,14},... | collective-permute-start | bytes 245768 | tf_op jit(solution)/shard_map/ppermute | solution.py:17
  22.0 12.2 %collective-permute-start.7 = (bf16[128,512]{1,0:T(8,128)(2,1)S(1)}, bf16[128,512]{1,0:T(8,128)(2,1)S(1)}, u32[]{:S(2)}, u32[]{:S(2)}) collective-permute-start(bf16[128,512]{1,0:T(8,128)(2,1)S(1)} %broadcast_select_fusion.refs_6_), channel_id=1, source_target_pairs={{0,1},{1,0},{2,3},{3,2},{4,5},{5,4},{6,7},{7,6},{8,9},{9,8},{10,11... | collective-permute-start | bytes 393224 | tf_op jit(solution)/shard_map/ppermute | solution.py:17
  26.3 6.2 %collective-permute-start.3 = (bf16[80,512]{1,0:T(8,128)(2,1)S(1)}, bf16[80,512]{1,0:T(8,128)(2,1)S(1)}, u32[]{:S(2)}, u32[]{:S(2)}) collective-permute-start(bf16[80,512]{1,0:T(8,128)(2,1)S(1)} %conv_far.1), channel_id=1, source_target_pairs={{0,12},{4,8},{8,4},{12,0},{1,13},{5,9},{9,5},{13,1},{2,14},{6,10},... | collective-permute-start | bytes 245768 | tf_op jit(solution)/shard_map/ppermute | solution.py:17
  37.2 2.0 %collective-permute-start.11 = (bf16[8,128,256]{2,1,0:T(8,128)(2,1)S(1)}, bf16[8,128,256]{2,1,0:T(8,128)(2,1)S(1)}, u32[]{:S(2)}, u32[]{:S(2)}) collective-permute-start(bf16[8,128,256]{2,1,0:T(8,128)(2,1)S(1)} %get-tuple-element.14), channel_id=1, source_target_pairs={{0,1},{1,0},{2,3},{3,2},{4,5},{5,4},{6,7},{7,6},{8,9},{9,8},{10,11... | collective-permute-start | bytes 1572872 | tf_op jit(solution)/shard_map/ppermute | solution.py:17
  39.5 5.6 %collective-permute-start.14 = (bf16[2,2,128,128]{3,2,1,0:T(8,128)(2,1)S(1)}, bf16[2,2,128,128]{3,2,1,0:T(8,128)(2,1)S(1)}, u32[]{:S(2)}, u32[]{:S(2)}) collective-permute-start(bf16[2,2,128,128]{3,2,1,0:T(8,128)(2,1)S(1)} %fusion.1), channel_id=1, source_target_pairs={{0,16},{16,0},{1,17},{17,1},{2,18},{18,2},{3,19},{19,3},{4,20},{20... | collective-permute-start | bytes 393224 | tf_op jit(solution)/shard_map/ppermute | solution.py:17
  41.1 5.6 %collective-permute-start.12 = (bf16[2,2,128,128]{3,2,1,0:T(8,128)(2,1)S(1)}, bf16[2,2,128,128]{3,2,1,0:T(8,128)(2,1)S(1)}, u32[]{:S(2)}, u32[]{:S(2)}) collective-permute-start(bf16[2,2,128,128]{3,2,1,0:T(8,128)(2,1)S(1)} %fusion), channel_id=1, source_target_pairs={{0,2},{1,3},{2,0},{3,1},{4,6},{5,7},{6,4},{7,5},{8,10},{9,11},{10,... | collective-permute-start | bytes 393224 | tf_op jit(solution)/shard_map/ppermute | solution.py:17
  45.1 4.3 %collective-permute-start.15 = (bf16[2,128,128]{2,1,0:T(8,128)(2,1)S(1)}, bf16[2,128,128]{2,1,0:T(8,128)(2,1)S(1)}, u32[]{:S(2)}, u32[]{:S(2)}) collective-permute-start(bf16[2,128,128]{2,1,0:T(8,128)(2,1)S(1)} %fusion.8), channel_id=1, source_target_pairs={{0,2},{1,3},{2,0},{3,1},{4,6},{5,7},{6,4},{7,5},{8,10},{9,11},{10,... | collective-permute-start | bytes 196616 | tf_op jit(solution)/shard_map/ppermute | solution.py:17
  46.8 4.3 %collective-permute-start.13 = (bf16[2,128,128]{2,1,0:T(8,128)(2,1)S(1)}, bf16[2,128,128]{2,1,0:T(8,128)(2,1)S(1)}, u32[]{:S(2)}, u32[]{:S(2)}) collective-permute-start(bf16[2,128,128]{2,1,0:T(8,128)(2,1)S(1)} %fusion.7), channel_id=1, source_target_pairs={{0,16},{16,0},{1,17},{17,1},{2,18},{18,2},{3,19},{19,3},{4,20},{20... | collective-permute-start | bytes 196616 | tf_op jit(solution)/shard_map/ppermute | solution.py:17
  51.1 5.9 %collective-permute-start.16 = (bf16[128,256]{1,0:T(8,128)(2,1)S(1)}, bf16[128,256]{1,0:T(8,128)(2,1)S(1)}, u32[]{:S(2)}, u32[]{:S(2)}) collective-permute-start(bf16[128,256]{1,0:T(8,128)(2,1)S(1)} %fusion.9), channel_id=1, source_target_pairs={{0,8},{4,12},{8,0},{12,4},{1,9},{5,13},{9,1},{13,5},{2,10},{6,14},... | collective-permute-start | bytes 196616 | tf_op jit(solution)/shard_map/ppermute | solution.py:17
  57.1 3.4 %collective-permute-start.17 = (bf16[64,256]{1,0:T(8,128)(2,1)S(1)}, bf16[64,256]{1,0:T(8,128)(2,1)S(1)}, u32[]{:S(2)}, u32[]{:S(2)}) collective-permute-start(bf16[64,256]{1,0:T(8,128)(2,1)S(1)} %fusion.10), channel_id=1, source_target_pairs={{0,5},{1,4},{2,7},{3,6},{4,1},{5,0},{6,3},{7,2},{8,13},{9,12},{10,... | collective-permute-start | bytes 98312 | tf_op jit(solution)/shard_map/ppermute | solution.py:361

commit v6 on v5

--- a/solution.py
+++ b/solution.py
@@ -99,15 +99,13 @@
     return pl.ds(pl.multiple_of(f * rows, 128), rows)
 
 
-def forward_kernel(*refs):
-    frames = 4
-    row_refs, shards, refs = refs[:4], refs[4:8], refs[8:]
-    qkv_ref, weights_ref, attended_ref, n_ref, w_ref, sems = refs
-    _, t, _, zh, _, _ = place()
-    pixels, channels = row_refs[0].shape
-    width = channels // 2
+def weights_kernel(own_ref, *refs):
+    shards, refs = refs[:4], refs[4:]
+    w_ref, qkv_ref, sems = refs
+    _, _, _, zh, _, _ = place()
+    width = w_ref.shape[1] // 3
     rows = shards[0].shape[0]
-    copies = [pltpu.make_async_copy(row_refs[k], n_ref.at[t ^ k], sems.at[k]) for k in range(frames)]
+    copies = []
     for k in range(4):
         for m in range(3):
             columns = pl.ds(pl.multiple_of((2 * m + zh) * width, 128), width)
@@ -115,16 +113,33 @@
                 pltpu.make_async_copy(
                     shards[k].at[:, columns],
                     w_ref.at[shard_rows(k, rows), pl.ds(m * width, width)],
-                    sems.at[frames + 3 * k + m],
+                    sems.at[3 * k + m],
                 )
             )
     start_all(copies)
     for copy in copies:
         copy.wait()
-    normed = n_ref[...].reshape(frames * pixels, channels)
-    qkv_ref[...] = jnp.dot(normed, w_ref[...], preferred_element_type=jnp.float32).astype(
-        jnp.bfloat16
-    )
+    qkv_ref[...] = jnp.dot(
+        own_ref[...], w_ref[...], preferred_element_type=jnp.float32
+    ).astype(jnp.bfloat16)
+
+
+def forward_kernel(own_ref, row_1_ref, row_2_ref, row_3_ref, own_qkv_ref, w_ref, *refs):
+    frames = 4
+    qkv_ref, weights_ref, attended_ref, n_ref = refs
+    _, t, _, _, _, _ = place()
+    pixels, channels = own_ref.shape
+    width = channels // 2
+    others = (row_1_ref, row_2_ref, row_3_ref)
+    for i, ref in enumerate((own_ref,) + others):
+        n_ref[t ^ i] = ref[...]
+    arrived = jnp.concatenate([ref[...] for ref in others], axis=0)
+    arrived = jnp.dot(arrived, w_ref[...], preferred_element_type=jnp.float32)
+    arrived = arrived.astype(jnp.bfloat16)
+    qkv_ref[pl.ds(pl.multiple_of(t * pixels, 16), pixels), :] = own_qkv_ref[...]
+    for i in range(1, frames):
+        start = pl.multiple_of((t ^ i) * pixels, 16)
+        qkv_ref[pl.ds(start, pixels), :] = arrived[(i - 1) * pixels : i * pixels]
     q, k, v = (
         [wide(qkv_ref, i, third, width, pixels) for i in range(frames)] for third in range(3)
     )
@@ -151,50 +166,59 @@
 
 def backward_kernel(*refs):
     frames = 4
-    row_refs, pair_refs, out_refs, refs = refs[:4], refs[4:6], refs[6:8], refs[8:]
-    qkv_ref, weights_ref, attended_ref, refs = refs[0], refs[1], refs[2], refs[3:]
-    keep_ref, send_ref, n_ref, u_ref, out_w_ref, sums_ref, out_sums_ref, sems = refs
+    pair_refs, out_refs, refs = refs[:2], refs[2:4], refs[4:]
+    n_ref, qkv_ref, weights_ref, attended_ref, refs = *refs[:4], refs[4:]
+    keep_ref, send_ref, u_ref, g_ref, sums_ref, out_sums_ref = refs
     _, t, _, zh, _, core = place()
-    pixels, channels = row_refs[0].shape
-    width = out_w_ref.shape[0]
-    rows = out_refs[0].shape[0]
-    row_copies = [
-        pltpu.make_async_copy(row_refs[k], n_ref.at[t ^ k], sems.at[k]) for k in range(frames)
-    ]
-    up_copies = [
-        pltpu.make_async_copy(pair_refs[k & 1].at[k >> 1], u_ref.at[t ^ k], sems.at[frames + k])
-        for k in range(frames)
-    ]
-
-    for k in range(2):
-        start = pl.multiple_of((core ^ k) * rows, 128)
-        up_copies.append(
-            pltpu.make_async_copy(
-                out_refs[k], out_w_ref.at[pl.ds(start, rows)], sems.at[2 * frames + k]
-            )
+    _, pixels, channels = n_ref.shape
+    width = out_sums_ref.shape[0]
+    first, second = out_refs[0][...], out_refs[1][...]
+    out_w = jnp.where(
+        core == 0,
+        jnp.concatenate([first, second], axis=0),
+        jnp.concatenate([second, first], axis=0),
+    )
+    for i, ref in enumerate(pair_refs):
+        pieces = ref[...].reshape(2 * pixels, channels)
+        products = lax.dot_general(
+            pieces, out_w, (((1,), (1,)), ((), ())), preferred_element_type=jnp.float32
         )
-    start_all(up_copies)
-    start_all(row_copies)
-    for copy in up_copies:
-        copy.wait()
+        for j in range(2):
+            at = t ^ (2 * j + i)
+            g_ref[at] = products[j * pixels : (j + 1) * pixels].astype(jnp.bfloat16)
+            u_ref[at] = ref[j]
+    normed = n_ref[...].reshape(frames * pixels, channels)
     upstream = u_ref[...].reshape(frames * pixels, channels)
-    grads = lax.dot_general(
-        upstream, out_w_ref[...], (((1,), (1,)), ((), ())), preferred_element_type=jnp.float32
-    ).astype(jnp.bfloat16)
-    g = [grads[i * pixels : (i + 1) * pixels].astype(jnp.float32) for i in range(frames)]
+    g = [g_ref[i].astype(jnp.float32) for i in range(frames)]
     q, k, v = (
         [wide(qkv_ref, i, third, width, pixels) for i in range(frames)] for third in range(3)
     )
-    dq, dk, dv = [], [None] * frames, [None] * frames
+
+    def over_rows(lhs, rhs):
+        return lax.dot_general(
+            lhs, rhs, (((0,), (0,)), ((), ())), preferred_element_type=jnp.float32
+        )
 
     def plus(total, term):
         return term if total is None else total + term
 
-    slot = 0
+    def keep_sum(m, pieces):
+        pieces = [piece.astype(jnp.bfloat16) for piece in pieces]
+        grad = over_rows(normed, jnp.concatenate(pieces, axis=0))
+        for lane in range(0, width, 128):
+            sums_ref[lane // 128, pl.ds(m, channels, stride=3), :] = grad[:, lane : lane + 128]
+
+    out_sums_ref[...] = over_rows(attended_ref[...], upstream)
+    firsts = [i * (i + 1) // 2 for i in range(frames)]
+    dv = [None] * frames
+    for i in range(frames):
+        for u in range(i + 1):
+            dv[u] = plus(dv[u], weights_ref[firsts[i] + u].astype(jnp.float32) * g[i])
+    keep_sum(2, dv)
+    dq, dk = [], [None] * frames
     for i in range(frames):
         dprob = head_sums([g[i] * v[u] for u in range(i + 1)], width)
-        weights = [weights_ref[slot + u].astype(jnp.float32) for u in range(i + 1)]
-        slot += i + 1
+        weights = [weights_ref[firsts[i] + u].astype(jnp.float32) for u in range(i + 1)]
         delta = weights[0] * dprob[0]
         for u in range(1, i + 1):
             delta = delta + weights[u] * dprob[u]
@@ -203,23 +227,9 @@
             ds = (weights[u] * (dprob[u] - delta)).astype(jnp.bfloat16).astype(jnp.float32)
             grad_q = plus(grad_q, ds * k[u])
             dk[u] = plus(dk[u], ds * q[i])
-            dv[u] = plus(dv[u], weights[u] * g[i])
-        dq.append(grad_q.astype(jnp.bfloat16))
-    for copy in row_copies:
-        copy.wait()
-    normed = n_ref[...].reshape(frames * pixels, channels)
-    thirds = (dq, [d.astype(jnp.bfloat16) for d in dk], [d.astype(jnp.bfloat16) for d in dv])
-
-    def over_rows(lhs, rhs):
-        return lax.dot_general(
-            lhs, rhs, (((0,), (0,)), ((), ())), preferred_element_type=jnp.float32
-        )
-
-    for m, pieces in enumerate(thirds):
-        grad = over_rows(normed, jnp.concatenate(pieces, axis=0))
-        for lane in range(0, width, 128):
-            sums_ref[lane // 128, pl.ds(m, channels, stride=3), :] = grad[:, lane : lane + 128]
-    out_sums_ref[...] = over_rows(attended_ref[...], upstream)
+        dq.append(grad_q)
+    keep_sum(0, dq)
+    keep_sum(1, dk)
 
     block = channels // HEADS
     for slot in range(8):
@@ -300,44 +310,48 @@
     out_rows = jnp.where(x == zh, out_weight, out_x)
     out_c = swap(out_rows, "fsdp", 1)
 
-    qkv, weights, attended = pl.pallas_call(
+    full_qkv, own_qkv = pl.pallas_call(
+        weights_kernel,
+        out_shape=(
+            jax.ShapeDtypeStruct((channels, 3 * width), narrow_type),
+            jax.ShapeDtypeStruct((half, 3 * width), narrow_type),
+        ),
+        in_specs=[in_vmem] + [anywhere] * 4,
+        out_specs=(in_vmem,) * 2,
+        scratch_shapes=[pltpu.SemaphoreType.DMA((12,))],
+        compiler_params=pltpu.CompilerParams(vmem_limit_bytes=16 << 20),
+        name="weights",
+    )(n_mine, qkv_weight, qkv_x, qkv_c, qkv_xc)
+    qkv, weights, attended, normed = pl.pallas_call(
         forward_kernel,
         out_shape=(
             jax.ShapeDtypeStruct((4 * half, 3 * width), narrow_type),
             jax.ShapeDtypeStruct((10, half, width), narrow_type),
             jax.ShapeDtypeStruct((4 * half, width), narrow_type),
+            jax.ShapeDtypeStruct((4, half, channels), narrow_type),
         ),
-        in_specs=[anywhere] * 8,
-        out_specs=(in_vmem,) * 3,
-        scratch_shapes=[
-            pltpu.VMEM((4, half, channels), narrow_type),
-            pltpu.VMEM((channels, 3 * width), narrow_type),
-            pltpu.SemaphoreType.DMA((16,)),
-        ],
+        in_specs=[in_vmem] * 6,
+        out_specs=(in_vmem,) * 4,
         compiler_params=pltpu.CompilerParams(vmem_limit_bytes=24 << 20),
         name="forward",
-    )(n_mine, row_1, row_2, row_3, qkv_weight, qkv_x, qkv_c, qkv_xc)
+    )(n_mine, row_1, row_2, row_3, own_qkv, full_qkv)
     keep, send = pl.pallas_call(
         backward_kernel,
         out_shape=(
             jax.ShapeDtypeStruct((8, 2 * block, width), jnp.float32),
             jax.ShapeDtypeStruct((8, 2 * block, width), narrow_type),
         ),
-        in_specs=[anywhere] * 8 + [in_vmem] * 3,
+        in_specs=[in_vmem] * 8,
         out_specs=(in_vmem, in_vmem),
         scratch_shapes=[
             pltpu.VMEM((4, half, channels), narrow_type),
-            pltpu.VMEM((4, half, channels), narrow_type),
-            pltpu.VMEM((width, channels), narrow_type),
+            pltpu.VMEM((4, half, width), narrow_type),
             pltpu.VMEM((width // 128, 3 * channels, 128), jnp.float32),
             pltpu.VMEM((width, channels), jnp.float32),
-            pltpu.SemaphoreType.DMA((10,)),
         ],
         compiler_params=pltpu.CompilerParams(vmem_limit_bytes=28 << 20),
         name="backward",
-    )(
-        n_mine, row_1, row_2, row_3, up_own, up_got, out_rows, out_c, qkv, weights, attended
-    )
+    )(up_own, up_got, out_rows, out_c, normed, qkv, weights, attended)
 
     def narrow(values):
         return values.astype(jnp.bfloat16)

time: 61.3 us -> 56.1 us (0.915)
  waiting for transfers between devices: 28.4 us -> 22.9 us
  Pallas kernels: 8.22 us -> 6.7 us
  starting transfers between devices: 22.8 us -> 24.3 us
    ppermute x17, waiting for transfers between devices: 25.1 us -> 19.4 us  [swap(): lax.ppermute(values, axis, [(i, i ^ mask) for i in range(lax.axis_size(ax...]
    ppermute x17, starting transfers between devices: 22.8 us -> 24.2 us  [swap(): lax.ppermute(values, axis, [(i, i ^ mask) for i in range(lax.axis_size(ax...]
    pallas_call x1, Pallas kernels: 3.07 us -> 1.72 us  [split_form(): pl.pallas_call(backward_kernel, out_shape=(jax.ShapeDtypeStruct((8, 2 * b...]
  transfers between devices with their start and end apart: 18 -> 18, of which waited for: 10 -> 9; matrix products, arithmetic and copies ran while one was open for 2% -> 2% of each run, Pallas kernels for 7% -> 8%
where the time goes in v6:
time: 56.1 us; the launch traced here: 55.9 us
  starting transfers between devices  24.3 us (43%)
  waiting for transfers between devices  22.9 us (41%)
  Pallas kernels  6.7 us (12%)
  local copies, waits for them, and re-layouts  1.58 us (3%)
    ppermute x17, starting transfers between devices, swap(): lax.ppermute(values, axis, [(i, i ^ mask) for i in range(lax.axis_size(ax...  24.2 us
    ppermute x17, waiting for transfers between devices, swap(): lax.ppermute(values, axis, [(i, i ^ mask) for i in range(lax.axis_size(ax...  19.4 us
    ppermute x1, waiting for transfers between devices, split_form(): got = lax.ppermute(narrow(pick(total, 1 - zh)), ('tm', 'fsdp'), crossed)  3.49 us
    pallas_call x2, Pallas kernels, conv(): pl.pallas_call(functools.partial(conv_kernel, far), out_shape=piece, in_s...  2.88 us
    pallas_call x1, Pallas kernels, split_form(): pl.pallas_call(backward_kernel, out_shape=(jax.ShapeDtypeStruct((8, 2 * b...  1.72 us
  transfers between devices with their start and end apart: 18, of which 9 were waited for; matrix products, arithmetic and copies ran while one was open for 2% of the time, Pallas kernels for 8%

profile of v6, /device:TPU:0, one launch (start us, length us, event | category | flops | bytes accessed | tf_op | source)
XLA Modules:
  0.0 55.9 jit_solution(11781913116505099254)
XLA Ops:
  0.0 3.0 %collective-permute-start.8 = (bf16[128,1536]{1,0:T(8,128)(2,1)}, bf16[128,1536]{1,0:T(8,128)(2,1)S(1)}, u32[]{:S(2)}, u32[]{:S(2)}) collective-permute-start(bf16[128,1536]{1,0:T(8,128)(2,1)} %refs_0_.1), channel_id=1, source_target_pairs={{0,2},{1,3},{2,0},{3,1},{4,6},{5,7},{6,4},{7,5},{8,10},{9,11},{10,... | collective-permute-start | bytes 1179656 | tf_op jit(solution)/shard_map/ppermute | solution.py:17
  3.0 1.0 %constant_dynamic-slice_fusion = (bf16[1,80,512]{2,1,0:T(8,128)(2,1)S(1)}, bf16[80,512]{1,0:T(8,128)(2,1)S(1)}) fusion(bf16[2,80,512]{2,1,0:T(8,128)(2,1)} %bitcast.50, s32[]{:T(128)S(6)} %select_n.41, s32[]{:T(128)S(6)} %select_n.42), kind=kLoop, calls=%fused_computation.28 | loop fusion | bytes 327688 | tf_op jit(solution)/shard_map/jit(dynamic_index_in_dim)/dynamic_slice | solution.py:21
  4.0 2.7 %collective-permute-start = (bf16[80,512]{1,0:T(8,128)(2,1)S(1)}, bf16[80,512]{1,0:T(8,128)(2,1)S(1)}, u32[]{:S(2)}, u32[]{:S(2)}) collective-permute-start(bf16[80,512]{1,0:T(8,128)(2,1)S(1)} %get-tuple-element.24), channel_id=1, source_target_pairs={{0,8},{4,12},{8,0},{12,4},{1,9},{5,13},{9,1},{13,5},{2,10},{6,14},... | collective-permute-start | bytes 245768 | tf_op jit(solution)/shard_map/ppermute | solution.py:17
  6.6 0.5 collective-permute-start.2
  7.2 1.5 %collective-permute-start.4 = (bf16[160,512]{1,0:T(8,128)(2,1)S(1)}, bf16[160,512]{1,0:T(8,128)(2,1)S(1)}, u32[]{:S(2)}, u32[]{:S(2)}) collective-permute-start(bf16[160,512]{1,0:T(8,128)(2,1)S(1)} %bitcast.42), channel_id=1, source_target_pairs={{0,16},{16,0},{1,17},{17,1},{2,18},{18,2},{3,19},{19,3},{4,20},{20... | collective-permute-start | bytes 491528 | tf_op jit(solution)/shard_map/ppermute | solution.py:17
  8.7 4.5 %collective-permute-done.8.refs_1_ = bf16[128,1536]{1,0:T(8,128)(2,1)S(1)} collective-permute-done((bf16[128,1536]{1,0:T(8,128)(2,1)}, bf16[128,1536]{1,0:T(8,128)(2,1)S(1)}, u32[]{:S(2)}, u32[]{:S(2)}) %collective-permute-start.8) | collective-permute-done | bytes 393248 | tf_op jit(solution)/shard_map/ppermute | solution.py:17
  13.2 2.2 %collective-permute-start.1 = (bf16[2,80,512]{2,1,0:T(8,128)(2,1)S(1)}, bf16[2,80,512]{2,1,0:T(8,128)(2,1)S(1)}, u32[]{:S(2)}, u32[]{:S(2)}) collective-permute-start(bf16[2,80,512]{2,1,0:T(8,128)(2,1)S(1)} %pad_maximum_fusion.refs_0_), channel_id=1, source_target_pairs={{0,4},{4,0},{8,12},{12,8},{1,5},{5,1},{9,13},{13,9},{2,6},{6,2},{1... | collective-permute-start | bytes 491528 | tf_op jit(solution)/shard_map/ppermute | solution.py:17
  15.4 0.3 collective-permute-start.3
  15.7 0.4 copy-done.3
  16.1 1.4 %conv_near.1.own_ref = bf16[80,512]{1,0:T(8,128)(2,1)S(1)} custom-call(s32[8,160]{1,0:T(8,128)S(1)} %bitcast.45, bf16[160,512]{1,0:T(8,128)(2,1)S(1)} %bitcast.43, bf16[160,512]{1,0:T(8,128)(2,1)S(1)} %collective-permute-done.4.band_hbm, f32[9,512]{1,0:T(8,128)S(1)} %copy-done.2, f32[1,512]{1,0:T(1,128)S(1)} %bitcast.47), custom_call_target="tpu_custom_call" | custom-call | tf_op jit(solution)/shard_map/conv_near/pallas_call | solution.py:284
  17.5 1.6 %collective-permute-start.5 = (bf16[80,512]{1,0:T(8,128)(2,1)S(1)}, bf16[80,512]{1,0:T(8,128)(2,1)S(1)}, u32[]{:S(2)}, u32[]{:S(2)}) collective-permute-start(bf16[80,512]{1,0:T(8,128)(2,1)S(1)} %conv_near.1.own_ref), channel_id=1, source_target_pairs={{0,4},{4,0},{8,12},{12,8},{1,5},{5,1},{9,13},{13,9},{2,6},{6,2},{1... | collective-permute-start | bytes 245768 | tf_op jit(solution)/shard_map/ppermute | solution.py:17
  19.2 1.4 %conv_far.1 = bf16[80,512]{1,0:T(8,128)(2,1)S(1)} custom-call(s32[8,160]{1,0:T(8,128)S(1)} %bitcast.46, bf16[160,512]{1,0:T(8,128)(2,1)S(1)} %bitcast.44, bf16[160,512]{1,0:T(8,128)(2,1)S(1)} %collective-permute-done.4.band_hbm, f32[9,512]{1,0:T(8,128)S(1)} %copy-done.2, f32[1,512]{1,0:T(1,128)S(1)} %bitcast.48), custom_call_target="tpu_custom_call" | custom-call | tf_op jit(solution)/shard_map/conv_far/pallas_call | solution.py:284
  20.6 2.7 %collective-permute-start.6 = (bf16[80,512]{1,0:T(8,128)(2,1)S(1)}, bf16[80,512]{1,0:T(8,128)(2,1)S(1)}, u32[]{:S(2)}, u32[]{:S(2)}) collective-permute-start(bf16[80,512]{1,0:T(8,128)(2,1)S(1)} %conv_far.1), channel_id=1, source_target_pairs={{0,8},{4,12},{8,0},{12,4},{1,9},{5,13},{9,1},{13,5},{2,10},{6,14},... | collective-permute-start | bytes 245768 | tf_op jit(solution)/shard_map/ppermute | solution.py:17
  23.3 0.2 collective-permute-start.7
  23.5 0.5 weights.1
  24.0 4.7 %collective-permute-done.6.row_2_ref = bf16[80,512]{1,0:T(8,128)(2,1)S(1)} collective-permute-done((bf16[80,512]{1,0:T(8,128)(2,1)S(1)}, bf16[80,512]{1,0:T(8,128)(2,1)S(1)}, u32[]{:S(2)}, u32[]{:S(2)}) %collective-permute-start.6) | collective-permute-done | bytes 81952 | tf_op jit(solution)/shard_map/ppermute | solution.py:17
  28.7 0.9 %collective-permute-done.7.row_3_ref = bf16[80,512]{1,0:T(8,128)(2,1)S(1)} collective-permute-done((bf16[80,512]{1,0:T(8,128)(2,1)S(1)}, bf16[80,512]{1,0:T(8,128)(2,1)S(1)}, u32[]{:S(2)}, u32[]{:S(2)}) %collective-permute-start.7) | collective-permute-done | bytes 81952 | tf_op jit(solution)/shard_map/ppermute | solution.py:17
  29.6 1.0 %forward.1 = (bf16[320,768]{1,0:T(8,128)(2,1)S(1)}, bf16[10,80,256]{2,1,0:T(8,128)(2,1)S(1)}, bf16[320,256]{1,0:T(8,128)(2,1)S(1)}, bf16[4,80,512]{2,1,0:T(8,128)(2,1)S(1)}) custom-call(bf16[80,512]{1,0:T(8,128)(2,1)S(1)} %conv_near.1.own_ref, bf16[80,512]{1,0:T(8,128)(2,1)S(1)} %collective-permute-done.5.row_1_ref, ...), custom_call_target="tpu_custom_call" | custom-call | tf_op jit(solution)/shard_map/forward/pallas_call | solution.py:325
  30.6 1.7 %backward.1 = (f32[8,128,256]{2,1,0:T(8,128)S(1)}, bf16[8,128,256]{2,1,0:T(8,128)(2,1)S(1)}) custom-call(bf16[2,80,512]{2,1,0:T(8,128)(2,1)S(1)} %pad_maximum_fusion.refs_0_, bf16[2,80,512]{2,1,0:T(8,128)(2,1)S(1)} %collective-permute-done.1.refs_1_, bf16[128,512]{1,0:T(8,128)(2,1)S(1)} %broadcast_select_fusion.refs_2_, ...), custom_call_target="tpu_custom_call" | custom-call | tf_op jit(solution)/shard_map/backward/pallas_call | solution.py:338
  32.4 1.9 %collective-permute-done.11 = bf16[8,128,256]{2,1,0:T(8,128)(2,1)S(1)} collective-permute-done((bf16[8,128,256]{2,1,0:T(8,128)(2,1)S(1)}, bf16[8,128,256]{2,1,0:T(8,128)(2,1)S(1)}, u32[]{:S(2)}, u32[]{:S(2)}) %collective-permute-start.11) | collective-permute-done | bytes 524320 | tf_op jit(solution)/shard_map/ppermute | solution.py:17
  34.3 0.1 convert_add_fusion
  34.6 1.6 %collective-permute-start.14 = (bf16[2,2,128,128]{3,2,1,0:T(8,128)(2,1)S(1)}, bf16[2,2,128,128]{3,2,1,0:T(8,128)(2,1)S(1)}, u32[]{:S(2)}, u32[]{:S(2)}) collective-permute-start(bf16[2,2,128,128]{3,2,1,0:T(8,128)(2,1)S(1)} %fusion.1), channel_id=1, source_target_pairs={{0,16},{16,0},{1,17},{17,1},{2,18},{18,2},{3,19},{19,3},{4,20},{20... | collective-permute-start | bytes 393224 | tf_op jit(solution)/shard_map/ppermute | solution.py:17
  36.2 1.6 %collective-permute-start.12 = (bf16[2,2,128,128]{3,2,1,0:T(8,128)(2,1)S(1)}, bf16[2,2,128,128]{3,2,1,0:T(8,128)(2,1)S(1)}, u32[]{:S(2)}, u32[]{:S(2)}) collective-permute-start(bf16[2,2,128,128]{3,2,1,0:T(8,128)(2,1)S(1)} %fusion), channel_id=1, source_target_pairs={{0,2},{1,3},{2,0},{3,1},{4,6},{5,7},{6,4},{7,5},{8,10},{9,11},{10,... | collective-permute-start | bytes 393224 | tf_op jit(solution)/shard_map/ppermute | solution.py:17
  37.7 2.4 %collective-permute-done.14 = bf16[2,2,128,128]{3,2,1,0:T(8,128)(2,1)S(1)} collective-permute-done((bf16[2,2,128,128]{3,2,1,0:T(8,128)(2,1)S(1)}, bf16[2,2,128,128]{3,2,1,0:T(8,128)(2,1)S(1)}, u32[]{:S(2)}, u32[]{:S(2)}) %collective-permute-start.14) | collective-permute-done | bytes 131104 | tf_op jit(solution)/shard_map/ppermute | solution.py:17
  40.2 1.6 %collective-permute-start.15 = (bf16[2,128,128]{2,1,0:T(8,128)(2,1)S(1)}, bf16[2,128,128]{2,1,0:T(8,128)(2,1)S(1)}, u32[]{:S(2)}, u32[]{:S(2)}) collective-permute-start(bf16[2,128,128]{2,1,0:T(8,128)(2,1)S(1)} %fusion.8), channel_id=1, source_target_pairs={{0,2},{1,3},{2,0},{3,1},{4,6},{5,7},{6,4},{7,5},{8,10},{9,11},{10,... | collective-permute-start | bytes 196616 | tf_op jit(solution)/shard_map/ppermute | solution.py:17
  41.8 1.6 %collective-permute-start.13 = (bf16[2,128,128]{2,1,0:T(8,128)(2,1)S(1)}, bf16[2,128,128]{2,1,0:T(8,128)(2,1)S(1)}, u32[]{:S(2)}, u32[]{:S(2)}) collective-permute-start(bf16[2,128,128]{2,1,0:T(8,128)(2,1)S(1)} %fusion.7), channel_id=1, source_target_pairs={{0,16},{16,0},{1,17},{17,1},{2,18},{18,2},{3,19},{19,3},{4,20},{20... | collective-permute-start | bytes 196616 | tf_op jit(solution)/shard_map/ppermute | solution.py:17
  43.4 1.1 %collective-permute-done.15 = bf16[2,128,128]{2,1,0:T(8,128)(2,1)S(1)} collective-permute-done((bf16[2,128,128]{2,1,0:T(8,128)(2,1)S(1)}, bf16[2,128,128]{2,1,0:T(8,128)(2,1)S(1)}, u32[]{:S(2)}, u32[]{:S(2)}) %collective-permute-start.15) | collective-permute-done | bytes 65568 | tf_op jit(solution)/shard_map/ppermute | solution.py:17
  44.6 1.6 %collective-permute-done.13 = bf16[2,128,128]{2,1,0:T(8,128)(2,1)S(1)} collective-permute-done((bf16[2,128,128]{2,1,0:T(8,128)(2,1)S(1)}, bf16[2,128,128]{2,1,0:T(8,128)(2,1)S(1)}, u32[]{:S(2)}, u32[]{:S(2)}) %collective-permute-start.13) | collective-permute-done | bytes 65568 | tf_op jit(solution)/shard_map/ppermute | solution.py:17
  46.2 3.2 %collective-permute-start.16 = (bf16[128,256]{1,0:T(8,128)(2,1)S(1)}, bf16[128,256]{1,0:T(8,128)(2,1)S(1)}, u32[]{:S(2)}, u32[]{:S(2)}) collective-permute-start(bf16[128,256]{1,0:T(8,128)(2,1)S(1)} %fusion.9), channel_id=1, source_target_pairs={{0,8},{4,12},{8,0},{12,4},{1,9},{5,13},{9,1},{13,5},{2,10},{6,14},... | collective-permute-start | bytes 196616 | tf_op jit(solution)/shard_map/ppermute | solution.py:17
  49.4 2.2 %collective-permute-done.16 = bf16[128,256]{1,0:T(8,128)(2,1)S(1)} collective-permute-done((bf16[128,256]{1,0:T(8,128)(2,1)S(1)}, bf16[128,256]{1,0:T(8,128)(2,1)S(1)}, u32[]{:S(2)}, u32[]{:S(2)}) %collective-permute-start.16) | collective-permute-done | bytes 65568 | tf_op jit(solution)/shard_map/ppermute | solution.py:17
  51.8 3.5 %collective-permute-done.17.got_ref = bf16[64,256]{1,0:T(8,128)(2,1)S(1)} collective-permute-done((bf16[64,256]{1,0:T(8,128)(2,1)S(1)}, bf16[64,256]{1,0:T(8,128)(2,1)S(1)}, u32[]{:S(2)}, u32[]{:S(2)}) %collective-permute-start.17) | collective-permute-done | bytes 32800 | tf_op jit(solution)/shard_map/ppermute | solution.py:375
  55.2 0.7 %join.1 = f32[256,128]{1,0:T(8,128)} custom-call(f32[2,64,256]{2,1,0:T(8,128)S(1)} %bitcast.41, bf16[64,256]{1,0:T(8,128)(2,1)S(1)} %collective-permute-done.17.got_ref), custom_call_target="tpu_custom_call" | custom-call | tf_op jit(solution)/shard_map/join/pallas_call | solution.py:377
  (38 shorter events, 0.6 us)
Async XLA Ops:
  0.0 13.1 %collective-permute-start.8 = (bf16[128,1536]{1,0:T(8,128)(2,1)}, bf16[128,1536]{1,0:T(8,128)(2,1)S(1)}, u32[]{:S(2)}, u32[]{:S(2)}) collective-permute-start(bf16[128,1536]{1,0:T(8,128)(2,1)} %refs_0_.1), channel_id=1, source_target_pairs={{0,2},{1,3},{2,0},{3,1},{4,6},{5,7},{6,4},{7,5},{8,10},{9,11},{10,... | collective-permute-start | bytes 1179656 | tf_op jit(solution)/shard_map/ppermute | solution.py:17
  3.0 3.6 %copy-start.5 = (bf16[128,512]{1,0:T(8,128)(2,1)S(1)}, bf16[128,512]{1,0:T(8,128)(2,1)}, u32[]{:S(2)}) copy-start(bf16[128,512]{1,0:T(8,128)(2,1)} %param.12) | copy-start | bytes 393220
  3.0 4.2 %copy-start = (bf16[1,1,160,512]{3,2,1,0:T(8,128)(2,1)S(1)}, bf16[1,1,160,512]{3,2,1,0:T(8,128)(2,1)}, u32[]{:S(2)}) copy-start(bf16[1,1,160,512]{3,2,1,0:T(8,128)(2,1)} %param.7) | copy-start | bytes 491524
  4.0 9.2 %collective-permute-start = (bf16[80,512]{1,0:T(8,128)(2,1)S(1)}, bf16[80,512]{1,0:T(8,128)(2,1)S(1)}, u32[]{:S(2)}, u32[]{:S(2)}) collective-permute-start(bf16[80,512]{1,0:T(8,128)(2,1)S(1)} %get-tuple-element.24), channel_id=1, source_target_pairs={{0,8},{4,12},{8,0},{12,4},{1,9},{5,13},{9,1},{13,5},{2,10},{6,14},... | collective-permute-start | bytes 245768 | tf_op jit(solution)/shard_map/ppermute | solution.py:17
  6.6 8.7 %collective-permute-start.2 = (bf16[128,512]{1,0:T(8,128)(2,1)S(1)}, bf16[128,512]{1,0:T(8,128)(2,1)S(1)}, u32[]{:S(2)}, u32[]{:S(2)}) collective-permute-start(bf16[128,512]{1,0:T(8,128)(2,1)S(1)} %copy-done.5), channel_id=1, source_target_pairs={{0,2},{1,3},{2,0},{3,1},{4,6},{5,7},{6,4},{7,5},{8,10},{9,11},{10,... | collective-permute-start | bytes 393224 | tf_op jit(solution)/shard_map/ppermute | solution.py:17
  7.2 13.4 %collective-permute-start.9 = (bf16[128,1536]{1,0:T(8,128)(2,1)}, bf16[128,1536]{1,0:T(8,128)(2,1)S(1)}, u32[]{:S(2)}, u32[]{:S(2)}) collective-permute-start(bf16[128,1536]{1,0:T(8,128)(2,1)} %refs_0_.1), channel_id=1, source_target_pairs={{0,1},{1,0},{2,3},{3,2},{4,5},{5,4},{6,7},{7,6},{8,9},{9,8},{10,11... | collective-permute-start | bytes 1179656 | tf_op jit(solution)/shard_map/ppermute | solution.py:17
  7.2 8.5 %collective-permute-start.4 = (bf16[160,512]{1,0:T(8,128)(2,1)S(1)}, bf16[160,512]{1,0:T(8,128)(2,1)S(1)}, u32[]{:S(2)}, u32[]{:S(2)}) collective-permute-start(bf16[160,512]{1,0:T(8,128)(2,1)S(1)} %bitcast.42), channel_id=1, source_target_pairs={{0,16},{16,0},{1,17},{17,1},{2,18},{18,2},{3,19},{19,3},{4,20},{20... | collective-permute-start | bytes 491528 | tf_op jit(solution)/shard_map/ppermute | solution.py:17
  13.1 10.1 %collective-permute-start.10 = (bf16[128,1536]{1,0:T(8,128)(2,1)S(1)}, bf16[128,1536]{1,0:T(8,128)(2,1)S(1)}, u32[]{:S(2)}, u32[]{:S(2)}) collective-permute-start(bf16[128,1536]{1,0:T(8,128)(2,1)S(1)} %collective-permute-done.8.refs_1_), channel_id=1, source_target_pairs={{0,1},{1,0},{2,3},{3,2},{4,5},{5,4},{6,7},{7,6},{8,9},{9,8},{10,11... | collective-permute-start | bytes 1179656 | tf_op jit(solution)/shard_map/ppermute | solution.py:17
  13.2 2.5 %copy-start.2 = (f32[9,512]{1,0:T(8,128)S(1)}, f32[9,512]{1,0:T(8,128)}, u32[]{:S(2)}) copy-start(f32[9,512]{1,0:T(8,128)} %taps_hbm.3) | copy-start | bytes 55300
  13.2 17.4 %collective-permute-start.1 = (bf16[2,80,512]{2,1,0:T(8,128)(2,1)S(1)}, bf16[2,80,512]{2,1,0:T(8,128)(2,1)S(1)}, u32[]{:S(2)}, u32[]{:S(2)}) collective-permute-start(bf16[2,80,512]{2,1,0:T(8,128)(2,1)S(1)} %pad_maximum_fusion.refs_0_), channel_id=1, source_target_pairs={{0,4},{4,0},{8,12},{12,8},{1,5},{5,1},{9,13},{13,9},{2,6},{6,2},{1... | collective-permute-start | bytes 491528 | tf_op jit(solution)/shard_map/ppermute | solution.py:17
  15.4 0.7 %copy-start.3 = (s32[160,8]{0,1:T(8,128)S(1)}, s32[160,8]{0,1:T(8,128)}, u32[]{:S(2)}) copy-start(s32[160,8]{0,1:T(8,128)} %param.8) | copy-start | bytes 15364
  15.4 0.7 %copy-start.4 = (f32[512]{0:T(512)S(1)}, f32[512]{0:T(512)}, u32[]{:S(2)}) copy-start(f32[512]{0:T(512)} %param.10) | copy-start | bytes 6148
  15.4 15.2 %collective-permute-start.3 = (bf16[128,512]{1,0:T(8,128)(2,1)S(1)}, bf16[128,512]{1,0:T(8,128)(2,1)S(1)}, u32[]{:S(2)}, u32[]{:S(2)}) collective-permute-start(bf16[128,512]{1,0:T(8,128)(2,1)S(1)} %broadcast_select_fusion.refs_2_), channel_id=1, source_target_pairs={{0,1},{1,0},{2,3},{3,2},{4,5},{5,4},{6,7},{7,6},{8,9},{9,8},{10,11... | collective-permute-start | bytes 393224 | tf_op jit(solution)/shard_map/ppermute | solution.py:17
  16.1 7.4 %copy-start.1 = (bf16[128,1536]{1,0:T(8,128)(2,1)S(1)}, bf16[128,1536]{1,0:T(8,128)(2,1)}, u32[]{:S(2)}) copy-start(bf16[128,1536]{1,0:T(8,128)(2,1)} %refs_0_.1) | copy-start | bytes 1179652
  17.5 6.5 %collective-permute-start.5 = (bf16[80,512]{1,0:T(8,128)(2,1)S(1)}, bf16[80,512]{1,0:T(8,128)(2,1)S(1)}, u32[]{:S(2)}, u32[]{:S(2)}) collective-permute-start(bf16[80,512]{1,0:T(8,128)(2,1)S(1)} %conv_near.1.own_ref), channel_id=1, source_target_pairs={{0,4},{4,0},{8,12},{12,8},{1,5},{5,1},{9,13},{13,9},{2,6},{6,2},{1... | collective-permute-start | bytes 245768 | tf_op jit(solution)/shard_map/ppermute | solution.py:17
  20.6 8.1 %collective-permute-start.6 = (bf16[80,512]{1,0:T(8,128)(2,1)S(1)}, bf16[80,512]{1,0:T(8,128)(2,1)S(1)}, u32[]{:S(2)}, u32[]{:S(2)}) collective-permute-start(bf16[80,512]{1,0:T(8,128)(2,1)S(1)} %conv_far.1), channel_id=1, source_target_pairs={{0,8},{4,12},{8,0},{12,4},{1,9},{5,13},{9,1},{13,5},{2,10},{6,14},... | collective-permute-start | bytes 245768 | tf_op jit(solution)/shard_map/ppermute | solution.py:17
  23.3 6.3 %collective-permute-start.7 = (bf16[80,512]{1,0:T(8,128)(2,1)S(1)}, bf16[80,512]{1,0:T(8,128)(2,1)S(1)}, u32[]{:S(2)}, u32[]{:S(2)}) collective-permute-start(bf16[80,512]{1,0:T(8,128)(2,1)S(1)} %conv_far.1), channel_id=1, source_target_pairs={{0,12},{4,8},{8,4},{12,0},{1,13},{5,9},{9,5},{13,1},{2,14},{6,10},... | collective-permute-start | bytes 245768 | tf_op jit(solution)/shard_map/ppermute | solution.py:17
  32.3 2.0 %collective-permute-start.11 = (bf16[8,128,256]{2,1,0:T(8,128)(2,1)S(1)}, bf16[8,128,256]{2,1,0:T(8,128)(2,1)S(1)}, u32[]{:S(2)}, u32[]{:S(2)}) collective-permute-start(bf16[8,128,256]{2,1,0:T(8,128)(2,1)S(1)} %get-tuple-element.20), channel_id=1, source_target_pairs={{0,1},{1,0},{2,3},{3,2},{4,5},{5,4},{6,7},{7,6},{8,9},{9,8},{10,11... | collective-permute-start | bytes 1572872 | tf_op jit(solution)/shard_map/ppermute | solution.py:17
  34.6 5.6 %collective-permute-start.14 = (bf16[2,2,128,128]{3,2,1,0:T(8,128)(2,1)S(1)}, bf16[2,2,128,128]{3,2,1,0:T(8,128)(2,1)S(1)}, u32[]{:S(2)}, u32[]{:S(2)}) collective-permute-start(bf16[2,2,128,128]{3,2,1,0:T(8,128)(2,1)S(1)} %fusion.1), channel_id=1, source_target_pairs={{0,16},{16,0},{1,17},{17,1},{2,18},{18,2},{3,19},{19,3},{4,20},{20... | collective-permute-start | bytes 393224 | tf_op jit(solution)/shard_map/ppermute | solution.py:17
  36.2 5.6 %collective-permute-start.12 = (bf16[2,2,128,128]{3,2,1,0:T(8,128)(2,1)S(1)}, bf16[2,2,128,128]{3,2,1,0:T(8,128)(2,1)S(1)}, u32[]{:S(2)}, u32[]{:S(2)}) collective-permute-start(bf16[2,2,128,128]{3,2,1,0:T(8,128)(2,1)S(1)} %fusion), channel_id=1, source_target_pairs={{0,2},{1,3},{2,0},{3,1},{4,6},{5,7},{6,4},{7,5},{8,10},{9,11},{10,... | collective-permute-start | bytes 393224 | tf_op jit(solution)/shard_map/ppermute | solution.py:17
  40.2 4.3 %collective-permute-start.15 = (bf16[2,128,128]{2,1,0:T(8,128)(2,1)S(1)}, bf16[2,128,128]{2,1,0:T(8,128)(2,1)S(1)}, u32[]{:S(2)}, u32[]{:S(2)}) collective-permute-start(bf16[2,128,128]{2,1,0:T(8,128)(2,1)S(1)} %fusion.8), channel_id=1, source_target_pairs={{0,2},{1,3},{2,0},{3,1},{4,6},{5,7},{6,4},{7,5},{8,10},{9,11},{10,... | collective-permute-start | bytes 196616 | tf_op jit(solution)/shard_map/ppermute | solution.py:17
  41.8 4.3 %collective-permute-start.13 = (bf16[2,128,128]{2,1,0:T(8,128)(2,1)S(1)}, bf16[2,128,128]{2,1,0:T(8,128)(2,1)S(1)}, u32[]{:S(2)}, u32[]{:S(2)}) collective-permute-start(bf16[2,128,128]{2,1,0:T(8,128)(2,1)S(1)} %fusion.7), channel_id=1, source_target_pairs={{0,16},{16,0},{1,17},{17,1},{2,18},{18,2},{3,19},{19,3},{4,20},{20... | collective-permute-start | bytes 196616 | tf_op jit(solution)/shard_map/ppermute | solution.py:17
  46.2 5.4 %collective-permute-start.16 = (bf16[128,256]{1,0:T(8,128)(2,1)S(1)}, bf16[128,256]{1,0:T(8,128)(2,1)S(1)}, u32[]{:S(2)}, u32[]{:S(2)}) collective-permute-start(bf16[128,256]{1,0:T(8,128)(2,1)S(1)} %fusion.9), channel_id=1, source_target_pairs={{0,8},{4,12},{8,0},{12,4},{1,9},{5,13},{9,1},{13,5},{2,10},{6,14},... | collective-permute-start | bytes 196616 | tf_op jit(solution)/shard_map/ppermute | solution.py:17
  51.7 3.6 %collective-permute-start.17 = (bf16[64,256]{1,0:T(8,128)(2,1)S(1)}, bf16[64,256]{1,0:T(8,128)(2,1)S(1)}, u32[]{:S(2)}, u32[]{:S(2)}) collective-permute-start(bf16[64,256]{1,0:T(8,128)(2,1)S(1)} %fusion.10), channel_id=1, source_target_pairs={{0,5},{1,4},{2,7},{3,6},{4,1},{5,0},{6,3},{7,2},{8,13},{9,12},{10,... | collective-permute-start | bytes 98312 | tf_op jit(solution)/shard_map/ppermute | solution.py:375

commit v7 on v6

--- a/solution.py
+++ b/solution.py
@@ -31,24 +31,11 @@
         copy.start()
 
 
-def conv_kernel(
-    far, near_hbm, own_hbm, band_hbm, taps_hbm, gain_hbm, out_ref,
-    near_ref, turned_ref, table_ref, taps_ref, gain_ref, sems,
-):
+def conv_kernel(far, near_ref, own_ref, band_ref, taps_ref, gain_ref, out_ref, turned_ref):
     y, _, zp, _, _, _ = place()
-    pixels, _ = own_hbm.shape
+    pixels, _ = own_ref.shape
     half = pixels // 2
     begin = pl.multiple_of((1 - zp if far else zp) * half, 16)
-    pairs = [
-        (near_hbm, near_ref),
-        (taps_hbm, taps_ref),
-        (gain_hbm, gain_ref),
-        (own_hbm, table_ref.at[pl.ds(0, pixels)]),
-        (band_hbm, table_ref.at[pl.ds(pixels, pixels)]),
-    ]
-    copies = [pltpu.make_async_copy(a, b, sems.at[i]) for i, (a, b) in enumerate(pairs)]
-    start_all(copies)
-    copies[0].wait()
     turned_ref[...] = near_ref[...].T
     near = turned_ref[pl.ds(begin, half), :]
     neighbours = near.shape[1]
@@ -62,10 +49,9 @@
         ],
         axis=0,
     )
-    for copy in copies[1:]:
-        copy.wait()
-    gathered = jnp.dot(chosen, table_ref[...], preferred_element_type=jnp.float32)
-    own = table_ref[pl.ds(begin, half), :].astype(jnp.float32)
+    table = jnp.concatenate([own_ref[...], band_ref[...]], axis=0)
+    gathered = jnp.dot(chosen, table, preferred_element_type=jnp.float32)
+    own = own_ref[pl.ds(begin, half), :].astype(jnp.float32)
     spatial = taps_ref[0:1, :] * own
     for k in range(neighbours):
         spatial = spatial + taps_ref[k + 1 : k + 2, :] * gathered[k * half : (k + 1) * half]
@@ -166,7 +152,7 @@
 
 def backward_kernel(*refs):
     frames = 4
-    pair_refs, out_refs, refs = refs[:2], refs[2:4], refs[4:]
+    piece_refs, out_refs, refs = refs[:4], refs[4:6], refs[6:]
     n_ref, qkv_ref, weights_ref, attended_ref, refs = *refs[:4], refs[4:]
     keep_ref, send_ref, u_ref, g_ref, sums_ref, out_sums_ref = refs
     _, t, _, zh, _, core = place()
@@ -178,15 +164,13 @@
         jnp.concatenate([first, second], axis=0),
         jnp.concatenate([second, first], axis=0),
     )
-    for i, ref in enumerate(pair_refs):
-        pieces = ref[...].reshape(2 * pixels, channels)
-        products = lax.dot_general(
-            pieces, out_w, (((1,), (1,)), ((), ())), preferred_element_type=jnp.float32
-        )
-        for j in range(2):
-            at = t ^ (2 * j + i)
-            g_ref[at] = products[j * pixels : (j + 1) * pixels].astype(jnp.bfloat16)
-            u_ref[at] = ref[j]
+    pieces = jnp.concatenate([ref[...] for ref in piece_refs], axis=0)
+    products = lax.dot_general(
+        pieces, out_w, (((1,), (1,)), ((), ())), preferred_element_type=jnp.float32
+    )
+    for i, ref in enumerate(piece_refs):
+        g_ref[t ^ i] = products[i * pixels : (i + 1) * pixels].astype(jnp.bfloat16)
+        u_ref[t ^ i] = ref[...]
     normed = n_ref[...].reshape(frames * pixels, channels)
     upstream = u_ref[...].reshape(frames * pixels, channels)
     g = [g_ref[i].astype(jnp.float32) for i in range(frames)]
@@ -284,16 +268,9 @@
         return pl.pallas_call(
             functools.partial(conv_kernel, far),
             out_shape=piece,
-            in_specs=[anywhere] * 5,
+            in_specs=[in_vmem] * 5,
             out_specs=in_vmem,
-            scratch_shapes=[
-                pltpu.VMEM((neighbours.shape[1], pixels), jnp.int32),
-                pltpu.VMEM((pixels, neighbours.shape[1]), jnp.int32),
-                pltpu.VMEM((2 * pixels, channels), narrow_type),
-                pltpu.VMEM(conv_taps.shape, jnp.float32),
-                pltpu.VMEM((1, channels), jnp.float32),
-                pltpu.SemaphoreType.DMA((5,)),
-            ],
+            scratch_shapes=[pltpu.VMEM((pixels, neighbours.shape[1]), jnp.int32)],
             compiler_params=pltpu.CompilerParams(vmem_limit_bytes=16 << 20),
             name="conv_far" if far else "conv_near",
         )(neighbours.T, own, band, conv_taps, norm_gain.reshape(1, channels))
@@ -303,8 +280,9 @@
     row_2 = swap(n_other, "tm", 2)
     n_mine = conv(False)
     row_1 = swap(n_mine, "tm", 1)
-    up_own = jnp.stack([pick(halves, zp), up_2])
-    up_got = swap(up_own, "tm", 1)
+    up_mine = pick(halves, zp)
+    up_1 = swap(up_mine, "tm", 1)
+    up_3 = swap(up_2, "tm", 1)
     qkv_c = swap(qkv_weight, "fsdp", 1)
     qkv_xc = swap(qkv_x, "fsdp", 1)
     out_rows = jnp.where(x == zh, out_weight, out_x)
@@ -341,7 +319,7 @@
             jax.ShapeDtypeStruct((8, 2 * block, width), jnp.float32),
             jax.ShapeDtypeStruct((8, 2 * block, width), narrow_type),
         ),
-        in_specs=[in_vmem] * 8,
+        in_specs=[in_vmem] * 10,
         out_specs=(in_vmem, in_vmem),
         scratch_shapes=[
             pltpu.VMEM((4, half, channels), narrow_type),
@@ -351,7 +329,7 @@
         ],
         compiler_params=pltpu.CompilerParams(vmem_limit_bytes=28 << 20),
         name="backward",
-    )(up_own, up_got, out_rows, out_c, normed, qkv, weights, attended)
+    )(up_mine, up_1, up_2, up_3, out_rows, out_c, normed, qkv, weights, attended)
 
     def narrow(values):
         return values.astype(jnp.bfloat16)

time: 56.1 us -> 59.7 us (1.064)
  waiting for transfers between devices: 22.9 us -> 29.4 us
  starting transfers between devices: 24.3 us -> 22.4 us
  Pallas kernels: 6.7 us -> 5.39 us
    ppermute x17 -> x18, waiting for transfers between devices: 19.4 us -> 26.1 us  [swap(): lax.ppermute(values, axis, [(i, i ^ mask) for i in range(lax.axis_size(ax...]
    ppermute x17 -> x18, starting transfers between devices: 24.2 us -> 22.4 us  [swap(): lax.ppermute(values, axis, [(i, i ^ mask) for i in range(lax.axis_size(ax...]
    pallas_call x2, Pallas kernels: 2.88 us -> 1.55 us  [conv(): pl.pallas_call(functools.partial(conv_kernel, far), out_shape=piece, in_s...]
    dynamic_slice x1 -> x0, local copies, waits for them, and re-layouts: 0.98 us -> none  [pick(): return lax.dynamic_index_in_dim(values, index, dim, keepdims=False)]
    squeeze x0 -> x1, local copies, waits for them, and re-layouts: none -> 0.98 us  [pick(): return lax.dynamic_index_in_dim(values, index, dim, keepdims=False)]
  transfers between devices with their start and end apart: 18 -> 19, of which waited for: 9 -> 12; matrix products, arithmetic and copies ran while one was open for 2% -> 2% of each run, Pallas kernels for 8% -> 5%
where the time goes in v7:
time: 59.7 us; the launch traced here: 59.5 us
  waiting for transfers between devices  29.4 us (49%)
  starting transfers between devices  22.4 us (38%)
  Pallas kernels  5.39 us (9%)
  local copies, waits for them, and re-layouts  1.87 us (3%)
    ppermute x18, waiting for transfers between devices, swap(): lax.ppermute(values, axis, [(i, i ^ mask) for i in range(lax.axis_size(ax...  26.1 us
    ppermute x18, starting transfers between devices, swap(): lax.ppermute(values, axis, [(i, i ^ mask) for i in range(lax.axis_size(ax...  22.4 us
    ppermute x1, waiting for transfers between devices, split_form(): got = lax.ppermute(narrow(pick(total, 1 - zh)), ('tm', 'fsdp'), crossed)  3.33 us
    pallas_call x1, Pallas kernels, split_form(): pl.pallas_call(backward_kernel, out_shape=(jax.ShapeDtypeStruct((8, 2 * b...  1.74 us
    pallas_call x2, Pallas kernels, conv(): pl.pallas_call(functools.partial(conv_kernel, far), out_shape=piece, in_s...  1.55 us
  transfers between devices with their start and end apart: 19, of which 12 were waited for; matrix products, arithmetic and copies ran while one was open for 2% of the time, Pallas kernels for 5%

profile of v7, /device:TPU:0, one launch (start us, length us, event | category | flops | bytes accessed | tf_op | source)
XLA Modules:
  0.0 59.5 jit_solution(11648616470200708745)
XLA Ops:
  0.0 3.0 %collective-permute-start.9 = (bf16[128,1536]{1,0:T(8,128)(2,1)}, bf16[128,1536]{1,0:T(8,128)(2,1)S(1)}, u32[]{:S(2)}, u32[]{:S(2)}) collective-permute-start(bf16[128,1536]{1,0:T(8,128)(2,1)} %refs_0_.1), channel_id=1, source_target_pairs={{0,2},{1,3},{2,0},{3,1},{4,6},{5,7},{6,4},{7,5},{8,10},{9,11},{10,... | collective-permute-start | bytes 1179656 | tf_op jit(solution)/shard_map/ppermute | solution.py:17
  3.0 1.5 %collective-permute-start.5 = (bf16[160,512]{1,0:T(8,128)(2,1)}, bf16[160,512]{1,0:T(8,128)(2,1)S(1)}, u32[]{:S(2)}, u32[]{:S(2)}) collective-permute-start(bf16[160,512]{1,0:T(8,128)(2,1)} %bitcast.43), channel_id=1, source_target_pairs={{0,16},{16,0},{1,17},{17,1},{2,18},{18,2},{3,19},{19,3},{4,20},{20... | collective-permute-start | bytes 491528 | tf_op jit(solution)/shard_map/ppermute | solution.py:17
  4.5 0.5 collective-permute-start.3
  5.0 8.1 %collective-permute-done.9.refs_1_ = bf16[128,1536]{1,0:T(8,128)(2,1)S(1)} collective-permute-done((bf16[128,1536]{1,0:T(8,128)(2,1)}, bf16[128,1536]{1,0:T(8,128)(2,1)S(1)}, u32[]{:S(2)}, u32[]{:S(2)}) %collective-permute-start.9) | collective-permute-done | bytes 393248 | tf_op jit(solution)/shard_map/ppermute | solution.py:17
  13.1 1.0 %dynamic-slice_bitcast_fusion = (bf16[80,512]{1,0:T(8,128)(2,1)S(1)}, bf16[80,512]{1,0:T(8,128)(2,1)S(1)}) fusion(bf16[2,80,512]{2,1,0:T(8,128)(2,1)} %bitcast.51, s32[]{:T(128)S(6)} %select_n.42, s32[]{:T(128)S(6)} %select_n.41), kind=kLoop, calls=%fused_computation.21 | loop fusion | bytes 327688 | tf_op jit(solution)/shard_map/jit(dynamic_index_in_dim)/squeeze | solution.py:21
  14.1 3.2 %collective-permute-start.1 = (bf16[80,512]{1,0:T(8,128)(2,1)S(1)}, bf16[80,512]{1,0:T(8,128)(2,1)S(1)}, u32[]{:S(2)}, u32[]{:S(2)}) collective-permute-start(bf16[80,512]{1,0:T(8,128)(2,1)S(1)} %get-tuple-element.23), channel_id=1, source_target_pairs={{0,8},{4,12},{8,0},{12,4},{1,9},{5,13},{9,1},{13,5},{2,10},{6,14},... | collective-permute-start | bytes 245768 | tf_op jit(solution)/shard_map/ppermute | solution.py:17
  17.4 0.7 %copy-done.4 = f32[512]{0:T(512)S(1)} copy-done((f32[512]{0:T(512)S(1)}, f32[512]{0:T(512)}, u32[]{:S(2)}) %copy-start.4) | copy-done | bytes 2072
  18.0 0.8 %conv_near.1.own_ref = bf16[80,512]{1,0:T(8,128)(2,1)S(1)} custom-call(s32[8,160]{1,0:T(8,128)S(1)} %bitcast.46, bf16[160,512]{1,0:T(8,128)(2,1)S(1)} %bitcast.44, bf16[160,512]{1,0:T(8,128)(2,1)S(1)} %collective-permute-done.5.band_ref, f32[9,512]{1,0:T(8,128)S(1)} %copy-done.2, f32[1,512]{1,0:T(1,128)S(1)} %bitcast.48), custom_call_target="tpu_custom_call" | custom-call | tf_op jit(solution)/shard_map/conv_near/pallas_call | solution.py:268
  18.8 1.6 %collective-permute-start.6 = (bf16[80,512]{1,0:T(8,128)(2,1)S(1)}, bf16[80,512]{1,0:T(8,128)(2,1)S(1)}, u32[]{:S(2)}, u32[]{:S(2)}) collective-permute-start(bf16[80,512]{1,0:T(8,128)(2,1)S(1)} %conv_near.1.own_ref), channel_id=1, source_target_pairs={{0,4},{4,0},{8,12},{12,8},{1,5},{5,1},{9,13},{13,9},{2,6},{6,2},{1... | collective-permute-start | bytes 245768 | tf_op jit(solution)/shard_map/ppermute | solution.py:17
  20.5 0.8 %conv_far.1 = bf16[80,512]{1,0:T(8,128)(2,1)S(1)} custom-call(s32[8,160]{1,0:T(8,128)S(1)} %bitcast.47, bf16[160,512]{1,0:T(8,128)(2,1)S(1)} %bitcast.45, bf16[160,512]{1,0:T(8,128)(2,1)S(1)} %collective-permute-done.5.band_ref, f32[9,512]{1,0:T(8,128)S(1)} %copy-done.2, f32[1,512]{1,0:T(1,128)S(1)} %bitcast.49), custom_call_target="tpu_custom_call" | custom-call | tf_op jit(solution)/shard_map/conv_far/pallas_call | solution.py:268
  21.3 0.9 %collective-permute-done.1.refs_2_ = bf16[80,512]{1,0:T(8,128)(2,1)S(1)} collective-permute-done((bf16[80,512]{1,0:T(8,128)(2,1)S(1)}, bf16[80,512]{1,0:T(8,128)(2,1)S(1)}, u32[]{:S(2)}, u32[]{:S(2)}) %collective-permute-start.1) | collective-permute-done | bytes 81952 | tf_op jit(solution)/shard_map/ppermute | solution.py:17
  22.3 0.9 %collective-permute-start.7 = (bf16[80,512]{1,0:T(8,128)(2,1)S(1)}, bf16[80,512]{1,0:T(8,128)(2,1)S(1)}, u32[]{:S(2)}, u32[]{:S(2)}) collective-permute-start(bf16[80,512]{1,0:T(8,128)(2,1)S(1)} %conv_far.1), channel_id=1, source_target_pairs={{0,8},{4,12},{8,0},{12,4},{1,9},{5,13},{9,1},{13,5},{2,10},{6,14},... | collective-permute-start | bytes 245768 | tf_op jit(solution)/shard_map/ppermute | solution.py:17
  23.2 0.8 %collective-permute-done.6.row_1_ref = bf16[80,512]{1,0:T(8,128)(2,1)S(1)} collective-permute-done((bf16[80,512]{1,0:T(8,128)(2,1)S(1)}, bf16[80,512]{1,0:T(8,128)(2,1)S(1)}, u32[]{:S(2)}, u32[]{:S(2)}) %collective-permute-start.6) | collective-permute-done | bytes 81952 | tf_op jit(solution)/shard_map/ppermute | solution.py:17
  24.0 2.5 %collective-permute-start.8 = (bf16[80,512]{1,0:T(8,128)(2,1)S(1)}, bf16[80,512]{1,0:T(8,128)(2,1)S(1)}, u32[]{:S(2)}, u32[]{:S(2)}) collective-permute-start(bf16[80,512]{1,0:T(8,128)(2,1)S(1)} %conv_far.1), channel_id=1, source_target_pairs={{0,12},{4,8},{8,4},{12,0},{1,13},{5,9},{9,5},{13,1},{2,14},{6,10},... | collective-permute-start | bytes 245768 | tf_op jit(solution)/shard_map/ppermute | solution.py:17
  26.5 2.0 %collective-permute-start.2 = (bf16[80,512]{1,0:T(8,128)(2,1)S(1)}, bf16[80,512]{1,0:T(8,128)(2,1)S(1)}, u32[]{:S(2)}, u32[]{:S(2)}) collective-permute-start(bf16[80,512]{1,0:T(8,128)(2,1)S(1)} %collective-permute-done.1.refs_2_), channel_id=1, source_target_pairs={{0,4},{4,0},{8,12},{12,8},{1,5},{5,1},{9,13},{13,9},{2,6},{6,2},{1... | collective-permute-start | bytes 245768 | tf_op jit(solution)/shard_map/ppermute | solution.py:17
  28.5 0.5 weights.1
  29.0 2.9 %collective-permute-done.7.row_2_ref = bf16[80,512]{1,0:T(8,128)(2,1)S(1)} collective-permute-done((bf16[80,512]{1,0:T(8,128)(2,1)S(1)}, bf16[80,512]{1,0:T(8,128)(2,1)S(1)}, u32[]{:S(2)}, u32[]{:S(2)}) %collective-permute-start.7) | collective-permute-done | bytes 81952 | tf_op jit(solution)/shard_map/ppermute | solution.py:17
  31.9 1.0 %forward.1 = (bf16[320,768]{1,0:T(8,128)(2,1)S(1)}, bf16[10,80,256]{2,1,0:T(8,128)(2,1)S(1)}, bf16[320,256]{1,0:T(8,128)(2,1)S(1)}, bf16[4,80,512]{2,1,0:T(8,128)(2,1)S(1)}) custom-call(bf16[80,512]{1,0:T(8,128)(2,1)S(1)} %conv_near.1.own_ref, bf16[80,512]{1,0:T(8,128)(2,1)S(1)} %collective-permute-done.6.row_1_ref, ...), custom_call_target="tpu_custom_call" | custom-call | tf_op jit(solution)/shard_map/forward/pallas_call | solution.py:303
  33.0 1.3 %collective-permute-done.2.refs_3_ = bf16[80,512]{1,0:T(8,128)(2,1)S(1)} collective-permute-done((bf16[80,512]{1,0:T(8,128)(2,1)S(1)}, bf16[80,512]{1,0:T(8,128)(2,1)S(1)}, u32[]{:S(2)}, u32[]{:S(2)}) %collective-permute-start.2) | collective-permute-done | bytes 81952 | tf_op jit(solution)/shard_map/ppermute | solution.py:17
  34.2 1.7 %backward.1 = (f32[8,128,256]{2,1,0:T(8,128)S(1)}, bf16[8,128,256]{2,1,0:T(8,128)(2,1)S(1)}) custom-call(bf16[80,512]{1,0:T(8,128)(2,1)S(1)} %get-tuple-element.24.refs_0_, bf16[80,512]{1,0:T(8,128)(2,1)S(1)} %collective-permute-done.refs_1_, bf16[80,512]{1,0:T(8,128)(2,1)S(1)} %collective-permute-done.1.refs_2_, ...), custom_call_target="tpu_custom_call" | custom-call | tf_op jit(solution)/shard_map/backward/pallas_call | solution.py:316
  36.1 1.9 %collective-permute-done.12 = bf16[8,128,256]{2,1,0:T(8,128)(2,1)S(1)} collective-permute-done((bf16[8,128,256]{2,1,0:T(8,128)(2,1)S(1)}, bf16[8,128,256]{2,1,0:T(8,128)(2,1)S(1)}, u32[]{:S(2)}, u32[]{:S(2)}) %collective-permute-start.12) | collective-permute-done | bytes 524320 | tf_op jit(solution)/shard_map/ppermute | solution.py:17
  38.2 1.6 %collective-permute-start.15 = (bf16[2,2,128,128]{3,2,1,0:T(8,128)(2,1)S(1)}, bf16[2,2,128,128]{3,2,1,0:T(8,128)(2,1)S(1)}, u32[]{:S(2)}, u32[]{:S(2)}) collective-permute-start(bf16[2,2,128,128]{3,2,1,0:T(8,128)(2,1)S(1)} %fusion.1), channel_id=1, source_target_pairs={{0,16},{16,0},{1,17},{17,1},{2,18},{18,2},{3,19},{19,3},{4,20},{20... | collective-permute-start | bytes 393224 | tf_op jit(solution)/shard_map/ppermute | solution.py:17
  39.8 1.6 %collective-permute-start.13 = (bf16[2,2,128,128]{3,2,1,0:T(8,128)(2,1)S(1)}, bf16[2,2,128,128]{3,2,1,0:T(8,128)(2,1)S(1)}, u32[]{:S(2)}, u32[]{:S(2)}) collective-permute-start(bf16[2,2,128,128]{3,2,1,0:T(8,128)(2,1)S(1)} %fusion), channel_id=1, source_target_pairs={{0,2},{1,3},{2,0},{3,1},{4,6},{5,7},{6,4},{7,5},{8,10},{9,11},{10,... | collective-permute-start | bytes 393224 | tf_op jit(solution)/shard_map/ppermute | solution.py:17
  41.4 2.4 %collective-permute-done.15 = bf16[2,2,128,128]{3,2,1,0:T(8,128)(2,1)S(1)} collective-permute-done((bf16[2,2,128,128]{3,2,1,0:T(8,128)(2,1)S(1)}, bf16[2,2,128,128]{3,2,1,0:T(8,128)(2,1)S(1)}, u32[]{:S(2)}, u32[]{:S(2)}) %collective-permute-start.15) | collective-permute-done | bytes 131104 | tf_op jit(solution)/shard_map/ppermute | solution.py:17
  43.9 1.6 %collective-permute-start.16 = (bf16[2,128,128]{2,1,0:T(8,128)(2,1)S(1)}, bf16[2,128,128]{2,1,0:T(8,128)(2,1)S(1)}, u32[]{:S(2)}, u32[]{:S(2)}) collective-permute-start(bf16[2,128,128]{2,1,0:T(8,128)(2,1)S(1)} %fusion.8), channel_id=1, source_target_pairs={{0,2},{1,3},{2,0},{3,1},{4,6},{5,7},{6,4},{7,5},{8,10},{9,11},{10,... | collective-permute-start | bytes 196616 | tf_op jit(solution)/shard_map/ppermute | solution.py:17
  45.5 1.6 %collective-permute-start.14 = (bf16[2,128,128]{2,1,0:T(8,128)(2,1)S(1)}, bf16[2,128,128]{2,1,0:T(8,128)(2,1)S(1)}, u32[]{:S(2)}, u32[]{:S(2)}) collective-permute-start(bf16[2,128,128]{2,1,0:T(8,128)(2,1)S(1)} %fusion.7), channel_id=1, source_target_pairs={{0,16},{16,0},{1,17},{17,1},{2,18},{18,2},{3,19},{19,3},{4,20},{20... | collective-permute-start | bytes 196616 | tf_op jit(solution)/shard_map/ppermute | solution.py:17
  47.1 1.1 %collective-permute-done.16 = bf16[2,128,128]{2,1,0:T(8,128)(2,1)S(1)} collective-permute-done((bf16[2,128,128]{2,1,0:T(8,128)(2,1)S(1)}, bf16[2,128,128]{2,1,0:T(8,128)(2,1)S(1)}, u32[]{:S(2)}, u32[]{:S(2)}) %collective-permute-start.16) | collective-permute-done | bytes 65568 | tf_op jit(solution)/shard_map/ppermute | solution.py:17
  48.2 1.6 %collective-permute-done.14 = bf16[2,128,128]{2,1,0:T(8,128)(2,1)S(1)} collective-permute-done((bf16[2,128,128]{2,1,0:T(8,128)(2,1)S(1)}, bf16[2,128,128]{2,1,0:T(8,128)(2,1)S(1)}, u32[]{:S(2)}, u32[]{:S(2)}) %collective-permute-start.14) | collective-permute-done | bytes 65568 | tf_op jit(solution)/shard_map/ppermute | solution.py:17
  49.9 0.6 %collective-permute-start.17 = (bf16[128,256]{1,0:T(8,128)(2,1)S(1)}, bf16[128,256]{1,0:T(8,128)(2,1)S(1)}, u32[]{:S(2)}, u32[]{:S(2)}) collective-permute-start(bf16[128,256]{1,0:T(8,128)(2,1)S(1)} %fusion.9), channel_id=1, source_target_pairs={{0,8},{4,12},{8,0},{12,4},{1,9},{5,13},{9,1},{13,5},{2,10},{6,14},... | collective-permute-start | bytes 196616 | tf_op jit(solution)/shard_map/ppermute | solution.py:17
  50.5 4.9 %collective-permute-done.17 = bf16[128,256]{1,0:T(8,128)(2,1)S(1)} collective-permute-done((bf16[128,256]{1,0:T(8,128)(2,1)S(1)}, bf16[128,256]{1,0:T(8,128)(2,1)S(1)}, u32[]{:S(2)}, u32[]{:S(2)}) %collective-permute-start.17) | collective-permute-done | bytes 65568 | tf_op jit(solution)/shard_map/ppermute | solution.py:17
  55.5 3.3 %collective-permute-done.18.got_ref = bf16[64,256]{1,0:T(8,128)(2,1)S(1)} collective-permute-done((bf16[64,256]{1,0:T(8,128)(2,1)S(1)}, bf16[64,256]{1,0:T(8,128)(2,1)S(1)}, u32[]{:S(2)}, u32[]{:S(2)}) %collective-permute-start.18) | collective-permute-done | bytes 32800 | tf_op jit(solution)/shard_map/ppermute | solution.py:353
  58.9 0.7 %join.1 = f32[256,128]{1,0:T(8,128)} custom-call(f32[2,64,256]{2,1,0:T(8,128)S(1)} %bitcast.42, bf16[64,256]{1,0:T(8,128)(2,1)S(1)} %collective-permute-done.18.got_ref), custom_call_target="tpu_custom_call" | custom-call | tf_op jit(solution)/shard_map/join/pallas_call | solution.py:355
  (39 shorter events, 0.8 us)
Async XLA Ops:
  0.0 13.1 %collective-permute-start.9 = (bf16[128,1536]{1,0:T(8,128)(2,1)}, bf16[128,1536]{1,0:T(8,128)(2,1)S(1)}, u32[]{:S(2)}, u32[]{:S(2)}) collective-permute-start(bf16[128,1536]{1,0:T(8,128)(2,1)} %refs_0_.1), channel_id=1, source_target_pairs={{0,2},{1,3},{2,0},{3,1},{4,6},{5,7},{6,4},{7,5},{8,10},{9,11},{10,... | collective-permute-start | bytes 1179656 | tf_op jit(solution)/shard_map/ppermute | solution.py:17
  3.0 14.4 %collective-permute-start.5 = (bf16[160,512]{1,0:T(8,128)(2,1)}, bf16[160,512]{1,0:T(8,128)(2,1)S(1)}, u32[]{:S(2)}, u32[]{:S(2)}) collective-permute-start(bf16[160,512]{1,0:T(8,128)(2,1)} %bitcast.43), channel_id=1, source_target_pairs={{0,16},{16,0},{1,17},{17,1},{2,18},{18,2},{3,19},{19,3},{4,20},{20... | collective-permute-start | bytes 491528 | tf_op jit(solution)/shard_map/ppermute | solution.py:17
  4.5 16.0 %collective-permute-start.3 = (bf16[128,512]{1,0:T(8,128)(2,1)}, bf16[128,512]{1,0:T(8,128)(2,1)S(1)}, u32[]{:S(2)}, u32[]{:S(2)}) collective-permute-start(bf16[128,512]{1,0:T(8,128)(2,1)} %param.12), channel_id=1, source_target_pairs={{0,2},{1,3},{2,0},{3,1},{4,6},{5,7},{6,4},{7,5},{8,10},{9,11},{10,... | collective-permute-start | bytes 393224 | tf_op jit(solution)/shard_map/ppermute | solution.py:17
  5.0 21.5 %collective-permute-start.10 = (bf16[128,1536]{1,0:T(8,128)(2,1)}, bf16[128,1536]{1,0:T(8,128)(2,1)S(1)}, u32[]{:S(2)}, u32[]{:S(2)}) collective-permute-start(bf16[128,1536]{1,0:T(8,128)(2,1)} %refs_0_.1), channel_id=1, source_target_pairs={{0,1},{1,0},{2,3},{3,2},{4,5},{5,4},{6,7},{7,6},{8,9},{9,8},{10,11... | collective-permute-start | bytes 1179656 | tf_op jit(solution)/shard_map/ppermute | solution.py:17
  13.1 13.3 %collective-permute-start.11 = (bf16[128,1536]{1,0:T(8,128)(2,1)S(1)}, bf16[128,1536]{1,0:T(8,128)(2,1)S(1)}, u32[]{:S(2)}, u32[]{:S(2)}) collective-permute-start(bf16[128,1536]{1,0:T(8,128)(2,1)S(1)} %collective-permute-done.9.refs_1_), channel_id=1, source_target_pairs={{0,1},{1,0},{2,3},{3,2},{4,5},{5,4},{6,7},{7,6},{8,9},{9,8},{10,11... | collective-permute-start | bytes 1179656 | tf_op jit(solution)/shard_map/ppermute | solution.py:17
  13.1 4.2 %copy-start = (bf16[1,1,160,512]{3,2,1,0:T(8,128)(2,1)S(1)}, bf16[1,1,160,512]{3,2,1,0:T(8,128)(2,1)}, u32[]{:S(2)}) copy-start(bf16[1,1,160,512]{3,2,1,0:T(8,128)(2,1)} %param.7) | copy-start | bytes 491524
  13.1 4.2 %copy-start.2 = (f32[9,512]{1,0:T(8,128)S(1)}, f32[9,512]{1,0:T(8,128)}, u32[]{:S(2)}) copy-start(f32[9,512]{1,0:T(8,128)} %taps_ref.3) | copy-start | bytes 55300
  14.1 3.2 %copy-start.3 = (s32[160,8]{0,1:T(8,128)S(1)}, s32[160,8]{0,1:T(8,128)}, u32[]{:S(2)}) copy-start(s32[160,8]{0,1:T(8,128)} %param.8) | copy-start | bytes 15364
  14.1 8.1 %collective-permute-start.1 = (bf16[80,512]{1,0:T(8,128)(2,1)S(1)}, bf16[80,512]{1,0:T(8,128)(2,1)S(1)}, u32[]{:S(2)}, u32[]{:S(2)}) collective-permute-start(bf16[80,512]{1,0:T(8,128)(2,1)S(1)} %get-tuple-element.23), channel_id=1, source_target_pairs={{0,8},{4,12},{8,0},{12,4},{1,9},{5,13},{9,1},{13,5},{2,10},{6,14},... | collective-permute-start | bytes 245768 | tf_op jit(solution)/shard_map/ppermute | solution.py:17
  17.3 0.7 %copy-start.4 = (f32[512]{0:T(512)S(1)}, f32[512]{0:T(512)}, u32[]{:S(2)}) copy-start(f32[512]{0:T(512)} %param.10) | copy-start | bytes 6148
  18.0 2.4 %copy-start.5 = (bf16[128,512]{1,0:T(8,128)(2,1)S(1)}, bf16[128,512]{1,0:T(8,128)(2,1)}, u32[]{:S(2)}) copy-start(bf16[128,512]{1,0:T(8,128)(2,1)} %param.12) | copy-start | bytes 393220
  18.8 9.7 %copy-start.1 = (bf16[128,1536]{1,0:T(8,128)(2,1)S(1)}, bf16[128,1536]{1,0:T(8,128)(2,1)}, u32[]{:S(2)}) copy-start(bf16[128,1536]{1,0:T(8,128)(2,1)} %refs_0_.1) | copy-start | bytes 1179652
  18.8 5.2 %collective-permute-start.6 = (bf16[80,512]{1,0:T(8,128)(2,1)S(1)}, bf16[80,512]{1,0:T(8,128)(2,1)S(1)}, u32[]{:S(2)}, u32[]{:S(2)}) collective-permute-start(bf16[80,512]{1,0:T(8,128)(2,1)S(1)} %conv_near.1.own_ref), channel_id=1, source_target_pairs={{0,4},{4,0},{8,12},{12,8},{1,5},{5,1},{9,13},{13,9},{2,6},{6,2},{1... | collective-permute-start | bytes 245768 | tf_op jit(solution)/shard_map/ppermute | solution.py:17
  20.5 13.8 %collective-permute-start.4 = (bf16[128,512]{1,0:T(8,128)(2,1)S(1)}, bf16[128,512]{1,0:T(8,128)(2,1)S(1)}, u32[]{:S(2)}, u32[]{:S(2)}) collective-permute-start(bf16[128,512]{1,0:T(8,128)(2,1)S(1)} %broadcast_select_fusion.refs_4_), channel_id=1, source_target_pairs={{0,1},{1,0},{2,3},{3,2},{4,5},{5,4},{6,7},{7,6},{8,9},{9,8},{10,11... | collective-permute-start | bytes 393224 | tf_op jit(solution)/shard_map/ppermute | solution.py:17
  22.3 9.6 %collective-permute-start.7 = (bf16[80,512]{1,0:T(8,128)(2,1)S(1)}, bf16[80,512]{1,0:T(8,128)(2,1)S(1)}, u32[]{:S(2)}, u32[]{:S(2)}) collective-permute-start(bf16[80,512]{1,0:T(8,128)(2,1)S(1)} %conv_far.1), channel_id=1, source_target_pairs={{0,8},{4,12},{8,0},{12,4},{1,9},{5,13},{9,1},{13,5},{2,10},{6,14},... | collective-permute-start | bytes 245768 | tf_op jit(solution)/shard_map/ppermute | solution.py:17
  24.0 7.9 %collective-permute-start.8 = (bf16[80,512]{1,0:T(8,128)(2,1)S(1)}, bf16[80,512]{1,0:T(8,128)(2,1)S(1)}, u32[]{:S(2)}, u32[]{:S(2)}) collective-permute-start(bf16[80,512]{1,0:T(8,128)(2,1)S(1)} %conv_far.1), channel_id=1, source_target_pairs={{0,12},{4,8},{8,4},{12,0},{1,13},{5,9},{9,5},{13,1},{2,14},{6,10},... | collective-permute-start | bytes 245768 | tf_op jit(solution)/shard_map/ppermute | solution.py:17
  26.5 6.5 %collective-permute-start = (bf16[80,512]{1,0:T(8,128)(2,1)S(1)}, bf16[80,512]{1,0:T(8,128)(2,1)S(1)}, u32[]{:S(2)}, u32[]{:S(2)}) collective-permute-start(bf16[80,512]{1,0:T(8,128)(2,1)S(1)} %get-tuple-element.24.refs_0_), channel_id=1, source_target_pairs={{0,4},{4,0},{8,12},{12,8},{1,5},{5,1},{9,13},{13,9},{2,6},{6,2},{1... | collective-permute-start | bytes 245768 | tf_op jit(solution)/shard_map/ppermute | solution.py:17
  26.5 7.7 %collective-permute-start.2 = (bf16[80,512]{1,0:T(8,128)(2,1)S(1)}, bf16[80,512]{1,0:T(8,128)(2,1)S(1)}, u32[]{:S(2)}, u32[]{:S(2)}) collective-permute-start(bf16[80,512]{1,0:T(8,128)(2,1)S(1)} %collective-permute-done.1.refs_2_), channel_id=1, source_target_pairs={{0,4},{4,0},{8,12},{12,8},{1,5},{5,1},{9,13},{13,9},{2,6},{6,2},{1... | collective-permute-start | bytes 245768 | tf_op jit(solution)/shard_map/ppermute | solution.py:17
  36.0 2.0 %collective-permute-start.12 = (bf16[8,128,256]{2,1,0:T(8,128)(2,1)S(1)}, bf16[8,128,256]{2,1,0:T(8,128)(2,1)S(1)}, u32[]{:S(2)}, u32[]{:S(2)}) collective-permute-start(bf16[8,128,256]{2,1,0:T(8,128)(2,1)S(1)} %get-tuple-element.20), channel_id=1, source_target_pairs={{0,1},{1,0},{2,3},{3,2},{4,5},{5,4},{6,7},{7,6},{8,9},{9,8},{10,11... | collective-permute-start | bytes 1572872 | tf_op jit(solution)/shard_map/ppermute | solution.py:17
  38.2 5.6 %collective-permute-start.15 = (bf16[2,2,128,128]{3,2,1,0:T(8,128)(2,1)S(1)}, bf16[2,2,128,128]{3,2,1,0:T(8,128)(2,1)S(1)}, u32[]{:S(2)}, u32[]{:S(2)}) collective-permute-start(bf16[2,2,128,128]{3,2,1,0:T(8,128)(2,1)S(1)} %fusion.1), channel_id=1, source_target_pairs={{0,16},{16,0},{1,17},{17,1},{2,18},{18,2},{3,19},{19,3},{4,20},{20... | collective-permute-start | bytes 393224 | tf_op jit(solution)/shard_map/ppermute | solution.py:17
  39.8 5.6 %collective-permute-start.13 = (bf16[2,2,128,128]{3,2,1,0:T(8,128)(2,1)S(1)}, bf16[2,2,128,128]{3,2,1,0:T(8,128)(2,1)S(1)}, u32[]{:S(2)}, u32[]{:S(2)}) collective-permute-start(bf16[2,2,128,128]{3,2,1,0:T(8,128)(2,1)S(1)} %fusion), channel_id=1, source_target_pairs={{0,2},{1,3},{2,0},{3,1},{4,6},{5,7},{6,4},{7,5},{8,10},{9,11},{10,... | collective-permute-start | bytes 393224 | tf_op jit(solution)/shard_map/ppermute | solution.py:17
  43.9 4.3 %collective-permute-start.16 = (bf16[2,128,128]{2,1,0:T(8,128)(2,1)S(1)}, bf16[2,128,128]{2,1,0:T(8,128)(2,1)S(1)}, u32[]{:S(2)}, u32[]{:S(2)}) collective-permute-start(bf16[2,128,128]{2,1,0:T(8,128)(2,1)S(1)} %fusion.8), channel_id=1, source_target_pairs={{0,2},{1,3},{2,0},{3,1},{4,6},{5,7},{6,4},{7,5},{8,10},{9,11},{10,... | collective-permute-start | bytes 196616 | tf_op jit(solution)/shard_map/ppermute | solution.py:17
  45.5 4.3 %collective-permute-start.14 = (bf16[2,128,128]{2,1,0:T(8,128)(2,1)S(1)}, bf16[2,128,128]{2,1,0:T(8,128)(2,1)S(1)}, u32[]{:S(2)}, u32[]{:S(2)}) collective-permute-start(bf16[2,128,128]{2,1,0:T(8,128)(2,1)S(1)} %fusion.7), channel_id=1, source_target_pairs={{0,16},{16,0},{1,17},{17,1},{2,18},{18,2},{3,19},{19,3},{4,20},{20... | collective-permute-start | bytes 196616 | tf_op jit(solution)/shard_map/ppermute | solution.py:17
  49.9 5.6 %collective-permute-start.17 = (bf16[128,256]{1,0:T(8,128)(2,1)S(1)}, bf16[128,256]{1,0:T(8,128)(2,1)S(1)}, u32[]{:S(2)}, u32[]{:S(2)}) collective-permute-start(bf16[128,256]{1,0:T(8,128)(2,1)S(1)} %fusion.9), channel_id=1, source_target_pairs={{0,8},{4,12},{8,0},{12,4},{1,9},{5,13},{9,1},{13,5},{2,10},{6,14},... | collective-permute-start | bytes 196616 | tf_op jit(solution)/shard_map/ppermute | solution.py:17
  55.5 3.4 %collective-permute-start.18 = (bf16[64,256]{1,0:T(8,128)(2,1)S(1)}, bf16[64,256]{1,0:T(8,128)(2,1)S(1)}, u32[]{:S(2)}, u32[]{:S(2)}) collective-permute-start(bf16[64,256]{1,0:T(8,128)(2,1)S(1)} %fusion.10), channel_id=1, source_target_pairs={{0,5},{1,4},{2,7},{3,6},{4,1},{5,0},{6,3},{7,2},{8,13},{9,12},{10,... | collective-permute-start | bytes 98312 | tf_op jit(solution)/shard_map/ppermute | solution.py:353

commit v8 on v7

--- a/solution.py
+++ b/solution.py
@@ -154,7 +154,7 @@
     frames = 4
     piece_refs, out_refs, refs = refs[:4], refs[4:6], refs[6:]
     n_ref, qkv_ref, weights_ref, attended_ref, refs = *refs[:4], refs[4:]
-    keep_ref, send_ref, u_ref, g_ref, sums_ref, out_sums_ref = refs
+    keep_refs, send_refs, (u_ref, g_ref, sums_ref, out_sums_ref) = refs[:2], refs[2:4], refs[4:]
     _, t, _, zh, _, core = place()
     _, pixels, channels = n_ref.shape
     width = out_sums_ref.shape[0]
@@ -218,34 +218,32 @@
     block = channels // HEADS
     for slot in range(8):
         at_x, at_y, at_zp = slot >> 2, (slot >> 1) & 1, slot & 1
-        for side, ref in ((core, keep_ref), (1 - core, send_ref)):
+        places = ((at_x, at_y, at_zp), (at_y, at_x, at_zp))
+        for side, path_refs in ((1 - core, send_refs), (core, keep_refs)):
             for low in range(2):
                 rows_at = slice(low * block, (low + 1) * block)
                 first = at_y * 16 + (2 * at_zp + low) * 4 + 2 * at_x
-                if first < 3 * HEADS:
-                    start = pl.multiple_of((first + (side ^ zh ^ low)) * block, block)
-                    for lane in range(width // 128):
-                        piece = sums_ref[lane, pl.ds(start, block), :]
-                        lanes_at = slice(lane * 128, (lane + 1) * 128)
-                        ref[slot, rows_at, lanes_at] = piece.astype(ref.dtype)
-                else:
-                    start = pl.multiple_of((2 * at_x + side) * block, block)
-                    piece = out_sums_ref[pl.ds(start, block), low * width : (low + 1) * width]
-                    ref[slot, rows_at, :] = piece.astype(ref.dtype)
-
-
-def join_kernel(total_ref, got_ref, out_ref):
+                for path, ref in enumerate(path_refs):
+                    if first < 3 * HEADS:
+                        start = pl.multiple_of((first + (side ^ zh ^ low)) * block, block)
+                        piece = sums_ref[path, pl.ds(start, block), :]
+                    else:
+                        start = pl.multiple_of((2 * at_x + side) * block, block)
+                        lanes_at = low * width + path * 128
+                        piece = out_sums_ref[pl.ds(start, block), lanes_at : lanes_at + 128]
+                    ref[(*places[path], rows_at)] = piece.astype(ref.dtype)
+
+
+def join_kernel(first_ref, second_ref, got_ref, out_ref):
     y, _, zp, zh, _, _ = place()
-    lanes = out_ref.shape[1]
-    rows, width = got_ref.shape
+    paths, rows, _ = got_ref.shape
     is_out = (y == 1) & (zp == 1)
-    got = got_ref[...].astype(jnp.float32)
-    for side in range(2):
-        joined = jnp.where(is_out | (zh == side), total_ref[side], got)
-        for lane in range(0, width, lanes):
-            first = (side * width + lane) // lanes
-            step = 2 * width // lanes
-            out_ref[pl.ds(first, rows, stride=step), :] = joined[:, lane : lane + lanes]
+    for path, total_ref in enumerate((first_ref, second_ref)):
+        got = got_ref[path].astype(jnp.float32)
+        for side in range(2):
+            mine = total_ref[side * rows : (side + 1) * rows, :]
+            joined = jnp.where(is_out | (zh == side), mine, got)
+            out_ref[pl.ds(side * paths + path, rows, stride=2 * paths), :] = joined
 
 
 def split_form(features, neighbours, conv_taps, norm_gain, qkv_weight, out_weight, cotangent):
@@ -280,7 +278,8 @@
     row_2 = swap(n_other, "tm", 2)
     n_mine = conv(False)
     row_1 = swap(n_mine, "tm", 1)
-    up_mine = pick(halves, zp)
+    later, _ = lax.optimization_barrier((halves, n_other))
+    up_mine = pick(later, zp)
     up_1 = swap(up_mine, "tm", 1)
     up_3 = swap(up_2, "tm", 1)
     qkv_c = swap(qkv_weight, "fsdp", 1)
@@ -313,14 +312,14 @@
         compiler_params=pltpu.CompilerParams(vmem_limit_bytes=24 << 20),
         name="forward",
     )(n_mine, row_1, row_2, row_3, own_qkv, full_qkv)
-    keep, send = pl.pallas_call(
+    *keep, send_0, send_1 = pl.pallas_call(
         backward_kernel,
         out_shape=(
-            jax.ShapeDtypeStruct((8, 2 * block, width), jnp.float32),
-            jax.ShapeDtypeStruct((8, 2 * block, width), narrow_type),
+            *(jax.ShapeDtypeStruct((2, 2, 2, 2 * block, 128), jnp.float32),) * 2,
+            *(jax.ShapeDtypeStruct((2, 2, 2, 2 * block, 128), narrow_type),) * 2,
         ),
         in_specs=[in_vmem] * 10,
-        out_specs=(in_vmem, in_vmem),
+        out_specs=(in_vmem,) * 4,
         scratch_shapes=[
             pltpu.VMEM((4, half, channels), narrow_type),
             pltpu.VMEM((4, half, width), narrow_type),
@@ -334,32 +333,31 @@
     def narrow(values):
         return values.astype(jnp.bfloat16)
 
-    total = keep + swap(send, "fsdp", 1).astype(jnp.float32)
-    total = total.reshape(2, 2, 2, 2 * block, width)
-    first, second = total[..., : width // 2], total[..., width // 2 :]
-    got_first = swap(narrow(pick(first, 1 - x, 0)), "fsdp", 2)
-    got_second = swap(narrow(pick(second, 1 - y, 1)), "blk", 1)
-    first = pick(first, x, 0) + got_first.astype(jnp.float32)
-    second = pick(second, y, 1) + got_second.astype(jnp.float32)
-    got_first = swap(narrow(pick(first, 1 - y, 0)), "blk", 1)
-    got_second = swap(narrow(pick(second, 1 - x, 0)), "fsdp", 2)
-    first = pick(first, y, 0) + got_first.astype(jnp.float32)
-    second = pick(second, x, 0) + got_second.astype(jnp.float32)
-    total = jnp.concatenate([first, second], axis=-1)
-    total = pick(total, zp) + swap(narrow(pick(total, 1 - zp)), "tm", 2).astype(jnp.float32)
-    total = total.reshape(2, block, width)
+    hops = (("fsdp", 2, x), ("blk", 1, y))
+    paths = [
+        total + swap(send, "fsdp", 1).astype(jnp.float32)
+        for total, send in zip(keep, (send_0, send_1))
+    ]
+    for stage in range(2):
+        for path in range(2):
+            axis, mask, index = hops[path ^ stage]
+            got = swap(narrow(pick(paths[path], 1 - index)), axis, mask)
+            paths[path] = pick(paths[path], index) + got.astype(jnp.float32)
+    for path in range(2):
+        got = swap(narrow(pick(paths[path], 1 - zp)), "tm", 2)
+        paths[path] = pick(paths[path], zp) + got.astype(jnp.float32)
+    far = jnp.stack([narrow(pick(total.reshape(2, block, 128), 1 - zh)) for total in paths])
     cores = lax.axis_size("fsdp")
     crossed = [(i, i ^ cores ^ 1) for i in range(lax.axis_size("tm") * cores)]
-    got = lax.ppermute(narrow(pick(total, 1 - zh)), ("tm", "fsdp"), crossed)
-    lanes = 128
+    got = lax.ppermute(far, ("tm", "fsdp"), crossed)
     out = pl.pallas_call(
         join_kernel,
-        out_shape=jax.ShapeDtypeStruct((block * channels // lanes, lanes), jnp.float32),
-        in_specs=[in_vmem] * 2,
+        out_shape=jax.ShapeDtypeStruct((block * channels // 128, 128), jnp.float32),
+        in_specs=[in_vmem] * 3,
         out_specs=in_vmem,
         compiler_params=pltpu.CompilerParams(vmem_limit_bytes=4 << 20),
         name="join",
-    )(total, got)
+    )(*paths, got)
     return out.reshape(-1)
 
 

time: 59.7 us -> 58.6 us (0.982)
  waiting for transfers between devices: 29.4 us -> 26.5 us
  starting transfers between devices: 22.4 us -> 24.5 us
    ppermute x18 -> x20, waiting for transfers between devices: 26.1 us -> 23.2 us  [swap(): lax.ppermute(values, axis, [(i, i ^ mask) for i in range(lax.axis_size(ax...]
    ppermute x18 -> x20, starting transfers between devices: 22.4 us -> 24.4 us  [swap(): lax.ppermute(values, axis, [(i, i ^ mask) for i in range(lax.axis_size(ax...]
    squeeze x1 -> x2, local copies, waits for them, and re-layouts: 0.98 us -> 0.02 us  [pick(): return lax.dynamic_index_in_dim(values, index, dim, keepdims=False)]
    unnamed x12 -> x14, local copies, waits for them, and re-layouts: 0.68 us -> 1.39 us
  transfers between devices with their start and end apart: 19 -> 21, of which waited for: 12 -> 13; matrix products, arithmetic and copies ran while one was open for 2% -> 1% of each run, Pallas kernels for 5% -> 5%
where the time goes in v8:
time: 58.6 us; the launch traced here: 58.4 us
  waiting for transfers between devices  26.5 us (45%)
  starting transfers between devices  24.5 us (42%)
  Pallas kernels  5.38 us (9%)
  local copies, waits for them, and re-layouts  1.55 us (3%)
    ppermute x20, starting transfers between devices, swap(): lax.ppermute(values, axis, [(i, i ^ mask) for i in range(lax.axis_size(ax...  24.4 us
    ppermute x20, waiting for transfers between devices, swap(): lax.ppermute(values, axis, [(i, i ^ mask) for i in range(lax.axis_size(ax...  23.2 us
    ppermute x1, waiting for transfers between devices, split_form(): got = lax.ppermute(far, ('tm', 'fsdp'), crossed)  3.33 us
    pallas_call x1, Pallas kernels, split_form(): pl.pallas_call(backward_kernel, out_shape=(*(jax.ShapeDtypeStruct((2, 2,...  1.74 us
    pallas_call x2, Pallas kernels, conv(): pl.pallas_call(functools.partial(conv_kernel, far), out_shape=piece, in_s...  1.54 us
    unnamed x14, local copies, waits for them, and re-layouts  1.39 us
  transfers between devices with their start and end apart: 21, of which 13 were waited for; matrix products, arithmetic and copies ran while one was open for 1% of the time, Pallas kernels for 5%

profile of v8, /device:TPU:0, one launch (start us, length us, event | category | flops | bytes accessed | tf_op | source)
XLA Modules:
  0.0 58.4 jit_solution(3010255642478174292)
XLA Ops:
  0.0 3.0 %collective-permute-start.9 = (bf16[128,1536]{1,0:T(8,128)(2,1)}, bf16[128,1536]{1,0:T(8,128)(2,1)S(1)}, u32[]{:S(2)}, u32[]{:S(2)}) collective-permute-start(bf16[128,1536]{1,0:T(8,128)(2,1)} %refs_0_.1), channel_id=1, source_target_pairs={{0,2},{1,3},{2,0},{3,1},{4,6},{5,7},{6,4},{7,5},{8,10},{9,11},{10,... | collective-permute-start | bytes 1179656 | tf_op jit(solution)/shard_map/ppermute | solution.py:17
  3.0 1.5 %collective-permute-start = (bf16[160,512]{1,0:T(8,128)(2,1)}, bf16[160,512]{1,0:T(8,128)(2,1)S(1)}, u32[]{:S(2)}, u32[]{:S(2)}) collective-permute-start(bf16[160,512]{1,0:T(8,128)(2,1)} %bitcast.37), channel_id=1, source_target_pairs={{0,16},{16,0},{1,17},{17,1},{2,18},{18,2},{3,19},{19,3},{4,20},{20... | collective-permute-start | bytes 491528 | tf_op jit(solution)/shard_map/ppermute | solution.py:17
  4.5 0.5 collective-permute-start.4
  5.0 8.1 %collective-permute-done.9.refs_1_ = bf16[128,1536]{1,0:T(8,128)(2,1)S(1)} collective-permute-done((bf16[128,1536]{1,0:T(8,128)(2,1)}, bf16[128,1536]{1,0:T(8,128)(2,1)S(1)}, u32[]{:S(2)}, u32[]{:S(2)}) %collective-permute-start.9) | collective-permute-done | bytes 393248 | tf_op jit(solution)/shard_map/ppermute | solution.py:17
  13.2 3.2 %collective-permute-start.2 = (bf16[80,512]{1,0:T(8,128)(2,1)S(1)}, bf16[80,512]{1,0:T(8,128)(2,1)S(1)}, u32[]{:S(2)}, u32[]{:S(2)}) collective-permute-start(bf16[80,512]{1,0:T(8,128)(2,1)S(1)} %dynamic-slice_bitcast_fusion), channel_id=1, source_target_pairs={{0,8},{4,12},{8,0},{12,4},{1,9},{5,13},{9,1},{13,5},{2,10},{6,14},... | collective-permute-start | bytes 245768 | tf_op jit(solution)/shard_map/ppermute | solution.py:17
  16.4 0.7 %copy-done.4 = s32[160,8]{0,1:T(8,128)S(1)} copy-done((s32[160,8]{0,1:T(8,128)S(1)}, s32[160,8]{0,1:T(8,128)}, u32[]{:S(2)}) %copy-start.4) | copy-done | bytes 5144
  17.1 0.7 %copy-done.5 = f32[512]{0:T(512)S(1)} copy-done((f32[512]{0:T(512)S(1)}, f32[512]{0:T(512)}, u32[]{:S(2)}) %copy-start.5) | copy-done | bytes 2072
  17.7 0.8 %conv_near.1.own_ref = bf16[80,512]{1,0:T(8,128)(2,1)S(1)} custom-call(s32[8,160]{1,0:T(8,128)S(1)} %bitcast.42, bf16[160,512]{1,0:T(8,128)(2,1)S(1)} %bitcast.38, bf16[160,512]{1,0:T(8,128)(2,1)S(1)} %collective-permute-done.band_ref, f32[9,512]{1,0:T(8,128)S(1)} %copy-done.3, f32[1,512]{1,0:T(1,128)S(1)} %bitcast.44), custom_call_target="tpu_custom_call" | custom-call | tf_op jit(solution)/shard_map/conv_near/pallas_call | solution.py:266
  18.5 1.6 %collective-permute-start.6 = (bf16[80,512]{1,0:T(8,128)(2,1)S(1)}, bf16[80,512]{1,0:T(8,128)(2,1)S(1)}, u32[]{:S(2)}, u32[]{:S(2)}) collective-permute-start(bf16[80,512]{1,0:T(8,128)(2,1)S(1)} %conv_near.1.own_ref), channel_id=1, source_target_pairs={{0,4},{4,0},{8,12},{12,8},{1,5},{5,1},{9,13},{13,9},{2,6},{6,2},{1... | collective-permute-start | bytes 245768 | tf_op jit(solution)/shard_map/ppermute | solution.py:17
  20.3 0.8 %conv_far.1 = bf16[80,512]{1,0:T(8,128)(2,1)S(1)} custom-call(s32[8,160]{1,0:T(8,128)S(1)} %bitcast.43, bf16[160,512]{1,0:T(8,128)(2,1)S(1)} %bitcast.39, bf16[160,512]{1,0:T(8,128)(2,1)S(1)} %collective-permute-done.band_ref, f32[9,512]{1,0:T(8,128)S(1)} %copy-done.3, f32[1,512]{1,0:T(1,128)S(1)} %bitcast.45), custom_call_target="tpu_custom_call" | custom-call | tf_op jit(solution)/shard_map/conv_far/pallas_call | solution.py:266
  21.2 1.0 %collective-permute-start.7 = (bf16[80,512]{1,0:T(8,128)(2,1)S(1)}, bf16[80,512]{1,0:T(8,128)(2,1)S(1)}, u32[]{:S(2)}, u32[]{:S(2)}) collective-permute-start(bf16[80,512]{1,0:T(8,128)(2,1)S(1)} %conv_far.1), channel_id=1, source_target_pairs={{0,8},{4,12},{8,0},{12,4},{1,9},{5,13},{9,1},{13,5},{2,10},{6,14},... | collective-permute-start | bytes 245768 | tf_op jit(solution)/shard_map/ppermute | solution.py:17
  22.2 0.9 %collective-permute-done.6.row_1_ref = bf16[80,512]{1,0:T(8,128)(2,1)S(1)} collective-permute-done((bf16[80,512]{1,0:T(8,128)(2,1)S(1)}, bf16[80,512]{1,0:T(8,128)(2,1)S(1)}, u32[]{:S(2)}, u32[]{:S(2)}) %collective-permute-start.6) | collective-permute-done | bytes 81952 | tf_op jit(solution)/shard_map/ppermute | solution.py:17
  23.1 3.0 %collective-permute-start.8 = (bf16[80,512]{1,0:T(8,128)(2,1)S(1)}, bf16[80,512]{1,0:T(8,128)(2,1)S(1)}, u32[]{:S(2)}, u32[]{:S(2)}) collective-permute-start(bf16[80,512]{1,0:T(8,128)(2,1)S(1)} %conv_far.1), channel_id=1, source_target_pairs={{0,12},{4,8},{8,4},{12,0},{1,13},{5,9},{9,5},{13,1},{2,14},{6,10},... | collective-permute-start | bytes 245768 | tf_op jit(solution)/shard_map/ppermute | solution.py:17
  26.3 2.0 %collective-permute-start.1 = (bf16[80,512]{1,0:T(8,128)(2,1)S(1)}, bf16[80,512]{1,0:T(8,128)(2,1)S(1)}, u32[]{:S(2)}, u32[]{:S(2)}) collective-permute-start(bf16[80,512]{1,0:T(8,128)(2,1)S(1)} %dynamic-slice_bitcast_fusion.1.refs_0_), channel_id=1, source_target_pairs={{0,4},{4,0},{8,12},{12,8},{1,5},{5,1},{9,13},{13,9},{2,6},{6,2},{1... | collective-permute-start | bytes 245768 | tf_op jit(solution)/shard_map/ppermute | solution.py:17
  28.7 2.2 %collective-permute-done.7.row_2_ref = bf16[80,512]{1,0:T(8,128)(2,1)S(1)} collective-permute-done((bf16[80,512]{1,0:T(8,128)(2,1)S(1)}, bf16[80,512]{1,0:T(8,128)(2,1)S(1)}, u32[]{:S(2)}, u32[]{:S(2)}) %collective-permute-start.7) | collective-permute-done | bytes 81952 | tf_op jit(solution)/shard_map/ppermute | solution.py:17
  31.0 1.0 %forward.1 = (bf16[320,768]{1,0:T(8,128)(2,1)S(1)}, bf16[10,80,256]{2,1,0:T(8,128)(2,1)S(1)}, bf16[320,256]{1,0:T(8,128)(2,1)S(1)}, bf16[4,80,512]{2,1,0:T(8,128)(2,1)S(1)}) custom-call(bf16[80,512]{1,0:T(8,128)(2,1)S(1)} %conv_near.1.own_ref, bf16[80,512]{1,0:T(8,128)(2,1)S(1)} %collective-permute-done.6.row_1_ref, ...), custom_call_target="tpu_custom_call" | custom-call | tf_op jit(solution)/shard_map/forward/pallas_call | solution.py:302
  32.3 1.6 %collective-permute-done.1.refs_1_ = bf16[80,512]{1,0:T(8,128)(2,1)S(1)} collective-permute-done((bf16[80,512]{1,0:T(8,128)(2,1)S(1)}, bf16[80,512]{1,0:T(8,128)(2,1)S(1)}, u32[]{:S(2)}, u32[]{:S(2)}) %collective-permute-start.1) | collective-permute-done | bytes 81952 | tf_op jit(solution)/shard_map/ppermute | solution.py:17
  33.9 1.7 %backward.1 = (f32[2,2,2,128,128]{4,3,2,1,0:T(8,128)S(1)}, f32[2,2,2,128,128]{4,3,2,1,0:T(8,128)S(1)}, bf16[2,2,2,128,128]{4,3,2,1,0:T(8,128)(2,1)S(1)}, bf16[2,2,2,128,128]{4,3,2,1,0:T(8,128)(2,1)S(1)}) custom-call(bf16[80,512]{1,0:T(8,128)(2,1)S(1)} %dynamic-slice_bitcast_fusion.1.refs_0_, bf16[80,512]{1,0:T(8,128)(2,1)S(1)} %collective-permute-done.1.refs_1_, ...), custom_call_target="tpu_custom_call" | custom-call | tf_op jit(solution)/shard_map/backward/pallas_call | solution.py:315
  35.7 0.5 collective-permute-start.12
  36.2 1.0 %collective-permute-done.16 = bf16[2,2,2,128,128]{4,3,2,1,0:T(8,128)(2,1)S(1)} collective-permute-done((bf16[2,2,2,128,128]{4,3,2,1,0:T(8,128)(2,1)S(1)}, bf16[2,2,2,128,128]{4,3,2,1,0:T(8,128)(2,1)S(1)}, u32[]{:S(2)}, u32[]{:S(2)}) %collective-permute-start.16) | collective-permute-done | bytes 262176 | tf_op jit(solution)/shard_map/ppermute | solution.py:17
  37.3 1.6 %collective-permute-start.17 = (bf16[2,2,128,128]{3,2,1,0:T(8,128)(2,1)S(1)}, bf16[2,2,128,128]{3,2,1,0:T(8,128)(2,1)S(1)}, u32[]{:S(2)}, u32[]{:S(2)}) collective-permute-start(bf16[2,2,128,128]{3,2,1,0:T(8,128)(2,1)S(1)} %fusion.1), channel_id=1, source_target_pairs={{0,16},{16,0},{1,17},{17,1},{2,18},{18,2},{3,19},{19,3},{4,20},{20... | collective-permute-start | bytes 393224 | tf_op jit(solution)/shard_map/ppermute | solution.py:17
  39.0 1.6 %collective-permute-start.13 = (bf16[2,2,128,128]{3,2,1,0:T(8,128)(2,1)S(1)}, bf16[2,2,128,128]{3,2,1,0:T(8,128)(2,1)S(1)}, u32[]{:S(2)}, u32[]{:S(2)}) collective-permute-start(bf16[2,2,128,128]{3,2,1,0:T(8,128)(2,1)S(1)} %fusion), channel_id=1, source_target_pairs={{0,2},{1,3},{2,0},{3,1},{4,6},{5,7},{6,4},{7,5},{8,10},{9,11},{10,... | collective-permute-start | bytes 393224 | tf_op jit(solution)/shard_map/ppermute | solution.py:17
  40.6 2.3 %collective-permute-done.17 = bf16[2,2,128,128]{3,2,1,0:T(8,128)(2,1)S(1)} collective-permute-done((bf16[2,2,128,128]{3,2,1,0:T(8,128)(2,1)S(1)}, bf16[2,2,128,128]{3,2,1,0:T(8,128)(2,1)S(1)}, u32[]{:S(2)}, u32[]{:S(2)}) %collective-permute-start.17) | collective-permute-done | bytes 131104 | tf_op jit(solution)/shard_map/ppermute | solution.py:17
  43.0 1.6 %collective-permute-start.18 = (bf16[2,128,128]{2,1,0:T(8,128)(2,1)S(1)}, bf16[2,128,128]{2,1,0:T(8,128)(2,1)S(1)}, u32[]{:S(2)}, u32[]{:S(2)}) collective-permute-start(bf16[2,128,128]{2,1,0:T(8,128)(2,1)S(1)} %fusion.3), channel_id=1, source_target_pairs={{0,2},{1,3},{2,0},{3,1},{4,6},{5,7},{6,4},{7,5},{8,10},{9,11},{10,... | collective-permute-start | bytes 196616 | tf_op jit(solution)/shard_map/ppermute | solution.py:17
  44.6 1.6 %collective-permute-start.14 = (bf16[2,128,128]{2,1,0:T(8,128)(2,1)S(1)}, bf16[2,128,128]{2,1,0:T(8,128)(2,1)S(1)}, u32[]{:S(2)}, u32[]{:S(2)}) collective-permute-start(bf16[2,128,128]{2,1,0:T(8,128)(2,1)S(1)} %fusion.2), channel_id=1, source_target_pairs={{0,16},{16,0},{1,17},{17,1},{2,18},{18,2},{3,19},{19,3},{4,20},{20... | collective-permute-start | bytes 196616 | tf_op jit(solution)/shard_map/ppermute | solution.py:17
  46.2 1.1 %collective-permute-done.18 = bf16[2,128,128]{2,1,0:T(8,128)(2,1)S(1)} collective-permute-done((bf16[2,128,128]{2,1,0:T(8,128)(2,1)S(1)}, bf16[2,128,128]{2,1,0:T(8,128)(2,1)S(1)}, u32[]{:S(2)}, u32[]{:S(2)}) %collective-permute-start.18) | collective-permute-done | bytes 65568 | tf_op jit(solution)/shard_map/ppermute | solution.py:17
  47.5 1.5 %collective-permute-done.14 = bf16[2,128,128]{2,1,0:T(8,128)(2,1)S(1)} collective-permute-done((bf16[2,128,128]{2,1,0:T(8,128)(2,1)S(1)}, bf16[2,128,128]{2,1,0:T(8,128)(2,1)S(1)}, u32[]{:S(2)}, u32[]{:S(2)}) %collective-permute-start.14) | collective-permute-done | bytes 65568 | tf_op jit(solution)/shard_map/ppermute | solution.py:17
  49.0 1.5 %collective-permute-start.15 = (bf16[128,128]{1,0:T(8,128)(2,1)S(1)}, bf16[128,128]{1,0:T(8,128)(2,1)S(1)}, u32[]{:S(2)}, u32[]{:S(2)}) collective-permute-start(bf16[128,128]{1,0:T(8,128)(2,1)S(1)} %fusion.4), channel_id=1, source_target_pairs={{0,8},{4,12},{8,0},{12,4},{1,9},{5,13},{9,1},{13,5},{2,10},{6,14},... | collective-permute-start | bytes 98312 | tf_op jit(solution)/shard_map/ppermute | solution.py:17
  50.5 1.8 %collective-permute-done.19 = bf16[128,128]{1,0:T(8,128)(2,1)S(1)} collective-permute-done((bf16[128,128]{1,0:T(8,128)(2,1)S(1)}, bf16[128,128]{1,0:T(8,128)(2,1)S(1)}, u32[]{:S(2)}, u32[]{:S(2)}) %collective-permute-start.19) | collective-permute-done | bytes 32800 | tf_op jit(solution)/shard_map/ppermute | solution.py:17
  52.3 2.0 %collective-permute-done.15 = bf16[128,128]{1,0:T(8,128)(2,1)S(1)} collective-permute-done((bf16[128,128]{1,0:T(8,128)(2,1)S(1)}, bf16[128,128]{1,0:T(8,128)(2,1)S(1)}, u32[]{:S(2)}, u32[]{:S(2)}) %collective-permute-start.15) | collective-permute-done | bytes 32800 | tf_op jit(solution)/shard_map/ppermute | solution.py:17
  54.4 3.3 %collective-permute-done.20.got_ref = bf16[2,64,128]{2,1,0:T(8,128)(2,1)S(1)} collective-permute-done((bf16[2,64,128]{2,1,0:T(8,128)(2,1)S(1)}, bf16[2,64,128]{2,1,0:T(8,128)(2,1)S(1)}, u32[]{:S(2)}, u32[]{:S(2)}) %collective-permute-start.20) | collective-permute-done | bytes 32800 | tf_op jit(solution)/shard_map/ppermute | solution.py:352
  57.7 0.7 %join.1 = f32[256,128]{1,0:T(8,128)} custom-call(f32[128,128]{1,0:T(8,128)S(1)} %bitcast_add_fusion.5.first_ref, f32[128,128]{1,0:T(8,128)S(1)} %bitcast_add_fusion.4.second_ref, bf16[2,64,128]{2,1,0:T(8,128)(2,1)S(1)} %collective-permute-done.20.got_ref), custom_call_target="tpu_custom_call" | custom-call | tf_op jit(solution)/shard_map/join/pallas_call | solution.py:353
  (49 shorter events, 1.7 us)
Async XLA Ops:
  0.0 13.2 %copy-start = (bf16[1,1,160,512]{3,2,1,0:T(8,128)(2,1)S(1)}, bf16[1,1,160,512]{3,2,1,0:T(8,128)(2,1)}, u32[]{:S(2)}) copy-start(bf16[1,1,160,512]{3,2,1,0:T(8,128)(2,1)} %param.13) | copy-start | bytes 491524
  0.0 16.4 %copy-start.1 = (bf16[1,1,160,512]{3,2,1,0:T(8,128)(2,1)S(1)}, bf16[1,1,160,512]{3,2,1,0:T(8,128)(2,1)}, u32[]{:S(2)}) copy-start(bf16[1,1,160,512]{3,2,1,0:T(8,128)(2,1)} %param.7) | copy-start | bytes 491524
  0.0 13.1 %collective-permute-start.9 = (bf16[128,1536]{1,0:T(8,128)(2,1)}, bf16[128,1536]{1,0:T(8,128)(2,1)S(1)}, u32[]{:S(2)}, u32[]{:S(2)}) collective-permute-start(bf16[128,1536]{1,0:T(8,128)(2,1)} %refs_0_.1), channel_id=1, source_target_pairs={{0,2},{1,3},{2,0},{3,1},{4,6},{5,7},{6,4},{7,5},{8,10},{9,11},{10,... | collective-permute-start | bytes 1179656 | tf_op jit(solution)/shard_map/ppermute | solution.py:17
  3.0 13.4 %collective-permute-start = (bf16[160,512]{1,0:T(8,128)(2,1)}, bf16[160,512]{1,0:T(8,128)(2,1)S(1)}, u32[]{:S(2)}, u32[]{:S(2)}) collective-permute-start(bf16[160,512]{1,0:T(8,128)(2,1)} %bitcast.37), channel_id=1, source_target_pairs={{0,16},{16,0},{1,17},{17,1},{2,18},{18,2},{3,19},{19,3},{4,20},{20... | collective-permute-start | bytes 491528 | tf_op jit(solution)/shard_map/ppermute | solution.py:17
  4.5 15.7 %collective-permute-start.4 = (bf16[128,512]{1,0:T(8,128)(2,1)}, bf16[128,512]{1,0:T(8,128)(2,1)S(1)}, u32[]{:S(2)}, u32[]{:S(2)}) collective-permute-start(bf16[128,512]{1,0:T(8,128)(2,1)} %param.12), channel_id=1, source_target_pairs={{0,2},{1,3},{2,0},{3,1},{4,6},{5,7},{6,4},{7,5},{8,10},{9,11},{10,... | collective-permute-start | bytes 393224 | tf_op jit(solution)/shard_map/ppermute | solution.py:17
  5.0 21.1 %collective-permute-start.10 = (bf16[128,1536]{1,0:T(8,128)(2,1)}, bf16[128,1536]{1,0:T(8,128)(2,1)S(1)}, u32[]{:S(2)}, u32[]{:S(2)}) collective-permute-start(bf16[128,1536]{1,0:T(8,128)(2,1)} %refs_0_.1), channel_id=1, source_target_pairs={{0,1},{1,0},{2,3},{3,2},{4,5},{5,4},{6,7},{7,6},{8,9},{9,8},{10,11... | collective-permute-start | bytes 1179656 | tf_op jit(solution)/shard_map/ppermute | solution.py:17
  13.1 13.1 %collective-permute-start.11 = (bf16[128,1536]{1,0:T(8,128)(2,1)S(1)}, bf16[128,1536]{1,0:T(8,128)(2,1)S(1)}, u32[]{:S(2)}, u32[]{:S(2)}) collective-permute-start(bf16[128,1536]{1,0:T(8,128)(2,1)S(1)} %collective-permute-done.9.refs_1_), channel_id=1, source_target_pairs={{0,1},{1,0},{2,3},{3,2},{4,5},{5,4},{6,7},{7,6},{8,9},{9,8},{10,11... | collective-permute-start | bytes 1179656 | tf_op jit(solution)/shard_map/ppermute | solution.py:17
  13.2 3.2 %copy-start.3 = (f32[9,512]{1,0:T(8,128)S(1)}, f32[9,512]{1,0:T(8,128)}, u32[]{:S(2)}) copy-start(f32[9,512]{1,0:T(8,128)} %taps_ref.3) | copy-start | bytes 55300
  13.2 8.0 %collective-permute-start.2 = (bf16[80,512]{1,0:T(8,128)(2,1)S(1)}, bf16[80,512]{1,0:T(8,128)(2,1)S(1)}, u32[]{:S(2)}, u32[]{:S(2)}) collective-permute-start(bf16[80,512]{1,0:T(8,128)(2,1)S(1)} %dynamic-slice_bitcast_fusion), channel_id=1, source_target_pairs={{0,8},{4,12},{8,0},{12,4},{1,9},{5,13},{9,1},{13,5},{2,10},{6,14},... | collective-permute-start | bytes 245768 | tf_op jit(solution)/shard_map/ppermute | solution.py:17
  16.4 0.7 %copy-start.4 = (s32[160,8]{0,1:T(8,128)S(1)}, s32[160,8]{0,1:T(8,128)}, u32[]{:S(2)}) copy-start(s32[160,8]{0,1:T(8,128)} %param.8) | copy-start | bytes 15364
  17.1 0.7 %copy-start.5 = (f32[512]{0:T(512)S(1)}, f32[512]{0:T(512)}, u32[]{:S(2)}) copy-start(f32[512]{0:T(512)} %param.10) | copy-start | bytes 6148
  17.7 2.4 %copy-start.6 = (bf16[128,512]{1,0:T(8,128)(2,1)S(1)}, bf16[128,512]{1,0:T(8,128)(2,1)}, u32[]{:S(2)}) copy-start(bf16[128,512]{1,0:T(8,128)(2,1)} %param.12) | copy-start | bytes 393220
  18.5 4.6 %collective-permute-start.6 = (bf16[80,512]{1,0:T(8,128)(2,1)S(1)}, bf16[80,512]{1,0:T(8,128)(2,1)S(1)}, u32[]{:S(2)}, u32[]{:S(2)}) collective-permute-start(bf16[80,512]{1,0:T(8,128)(2,1)S(1)} %conv_near.1.own_ref), channel_id=1, source_target_pairs={{0,4},{4,0},{8,12},{12,8},{1,5},{5,1},{9,13},{13,9},{2,6},{6,2},{1... | collective-permute-start | bytes 245768 | tf_op jit(solution)/shard_map/ppermute | solution.py:17
  20.2 8.1 %copy-start.2 = (bf16[128,1536]{1,0:T(8,128)(2,1)S(1)}, bf16[128,1536]{1,0:T(8,128)(2,1)}, u32[]{:S(2)}) copy-start(bf16[128,1536]{1,0:T(8,128)(2,1)} %refs_0_.1) | copy-start | bytes 1179652
  20.2 13.7 %collective-permute-start.5 = (bf16[128,512]{1,0:T(8,128)(2,1)S(1)}, bf16[128,512]{1,0:T(8,128)(2,1)S(1)}, u32[]{:S(2)}, u32[]{:S(2)}) collective-permute-start(bf16[128,512]{1,0:T(8,128)(2,1)S(1)} %broadcast_select_fusion.refs_4_), channel_id=1, source_target_pairs={{0,1},{1,0},{2,3},{3,2},{4,5},{5,4},{6,7},{7,6},{8,9},{9,8},{10,11... | collective-permute-start | bytes 393224 | tf_op jit(solution)/shard_map/ppermute | solution.py:17
  21.2 9.8 %collective-permute-start.7 = (bf16[80,512]{1,0:T(8,128)(2,1)S(1)}, bf16[80,512]{1,0:T(8,128)(2,1)S(1)}, u32[]{:S(2)}, u32[]{:S(2)}) collective-permute-start(bf16[80,512]{1,0:T(8,128)(2,1)S(1)} %conv_far.1), channel_id=1, source_target_pairs={{0,8},{4,12},{8,0},{12,4},{1,9},{5,13},{9,1},{13,5},{2,10},{6,14},... | collective-permute-start | bytes 245768 | tf_op jit(solution)/shard_map/ppermute | solution.py:17
  23.1 7.9 %collective-permute-start.8 = (bf16[80,512]{1,0:T(8,128)(2,1)S(1)}, bf16[80,512]{1,0:T(8,128)(2,1)S(1)}, u32[]{:S(2)}, u32[]{:S(2)}) collective-permute-start(bf16[80,512]{1,0:T(8,128)(2,1)S(1)} %conv_far.1), channel_id=1, source_target_pairs={{0,12},{4,8},{8,4},{12,0},{1,13},{5,9},{9,5},{13,1},{2,14},{6,10},... | collective-permute-start | bytes 245768 | tf_op jit(solution)/shard_map/ppermute | solution.py:17
  26.2 6.1 %collective-permute-start.3 = (bf16[80,512]{1,0:T(8,128)(2,1)S(1)}, bf16[80,512]{1,0:T(8,128)(2,1)S(1)}, u32[]{:S(2)}, u32[]{:S(2)}) collective-permute-start(bf16[80,512]{1,0:T(8,128)(2,1)S(1)} %collective-permute-done.2.refs_2_), channel_id=1, source_target_pairs={{0,4},{4,0},{8,12},{12,8},{1,5},{5,1},{9,13},{13,9},{2,6},{6,2},{1... | collective-permute-start | bytes 245768 | tf_op jit(solution)/shard_map/ppermute | solution.py:17
  26.3 7.6 %collective-permute-start.1 = (bf16[80,512]{1,0:T(8,128)(2,1)S(1)}, bf16[80,512]{1,0:T(8,128)(2,1)S(1)}, u32[]{:S(2)}, u32[]{:S(2)}) collective-permute-start(bf16[80,512]{1,0:T(8,128)(2,1)S(1)} %dynamic-slice_bitcast_fusion.1.refs_0_), channel_id=1, source_target_pairs={{0,4},{4,0},{8,12},{12,8},{1,5},{5,1},{9,13},{13,9},{2,6},{6,2},{1... | collective-permute-start | bytes 245768 | tf_op jit(solution)/shard_map/ppermute | solution.py:17
  35.7 1.6 %collective-permute-start.16 = (bf16[2,2,2,128,128]{4,3,2,1,0:T(8,128)(2,1)S(1)}, bf16[2,2,2,128,128]{4,3,2,1,0:T(8,128)(2,1)S(1)}, u32[]{:S(2)}, u32[]{:S(2)}) collective-permute-start(bf16[2,2,2,128,128]{4,3,2,1,0:T(8,128)(2,1)S(1)} %get-tuple-element.26), channel_id=1, source_target_pairs={{0,1},{1,0},{2,3},{3,2},{4,5},{5,4},{6,7},{7,6},{8,9},{9,8},{10,11... | collective-permute-start | bytes 786440 | tf_op jit(solution)/shard_map/ppermute | solution.py:17
  35.7 3.2 %collective-permute-start.12 = (bf16[2,2,2,128,128]{4,3,2,1,0:T(8,128)(2,1)S(1)}, bf16[2,2,2,128,128]{4,3,2,1,0:T(8,128)(2,1)S(1)}, u32[]{:S(2)}, u32[]{:S(2)}) collective-permute-start(bf16[2,2,2,128,128]{4,3,2,1,0:T(8,128)(2,1)S(1)} %get-tuple-element.24), channel_id=1, source_target_pairs={{0,1},{1,0},{2,3},{3,2},{4,5},{5,4},{6,7},{7,6},{8,9},{9,8},{10,11... | collective-permute-start | bytes 786440 | tf_op jit(solution)/shard_map/ppermute | solution.py:17
  37.3 5.6 %collective-permute-start.17 = (bf16[2,2,128,128]{3,2,1,0:T(8,128)(2,1)S(1)}, bf16[2,2,128,128]{3,2,1,0:T(8,128)(2,1)S(1)}, u32[]{:S(2)}, u32[]{:S(2)}) collective-permute-start(bf16[2,2,128,128]{3,2,1,0:T(8,128)(2,1)S(1)} %fusion.1), channel_id=1, source_target_pairs={{0,16},{16,0},{1,17},{17,1},{2,18},{18,2},{3,19},{19,3},{4,20},{20... | collective-permute-start | bytes 393224 | tf_op jit(solution)/shard_map/ppermute | solution.py:17
  39.0 5.5 %collective-permute-start.13 = (bf16[2,2,128,128]{3,2,1,0:T(8,128)(2,1)S(1)}, bf16[2,2,128,128]{3,2,1,0:T(8,128)(2,1)S(1)}, u32[]{:S(2)}, u32[]{:S(2)}) collective-permute-start(bf16[2,2,128,128]{3,2,1,0:T(8,128)(2,1)S(1)} %fusion), channel_id=1, source_target_pairs={{0,2},{1,3},{2,0},{3,1},{4,6},{5,7},{6,4},{7,5},{8,10},{9,11},{10,... | collective-permute-start | bytes 393224 | tf_op jit(solution)/shard_map/ppermute | solution.py:17
  43.0 4.3 %collective-permute-start.18 = (bf16[2,128,128]{2,1,0:T(8,128)(2,1)S(1)}, bf16[2,128,128]{2,1,0:T(8,128)(2,1)S(1)}, u32[]{:S(2)}, u32[]{:S(2)}) collective-permute-start(bf16[2,128,128]{2,1,0:T(8,128)(2,1)S(1)} %fusion.3), channel_id=1, source_target_pairs={{0,2},{1,3},{2,0},{3,1},{4,6},{5,7},{6,4},{7,5},{8,10},{9,11},{10,... | collective-permute-start | bytes 196616 | tf_op jit(solution)/shard_map/ppermute | solution.py:17
  44.6 4.3 %collective-permute-start.14 = (bf16[2,128,128]{2,1,0:T(8,128)(2,1)S(1)}, bf16[2,128,128]{2,1,0:T(8,128)(2,1)S(1)}, u32[]{:S(2)}, u32[]{:S(2)}) collective-permute-start(bf16[2,128,128]{2,1,0:T(8,128)(2,1)S(1)} %fusion.2), channel_id=1, source_target_pairs={{0,16},{16,0},{1,17},{17,1},{2,18},{18,2},{3,19},{19,3},{4,20},{20... | collective-permute-start | bytes 196616 | tf_op jit(solution)/shard_map/ppermute | solution.py:17
  47.4 4.9 %collective-permute-start.19 = (bf16[128,128]{1,0:T(8,128)(2,1)S(1)}, bf16[128,128]{1,0:T(8,128)(2,1)S(1)}, u32[]{:S(2)}, u32[]{:S(2)}) collective-permute-start(bf16[128,128]{1,0:T(8,128)(2,1)S(1)} %fusion.5), channel_id=1, source_target_pairs={{0,8},{4,12},{8,0},{12,4},{1,9},{5,13},{9,1},{13,5},{2,10},{6,14},... | collective-permute-start | bytes 98312 | tf_op jit(solution)/shard_map/ppermute | solution.py:17
  49.0 5.2 %collective-permute-start.15 = (bf16[128,128]{1,0:T(8,128)(2,1)S(1)}, bf16[128,128]{1,0:T(8,128)(2,1)S(1)}, u32[]{:S(2)}, u32[]{:S(2)}) collective-permute-start(bf16[128,128]{1,0:T(8,128)(2,1)S(1)} %fusion.4), channel_id=1, source_target_pairs={{0,8},{4,12},{8,0},{12,4},{1,9},{5,13},{9,1},{13,5},{2,10},{6,14},... | collective-permute-start | bytes 98312 | tf_op jit(solution)/shard_map/ppermute | solution.py:17
  54.3 3.4 %collective-permute-start.20 = (bf16[2,64,128]{2,1,0:T(8,128)(2,1)S(1)}, bf16[2,64,128]{2,1,0:T(8,128)(2,1)S(1)}, u32[]{:S(2)}, u32[]{:S(2)}) collective-permute-start(bf16[2,64,128]{2,1,0:T(8,128)(2,1)S(1)} %pad_maximum_fusion), channel_id=1, source_target_pairs={{0,5},{1,4},{2,7},{3,6},{4,1},{5,0},{6,3},{7,2},{8,13},{9,12},{10,... | collective-permute-start | bytes 98312 | tf_op jit(solution)/shard_map/ppermute | solution.py:352

commit v9 on v8

--- a/solution.py
+++ b/solution.py
@@ -12,9 +12,19 @@
 HALO = 130
 VMEM = pltpu.MemorySpace.VMEM
 
+CROSSED = (1, 1, 1, 1)
+
 
 def swap(values, axis, mask):
     return lax.ppermute(values, axis, [(i, i ^ mask) for i in range(lax.axis_size(axis))])
+
+
+def hop(values, axis, mask, crossed):
+    cores = lax.axis_size("fsdp")
+    if axis == "fsdp":
+        return swap(values, axis, mask ^ crossed)
+    pairs = [(i, i ^ mask * cores ^ crossed) for i in range(lax.axis_size(axis) * cores)]
+    return lax.ppermute(values, (axis, "fsdp"), pairs)
 
 
 def pick(values, index, dim=0):
@@ -155,7 +165,7 @@
     piece_refs, out_refs, refs = refs[:4], refs[4:6], refs[6:]
     n_ref, qkv_ref, weights_ref, attended_ref, refs = *refs[:4], refs[4:]
     keep_refs, send_refs, (u_ref, g_ref, sums_ref, out_sums_ref) = refs[:2], refs[2:4], refs[4:]
-    _, t, _, zh, _, core = place()
+    y, t, zp, zh, x, core = place()
     _, pixels, channels = n_ref.shape
     width = out_sums_ref.shape[0]
     first, second = out_refs[0][...], out_refs[1][...]
@@ -219,16 +229,22 @@
     for slot in range(8):
         at_x, at_y, at_zp = slot >> 2, (slot >> 1) & 1, slot & 1
         places = ((at_x, at_y, at_zp), (at_y, at_x, at_zp))
+        first_flip, second_flip, z_flip = x ^ at_x, y ^ at_y, zp ^ at_zp
+        flips = [
+            CROSSED[0] * pair[0] ^ CROSSED[1] * pair[1] ^ CROSSED[2] * z_flip
+            for pair in ((first_flip, second_flip), (second_flip, first_flip))
+        ]
         for side, path_refs in ((1 - core, send_refs), (core, keep_refs)):
             for low in range(2):
                 rows_at = slice(low * block, (low + 1) * block)
                 first = at_y * 16 + (2 * at_zp + low) * 4 + 2 * at_x
                 for path, ref in enumerate(path_refs):
                     if first < 3 * HEADS:
-                        start = pl.multiple_of((first + (side ^ zh ^ low)) * block, block)
+                        owner = side ^ flips[path] ^ CROSSED[3] * (zh ^ low)
+                        start = pl.multiple_of((first + owner) * block, block)
                         piece = sums_ref[path, pl.ds(start, block), :]
                     else:
-                        start = pl.multiple_of((2 * at_x + side) * block, block)
+                        start = pl.multiple_of((2 * at_x + (side ^ flips[path])) * block, block)
                         lanes_at = low * width + path * 128
                         piece = out_sums_ref[pl.ds(start, block), lanes_at : lanes_at + 128]
                     ref[(*places[path], rows_at)] = piece.astype(ref.dtype)
@@ -341,15 +357,13 @@
     for stage in range(2):
         for path in range(2):
             axis, mask, index = hops[path ^ stage]
-            got = swap(narrow(pick(paths[path], 1 - index)), axis, mask)
+            got = hop(narrow(pick(paths[path], 1 - index)), axis, mask, CROSSED[stage])
             paths[path] = pick(paths[path], index) + got.astype(jnp.float32)
     for path in range(2):
-        got = swap(narrow(pick(paths[path], 1 - zp)), "tm", 2)
+        got = hop(narrow(pick(paths[path], 1 - zp)), "tm", 2, CROSSED[2])
         paths[path] = pick(paths[path], zp) + got.astype(jnp.float32)
     far = jnp.stack([narrow(pick(total.reshape(2, block, 128), 1 - zh)) for total in paths])
-    cores = lax.axis_size("fsdp")
-    crossed = [(i, i ^ cores ^ 1) for i in range(lax.axis_size("tm") * cores)]
-    got = lax.ppermute(far, ("tm", "fsdp"), crossed)
+    got = hop(far, "tm", 1, CROSSED[3])
     out = pl.pallas_call(
         join_kernel,
         out_shape=jax.ShapeDtypeStruct((block * channels // 128, 128), jnp.float32),

time: 58.6 us -> 58.2 us (level)
  starting transfers between devices: 24.5 us -> 23.2 us
  waiting for transfers between devices: 26.5 us -> 27.4 us
    ppermute x1 -> x5, waiting for transfers between devices: 3.33 us -> 12.1 us  [hop(): return lax.ppermute(values, (axis, 'fsdp'), pairs)]
    ppermute x20 -> x16, waiting for transfers between devices: 23.2 us -> 15.4 us  [swap(): lax.ppermute(values, axis, [(i, i ^ mask) for i in range(lax.axis_size(ax...]
    ppermute x20 -> x16, starting transfers between devices: 24.4 us -> 19.7 us  [swap(): lax.ppermute(values, axis, [(i, i ^ mask) for i in range(lax.axis_size(ax...]
    ppermute x1 -> x5, starting transfers between devices: 0.07 us -> 3.54 us  [hop(): return lax.ppermute(values, (axis, 'fsdp'), pairs)]
where the time goes in v9:
time: 58.2 us; the launch traced here: 58 us
  waiting for transfers between devices  27.4 us (47%)
  starting transfers between devices  23.2 us (40%)
  Pallas kernels  5.3 us (9%)
  local copies, waits for them, and re-layouts  1.55 us (3%)
    ppermute x16, starting transfers between devices, swap(): lax.ppermute(values, axis, [(i, i ^ mask) for i in range(lax.axis_size(ax...  19.7 us
    ppermute x16, waiting for transfers between devices, swap(): lax.ppermute(values, axis, [(i, i ^ mask) for i in range(lax.axis_size(ax...  15.4 us
    ppermute x5, waiting for transfers between devices, hop(): return lax.ppermute(values, (axis, 'fsdp'), pairs)  12.1 us
    ppermute x5, starting transfers between devices, hop(): return lax.ppermute(values, (axis, 'fsdp'), pairs)  3.54 us
    pallas_call x1, Pallas kernels, split_form(): pl.pallas_call(backward_kernel, out_shape=(*(jax.ShapeDtypeStruct((2, 2,...  1.67 us
    pallas_call x2, Pallas kernels, conv(): pl.pallas_call(functools.partial(conv_kernel, far), out_shape=piece, in_s...  1.54 us
    unnamed x14, local copies, waits for them, and re-layouts  1.39 us
  transfers between devices with their start and end apart: 21, of which 13 were waited for; matrix products, arithmetic and copies ran while one was open for 1% of the time, Pallas kernels for 5%

profile of v9, /device:TPU:0, one launch (start us, length us, event | category | flops | bytes accessed | tf_op | source)
XLA Modules:
  0.0 58.0 jit_solution(18246786100654887572)
XLA Ops:
  0.0 3.0 %collective-permute-start.9 = (bf16[128,1536]{1,0:T(8,128)(2,1)}, bf16[128,1536]{1,0:T(8,128)(2,1)S(1)}, u32[]{:S(2)}, u32[]{:S(2)}) collective-permute-start(bf16[128,1536]{1,0:T(8,128)(2,1)} %refs_0_.1), channel_id=1, source_target_pairs={{0,2},{1,3},{2,0},{3,1},{4,6},{5,7},{6,4},{7,5},{8,10},{9,11},{10,... | collective-permute-start | bytes 1179656 | tf_op jit(solution)/shard_map/ppermute | solution.py:19
  3.0 1.5 %collective-permute-start = (bf16[160,512]{1,0:T(8,128)(2,1)}, bf16[160,512]{1,0:T(8,128)(2,1)S(1)}, u32[]{:S(2)}, u32[]{:S(2)}) collective-permute-start(bf16[160,512]{1,0:T(8,128)(2,1)} %bitcast.37), channel_id=1, source_target_pairs={{0,16},{16,0},{1,17},{17,1},{2,18},{18,2},{3,19},{19,3},{4,20},{20... | collective-permute-start | bytes 491528 | tf_op jit(solution)/shard_map/ppermute | solution.py:19
  4.5 0.5 collective-permute-start.4
  5.0 8.1 %collective-permute-done.9.refs_1_ = bf16[128,1536]{1,0:T(8,128)(2,1)S(1)} collective-permute-done((bf16[128,1536]{1,0:T(8,128)(2,1)}, bf16[128,1536]{1,0:T(8,128)(2,1)S(1)}, u32[]{:S(2)}, u32[]{:S(2)}) %collective-permute-start.9) | collective-permute-done | bytes 393248 | tf_op jit(solution)/shard_map/ppermute | solution.py:19
  13.2 3.2 %collective-permute-start.2 = (bf16[80,512]{1,0:T(8,128)(2,1)S(1)}, bf16[80,512]{1,0:T(8,128)(2,1)S(1)}, u32[]{:S(2)}, u32[]{:S(2)}) collective-permute-start(bf16[80,512]{1,0:T(8,128)(2,1)S(1)} %dynamic-slice_bitcast_fusion), channel_id=1, source_target_pairs={{0,8},{4,12},{8,0},{12,4},{1,9},{5,13},{9,1},{13,5},{2,10},{6,14},... | collective-permute-start | bytes 245768 | tf_op jit(solution)/shard_map/ppermute | solution.py:19
  16.4 0.7 %copy-done.4 = s32[160,8]{0,1:T(8,128)S(1)} copy-done((s32[160,8]{0,1:T(8,128)S(1)}, s32[160,8]{0,1:T(8,128)}, u32[]{:S(2)}) %copy-start.4) | copy-done | bytes 5144
  17.1 0.7 %copy-done.5 = f32[512]{0:T(512)S(1)} copy-done((f32[512]{0:T(512)S(1)}, f32[512]{0:T(512)}, u32[]{:S(2)}) %copy-start.5) | copy-done | bytes 2072
  17.7 0.8 %conv_near.1.own_ref = bf16[80,512]{1,0:T(8,128)(2,1)S(1)} custom-call(s32[8,160]{1,0:T(8,128)S(1)} %bitcast.42, bf16[160,512]{1,0:T(8,128)(2,1)S(1)} %bitcast.38, bf16[160,512]{1,0:T(8,128)(2,1)S(1)} %collective-permute-done.band_ref, f32[9,512]{1,0:T(8,128)S(1)} %copy-done.3, f32[1,512]{1,0:T(1,128)S(1)} %bitcast.44), custom_call_target="tpu_custom_call" | custom-call | tf_op jit(solution)/shard_map/conv_near/pallas_call | solution.py:282
  18.5 1.6 %collective-permute-start.6 = (bf16[80,512]{1,0:T(8,128)(2,1)S(1)}, bf16[80,512]{1,0:T(8,128)(2,1)S(1)}, u32[]{:S(2)}, u32[]{:S(2)}) collective-permute-start(bf16[80,512]{1,0:T(8,128)(2,1)S(1)} %conv_near.1.own_ref), channel_id=1, source_target_pairs={{0,4},{4,0},{8,12},{12,8},{1,5},{5,1},{9,13},{13,9},{2,6},{6,2},{1... | collective-permute-start | bytes 245768 | tf_op jit(solution)/shard_map/ppermute | solution.py:19
  20.3 0.8 %conv_far.1 = bf16[80,512]{1,0:T(8,128)(2,1)S(1)} custom-call(s32[8,160]{1,0:T(8,128)S(1)} %bitcast.43, bf16[160,512]{1,0:T(8,128)(2,1)S(1)} %bitcast.39, bf16[160,512]{1,0:T(8,128)(2,1)S(1)} %collective-permute-done.band_ref, f32[9,512]{1,0:T(8,128)S(1)} %copy-done.3, f32[1,512]{1,0:T(1,128)S(1)} %bitcast.45), custom_call_target="tpu_custom_call" | custom-call | tf_op jit(solution)/shard_map/conv_far/pallas_call | solution.py:282
  21.2 1.0 %collective-permute-start.7 = (bf16[80,512]{1,0:T(8,128)(2,1)S(1)}, bf16[80,512]{1,0:T(8,128)(2,1)S(1)}, u32[]{:S(2)}, u32[]{:S(2)}) collective-permute-start(bf16[80,512]{1,0:T(8,128)(2,1)S(1)} %conv_far.1), channel_id=1, source_target_pairs={{0,8},{4,12},{8,0},{12,4},{1,9},{5,13},{9,1},{13,5},{2,10},{6,14},... | collective-permute-start | bytes 245768 | tf_op jit(solution)/shard_map/ppermute | solution.py:19
  22.2 0.9 %collective-permute-done.6.row_1_ref = bf16[80,512]{1,0:T(8,128)(2,1)S(1)} collective-permute-done((bf16[80,512]{1,0:T(8,128)(2,1)S(1)}, bf16[80,512]{1,0:T(8,128)(2,1)S(1)}, u32[]{:S(2)}, u32[]{:S(2)}) %collective-permute-start.6) | collective-permute-done | bytes 81952 | tf_op jit(solution)/shard_map/ppermute | solution.py:19
  23.1 3.0 %collective-permute-start.8 = (bf16[80,512]{1,0:T(8,128)(2,1)S(1)}, bf16[80,512]{1,0:T(8,128)(2,1)S(1)}, u32[]{:S(2)}, u32[]{:S(2)}) collective-permute-start(bf16[80,512]{1,0:T(8,128)(2,1)S(1)} %conv_far.1), channel_id=1, source_target_pairs={{0,12},{4,8},{8,4},{12,0},{1,13},{5,9},{9,5},{13,1},{2,14},{6,10},... | collective-permute-start | bytes 245768 | tf_op jit(solution)/shard_map/ppermute | solution.py:19
  26.3 2.0 %collective-permute-start.1 = (bf16[80,512]{1,0:T(8,128)(2,1)S(1)}, bf16[80,512]{1,0:T(8,128)(2,1)S(1)}, u32[]{:S(2)}, u32[]{:S(2)}) collective-permute-start(bf16[80,512]{1,0:T(8,128)(2,1)S(1)} %dynamic-slice_bitcast_fusion.1.refs_0_), channel_id=1, source_target_pairs={{0,4},{4,0},{8,12},{12,8},{1,5},{5,1},{9,13},{13,9},{2,6},{6,2},{1... | collective-permute-start | bytes 245768 | tf_op jit(solution)/shard_map/ppermute | solution.py:19
  28.7 2.2 %collective-permute-done.7.row_2_ref = bf16[80,512]{1,0:T(8,128)(2,1)S(1)} collective-permute-done((bf16[80,512]{1,0:T(8,128)(2,1)S(1)}, bf16[80,512]{1,0:T(8,128)(2,1)S(1)}, u32[]{:S(2)}, u32[]{:S(2)}) %collective-permute-start.7) | collective-permute-done | bytes 81952 | tf_op jit(solution)/shard_map/ppermute | solution.py:19
  31.0 1.0 %forward.1 = (bf16[320,768]{1,0:T(8,128)(2,1)S(1)}, bf16[10,80,256]{2,1,0:T(8,128)(2,1)S(1)}, bf16[320,256]{1,0:T(8,128)(2,1)S(1)}, bf16[4,80,512]{2,1,0:T(8,128)(2,1)S(1)}) custom-call(bf16[80,512]{1,0:T(8,128)(2,1)S(1)} %conv_near.1.own_ref, bf16[80,512]{1,0:T(8,128)(2,1)S(1)} %collective-permute-done.6.row_1_ref, ...), custom_call_target="tpu_custom_call" | custom-call | tf_op jit(solution)/shard_map/forward/pallas_call | solution.py:318
  32.3 1.6 %collective-permute-done.1.refs_1_ = bf16[80,512]{1,0:T(8,128)(2,1)S(1)} collective-permute-done((bf16[80,512]{1,0:T(8,128)(2,1)S(1)}, bf16[80,512]{1,0:T(8,128)(2,1)S(1)}, u32[]{:S(2)}, u32[]{:S(2)}) %collective-permute-start.1) | collective-permute-done | bytes 81952 | tf_op jit(solution)/shard_map/ppermute | solution.py:19
  33.9 1.7 %backward.1 = (f32[2,2,2,128,128]{4,3,2,1,0:T(8,128)S(1)}, f32[2,2,2,128,128]{4,3,2,1,0:T(8,128)S(1)}, bf16[2,2,2,128,128]{4,3,2,1,0:T(8,128)(2,1)S(1)}, bf16[2,2,2,128,128]{4,3,2,1,0:T(8,128)(2,1)S(1)}) custom-call(bf16[80,512]{1,0:T(8,128)(2,1)S(1)} %dynamic-slice_bitcast_fusion.1.refs_0_, bf16[80,512]{1,0:T(8,128)(2,1)S(1)} %collective-permute-done.1.refs_1_, ...), custom_call_target="tpu_custom_call" | custom-call | tf_op jit(solution)/shard_map/backward/pallas_call | solution.py:331
  35.7 0.5 collective-permute-start.12
  36.2 1.0 %collective-permute-done.16 = bf16[2,2,2,128,128]{4,3,2,1,0:T(8,128)(2,1)S(1)} collective-permute-done((bf16[2,2,2,128,128]{4,3,2,1,0:T(8,128)(2,1)S(1)}, bf16[2,2,2,128,128]{4,3,2,1,0:T(8,128)(2,1)S(1)}, u32[]{:S(2)}, u32[]{:S(2)}) %collective-permute-start.16) | collective-permute-done | bytes 262176 | tf_op jit(solution)/shard_map/ppermute | solution.py:19
  37.3 1.3 %collective-permute-start.17 = (bf16[2,2,128,128]{3,2,1,0:T(8,128)(2,1)S(1)}, bf16[2,2,128,128]{3,2,1,0:T(8,128)(2,1)S(1)}, u32[]{:S(2)}, u32[]{:S(2)}) collective-permute-start(bf16[2,2,128,128]{3,2,1,0:T(8,128)(2,1)S(1)} %fusion.1), channel_id=1, source_target_pairs={{0,17},{1,16},{2,19},{3,18},{16,1},{17,0},{18,3},{19,2},{4,21},{5,... | collective-permute-start | bytes 393224 | tf_op jit(solution)/shard_map/ppermute | solution.py:27
  38.7 1.5 %collective-permute-start.13 = (bf16[2,2,128,128]{3,2,1,0:T(8,128)(2,1)S(1)}, bf16[2,2,128,128]{3,2,1,0:T(8,128)(2,1)S(1)}, u32[]{:S(2)}, u32[]{:S(2)}) collective-permute-start(bf16[2,2,128,128]{3,2,1,0:T(8,128)(2,1)S(1)} %fusion), channel_id=1, source_target_pairs={{0,3},{1,2},{2,1},{3,0},{4,7},{5,6},{6,5},{7,4},{8,11},{9,10},{10,... | collective-permute-start | bytes 393224 | tf_op jit(solution)/shard_map/ppermute | solution.py:19
  40.2 2.6 %collective-permute-done.17 = bf16[2,2,128,128]{3,2,1,0:T(8,128)(2,1)S(1)} collective-permute-done((bf16[2,2,128,128]{3,2,1,0:T(8,128)(2,1)S(1)}, bf16[2,2,128,128]{3,2,1,0:T(8,128)(2,1)S(1)}, u32[]{:S(2)}, u32[]{:S(2)}) %collective-permute-start.17) | collective-permute-done | bytes 131104 | tf_op jit(solution)/shard_map/ppermute | solution.py:27
  42.9 1.6 %collective-permute-start.18 = (bf16[2,128,128]{2,1,0:T(8,128)(2,1)S(1)}, bf16[2,128,128]{2,1,0:T(8,128)(2,1)S(1)}, u32[]{:S(2)}, u32[]{:S(2)}) collective-permute-start(bf16[2,128,128]{2,1,0:T(8,128)(2,1)S(1)} %fusion.3), channel_id=1, source_target_pairs={{0,3},{1,2},{2,1},{3,0},{4,7},{5,6},{6,5},{7,4},{8,11},{9,10},{10,... | collective-permute-start | bytes 196616 | tf_op jit(solution)/shard_map/ppermute | solution.py:19
  44.5 1.3 %collective-permute-start.14 = (bf16[2,128,128]{2,1,0:T(8,128)(2,1)S(1)}, bf16[2,128,128]{2,1,0:T(8,128)(2,1)S(1)}, u32[]{:S(2)}, u32[]{:S(2)}) collective-permute-start(bf16[2,128,128]{2,1,0:T(8,128)(2,1)S(1)} %fusion.2), channel_id=1, source_target_pairs={{0,17},{1,16},{2,19},{3,18},{16,1},{17,0},{18,3},{19,2},{4,21},{5,... | collective-permute-start | bytes 196616 | tf_op jit(solution)/shard_map/ppermute | solution.py:27
  45.8 0.9 %collective-permute-done.18 = bf16[2,128,128]{2,1,0:T(8,128)(2,1)S(1)} collective-permute-done((bf16[2,128,128]{2,1,0:T(8,128)(2,1)S(1)}, bf16[2,128,128]{2,1,0:T(8,128)(2,1)S(1)}, u32[]{:S(2)}, u32[]{:S(2)}) %collective-permute-start.18) | collective-permute-done | bytes 65568 | tf_op jit(solution)/shard_map/ppermute | solution.py:19
  46.8 1.9 %collective-permute-done.14 = bf16[2,128,128]{2,1,0:T(8,128)(2,1)S(1)} collective-permute-done((bf16[2,128,128]{2,1,0:T(8,128)(2,1)S(1)}, bf16[2,128,128]{2,1,0:T(8,128)(2,1)S(1)}, u32[]{:S(2)}, u32[]{:S(2)}) %collective-permute-start.14) | collective-permute-done | bytes 65568 | tf_op jit(solution)/shard_map/ppermute | solution.py:27
  48.8 0.8 %collective-permute-start.15 = (bf16[128,128]{1,0:T(8,128)(2,1)S(1)}, bf16[128,128]{1,0:T(8,128)(2,1)S(1)}, u32[]{:S(2)}, u32[]{:S(2)}) collective-permute-start(bf16[128,128]{1,0:T(8,128)(2,1)S(1)} %fusion.4), channel_id=1, source_target_pairs={{0,9},{1,8},{2,11},{3,10},{4,13},{5,12},{6,15},{7,14},{8,1},{9,0},... | collective-permute-start | bytes 98312 | tf_op jit(solution)/shard_map/ppermute | solution.py:27
  49.6 1.7 %collective-permute-done.19 = bf16[128,128]{1,0:T(8,128)(2,1)S(1)} collective-permute-done((bf16[128,128]{1,0:T(8,128)(2,1)S(1)}, bf16[128,128]{1,0:T(8,128)(2,1)S(1)}, u32[]{:S(2)}, u32[]{:S(2)}) %collective-permute-start.19) | collective-permute-done | bytes 32800 | tf_op jit(solution)/shard_map/ppermute | solution.py:27
  51.3 2.5 %collective-permute-done.15 = bf16[128,128]{1,0:T(8,128)(2,1)S(1)} collective-permute-done((bf16[128,128]{1,0:T(8,128)(2,1)S(1)}, bf16[128,128]{1,0:T(8,128)(2,1)S(1)}, u32[]{:S(2)}, u32[]{:S(2)}) %collective-permute-start.15) | collective-permute-done | bytes 32800 | tf_op jit(solution)/shard_map/ppermute | solution.py:27
  53.9 3.4 %collective-permute-done.20.got_ref = bf16[2,64,128]{2,1,0:T(8,128)(2,1)S(1)} collective-permute-done((bf16[2,64,128]{2,1,0:T(8,128)(2,1)S(1)}, bf16[2,64,128]{2,1,0:T(8,128)(2,1)S(1)}, u32[]{:S(2)}, u32[]{:S(2)}) %collective-permute-start.20) | collective-permute-done | bytes 32800 | tf_op jit(solution)/shard_map/ppermute | solution.py:27
  57.3 0.7 %join.1 = f32[256,128]{1,0:T(8,128)} custom-call(f32[128,128]{1,0:T(8,128)S(1)} %bitcast_add_fusion.5.first_ref, f32[128,128]{1,0:T(8,128)S(1)} %bitcast_add_fusion.4.second_ref, bf16[2,64,128]{2,1,0:T(8,128)(2,1)S(1)} %collective-permute-done.20.got_ref), custom_call_target="tpu_custom_call" | custom-call | tf_op jit(solution)/shard_map/join/pallas_call | solution.py:367
  (49 shorter events, 1.7 us)
Async XLA Ops:
  0.0 13.2 %copy-start = (bf16[1,1,160,512]{3,2,1,0:T(8,128)(2,1)S(1)}, bf16[1,1,160,512]{3,2,1,0:T(8,128)(2,1)}, u32[]{:S(2)}) copy-start(bf16[1,1,160,512]{3,2,1,0:T(8,128)(2,1)} %param.13) | copy-start | bytes 491524
  0.0 16.4 %copy-start.1 = (bf16[1,1,160,512]{3,2,1,0:T(8,128)(2,1)S(1)}, bf16[1,1,160,512]{3,2,1,0:T(8,128)(2,1)}, u32[]{:S(2)}) copy-start(bf16[1,1,160,512]{3,2,1,0:T(8,128)(2,1)} %param.7) | copy-start | bytes 491524
  0.0 13.1 %collective-permute-start.9 = (bf16[128,1536]{1,0:T(8,128)(2,1)}, bf16[128,1536]{1,0:T(8,128)(2,1)S(1)}, u32[]{:S(2)}, u32[]{:S(2)}) collective-permute-start(bf16[128,1536]{1,0:T(8,128)(2,1)} %refs_0_.1), channel_id=1, source_target_pairs={{0,2},{1,3},{2,0},{3,1},{4,6},{5,7},{6,4},{7,5},{8,10},{9,11},{10,... | collective-permute-start | bytes 1179656 | tf_op jit(solution)/shard_map/ppermute | solution.py:19
  3.0 13.4 %collective-permute-start = (bf16[160,512]{1,0:T(8,128)(2,1)}, bf16[160,512]{1,0:T(8,128)(2,1)S(1)}, u32[]{:S(2)}, u32[]{:S(2)}) collective-permute-start(bf16[160,512]{1,0:T(8,128)(2,1)} %bitcast.37), channel_id=1, source_target_pairs={{0,16},{16,0},{1,17},{17,1},{2,18},{18,2},{3,19},{19,3},{4,20},{20... | collective-permute-start | bytes 491528 | tf_op jit(solution)/shard_map/ppermute | solution.py:19
  4.5 15.7 %collective-permute-start.4 = (bf16[128,512]{1,0:T(8,128)(2,1)}, bf16[128,512]{1,0:T(8,128)(2,1)S(1)}, u32[]{:S(2)}, u32[]{:S(2)}) collective-permute-start(bf16[128,512]{1,0:T(8,128)(2,1)} %param.12), channel_id=1, source_target_pairs={{0,2},{1,3},{2,0},{3,1},{4,6},{5,7},{6,4},{7,5},{8,10},{9,11},{10,... | collective-permute-start | bytes 393224 | tf_op jit(solution)/shard_map/ppermute | solution.py:19
  5.0 21.1 %collective-permute-start.10 = (bf16[128,1536]{1,0:T(8,128)(2,1)}, bf16[128,1536]{1,0:T(8,128)(2,1)S(1)}, u32[]{:S(2)}, u32[]{:S(2)}) collective-permute-start(bf16[128,1536]{1,0:T(8,128)(2,1)} %refs_0_.1), channel_id=1, source_target_pairs={{0,1},{1,0},{2,3},{3,2},{4,5},{5,4},{6,7},{7,6},{8,9},{9,8},{10,11... | collective-permute-start | bytes 1179656 | tf_op jit(solution)/shard_map/ppermute | solution.py:19
  13.1 13.1 %collective-permute-start.11 = (bf16[128,1536]{1,0:T(8,128)(2,1)S(1)}, bf16[128,1536]{1,0:T(8,128)(2,1)S(1)}, u32[]{:S(2)}, u32[]{:S(2)}) collective-permute-start(bf16[128,1536]{1,0:T(8,128)(2,1)S(1)} %collective-permute-done.9.refs_1_), channel_id=1, source_target_pairs={{0,1},{1,0},{2,3},{3,2},{4,5},{5,4},{6,7},{7,6},{8,9},{9,8},{10,11... | collective-permute-start | bytes 1179656 | tf_op jit(solution)/shard_map/ppermute | solution.py:19
  13.2 3.2 %copy-start.3 = (f32[9,512]{1,0:T(8,128)S(1)}, f32[9,512]{1,0:T(8,128)}, u32[]{:S(2)}) copy-start(f32[9,512]{1,0:T(8,128)} %taps_ref.3) | copy-start | bytes 55300
  13.2 8.0 %collective-permute-start.2 = (bf16[80,512]{1,0:T(8,128)(2,1)S(1)}, bf16[80,512]{1,0:T(8,128)(2,1)S(1)}, u32[]{:S(2)}, u32[]{:S(2)}) collective-permute-start(bf16[80,512]{1,0:T(8,128)(2,1)S(1)} %dynamic-slice_bitcast_fusion), channel_id=1, source_target_pairs={{0,8},{4,12},{8,0},{12,4},{1,9},{5,13},{9,1},{13,5},{2,10},{6,14},... | collective-permute-start | bytes 245768 | tf_op jit(solution)/shard_map/ppermute | solution.py:19
  16.4 0.7 %copy-start.4 = (s32[160,8]{0,1:T(8,128)S(1)}, s32[160,8]{0,1:T(8,128)}, u32[]{:S(2)}) copy-start(s32[160,8]{0,1:T(8,128)} %param.8) | copy-start | bytes 15364
  17.1 0.7 %copy-start.5 = (f32[512]{0:T(512)S(1)}, f32[512]{0:T(512)}, u32[]{:S(2)}) copy-start(f32[512]{0:T(512)} %param.10) | copy-start | bytes 6148
  17.7 2.4 %copy-start.6 = (bf16[128,512]{1,0:T(8,128)(2,1)S(1)}, bf16[128,512]{1,0:T(8,128)(2,1)}, u32[]{:S(2)}) copy-start(bf16[128,512]{1,0:T(8,128)(2,1)} %param.12) | copy-start | bytes 393220
  18.5 4.6 %collective-permute-start.6 = (bf16[80,512]{1,0:T(8,128)(2,1)S(1)}, bf16[80,512]{1,0:T(8,128)(2,1)S(1)}, u32[]{:S(2)}, u32[]{:S(2)}) collective-permute-start(bf16[80,512]{1,0:T(8,128)(2,1)S(1)} %conv_near.1.own_ref), channel_id=1, source_target_pairs={{0,4},{4,0},{8,12},{12,8},{1,5},{5,1},{9,13},{13,9},{2,6},{6,2},{1... | collective-permute-start | bytes 245768 | tf_op jit(solution)/shard_map/ppermute | solution.py:19
  20.2 8.1 %copy-start.2 = (bf16[128,1536]{1,0:T(8,128)(2,1)S(1)}, bf16[128,1536]{1,0:T(8,128)(2,1)}, u32[]{:S(2)}) copy-start(bf16[128,1536]{1,0:T(8,128)(2,1)} %refs_0_.1) | copy-start | bytes 1179652
  20.2 13.7 %collective-permute-start.5 = (bf16[128,512]{1,0:T(8,128)(2,1)S(1)}, bf16[128,512]{1,0:T(8,128)(2,1)S(1)}, u32[]{:S(2)}, u32[]{:S(2)}) collective-permute-start(bf16[128,512]{1,0:T(8,128)(2,1)S(1)} %broadcast_select_fusion.refs_4_), channel_id=1, source_target_pairs={{0,1},{1,0},{2,3},{3,2},{4,5},{5,4},{6,7},{7,6},{8,9},{9,8},{10,11... | collective-permute-start | bytes 393224 | tf_op jit(solution)/shard_map/ppermute | solution.py:19
  21.2 9.8 %collective-permute-start.7 = (bf16[80,512]{1,0:T(8,128)(2,1)S(1)}, bf16[80,512]{1,0:T(8,128)(2,1)S(1)}, u32[]{:S(2)}, u32[]{:S(2)}) collective-permute-start(bf16[80,512]{1,0:T(8,128)(2,1)S(1)} %conv_far.1), channel_id=1, source_target_pairs={{0,8},{4,12},{8,0},{12,4},{1,9},{5,13},{9,1},{13,5},{2,10},{6,14},... | collective-permute-start | bytes 245768 | tf_op jit(solution)/shard_map/ppermute | solution.py:19
  23.1 7.9 %collective-permute-start.8 = (bf16[80,512]{1,0:T(8,128)(2,1)S(1)}, bf16[80,512]{1,0:T(8,128)(2,1)S(1)}, u32[]{:S(2)}, u32[]{:S(2)}) collective-permute-start(bf16[80,512]{1,0:T(8,128)(2,1)S(1)} %conv_far.1), channel_id=1, source_target_pairs={{0,12},{4,8},{8,4},{12,0},{1,13},{5,9},{9,5},{13,1},{2,14},{6,10},... | collective-permute-start | bytes 245768 | tf_op jit(solution)/shard_map/ppermute | solution.py:19
  26.2 6.1 %collective-permute-start.3 = (bf16[80,512]{1,0:T(8,128)(2,1)S(1)}, bf16[80,512]{1,0:T(8,128)(2,1)S(1)}, u32[]{:S(2)}, u32[]{:S(2)}) collective-permute-start(bf16[80,512]{1,0:T(8,128)(2,1)S(1)} %collective-permute-done.2.refs_2_), channel_id=1, source_target_pairs={{0,4},{4,0},{8,12},{12,8},{1,5},{5,1},{9,13},{13,9},{2,6},{6,2},{1... | collective-permute-start | bytes 245768 | tf_op jit(solution)/shard_map/ppermute | solution.py:19
  26.3 7.6 %collective-permute-start.1 = (bf16[80,512]{1,0:T(8,128)(2,1)S(1)}, bf16[80,512]{1,0:T(8,128)(2,1)S(1)}, u32[]{:S(2)}, u32[]{:S(2)}) collective-permute-start(bf16[80,512]{1,0:T(8,128)(2,1)S(1)} %dynamic-slice_bitcast_fusion.1.refs_0_), channel_id=1, source_target_pairs={{0,4},{4,0},{8,12},{12,8},{1,5},{5,1},{9,13},{13,9},{2,6},{6,2},{1... | collective-permute-start | bytes 245768 | tf_op jit(solution)/shard_map/ppermute | solution.py:19
  35.6 1.6 %collective-permute-start.16 = (bf16[2,2,2,128,128]{4,3,2,1,0:T(8,128)(2,1)S(1)}, bf16[2,2,2,128,128]{4,3,2,1,0:T(8,128)(2,1)S(1)}, u32[]{:S(2)}, u32[]{:S(2)}) collective-permute-start(bf16[2,2,2,128,128]{4,3,2,1,0:T(8,128)(2,1)S(1)} %get-tuple-element.26), channel_id=1, source_target_pairs={{0,1},{1,0},{2,3},{3,2},{4,5},{5,4},{6,7},{7,6},{8,9},{9,8},{10,11... | collective-permute-start | bytes 786440 | tf_op jit(solution)/shard_map/ppermute | solution.py:19
  35.7 2.9 %collective-permute-start.12 = (bf16[2,2,2,128,128]{4,3,2,1,0:T(8,128)(2,1)S(1)}, bf16[2,2,2,128,128]{4,3,2,1,0:T(8,128)(2,1)S(1)}, u32[]{:S(2)}, u32[]{:S(2)}) collective-permute-start(bf16[2,2,2,128,128]{4,3,2,1,0:T(8,128)(2,1)S(1)} %get-tuple-element.24), channel_id=1, source_target_pairs={{0,1},{1,0},{2,3},{3,2},{4,5},{5,4},{6,7},{7,6},{8,9},{9,8},{10,11... | collective-permute-start | bytes 786440 | tf_op jit(solution)/shard_map/ppermute | solution.py:19
  37.3 5.5 %collective-permute-start.17 = (bf16[2,2,128,128]{3,2,1,0:T(8,128)(2,1)S(1)}, bf16[2,2,128,128]{3,2,1,0:T(8,128)(2,1)S(1)}, u32[]{:S(2)}, u32[]{:S(2)}) collective-permute-start(bf16[2,2,128,128]{3,2,1,0:T(8,128)(2,1)S(1)} %fusion.1), channel_id=1, source_target_pairs={{0,17},{1,16},{2,19},{3,18},{16,1},{17,0},{18,3},{19,2},{4,21},{5,... | collective-permute-start | bytes 393224 | tf_op jit(solution)/shard_map/ppermute | solution.py:27
  38.7 5.8 %collective-permute-start.13 = (bf16[2,2,128,128]{3,2,1,0:T(8,128)(2,1)S(1)}, bf16[2,2,128,128]{3,2,1,0:T(8,128)(2,1)S(1)}, u32[]{:S(2)}, u32[]{:S(2)}) collective-permute-start(bf16[2,2,128,128]{3,2,1,0:T(8,128)(2,1)S(1)} %fusion), channel_id=1, source_target_pairs={{0,3},{1,2},{2,1},{3,0},{4,7},{5,6},{6,5},{7,4},{8,11},{9,10},{10,... | collective-permute-start | bytes 393224 | tf_op jit(solution)/shard_map/ppermute | solution.py:19
  42.9 3.8 %collective-permute-start.18 = (bf16[2,128,128]{2,1,0:T(8,128)(2,1)S(1)}, bf16[2,128,128]{2,1,0:T(8,128)(2,1)S(1)}, u32[]{:S(2)}, u32[]{:S(2)}) collective-permute-start(bf16[2,128,128]{2,1,0:T(8,128)(2,1)S(1)} %fusion.3), channel_id=1, source_target_pairs={{0,3},{1,2},{2,1},{3,0},{4,7},{5,6},{6,5},{7,4},{8,11},{9,10},{10,... | collective-permute-start | bytes 196616 | tf_op jit(solution)/shard_map/ppermute | solution.py:19
  44.5 4.2 %collective-permute-start.14 = (bf16[2,128,128]{2,1,0:T(8,128)(2,1)S(1)}, bf16[2,128,128]{2,1,0:T(8,128)(2,1)S(1)}, u32[]{:S(2)}, u32[]{:S(2)}) collective-permute-start(bf16[2,128,128]{2,1,0:T(8,128)(2,1)S(1)} %fusion.2), channel_id=1, source_target_pairs={{0,17},{1,16},{2,19},{3,18},{16,1},{17,0},{18,3},{19,2},{4,21},{5,... | collective-permute-start | bytes 196616 | tf_op jit(solution)/shard_map/ppermute | solution.py:27
  46.8 4.6 %collective-permute-start.19 = (bf16[128,128]{1,0:T(8,128)(2,1)S(1)}, bf16[128,128]{1,0:T(8,128)(2,1)S(1)}, u32[]{:S(2)}, u32[]{:S(2)}) collective-permute-start(bf16[128,128]{1,0:T(8,128)(2,1)S(1)} %fusion.5), channel_id=1, source_target_pairs={{0,9},{1,8},{2,11},{3,10},{4,13},{5,12},{6,15},{7,14},{8,1},{9,0},... | collective-permute-start | bytes 98312 | tf_op jit(solution)/shard_map/ppermute | solution.py:27
  48.8 5.0 %collective-permute-start.15 = (bf16[128,128]{1,0:T(8,128)(2,1)S(1)}, bf16[128,128]{1,0:T(8,128)(2,1)S(1)}, u32[]{:S(2)}, u32[]{:S(2)}) collective-permute-start(bf16[128,128]{1,0:T(8,128)(2,1)S(1)} %fusion.4), channel_id=1, source_target_pairs={{0,9},{1,8},{2,11},{3,10},{4,13},{5,12},{6,15},{7,14},{8,1},{9,0},... | collective-permute-start | bytes 98312 | tf_op jit(solution)/shard_map/ppermute | solution.py:27
  53.9 3.5 %collective-permute-start.20 = (bf16[2,64,128]{2,1,0:T(8,128)(2,1)S(1)}, bf16[2,64,128]{2,1,0:T(8,128)(2,1)S(1)}, u32[]{:S(2)}, u32[]{:S(2)}) collective-permute-start(bf16[2,64,128]{2,1,0:T(8,128)(2,1)S(1)} %pad_maximum_fusion), channel_id=1, source_target_pairs={{0,5},{1,4},{2,7},{3,6},{4,1},{5,0},{6,3},{7,2},{8,13},{9,12},{10,... | collective-permute-start | bytes 98312 | tf_op jit(solution)/shard_map/ppermute | solution.py:27

commit v10 on v9

--- a/solution.py
+++ b/solution.py
@@ -41,7 +41,7 @@
         copy.start()
 
 
-def conv_kernel(far, near_ref, own_ref, band_ref, taps_ref, gain_ref, out_ref, turned_ref):
+def conv_kernel(far, near_ref, own_ref, band_ref, taps_ref, out_ref, turned_ref):
     y, _, zp, _, _, _ = place()
     pixels, _ = own_ref.shape
     half = pixels // 2
@@ -67,7 +67,7 @@
         spatial = spatial + taps_ref[k + 1 : k + 2, :] * gathered[k * half : (k + 1) * half]
     hidden = (own + spatial).astype(jnp.bfloat16).astype(jnp.float32)
     inverse = lax.rsqrt(jnp.mean(hidden * hidden, axis=-1, keepdims=True) + 1e-05)
-    out_ref[...] = (hidden * inverse * gain_ref[...]).astype(jnp.bfloat16)
+    out_ref[...] = (hidden * inverse * taps_ref[neighbours + 1 :, :]).astype(jnp.bfloat16)
 
 
 def head_sums(products, width):
@@ -250,12 +250,14 @@
                     ref[(*places[path], rows_at)] = piece.astype(ref.dtype)
 
 
-def join_kernel(first_ref, second_ref, got_ref, out_ref):
+def join_kernel(first_ref, second_ref, got_first_ref, got_second_ref, out_ref):
     y, _, zp, zh, _, _ = place()
-    paths, rows, _ = got_ref.shape
+    rows, _ = got_first_ref.shape
+    got_refs = (got_first_ref, got_second_ref)
+    paths = len(got_refs)
     is_out = (y == 1) & (zp == 1)
     for path, total_ref in enumerate((first_ref, second_ref)):
-        got = got_ref[path].astype(jnp.float32)
+        got = got_refs[path][...].astype(jnp.float32)
         for side in range(2):
             mine = total_ref[side * rows : (side + 1) * rows, :]
             joined = jnp.where(is_out | (zh == side), mine, got)
@@ -278,16 +280,18 @@
     halves = cotangent[0, 0].reshape(2, half, channels)
     up_2 = swap(pick(halves, 1 - zp), "tm", 2)
 
+    scales = jnp.concatenate([conv_taps, norm_gain.reshape(1, channels)], axis=0)
+
     def conv(far):
         return pl.pallas_call(
             functools.partial(conv_kernel, far),
             out_shape=piece,
-            in_specs=[in_vmem] * 5,
+            in_specs=[in_vmem] * 4,
             out_specs=in_vmem,
             scratch_shapes=[pltpu.VMEM((pixels, neighbours.shape[1]), jnp.int32)],
             compiler_params=pltpu.CompilerParams(vmem_limit_bytes=16 << 20),
             name="conv_far" if far else "conv_near",
-        )(neighbours.T, own, band, conv_taps, norm_gain.reshape(1, channels))
+        )(neighbours.T, own, band, scales)
 
     n_other = conv(True)
     row_3 = swap(n_other, "tm", 3)
@@ -362,16 +366,18 @@
     for path in range(2):
         got = hop(narrow(pick(paths[path], 1 - zp)), "tm", 2, CROSSED[2])
         paths[path] = pick(paths[path], zp) + got.astype(jnp.float32)
-    far = jnp.stack([narrow(pick(total.reshape(2, block, 128), 1 - zh)) for total in paths])
-    got = hop(far, "tm", 1, CROSSED[3])
+    got = [
+        hop(narrow(pick(total.reshape(2, block, 128), 1 - zh)), "tm", 1, CROSSED[3])
+        for total in paths
+    ]
     out = pl.pallas_call(
         join_kernel,
         out_shape=jax.ShapeDtypeStruct((block * channels // 128, 128), jnp.float32),
-        in_specs=[in_vmem] * 3,
+        in_specs=[in_vmem] * 4,
         out_specs=in_vmem,
         compiler_params=pltpu.CompilerParams(vmem_limit_bytes=4 << 20),
         name="join",
-    )(*paths, got)
+    )(*paths, *got)
     return out.reshape(-1)
 
 

time: 58.2 us -> 55.4 us (0.952)
  waiting for transfers between devices: 27.4 us -> 21.7 us
  starting transfers between devices: 23.2 us -> 26.1 us
  other arithmetic: 0.23 us -> 1 us
  local copies, waits for them, and re-layouts: 1.55 us -> 0.84 us
    ppermute x16, waiting for transfers between devices: 15.4 us -> 10.8 us  [swap(): lax.ppermute(values, axis, [(i, i ^ mask) for i in range(lax.axis_size(ax...]
    ppermute x16, starting transfers between devices: 19.7 us -> 21.7 us  [swap(): lax.ppermute(values, axis, [(i, i ^ mask) for i in range(lax.axis_size(ax...]
    ppermute x5 -> x6, waiting for transfers between devices: 12.1 us -> 11 us  [hop(): return lax.ppermute(values, (axis, 'fsdp'), pairs)]
    ppermute x5 -> x6, starting transfers between devices: 3.54 us -> 4.44 us  [hop(): return lax.ppermute(values, (axis, 'fsdp'), pairs)]
    concatenate x0 -> x1, other arithmetic: none -> 0.77 us  [split_form(): jnp.concatenate([conv_taps, norm_gain.reshape(1, channels)], axis=0)]
    unnamed x14 -> x12, local copies, waits for them, and re-layouts: 1.39 us -> 0.68 us
  transfers between devices with their start and end apart: 21 -> 22, of which waited for: 13 -> 13; matrix products, arithmetic and copies ran while one was open for 1% -> 2% of each run, Pallas kernels for 5% -> 5%
where the time goes in v10:
time: 55.4 us; the launch traced here: 55.2 us
  starting transfers between devices  26.1 us (47%)
  waiting for transfers between devices  21.7 us (39%)
  Pallas kernels  5.3 us (10%)
  other arithmetic  1 us (2%)
  local copies, waits for them, and re-layouts  0.84 us (2%)
    ppermute x16, starting transfers between devices, swap(): lax.ppermute(values, axis, [(i, i ^ mask) for i in range(lax.axis_size(ax...  21.7 us
    ppermute x6, waiting for transfers between devices, hop(): return lax.ppermute(values, (axis, 'fsdp'), pairs)  11 us
    ppermute x16, waiting for transfers between devices, swap(): lax.ppermute(values, axis, [(i, i ^ mask) for i in range(lax.axis_size(ax...  10.8 us
    ppermute x6, starting transfers between devices, hop(): return lax.ppermute(values, (axis, 'fsdp'), pairs)  4.44 us
    pallas_call x1, Pallas kernels, split_form(): pl.pallas_call(backward_kernel, out_shape=(*(jax.ShapeDtypeStruct((2, 2,...  1.67 us
    pallas_call x2, Pallas kernels, conv(): pl.pallas_call(functools.partial(conv_kernel, far), out_shape=piece, in_s...  1.53 us
  transfers between devices with their start and end apart: 22, of which 13 were waited for; matrix products, arithmetic and copies ran while one was open for 2% of the time, Pallas kernels for 5%

profile of v10, /device:TPU:0, one launch (start us, length us, event | category | flops | bytes accessed | tf_op | source)
XLA Modules:
  0.0 55.2 jit_solution(3809177573166528433)
XLA Ops:
  0.0 3.0 %collective-permute-start.9 = (bf16[128,1536]{1,0:T(8,128)(2,1)}, bf16[128,1536]{1,0:T(8,128)(2,1)S(1)}, u32[]{:S(2)}, u32[]{:S(2)}) collective-permute-start(bf16[128,1536]{1,0:T(8,128)(2,1)} %refs_0_.1), channel_id=1, source_target_pairs={{0,2},{1,3},{2,0},{3,1},{4,6},{5,7},{6,4},{7,5},{8,10},{9,11},{10,... | collective-permute-start | bytes 1179656 | tf_op jit(solution)/shard_map/ppermute | solution.py:19
  3.0 1.5 %collective-permute-start = (bf16[160,512]{1,0:T(8,128)(2,1)}, bf16[160,512]{1,0:T(8,128)(2,1)S(1)}, u32[]{:S(2)}, u32[]{:S(2)}) collective-permute-start(bf16[160,512]{1,0:T(8,128)(2,1)} %bitcast.41), channel_id=1, source_target_pairs={{0,16},{16,0},{1,17},{17,1},{2,18},{18,2},{3,19},{19,3},{4,20},{20... | collective-permute-start | bytes 491528 | tf_op jit(solution)/shard_map/ppermute | solution.py:19
  5.0 2.7 %collective-permute-start.2 = (bf16[80,512]{1,0:T(8,128)(2,1)S(1)}, bf16[80,512]{1,0:T(8,128)(2,1)S(1)}, u32[]{:S(2)}, u32[]{:S(2)}) collective-permute-start(bf16[80,512]{1,0:T(8,128)(2,1)S(1)} %dynamic-slice_bitcast_fusion), channel_id=1, source_target_pairs={{0,8},{4,12},{8,0},{12,4},{1,9},{5,13},{9,1},{13,5},{2,10},{6,14},... | collective-permute-start | bytes 245768 | tf_op jit(solution)/shard_map/ppermute | solution.py:19
  7.7 5.4 %collective-permute-done.9.refs_1_ = bf16[128,1536]{1,0:T(8,128)(2,1)S(1)} collective-permute-done((bf16[128,1536]{1,0:T(8,128)(2,1)}, bf16[128,1536]{1,0:T(8,128)(2,1)S(1)}, u32[]{:S(2)}, u32[]{:S(2)}) %collective-permute-start.9) | collective-permute-done | bytes 393248 | tf_op jit(solution)/shard_map/ppermute | solution.py:19
  13.2 0.8 %pad_maximum_fusion.taps_ref = f32[10,512]{1,0:T(8,128)S(1)} fusion(f32[1,512]{1,0:T(1,128)S(1)} %bitcast.48, f32[9,512]{1,0:T(8,128)} %param.9), kind=kLoop, calls=%fused_computation.23 | loop fusion | flops 5120 | bytes 40960 | tf_op jit(solution)/shard_map/concatenate | solution.py:283
  14.0 0.7 %copy-done.3 = s32[160,8]{0,1:T(8,128)S(1)} copy-done((s32[160,8]{0,1:T(8,128)S(1)}, s32[160,8]{0,1:T(8,128)}, u32[]{:S(2)}) %copy-start.3) | copy-done | bytes 5144
  14.6 0.8 %conv_near.1.own_ref = bf16[80,512]{1,0:T(8,128)(2,1)S(1)} custom-call(s32[8,160]{1,0:T(8,128)S(1)} %bitcast.46, bf16[160,512]{1,0:T(8,128)(2,1)S(1)} %bitcast.42, bf16[160,512]{1,0:T(8,128)(2,1)S(1)} %collective-permute-done.band_ref, f32[10,512]{1,0:T(8,128)S(1)} %pad_maximum_fusion.taps_ref), custom_call_target="tpu_custom_call" | custom-call | tf_op jit(solution)/shard_map/conv_near/pallas_call | solution.py:286
  15.4 2.2 %collective-permute-start.6 = (bf16[80,512]{1,0:T(8,128)(2,1)S(1)}, bf16[80,512]{1,0:T(8,128)(2,1)S(1)}, u32[]{:S(2)}, u32[]{:S(2)}) collective-permute-start(bf16[80,512]{1,0:T(8,128)(2,1)S(1)} %conv_near.1.own_ref), channel_id=1, source_target_pairs={{0,4},{4,0},{8,12},{12,8},{1,5},{5,1},{9,13},{13,9},{2,6},{6,2},{1... | collective-permute-start | bytes 245768 | tf_op jit(solution)/shard_map/ppermute | solution.py:19
  17.9 0.8 %conv_far.1 = bf16[80,512]{1,0:T(8,128)(2,1)S(1)} custom-call(s32[8,160]{1,0:T(8,128)S(1)} %bitcast.47, bf16[160,512]{1,0:T(8,128)(2,1)S(1)} %bitcast.43, bf16[160,512]{1,0:T(8,128)(2,1)S(1)} %collective-permute-done.band_ref, f32[10,512]{1,0:T(8,128)S(1)} %pad_maximum_fusion.taps_ref), custom_call_target="tpu_custom_call" | custom-call | tf_op jit(solution)/shard_map/conv_far/pallas_call | solution.py:286
  18.7 2.6 %collective-permute-start.7 = (bf16[80,512]{1,0:T(8,128)(2,1)S(1)}, bf16[80,512]{1,0:T(8,128)(2,1)S(1)}, u32[]{:S(2)}, u32[]{:S(2)}) collective-permute-start(bf16[80,512]{1,0:T(8,128)(2,1)S(1)} %conv_far.1), channel_id=1, source_target_pairs={{0,8},{4,12},{8,0},{12,4},{1,9},{5,13},{9,1},{13,5},{2,10},{6,14},... | collective-permute-start | bytes 245768 | tf_op jit(solution)/shard_map/ppermute | solution.py:19
  21.3 3.1 %collective-permute-start.8 = (bf16[80,512]{1,0:T(8,128)(2,1)S(1)}, bf16[80,512]{1,0:T(8,128)(2,1)S(1)}, u32[]{:S(2)}, u32[]{:S(2)}) collective-permute-start(bf16[80,512]{1,0:T(8,128)(2,1)S(1)} %conv_far.1), channel_id=1, source_target_pairs={{0,12},{4,8},{8,4},{12,0},{1,13},{5,9},{9,5},{13,1},{2,14},{6,10},... | collective-permute-start | bytes 245768 | tf_op jit(solution)/shard_map/ppermute | solution.py:19
  24.6 2.0 %collective-permute-start.1 = (bf16[80,512]{1,0:T(8,128)(2,1)S(1)}, bf16[80,512]{1,0:T(8,128)(2,1)S(1)}, u32[]{:S(2)}, u32[]{:S(2)}) collective-permute-start(bf16[80,512]{1,0:T(8,128)(2,1)S(1)} %dynamic-slice_bitcast_fusion.1.refs_0_), channel_id=1, source_target_pairs={{0,4},{4,0},{8,12},{12,8},{1,5},{5,1},{9,13},{13,9},{2,6},{6,2},{1... | collective-permute-start | bytes 245768 | tf_op jit(solution)/shard_map/ppermute | solution.py:19
  27.0 0.6 %collective-permute-done.7.row_2_ref = bf16[80,512]{1,0:T(8,128)(2,1)S(1)} collective-permute-done((bf16[80,512]{1,0:T(8,128)(2,1)S(1)}, bf16[80,512]{1,0:T(8,128)(2,1)S(1)}, u32[]{:S(2)}, u32[]{:S(2)}) %collective-permute-start.7) | collective-permute-done | bytes 81952 | tf_op jit(solution)/shard_map/ppermute | solution.py:19
  27.7 0.8 %collective-permute-done.8.row_3_ref = bf16[80,512]{1,0:T(8,128)(2,1)S(1)} collective-permute-done((bf16[80,512]{1,0:T(8,128)(2,1)S(1)}, bf16[80,512]{1,0:T(8,128)(2,1)S(1)}, u32[]{:S(2)}, u32[]{:S(2)}) %collective-permute-start.8) | collective-permute-done | bytes 81952 | tf_op jit(solution)/shard_map/ppermute | solution.py:19
  28.5 1.0 %forward.1 = (bf16[320,768]{1,0:T(8,128)(2,1)S(1)}, bf16[10,80,256]{2,1,0:T(8,128)(2,1)S(1)}, bf16[320,256]{1,0:T(8,128)(2,1)S(1)}, bf16[4,80,512]{2,1,0:T(8,128)(2,1)S(1)}) custom-call(bf16[80,512]{1,0:T(8,128)(2,1)S(1)} %conv_near.1.own_ref, bf16[80,512]{1,0:T(8,128)(2,1)S(1)} %collective-permute-done.6.row_1_ref, ...), custom_call_target="tpu_custom_call" | custom-call | tf_op jit(solution)/shard_map/forward/pallas_call | solution.py:322
  30.0 1.3 %collective-permute-done.1.refs_1_ = bf16[80,512]{1,0:T(8,128)(2,1)S(1)} collective-permute-done((bf16[80,512]{1,0:T(8,128)(2,1)S(1)}, bf16[80,512]{1,0:T(8,128)(2,1)S(1)}, u32[]{:S(2)}, u32[]{:S(2)}) %collective-permute-start.1) | collective-permute-done | bytes 81952 | tf_op jit(solution)/shard_map/ppermute | solution.py:19
  31.4 1.7 %backward.1 = (f32[2,2,2,128,128]{4,3,2,1,0:T(8,128)S(1)}, f32[2,2,2,128,128]{4,3,2,1,0:T(8,128)S(1)}, bf16[2,2,2,128,128]{4,3,2,1,0:T(8,128)(2,1)S(1)}, bf16[2,2,2,128,128]{4,3,2,1,0:T(8,128)(2,1)S(1)}) custom-call(bf16[80,512]{1,0:T(8,128)(2,1)S(1)} %dynamic-slice_bitcast_fusion.1.refs_0_, bf16[80,512]{1,0:T(8,128)(2,1)S(1)} %collective-permute-done.1.refs_1_, ...), custom_call_target="tpu_custom_call" | custom-call | tf_op jit(solution)/shard_map/backward/pallas_call | solution.py:335
  33.6 1.0 %collective-permute-done.16 = bf16[2,2,2,128,128]{4,3,2,1,0:T(8,128)(2,1)S(1)} collective-permute-done((bf16[2,2,2,128,128]{4,3,2,1,0:T(8,128)(2,1)S(1)}, bf16[2,2,2,128,128]{4,3,2,1,0:T(8,128)(2,1)S(1)}, u32[]{:S(2)}, u32[]{:S(2)}) %collective-permute-start.16) | collective-permute-done | bytes 262176 | tf_op jit(solution)/shard_map/ppermute | solution.py:19
  34.7 1.3 %collective-permute-start.17 = (bf16[2,2,128,128]{3,2,1,0:T(8,128)(2,1)S(1)}, bf16[2,2,128,128]{3,2,1,0:T(8,128)(2,1)S(1)}, u32[]{:S(2)}, u32[]{:S(2)}) collective-permute-start(bf16[2,2,128,128]{3,2,1,0:T(8,128)(2,1)S(1)} %fusion.1), channel_id=1, source_target_pairs={{0,17},{1,16},{2,19},{3,18},{16,1},{17,0},{18,3},{19,2},{4,21},{5,... | collective-permute-start | bytes 393224 | tf_op jit(solution)/shard_map/ppermute | solution.py:27
  36.2 1.5 %collective-permute-start.13 = (bf16[2,2,128,128]{3,2,1,0:T(8,128)(2,1)S(1)}, bf16[2,2,128,128]{3,2,1,0:T(8,128)(2,1)S(1)}, u32[]{:S(2)}, u32[]{:S(2)}) collective-permute-start(bf16[2,2,128,128]{3,2,1,0:T(8,128)(2,1)S(1)} %fusion), channel_id=1, source_target_pairs={{0,3},{1,2},{2,1},{3,0},{4,7},{5,6},{6,5},{7,4},{8,11},{9,10},{10,... | collective-permute-start | bytes 393224 | tf_op jit(solution)/shard_map/ppermute | solution.py:19
  37.7 2.6 %collective-permute-done.17 = bf16[2,2,128,128]{3,2,1,0:T(8,128)(2,1)S(1)} collective-permute-done((bf16[2,2,128,128]{3,2,1,0:T(8,128)(2,1)S(1)}, bf16[2,2,128,128]{3,2,1,0:T(8,128)(2,1)S(1)}, u32[]{:S(2)}, u32[]{:S(2)}) %collective-permute-start.17) | collective-permute-done | bytes 131104 | tf_op jit(solution)/shard_map/ppermute | solution.py:27
  40.3 1.6 %collective-permute-start.18 = (bf16[2,128,128]{2,1,0:T(8,128)(2,1)S(1)}, bf16[2,128,128]{2,1,0:T(8,128)(2,1)S(1)}, u32[]{:S(2)}, u32[]{:S(2)}) collective-permute-start(bf16[2,128,128]{2,1,0:T(8,128)(2,1)S(1)} %fusion.3), channel_id=1, source_target_pairs={{0,3},{1,2},{2,1},{3,0},{4,7},{5,6},{6,5},{7,4},{8,11},{9,10},{10,... | collective-permute-start | bytes 196616 | tf_op jit(solution)/shard_map/ppermute | solution.py:19
  42.0 1.3 %collective-permute-start.14 = (bf16[2,128,128]{2,1,0:T(8,128)(2,1)S(1)}, bf16[2,128,128]{2,1,0:T(8,128)(2,1)S(1)}, u32[]{:S(2)}, u32[]{:S(2)}) collective-permute-start(bf16[2,128,128]{2,1,0:T(8,128)(2,1)S(1)} %fusion.2), channel_id=1, source_target_pairs={{0,17},{1,16},{2,19},{3,18},{16,1},{17,0},{18,3},{19,2},{4,21},{5,... | collective-permute-start | bytes 196616 | tf_op jit(solution)/shard_map/ppermute | solution.py:27
  43.2 0.9 %collective-permute-done.18 = bf16[2,128,128]{2,1,0:T(8,128)(2,1)S(1)} collective-permute-done((bf16[2,128,128]{2,1,0:T(8,128)(2,1)S(1)}, bf16[2,128,128]{2,1,0:T(8,128)(2,1)S(1)}, u32[]{:S(2)}, u32[]{:S(2)}) %collective-permute-start.18) | collective-permute-done | bytes 65568 | tf_op jit(solution)/shard_map/ppermute | solution.py:19
  44.2 0.9 %collective-permute-start.19 = (bf16[128,128]{1,0:T(8,128)(2,1)S(1)}, bf16[128,128]{1,0:T(8,128)(2,1)S(1)}, u32[]{:S(2)}, u32[]{:S(2)}) collective-permute-start(bf16[128,128]{1,0:T(8,128)(2,1)S(1)} %fusion.5), channel_id=1, source_target_pairs={{0,9},{1,8},{2,11},{3,10},{4,13},{5,12},{6,15},{7,14},{8,1},{9,0},... | collective-permute-start | bytes 98312 | tf_op jit(solution)/shard_map/ppermute | solution.py:27
  45.1 1.1 %collective-permute-done.14 = bf16[2,128,128]{2,1,0:T(8,128)(2,1)S(1)} collective-permute-done((bf16[2,128,128]{2,1,0:T(8,128)(2,1)S(1)}, bf16[2,128,128]{2,1,0:T(8,128)(2,1)S(1)}, u32[]{:S(2)}, u32[]{:S(2)}) %collective-permute-start.14) | collective-permute-done | bytes 65568 | tf_op jit(solution)/shard_map/ppermute | solution.py:27
  46.2 0.8 %collective-permute-start.15 = (bf16[128,128]{1,0:T(8,128)(2,1)S(1)}, bf16[128,128]{1,0:T(8,128)(2,1)S(1)}, u32[]{:S(2)}, u32[]{:S(2)}) collective-permute-start(bf16[128,128]{1,0:T(8,128)(2,1)S(1)} %fusion.4), channel_id=1, source_target_pairs={{0,9},{1,8},{2,11},{3,10},{4,13},{5,12},{6,15},{7,14},{8,1},{9,0},... | collective-permute-start | bytes 98312 | tf_op jit(solution)/shard_map/ppermute | solution.py:27
  47.0 2.3 %collective-permute-done.19 = bf16[128,128]{1,0:T(8,128)(2,1)S(1)} collective-permute-done((bf16[128,128]{1,0:T(8,128)(2,1)S(1)}, bf16[128,128]{1,0:T(8,128)(2,1)S(1)}, u32[]{:S(2)}, u32[]{:S(2)}) %collective-permute-start.19) | collective-permute-done | bytes 32800 | tf_op jit(solution)/shard_map/ppermute | solution.py:27
  49.4 1.9 %collective-permute-done.15 = bf16[128,128]{1,0:T(8,128)(2,1)S(1)} collective-permute-done((bf16[128,128]{1,0:T(8,128)(2,1)S(1)}, bf16[128,128]{1,0:T(8,128)(2,1)S(1)}, u32[]{:S(2)}, u32[]{:S(2)}) %collective-permute-start.15) | collective-permute-done | bytes 32800 | tf_op jit(solution)/shard_map/ppermute | solution.py:27
  51.4 1.2 %collective-permute-done.21.got_second_ref = bf16[64,128]{1,0:T(8,128)(2,1)S(1)} collective-permute-done((bf16[64,128]{1,0:T(8,128)(2,1)S(1)}, bf16[64,128]{1,0:T(8,128)(2,1)S(1)}, u32[]{:S(2)}, u32[]{:S(2)}) %collective-permute-start.21) | collective-permute-done | bytes 16416 | tf_op jit(solution)/shard_map/ppermute | solution.py:27
  52.6 2.0 %collective-permute-done.20.got_first_ref = bf16[64,128]{1,0:T(8,128)(2,1)S(1)} collective-permute-done((bf16[64,128]{1,0:T(8,128)(2,1)S(1)}, bf16[64,128]{1,0:T(8,128)(2,1)S(1)}, u32[]{:S(2)}, u32[]{:S(2)}) %collective-permute-start.20) | collective-permute-done | bytes 16416 | tf_op jit(solution)/shard_map/ppermute | solution.py:27
  54.6 0.7 %join.1 = f32[256,128]{1,0:T(8,128)} custom-call(f32[128,128]{1,0:T(8,128)S(1)} %bitcast_add_fusion.5.first_ref, f32[128,128]{1,0:T(8,128)S(1)} %bitcast_add_fusion.4.second_ref, bf16[64,128]{1,0:T(8,128)(2,1)S(1)} %collective-permute-done.20.got_first_ref, bf16[64,128]{1,0:T(8,128)(2,1)S(1)} %collective-permute-done.21.got_second_ref), custom_call_target="tpu_custom_call" | custom-call | tf_op jit(solution)/shard_map/join/pallas_call | solution.py:373
  (50 shorter events, 3.1 us)
Async XLA Ops:
  0.0 5.0 %copy-start = (bf16[1,1,160,512]{3,2,1,0:T(8,128)(2,1)S(1)}, bf16[1,1,160,512]{3,2,1,0:T(8,128)(2,1)}, u32[]{:S(2)}) copy-start(bf16[1,1,160,512]{3,2,1,0:T(8,128)(2,1)} %param.13) | copy-start | bytes 491524
  0.0 13.9 %copy-start.1 = (bf16[1,1,160,512]{3,2,1,0:T(8,128)(2,1)S(1)}, bf16[1,1,160,512]{3,2,1,0:T(8,128)(2,1)}, u32[]{:S(2)}) copy-start(bf16[1,1,160,512]{3,2,1,0:T(8,128)(2,1)} %param.7) | copy-start | bytes 491524
  0.0 13.1 %collective-permute-start.9 = (bf16[128,1536]{1,0:T(8,128)(2,1)}, bf16[128,1536]{1,0:T(8,128)(2,1)S(1)}, u32[]{:S(2)}, u32[]{:S(2)}) collective-permute-start(bf16[128,1536]{1,0:T(8,128)(2,1)} %refs_0_.1), channel_id=1, source_target_pairs={{0,2},{1,3},{2,0},{3,1},{4,6},{5,7},{6,4},{7,5},{8,10},{9,11},{10,... | collective-permute-start | bytes 1179656 | tf_op jit(solution)/shard_map/ppermute | solution.py:19
  3.0 21.5 %collective-permute-start.10 = (bf16[128,1536]{1,0:T(8,128)(2,1)}, bf16[128,1536]{1,0:T(8,128)(2,1)S(1)}, u32[]{:S(2)}, u32[]{:S(2)}) collective-permute-start(bf16[128,1536]{1,0:T(8,128)(2,1)} %refs_0_.1), channel_id=1, source_target_pairs={{0,1},{1,0},{2,3},{3,2},{4,5},{5,4},{6,7},{7,6},{8,9},{9,8},{10,11... | collective-permute-start | bytes 1179656 | tf_op jit(solution)/shard_map/ppermute | solution.py:19
  3.0 11.0 %collective-permute-start = (bf16[160,512]{1,0:T(8,128)(2,1)}, bf16[160,512]{1,0:T(8,128)(2,1)S(1)}, u32[]{:S(2)}, u32[]{:S(2)}) collective-permute-start(bf16[160,512]{1,0:T(8,128)(2,1)} %bitcast.41), channel_id=1, source_target_pairs={{0,16},{16,0},{1,17},{17,1},{2,18},{18,2},{3,19},{19,3},{4,20},{20... | collective-permute-start | bytes 491528 | tf_op jit(solution)/shard_map/ppermute | solution.py:19
  4.5 13.1 %collective-permute-start.4 = (bf16[128,512]{1,0:T(8,128)(2,1)}, bf16[128,512]{1,0:T(8,128)(2,1)S(1)}, u32[]{:S(2)}, u32[]{:S(2)}) collective-permute-start(bf16[128,512]{1,0:T(8,128)(2,1)} %param.12), channel_id=1, source_target_pairs={{0,2},{1,3},{2,0},{3,1},{4,6},{5,7},{6,4},{7,5},{8,10},{9,11},{10,... | collective-permute-start | bytes 393224 | tf_op jit(solution)/shard_map/ppermute | solution.py:19
  5.0 8.1 %copy-start.5 = (f32[512]{0:T(512)S(1)}, f32[512]{0:T(512)}, u32[]{:S(2)}) copy-start(f32[512]{0:T(512)} %param.10) | copy-start | bytes 6148
  5.0 13.6 %collective-permute-start.2 = (bf16[80,512]{1,0:T(8,128)(2,1)S(1)}, bf16[80,512]{1,0:T(8,128)(2,1)S(1)}, u32[]{:S(2)}, u32[]{:S(2)}) collective-permute-start(bf16[80,512]{1,0:T(8,128)(2,1)S(1)} %dynamic-slice_bitcast_fusion), channel_id=1, source_target_pairs={{0,8},{4,12},{8,0},{12,4},{1,9},{5,13},{9,1},{13,5},{2,10},{6,14},... | collective-permute-start | bytes 245768 | tf_op jit(solution)/shard_map/ppermute | solution.py:19
  13.1 11.4 %collective-permute-start.11 = (bf16[128,1536]{1,0:T(8,128)(2,1)S(1)}, bf16[128,1536]{1,0:T(8,128)(2,1)S(1)}, u32[]{:S(2)}, u32[]{:S(2)}) collective-permute-start(bf16[128,1536]{1,0:T(8,128)(2,1)S(1)} %collective-permute-done.9.refs_1_), channel_id=1, source_target_pairs={{0,1},{1,0},{2,3},{3,2},{4,5},{5,4},{6,7},{7,6},{8,9},{9,8},{10,11... | collective-permute-start | bytes 1179656 | tf_op jit(solution)/shard_map/ppermute | solution.py:19
  13.9 0.7 %copy-start.3 = (s32[160,8]{0,1:T(8,128)S(1)}, s32[160,8]{0,1:T(8,128)}, u32[]{:S(2)}) copy-start(s32[160,8]{0,1:T(8,128)} %param.8) | copy-start | bytes 15364
  14.6 3.0 %copy-start.4 = (bf16[128,512]{1,0:T(8,128)(2,1)S(1)}, bf16[128,512]{1,0:T(8,128)(2,1)}, u32[]{:S(2)}) copy-start(bf16[128,512]{1,0:T(8,128)(2,1)} %param.12) | copy-start | bytes 393220
  15.4 5.9 %collective-permute-start.6 = (bf16[80,512]{1,0:T(8,128)(2,1)S(1)}, bf16[80,512]{1,0:T(8,128)(2,1)S(1)}, u32[]{:S(2)}, u32[]{:S(2)}) collective-permute-start(bf16[80,512]{1,0:T(8,128)(2,1)S(1)} %conv_near.1.own_ref), channel_id=1, source_target_pairs={{0,4},{4,0},{8,12},{12,8},{1,5},{5,1},{9,13},{13,9},{2,6},{6,2},{1... | collective-permute-start | bytes 245768 | tf_op jit(solution)/shard_map/ppermute | solution.py:19
  17.6 9.0 %copy-start.2 = (bf16[128,1536]{1,0:T(8,128)(2,1)S(1)}, bf16[128,1536]{1,0:T(8,128)(2,1)}, u32[]{:S(2)}) copy-start(bf16[128,1536]{1,0:T(8,128)(2,1)} %refs_0_.1) | copy-start | bytes 1179652
  17.6 13.8 %collective-permute-start.5 = (bf16[128,512]{1,0:T(8,128)(2,1)S(1)}, bf16[128,512]{1,0:T(8,128)(2,1)S(1)}, u32[]{:S(2)}, u32[]{:S(2)}) collective-permute-start(bf16[128,512]{1,0:T(8,128)(2,1)S(1)} %broadcast_select_fusion.refs_4_), channel_id=1, source_target_pairs={{0,1},{1,0},{2,3},{3,2},{4,5},{5,4},{6,7},{7,6},{8,9},{9,8},{10,11... | collective-permute-start | bytes 393224 | tf_op jit(solution)/shard_map/ppermute | solution.py:19
  18.7 9.0 %collective-permute-start.7 = (bf16[80,512]{1,0:T(8,128)(2,1)S(1)}, bf16[80,512]{1,0:T(8,128)(2,1)S(1)}, u32[]{:S(2)}, u32[]{:S(2)}) collective-permute-start(bf16[80,512]{1,0:T(8,128)(2,1)S(1)} %conv_far.1), channel_id=1, source_target_pairs={{0,8},{4,12},{8,0},{12,4},{1,9},{5,13},{9,1},{13,5},{2,10},{6,14},... | collective-permute-start | bytes 245768 | tf_op jit(solution)/shard_map/ppermute | solution.py:19
  21.3 7.1 %collective-permute-start.8 = (bf16[80,512]{1,0:T(8,128)(2,1)S(1)}, bf16[80,512]{1,0:T(8,128)(2,1)S(1)}, u32[]{:S(2)}, u32[]{:S(2)}) collective-permute-start(bf16[80,512]{1,0:T(8,128)(2,1)S(1)} %conv_far.1), channel_id=1, source_target_pairs={{0,12},{4,8},{8,4},{12,0},{1,13},{5,9},{9,5},{13,1},{2,14},{6,10},... | collective-permute-start | bytes 245768 | tf_op jit(solution)/shard_map/ppermute | solution.py:19
  24.5 5.6 %collective-permute-start.3 = (bf16[80,512]{1,0:T(8,128)(2,1)S(1)}, bf16[80,512]{1,0:T(8,128)(2,1)S(1)}, u32[]{:S(2)}, u32[]{:S(2)}) collective-permute-start(bf16[80,512]{1,0:T(8,128)(2,1)S(1)} %collective-permute-done.2.refs_2_), channel_id=1, source_target_pairs={{0,4},{4,0},{8,12},{12,8},{1,5},{5,1},{9,13},{13,9},{2,6},{6,2},{1... | collective-permute-start | bytes 245768 | tf_op jit(solution)/shard_map/ppermute | solution.py:19
  24.6 6.8 %collective-permute-start.1 = (bf16[80,512]{1,0:T(8,128)(2,1)S(1)}, bf16[80,512]{1,0:T(8,128)(2,1)S(1)}, u32[]{:S(2)}, u32[]{:S(2)}) collective-permute-start(bf16[80,512]{1,0:T(8,128)(2,1)S(1)} %dynamic-slice_bitcast_fusion.1.refs_0_), channel_id=1, source_target_pairs={{0,4},{4,0},{8,12},{12,8},{1,5},{5,1},{9,13},{13,9},{2,6},{6,2},{1... | collective-permute-start | bytes 245768 | tf_op jit(solution)/shard_map/ppermute | solution.py:19
  33.0 1.6 %collective-permute-start.16 = (bf16[2,2,2,128,128]{4,3,2,1,0:T(8,128)(2,1)S(1)}, bf16[2,2,2,128,128]{4,3,2,1,0:T(8,128)(2,1)S(1)}, u32[]{:S(2)}, u32[]{:S(2)}) collective-permute-start(bf16[2,2,2,128,128]{4,3,2,1,0:T(8,128)(2,1)S(1)} %get-tuple-element.26), channel_id=1, source_target_pairs={{0,1},{1,0},{2,3},{3,2},{4,5},{5,4},{6,7},{7,6},{8,9},{9,8},{10,11... | collective-permute-start | bytes 786440 | tf_op jit(solution)/shard_map/ppermute | solution.py:19
  33.1 2.9 %collective-permute-start.12 = (bf16[2,2,2,128,128]{4,3,2,1,0:T(8,128)(2,1)S(1)}, bf16[2,2,2,128,128]{4,3,2,1,0:T(8,128)(2,1)S(1)}, u32[]{:S(2)}, u32[]{:S(2)}) collective-permute-start(bf16[2,2,2,128,128]{4,3,2,1,0:T(8,128)(2,1)S(1)} %get-tuple-element.24), channel_id=1, source_target_pairs={{0,1},{1,0},{2,3},{3,2},{4,5},{5,4},{6,7},{7,6},{8,9},{9,8},{10,11... | collective-permute-start | bytes 786440 | tf_op jit(solution)/shard_map/ppermute | solution.py:19
  34.7 5.5 %collective-permute-start.17 = (bf16[2,2,128,128]{3,2,1,0:T(8,128)(2,1)S(1)}, bf16[2,2,128,128]{3,2,1,0:T(8,128)(2,1)S(1)}, u32[]{:S(2)}, u32[]{:S(2)}) collective-permute-start(bf16[2,2,128,128]{3,2,1,0:T(8,128)(2,1)S(1)} %fusion.1), channel_id=1, source_target_pairs={{0,17},{1,16},{2,19},{3,18},{16,1},{17,0},{18,3},{19,2},{4,21},{5,... | collective-permute-start | bytes 393224 | tf_op jit(solution)/shard_map/ppermute | solution.py:27
  36.2 5.8 %collective-permute-start.13 = (bf16[2,2,128,128]{3,2,1,0:T(8,128)(2,1)S(1)}, bf16[2,2,128,128]{3,2,1,0:T(8,128)(2,1)S(1)}, u32[]{:S(2)}, u32[]{:S(2)}) collective-permute-start(bf16[2,2,128,128]{3,2,1,0:T(8,128)(2,1)S(1)} %fusion), channel_id=1, source_target_pairs={{0,3},{1,2},{2,1},{3,0},{4,7},{5,6},{6,5},{7,4},{8,11},{9,10},{10,... | collective-permute-start | bytes 393224 | tf_op jit(solution)/shard_map/ppermute | solution.py:19
  40.3 3.8 %collective-permute-start.18 = (bf16[2,128,128]{2,1,0:T(8,128)(2,1)S(1)}, bf16[2,128,128]{2,1,0:T(8,128)(2,1)S(1)}, u32[]{:S(2)}, u32[]{:S(2)}) collective-permute-start(bf16[2,128,128]{2,1,0:T(8,128)(2,1)S(1)} %fusion.3), channel_id=1, source_target_pairs={{0,3},{1,2},{2,1},{3,0},{4,7},{5,6},{6,5},{7,4},{8,11},{9,10},{10,... | collective-permute-start | bytes 196616 | tf_op jit(solution)/shard_map/ppermute | solution.py:19
  42.0 4.2 %collective-permute-start.14 = (bf16[2,128,128]{2,1,0:T(8,128)(2,1)S(1)}, bf16[2,128,128]{2,1,0:T(8,128)(2,1)S(1)}, u32[]{:S(2)}, u32[]{:S(2)}) collective-permute-start(bf16[2,128,128]{2,1,0:T(8,128)(2,1)S(1)} %fusion.2), channel_id=1, source_target_pairs={{0,17},{1,16},{2,19},{3,18},{16,1},{17,0},{18,3},{19,2},{4,21},{5,... | collective-permute-start | bytes 196616 | tf_op jit(solution)/shard_map/ppermute | solution.py:27
  44.2 5.1 %collective-permute-start.19 = (bf16[128,128]{1,0:T(8,128)(2,1)S(1)}, bf16[128,128]{1,0:T(8,128)(2,1)S(1)}, u32[]{:S(2)}, u32[]{:S(2)}) collective-permute-start(bf16[128,128]{1,0:T(8,128)(2,1)S(1)} %fusion.5), channel_id=1, source_target_pairs={{0,9},{1,8},{2,11},{3,10},{4,13},{5,12},{6,15},{7,14},{8,1},{9,0},... | collective-permute-start | bytes 98312 | tf_op jit(solution)/shard_map/ppermute | solution.py:27
  46.2 5.1 %collective-permute-start.15 = (bf16[128,128]{1,0:T(8,128)(2,1)S(1)}, bf16[128,128]{1,0:T(8,128)(2,1)S(1)}, u32[]{:S(2)}, u32[]{:S(2)}) collective-permute-start(bf16[128,128]{1,0:T(8,128)(2,1)S(1)} %fusion.4), channel_id=1, source_target_pairs={{0,9},{1,8},{2,11},{3,10},{4,13},{5,12},{6,15},{7,14},{8,1},{9,0},... | collective-permute-start | bytes 98312 | tf_op jit(solution)/shard_map/ppermute | solution.py:27
  49.3 3.2 %collective-permute-start.21 = (bf16[64,128]{1,0:T(8,128)(2,1)S(1)}, bf16[64,128]{1,0:T(8,128)(2,1)S(1)}, u32[]{:S(2)}, u32[]{:S(2)}) collective-permute-start(bf16[64,128]{1,0:T(8,128)(2,1)S(1)} %fusion.7), channel_id=1, source_target_pairs={{0,5},{1,4},{2,7},{3,6},{4,1},{5,0},{6,3},{7,2},{8,13},{9,12},{10,... | collective-permute-start | bytes 49160 | tf_op jit(solution)/shard_map/ppermute | solution.py:27
  51.3 3.2 %collective-permute-start.20 = (bf16[64,128]{1,0:T(8,128)(2,1)S(1)}, bf16[64,128]{1,0:T(8,128)(2,1)S(1)}, u32[]{:S(2)}, u32[]{:S(2)}) collective-permute-start(bf16[64,128]{1,0:T(8,128)(2,1)S(1)} %fusion.6), channel_id=1, source_target_pairs={{0,5},{1,4},{2,7},{3,6},{4,1},{5,0},{6,3},{7,2},{8,13},{9,12},{10,... | collective-permute-start | bytes 49160 | tf_op jit(solution)/shard_map/ppermute | solution.py:27
